TPU v7x, 32 devices: a whole 2x2x4 slice. The times are simulated.
32 devices in a mesh: dp: 8 (over y, x, core), mp: 4 (over z).
Axes of the slice: x: 2, y: 2, z: 4, core: 2. Of those that a mesh axis runs over, the one named last changes fastest.
Arguments:
- latents: float32 [3, 8192, 1024], P(None, ('dp', 'mp')), may hold values from -6 to 6
- group_ids: int32 [3, 8, 1024], P(None, 'dp'), may hold values from 0 to 15, never falling along the last dimension, each value on 1 to 128 neighbouring positions
- pad_mask: int32 [3, 8, 1024], P(None, 'dp'), may hold values 0 or 1
- w_qkv: bfloat16 [3, 1024, 1024], P(None, 'dp', 'mp'), may hold values from -0.1875 to 0.1875
- w_out: bfloat16 [1024, 1024], P('dp', 'mp'), may hold values from -0.5 to 0.5
- w_up: bfloat16 [1024, 4096], P('dp', 'mp'), may hold values from -0.1875 to 0.1875
- w_down: bfloat16 [1024, 4096], P('dp', 'mp'), may hold values from -0.09375 to 0.09375
- norm_gain: bfloat16 [2, 1024], P(None, 'dp'), may hold values from 0.099609375 to 1.8984375
- norm_bias: bfloat16 [2, 1024], P(None, 'dp'), may hold values from -3 to 3
- out_grad: float32 [3, 8192, 1024], P(None, ('dp', 'mp')), may hold values from -6 to 6
Outputs:
- latents_out: float32 [3, 8192, 1024], P(None, ('dp', 'mp'))
- latents_grad: float32 [3, 8192, 1024], P(None, ('dp', 'mp'))
- grad_qkv: float32 [3, 1024, 1024], P(None, 'dp', 'mp')
- grad_out: float32 [1024, 1024], P('dp', 'mp')
- grad_up: float32 [1024, 4096], P('dp', 'mp')
- grad_down: float32 [1024, 4096], P('dp', 'mp')
- grad_gain: float32 [2, 1024], P(None, 'dp')
- grad_bias: float32 [2, 1024], P(None, 'dp')
Inputs may be any that keep to these rules, and one draw needn't show every extreme that they name: `group_ids`: group numbers along one clip never fall; each group of a clip holds 1 to 128 latents and one holds exactly 128.
All inputs are finite; a program needn't handle non-finite values. No bound on the sum of `pad_mask` on one device may be relied on, other than what follows from the above.
Results may differ from a plain program's by a relative error of at most 0.0095.
Values may be sent and summed in bfloat16 or wider, within the bound.
No kernel may reach another device: no remote copies, remote signals or barrier semaphores. Data moves between devices by JAX's collectives and lax.ppermute only.
A program may use at most 192 MiB of HBM per device.

v0:
```python
import jax
import jax.numpy as jnp
from jax import lax
from jax.sharding import PartitionSpec as P

HEAD_DIM = 128


epsilon = 1e-05


def norm_rows(values, scaling, offset):
    row_mean = jnp.mean(values, axis=-1, keepdims=True)
    centred = values - row_mean
    row_var = jnp.mean(centred * centred, axis=-1, keepdims=True)
    return centred * lax.rsqrt(row_var + epsilon) * scaling + offset


def spread_rows(rows_local):
    return lax.all_gather(rows_local, "mp", axis=0, tiled=True)


def settle_rows(partial_rows):
    return lax.psum_scatter(partial_rows, "mp", scatter_dimension=0, tiled=True)


def block_mask(group_row, live_row, first_row, block_rows):
    positions = jnp.arange(group_row.shape[0], dtype=jnp.int32)
    query_positions = first_row + jnp.arange(block_rows, dtype=jnp.int32)
    query_groups = lax.dynamic_slice_in_dim(group_row, first_row, block_rows)
    same_group = query_groups[:, None] == group_row[None, :]
    return same_group & (
        (live_row[None, :] == 1) | (query_positions[:, None] == positions[None, :])
    )


def block_scores(query_block, keys, allowed, factor):
    scores = (
        jnp.einsum("qhd,khd->hqk", query_block, keys, preferred_element_type=jnp.float32) * factor
    )
    return jnp.where(allowed[None], scores, -1e30)


def attend_forward(queries, keys, values, group_row, live_row, block_rows, factor):
    seq_len = keys.shape[0]
    block_count = seq_len // block_rows

    def one_block(block_index):
        first_row = block_index * block_rows
        query_block = lax.dynamic_slice_in_dim(queries, first_row, block_rows, 0)
        scores = block_scores(
            query_block, keys, block_mask(group_row, live_row, first_row, block_rows), factor
        )
        row_peak = jnp.max(scores, axis=-1, keepdims=True)
        weights = jnp.exp(scores - row_peak)
        totals = jnp.sum(weights, axis=-1, keepdims=True)
        probabilities = (weights / totals).astype(jnp.bfloat16)
        mixture = jnp.einsum(
            "hqk,khd->qhd", probabilities, values, preferred_element_type=jnp.float32
        )
        return (mixture, (row_peak + jnp.log(totals))[..., 0])

    mixture, log_totals = lax.map(one_block, jnp.arange(block_count, dtype=jnp.int32))
    return (mixture.reshape(seq_len, mixture.shape[2], mixture.shape[3]), log_totals)


def attend_backward(
    queries, keys, values, grad_mix, log_totals, group_row, live_row, block_rows, factor
):
    seq_len = keys.shape[0]
    block_count = seq_len // block_rows

    def one_block(carry, block_index):
        grad_keys, grad_values = carry
        first_row = block_index * block_rows
        query_block = lax.dynamic_slice_in_dim(queries, first_row, block_rows, 0)
        grad_block = lax.dynamic_slice_in_dim(grad_mix, first_row, block_rows, 0)
        scores = block_scores(
            query_block, keys, block_mask(group_row, live_row, first_row, block_rows), factor
        )
        probabilities = jnp.exp(scores - log_totals[block_index][:, :, None])
        grad_probs = jnp.einsum(
            "qhd,khd->hqk", grad_block, values, preferred_element_type=jnp.float32
        )
        weighted = jnp.sum(probabilities * grad_probs, axis=-1, keepdims=True)
        grad_scores = (probabilities * (grad_probs - weighted)).astype(jnp.bfloat16)
        grad_query = (
            jnp.einsum("hqk,khd->qhd", grad_scores, keys, preferred_element_type=jnp.float32)
            * factor
        )
        grad_keys = (
            grad_keys
            + jnp.einsum(
                "hqk,qhd->khd", grad_scores, query_block, preferred_element_type=jnp.float32
            )
            * factor
        )
        grad_values = grad_values + jnp.einsum(
            "hqk,qhd->khd",
            probabilities.astype(jnp.bfloat16),
            grad_block,
            preferred_element_type=jnp.float32,
        )
        return ((grad_keys, grad_values), grad_query)

    zeros_kv = jnp.zeros(keys.shape, jnp.float32)
    (grad_keys, grad_values), grad_query = lax.scan(
        one_block, (zeros_kv, zeros_kv), jnp.arange(block_count, dtype=jnp.int32)
    )
    return (grad_query.reshape(keys.shape), grad_keys, grad_values)


def forward_pass(latent_rows, weights, groups, masks, block_rows, factor):
    qkv_rows, out_rows, up_rows, down_rows, gains, offsets = weights
    gains_full = gains.astype(jnp.float32)
    offsets_full = offsets.astype(jnp.float32)
    seq_count = groups.shape[0]
    seq_len = groups.shape[1]
    inputs_a = spread_rows(
        norm_rows(latent_rows, gains_full[0], offsets_full[0]).astype(jnp.bfloat16)
    )
    projected = jnp.einsum(
        "rd,tde->tre", inputs_a, qkv_rows, preferred_element_type=jnp.float32
    ).astype(jnp.bfloat16)
    local_heads = projected.shape[2] // HEAD_DIM
    shaped = projected.reshape(3, seq_count, seq_len, local_heads, HEAD_DIM)
    mixture, log_totals = lax.map(
        lambda element: attend_forward(
            element[0], element[1], element[2], element[3], element[4], block_rows, factor
        ),
        (shaped[0], shaped[1], shaped[2], groups, masks),
    )
    attended = mixture.reshape(seq_count * seq_len, local_heads * HEAD_DIM).astype(jnp.bfloat16)
    resid = latent_rows + settle_rows(
        jnp.einsum("rk,dk->rd", attended, out_rows, preferred_element_type=jnp.float32)
    )
    inputs_c = spread_rows(norm_rows(resid, gains_full[1], offsets_full[1]).astype(jnp.bfloat16))
    upward = jnp.dot(inputs_c, up_rows, preferred_element_type=jnp.float32)
    hidden = jax.nn.gelu(upward).astype(jnp.bfloat16)
    output = resid + settle_rows(
        jnp.einsum("rf,df->rd", hidden, down_rows, preferred_element_type=jnp.float32)
    )
    saved = (inputs_a, shaped, log_totals, attended, resid, inputs_c, upward, hidden)
    return (output, saved)


def backward_pass(latent_rows, grad_rows, weights, saved, groups, masks, block_rows, factor):
    qkv_rows, out_rows, up_rows, down_rows, gains, offsets = weights
    gains_full = gains.astype(jnp.float32)
    offsets_full = offsets.astype(jnp.float32)
    inputs_a, shaped, log_totals, attended, resid, inputs_c, upward, hidden = saved
    seq_count = groups.shape[0]
    seq_len = groups.shape[1]
    local_heads = shaped.shape[3]
    grad_z = spread_rows(grad_rows.astype(jnp.bfloat16))
    grad_down = jnp.einsum("rd,rf->df", grad_z, hidden, preferred_element_type=jnp.float32)
    grad_hidden = jnp.einsum("rd,df->rf", grad_z, down_rows, preferred_element_type=jnp.float32)
    gelu_pull = jax.vjp(jax.nn.gelu, upward)[1]
    grad_upward = gelu_pull(grad_hidden)[0].astype(jnp.bfloat16)
    grad_up = jnp.einsum("rd,rf->df", inputs_c, grad_upward, preferred_element_type=jnp.float32)
    grad_norm_two = settle_rows(
        jnp.einsum("rf,df->rd", grad_upward, up_rows, preferred_element_type=jnp.float32)
    )
    norm_pull_two = jax.vjp(norm_rows, resid, gains_full[1], offsets_full[1])[1]
    resid_part, gain_two, offset_two = norm_pull_two(grad_norm_two)
    grad_resid = grad_rows + resid_part
    grad_branch = spread_rows(grad_resid.astype(jnp.bfloat16))
    grad_out = jnp.einsum("rd,rk->dk", grad_branch, attended, preferred_element_type=jnp.float32)
    grad_attended = jnp.einsum(
        "rd,dk->rk", grad_branch, out_rows, preferred_element_type=jnp.float32
    )
    grad_attended = grad_attended.astype(jnp.bfloat16).reshape(
        seq_count, seq_len, local_heads, HEAD_DIM
    )
    grad_queries, grad_keys, grad_values = lax.map(
        lambda element: attend_backward(
            element[0],
            element[1],
            element[2],
            element[3],
            element[4],
            element[5],
            element[6],
            block_rows,
            factor,
        ),
        (shaped[0], shaped[1], shaped[2], grad_attended, log_totals, groups, masks),
    )
    grad_projected = (
        jnp.stack([grad_queries, grad_keys, grad_values])
        .reshape(3, seq_count * seq_len, local_heads * HEAD_DIM)
        .astype(jnp.bfloat16)
    )
    grad_qkv = jnp.einsum(
        "rd,tre->tde", inputs_a, grad_projected, preferred_element_type=jnp.float32
    )
    grad_norm_one = settle_rows(
        jnp.einsum("tre,tde->rd", grad_projected, qkv_rows, preferred_element_type=jnp.float32)
    )
    norm_pull_one = jax.vjp(norm_rows, latent_rows, gains_full[0], offsets_full[0])[1]
    rows_part, gain_one, offset_one = norm_pull_one(grad_norm_one)
    grad_latents = grad_resid + rows_part
    grad_gains = jnp.stack([gain_one, gain_two])
    grad_offsets = jnp.stack([offset_one, offset_two])
    return (grad_latents, (grad_qkv, grad_out, grad_up, grad_down, grad_gains, grad_offsets))


def add_trees(first_tree, second_tree):
    if first_tree is None:
        return second_tree
    return tuple((left + right for left, right in zip(first_tree, second_tree)))


def body(latents, group_ids, pad_mask, w_qkv, w_out, w_up, w_down, norm_gain, norm_bias, out_grad):
    micro_count = latents.shape[0]
    seq_len = group_ids.shape[2]
    block_rows = min(512, seq_len)
    factor = HEAD_DIM ** (-0.5)
    outputs = []
    input_grads = []
    totals = None
    for batch_index in range(micro_count):
        latent_rows = latents[batch_index]
        groups = group_ids[batch_index]
        masks = pad_mask[batch_index]
        forward_weights = (
            lax.all_gather(w_qkv, "dp", axis=1, tiled=True),
            lax.all_gather(w_out, "dp", axis=0, tiled=True),
            lax.all_gather(w_up, "dp", axis=0, tiled=True),
            lax.all_gather(w_down, "dp", axis=0, tiled=True),
            lax.all_gather(norm_gain, "dp", axis=1, tiled=True),
            lax.all_gather(norm_bias, "dp", axis=1, tiled=True),
        )
        output, saved = forward_pass(
            latent_rows, forward_weights, groups, masks, block_rows, factor
        )
        outputs.append(output)
        backward_weights = (
            lax.all_gather(w_qkv, "dp", axis=1, tiled=True),
            lax.all_gather(w_out, "dp", axis=0, tiled=True),
            lax.all_gather(w_up, "dp", axis=0, tiled=True),
            lax.all_gather(w_down, "dp", axis=0, tiled=True),
            lax.all_gather(norm_gain, "dp", axis=1, tiled=True),
            lax.all_gather(norm_bias, "dp", axis=1, tiled=True),
        )
        grad_latents, partials = backward_pass(
            latent_rows,
            out_grad[batch_index],
            backward_weights,
            saved,
            groups,
            masks,
            block_rows,
            factor,
        )
        input_grads.append(grad_latents)
        norm_sums = lax.psum((partials[4], partials[5]), "mp")
        shares = (
            lax.psum_scatter(partials[0], "dp", scatter_dimension=1, tiled=True),
            lax.psum_scatter(partials[1], "dp", scatter_dimension=0, tiled=True),
            lax.psum_scatter(partials[2], "dp", scatter_dimension=0, tiled=True),
            lax.psum_scatter(partials[3], "dp", scatter_dimension=0, tiled=True),
            lax.psum_scatter(norm_sums[0], "dp", scatter_dimension=1, tiled=True),
            lax.psum_scatter(norm_sums[1], "dp", scatter_dimension=1, tiled=True),
        )
        totals = add_trees(totals, shares)
    return (
        jnp.stack(outputs),
        jnp.stack(input_grads),
        totals[0],
        totals[1],
        totals[2],
        totals[3],
        totals[4],
        totals[5],
    )


def solution(mesh):
    return jax.shard_map(
        body,
        mesh=mesh,
        in_specs=(
            P(None, ("dp", "mp"), None),
            P(None, "dp", None),
            P(None, "dp", None),
            P(None, "dp", "mp"),
            P("dp", "mp"),
            P("dp", "mp"),
            P("dp", "mp"),
            P(None, "dp"),
            P(None, "dp"),
            P(None, ("dp", "mp"), None),
        ),
        out_specs=(
            P(None, ("dp", "mp"), None),
            P(None, ("dp", "mp"), None),
            P(None, "dp", "mp"),
            P("dp", "mp"),
            P("dp", "mp"),
            P("dp", "mp"),
            P(None, "dp"),
            P(None, "dp"),
        ),
        check_vma=False,
    )
```

profile of v0, /device:TPU:0, one launch (start us, length us, event | category | flops | bytes accessed | tf_op | source)
XLA Modules:
  0.0 1898.9 jit_solution(16451634394889164312)
XLA Ops:
  9.2 10.3 all_gather.36
  19.5 8.6 all_gather.37
  35.2 9.0 all_gather.40
  44.2 43.0 %all-gather.16.cloned.1.call-done = bf16[1024,1024]{1,0:T(8,128)(2,1)} async-done(((bf16[256,1024]{1,0:T(8,128)(2,1)}), bf16[1024,1024]{1,0:T(8,128)(2,1)}) %all-gather.16.cloned.1.call-update) | async-done | bytes 2097168 | tf_op jit(solution)/shard_map/all_gather | solution.py:20
  92.1 12.2 while.141
  108.8 25.2 %all-gather.26.cloned.1.call-done = bf16[1024,1024]{1,0:T(8,128)(2,1)} async-done(((bf16[256,1024]{1,0:T(8,128)(2,1)}), bf16[1024,1024]{1,0:T(8,128)(2,1)}) %all-gather.26.cloned.1.call-update) | async-done | bytes 2097168 | tf_op jit(solution)/shard_map/all_gather | solution.py:20
  139.0 12.1 while.142
  155.8 25.0 %all-gather.30.cloned.1.call-done = bf16[1024,1024]{1,0:T(8,128)(2,1)} async-done(((bf16[256,1024]{1,0:T(8,128)(2,1)}), bf16[1024,1024]{1,0:T(8,128)(2,1)}) %all-gather.30.cloned.1.call-update) | async-done | bytes 2097168 | tf_op jit(solution)/shard_map/all_gather | solution.py:20
  185.7 12.1 while.143
  207.0 51.5 %reduce-scatter.23.cloned.1.call-done = f32[256,1024]{1,0:T(8,128)} async-done(((f32[1024,1024]{1,0:T(8,128)}), f32[256,1024]{1,0:T(8,128)}) %reduce-scatter.23.cloned.1.call-update) | async-done | bytes 1048592 | tf_op jit(solution)/shard_map/reduce_scatter | solution.py:24
  258.4 79.5 %reduce-scatter.27.cloned.1.call-done = f32[256,1024]{1,0:T(8,128)} async-done(((f32[1024,1024]{1,0:T(8,128)}), f32[256,1024]{1,0:T(8,128)}) %reduce-scatter.27.cloned.1.call-update) | async-done | bytes 1048592 | tf_op jit(solution)/shard_map/reduce_scatter | solution.py:24
  338.0 79.6 %reduce-scatter.31.cloned.1.call-done = f32[256,1024]{1,0:T(8,128)} async-done(((f32[1024,1024]{1,0:T(8,128)}), f32[256,1024]{1,0:T(8,128)}) %reduce-scatter.31.cloned.1.call-update) | async-done | bytes 1048592 | tf_op jit(solution)/shard_map/reduce_scatter | solution.py:24
  425.5 40.8 %all-gather.38.cloned.1.call-done = bf16[1024,1024]{1,0:T(8,128)(2,1)} async-done(((bf16[256,1024]{1,0:T(8,128)(2,1)}), bf16[1024,1024]{1,0:T(8,128)(2,1)}) %all-gather.38.cloned.1.call-update) | async-done | bytes 2097168 | tf_op jit(solution)/shard_map/all_gather | solution.py:20
  466.2 28.7 %all-gather.24.cloned.1.call-done = bf16[1024,1024]{1,0:T(8,128)(2,1)} async-done(((bf16[128,1024]{1,0:T(8,128)(2,1)}), bf16[1024,1024]{1,0:T(8,128)(2,1)}) %all-gather.24.cloned.1.call-update) | async-done | bytes 2097168 | tf_op jit(solution)/shard_map/all_gather | solution.py:230
  494.9 6.7 fusion.238
  501.6 23.2 %all-gather.22.cloned.1.call-done = bf16[1024,1024]{1,0:T(8,128)(2,1)} async-done(((bf16[128,1024]{1,0:T(8,128)(2,1)}), bf16[1024,1024]{1,0:T(8,128)(2,1)}) %all-gather.22.cloned.1.call-update) | async-done | bytes 2097168 | tf_op jit(solution)/shard_map/all_gather | solution.py:229
  524.8 47.6 %all-gather.28.cloned.1.call-done = bf16[1024,1024]{1,0:T(8,128)(2,1)} async-done(((bf16[256,1024]{1,0:T(8,128)(2,1)}), bf16[1024,1024]{1,0:T(8,128)(2,1)}) %all-gather.28.cloned.1.call-update) | async-done | bytes 2097168 | tf_op jit(solution)/shard_map/all_gather | solution.py:20
  572.4 10.0 fusion.142
  583.7 4.5 fusion.239
  588.4 30.7 %all-gather.34.cloned.1.call-done = bf16[1024,1024]{1,0:T(8,128)(2,1)} async-done(((bf16[256,1024]{1,0:T(8,128)(2,1)}), bf16[1024,1024]{1,0:T(8,128)(2,1)}) %all-gather.34.cloned.1.call-update) | async-done | bytes 2097168 | tf_op jit(solution)/shard_map/all_gather | solution.py:20
  619.2 5.9 fusion.236
  625.1 41.0 %all-gather.20.cloned.1.call-done = bf16[1024,1024]{1,0:T(8,128)(2,1)} async-done(((bf16[256,1024]{1,0:T(8,128)(2,1)}), bf16[1024,1024]{1,0:T(8,128)(2,1)}) %all-gather.20.cloned.1.call-update) | async-done | bytes 2097168 | tf_op jit(solution)/shard_map/all_gather | solution.py:20
  666.1 10.0 fusion.135
  677.4 4.3 fusion.237
  681.8 7.0 fusion.218
  689.1 23.2 %all-gather.42.cloned.1.call-done = bf16[1024,1024]{1,0:T(8,128)(2,1)} async-done(((bf16[256,1024]{1,0:T(8,128)(2,1)}), bf16[1024,1024]{1,0:T(8,128)(2,1)}) %all-gather.42.cloned.1.call-update) | async-done | bytes 2097168 | tf_op jit(solution)/shard_map/all_gather | solution.py:20
  712.2 5.9 fusion.240
  718.1 40.3 %all-gather.32.cloned.1.call-done = bf16[1024,1024]{1,0:T(8,128)(2,1)} async-done(((bf16[256,1024]{1,0:T(8,128)(2,1)}), bf16[1024,1024]{1,0:T(8,128)(2,1)}) %all-gather.32.cloned.1.call-update) | async-done | bytes 2097168 | tf_op jit(solution)/shard_map/all_gather | solution.py:20
  758.4 10.0 fusion.149
  769.7 4.4 fusion.241
  774.2 6.9 fusion.216
  781.2 6.9 fusion.219
  788.6 47.6 %reduce-scatter.39.cloned.1.call-done = f32[256,1024]{1,0:T(8,128)} async-done(((f32[1024,1024]{1,0:T(8,128)}), f32[256,1024]{1,0:T(8,128)}) %reduce-scatter.39.cloned.1.call-update) | async-done | bytes 1048592 | tf_op jit(solution)/shard_map/reduce_scatter | solution.py:24
  836.2 79.4 %reduce-scatter.35.cloned.1.call-done = f32[256,1024]{1,0:T(8,128)} async-done(((f32[1024,1024]{1,0:T(8,128)}), f32[256,1024]{1,0:T(8,128)}) %reduce-scatter.35.cloned.1.call-update) | async-done | bytes 1048592 | tf_op jit(solution)/shard_map/reduce_scatter | solution.py:24
  918.6 76.6 %reduce-scatter.29.cloned.1.call-done = f32[256,1024]{1,0:T(8,128)} async-done(((f32[1024,1024]{1,0:T(8,128)}), f32[256,1024]{1,0:T(8,128)}) %reduce-scatter.29.cloned.1.call-update) | async-done | bytes 1048592 | tf_op jit(solution)/shard_map/reduce_scatter | solution.py:24
  995.2 79.6 %reduce-scatter.43.cloned.1.call-done = f32[256,1024]{1,0:T(8,128)} async-done(((f32[1024,1024]{1,0:T(8,128)}), f32[256,1024]{1,0:T(8,128)}) %reduce-scatter.43.cloned.1.call-update) | async-done | bytes 1048592 | tf_op jit(solution)/shard_map/reduce_scatter | solution.py:24
  1074.8 79.5 %reduce-scatter.25.cloned.1.call-done = f32[256,1024]{1,0:T(8,128)} async-done(((f32[1024,1024]{1,0:T(8,128)}), f32[256,1024]{1,0:T(8,128)}) %reduce-scatter.25.cloned.1.call-update) | async-done | bytes 1048592 | tf_op jit(solution)/shard_map/reduce_scatter | solution.py:24
  1154.3 4.9 fusion.223
  1159.3 74.6 %reduce-scatter.33.cloned.1.call-done = f32[256,1024]{1,0:T(8,128)} async-done(((f32[1024,1024]{1,0:T(8,128)}), f32[256,1024]{1,0:T(8,128)}) %reduce-scatter.33.cloned.1.call-update) | async-done | bytes 1048592 | tf_op jit(solution)/shard_map/reduce_scatter | solution.py:24
  1240.6 45.2 %all-gather.36.cloned.1.call-done = bf16[1024,1024]{1,0:T(8,128)(2,1)} async-done(((bf16[256,1024]{1,0:T(8,128)(2,1)}), bf16[1024,1024]{1,0:T(8,128)(2,1)}) %all-gather.36.cloned.1.call-update) | async-done | bytes 2097168 | tf_op jit(solution)/shard_map/all_gather | solution.py:20
  1289.2 22.6 %while.144 = (s32[]{:T(128)}, f32[1024,2,128]{0,2,1:T(8,128)S(1)}, f32[1024,2,128]{0,2,1:T(8,128)}, bf16[2,512,2,128]{3,1,2,0:T(8,128)(2,1)}, s32[2]{0:T(128)S(1...) while((s32[]{:T(128)}, f32[1024,2,128]{0,2,1:T(8,128)S(1)}, ...), condition=%wide.region_35.36_spmd.clone, body=%wide.region_33.35_spmd.clone.sunk | while | flops 1361445376 | bytes 53526936 | solution.py:107
  1314.8 5.4 convolution_bitcast_fusion.2
  1320.6 11.6 all-gather.44.cloned.1.call-done
  1336.2 22.6 %while.146 = (s32[]{:T(128)}, f32[1024,2,128]{0,2,1:T(8,128)S(1)}, f32[1024,2,128]{0,2,1:T(8,128)}, bf16[2,512,2,128]{3,1,2,0:T(8,128)(2,1)}, s32[2]{0:T(128)S(1...) while((s32[]{:T(128)}, f32[1024,2,128]{0,2,1:T(8,128)S(1)}, ...), condition=%wide.region_53.54_spmd.clone, body=%wide.region_51.53_spmd.clone.sunk | while | flops 1361445376 | bytes 55624116 | solution.py:107
  1363.0 5.5 convolution_bitcast_fusion
  1368.9 10.4 all-gather.40.cloned.1.call-done
  1383.3 22.6 %while.145 = (s32[]{:T(128)}, f32[1024,2,128]{0,2,1:T(8,128)S(1)}, f32[1024,2,128]{0,2,1:T(8,128)}, bf16[2,512,2,128]{3,1,2,0:T(8,128)(2,1)}, s32[2]{0:T(128)S(1...) while((s32[]{:T(128)}, f32[1024,2,128]{0,2,1:T(8,128)S(1)}, ...), condition=%wide.region_44.45_spmd.clone, body=%wide.region_42.44_spmd.clone.sunk | while | flops 1361445376 | bytes 55624116 | solution.py:107
  1408.5 5.2 convolution_bitcast_fusion.1
  1414.2 5.9 fusion.217
  1423.0 5.2 add_bitcast_fusion
  1438.0 6.2 fusion.243
  1444.3 4.5 fusion.242
  1448.8 8.3 reduce-scatter.37.cloned.1.call-done
  1457.1 79.5 %reduce-scatter.45.cloned.1.call-done = f32[256,1024]{1,0:T(8,128)} async-done(((f32[1024,1024]{1,0:T(8,128)}), f32[256,1024]{1,0:T(8,128)}) %reduce-scatter.45.cloned.1.call-update) | async-done | bytes 1048592 | tf_op jit(solution)/shard_map/reduce_scatter | solution.py:24
  1536.5 79.5 %reduce-scatter.41.cloned.1.call-done = f32[256,1024]{1,0:T(8,128)} async-done(((f32[1024,1024]{1,0:T(8,128)}), f32[256,1024]{1,0:T(8,128)}) %reduce-scatter.41.cloned.1.call-update) | async-done | bytes 1048592 | tf_op jit(solution)/shard_map/reduce_scatter | solution.py:24
  1621.3 9.5 add_add_fusion
  1630.9 40.3 %reduce-scatter.53.cloned.1.call-done = f32[128,1024]{0,1:T(8,128)} async-done(((f32[1024,1024]{0,1:T(8,128)}), f32[128,1024]{0,1:T(8,128)}) %reduce-scatter.53.cloned.1.call-update) | async-done | bytes 524304 | tf_op jit(solution)/shard_map/reduce_scatter | solution.py:262
  1673.3 4.1 pad_maximum_fusion
  1682.7 39.2 %reduce-scatter.47.cloned.1.call-done = f32[3,128,256]{1,2,0:T(8,128)} async-done(((f32[3,1024,256]{1,2,0:T(8,128)}), f32[3,128,256]{1,2,0:T(8,128)}) %reduce-scatter.47.cloned.1.call-update) | async-done | bytes 393232 | tf_op jit(solution)/shard_map/reduce_scatter | solution.py:259
  1730.3 28.7 %reduce-scatter.55.cloned.1.call-done = f32[128,2]{1,0:T(8,128)} async-done(((f32[1024,2]{1,0:T(8,128)}), f32[128,2]{1,0:T(8,128)}) %reduce-scatter.55.cloned.1.call-update) | async-done | bytes 1040
  1759.9 36.7 %reduce-scatter.57.cloned.1.call-done = f32[128,2]{1,0:T(8,128)} async-done(((f32[1024,2]{1,0:T(8,128)}), f32[128,2]{1,0:T(8,128)}) %reduce-scatter.57.cloned.1.call-update) | async-done | bytes 1040
  1797.4 12.3 all-reduce
  1809.7 42.1 %reduce-scatter.51.cloned.1.call-done = f32[128,1024]{1,0:T(8,128)} async-done(((f32[1024,1024]{1,0:T(8,128)}), f32[128,1024]{1,0:T(8,128)}) %reduce-scatter.51.cloned.1.call-update) | async-done | bytes 524304 | tf_op jit(solution)/shard_map/reduce_scatter | solution.py:261
  1851.8 40.0 %reduce-scatter.49.cloned.1.call-done = f32[128,256]{1,0:T(8,128)} async-done(((f32[1024,256]{1,0:T(8,128)}), f32[128,256]{1,0:T(8,128)}) %reduce-scatter.49.cloned.1.call-update) | async-done | bytes 131088 | tf_op jit(solution)/shard_map/reduce_scatter | solution.py:260
  (633 shorter events, 204.4 us)
Async XLA Ops:
  7.2 37.0 %all-gather.18.cloned.1.call-start = ((), (), s32[]{:S(2)}) async-start(), calls=%async_computation.19 | async-start | bytes 1769472 | tf_op jit(solution)/shard_map/all_gather | solution.py:227
  9.1 78.1 %all-gather.16.cloned.1.call-start = ((), (), s32[]{:S(2)}) async-start(), calls=%async_computation.18 | async-start | bytes 2621440 | tf_op jit(solution)/shard_map/all_gather | solution.py:20
  33.8 100.3 %all-gather.26.cloned.1.call-start = ((), (), s32[]{:S(2)}) async-start(), calls=%async_computation.25 | async-start | bytes 2621440 | tf_op jit(solution)/shard_map/all_gather | solution.py:20
  34.5 146.3 %all-gather.30.cloned.1.call-start = ((), (), s32[]{:S(2)}) async-start(), calls=%async_computation.29 | async-start | bytes 2621440 | tf_op jit(solution)/shard_map/all_gather | solution.py:20
  35.1 223.3 %reduce-scatter.23.cloned.1.call-start = ((), (), s32[]{:S(2)}) async-start(), calls=%async_computation.20 | async-start | bytes 5242880 | tf_op jit(solution)/shard_map/reduce_scatter | solution.py:24
  44.2 154.3 %copy-start.35 = (bf16[1024,256]{1,0:T(8,128)(2,1)}, bf16[1024,256]{1,0:T(8,128)(2,1)S(1)}, u32[]{:S(2)}) copy-start(bf16[1024,256]{1,0:T(8,128)(2,1)S(1)} %all_gather.40) | copy-start | bytes 1572868
  108.6 229.4 %reduce-scatter.27.cloned.1.call-start = ((), (), s32[]{:S(2)}) async-start(), calls=%async_computation.26 | async-start | bytes 5242880 | tf_op jit(solution)/shard_map/reduce_scatter | solution.py:24
  155.5 262.1 %reduce-scatter.31.cloned.1.call-start = ((), (), s32[]{:S(2)}) async-start(), calls=%async_computation.30 | async-start | bytes 5242880 | tf_op jit(solution)/shard_map/reduce_scatter | solution.py:24
  202.2 215.3 %copy-start.1 = (f32[3,256,1024]{2,1,0:T(8,128)S(1)}, f32[3,256,1024]{2,1,0:T(8,128)}, u32[]{:S(2)}) copy-start(f32[3,256,1024]{2,1,0:T(8,128)} %param.22) | copy-start | bytes 9437188
  202.2 264.0 %all-gather.38.cloned.1.call-start = ((), (), s32[]{:S(2)}) async-start(), calls=%async_computation.37 | async-start | bytes 2621440 | tf_op jit(solution)/shard_map/all_gather | solution.py:20
  205.6 289.4 %all-gather.24.cloned.1.call-start = ((), (), s32[]{:S(2)}) async-start(), calls=%async_computation.23 | async-start | bytes 2359296 | tf_op jit(solution)/shard_map/all_gather | solution.py:230
  206.3 318.5 %all-gather.22.cloned.1.call-start = ((), (), s32[]{:S(2)}) async-start(), calls=%async_computation.22 | async-start | bytes 2359296 | tf_op jit(solution)/shard_map/all_gather | solution.py:229
  206.9 213.9 %copy-start.83 = (f32[1,1024]{1,0:T(1,128)S(1)}, f32[1,1024]{1,0:T(1,128)}, u32[]{:S(2)}) copy-start(f32[1,1024]{1,0:T(1,128)} %get-tuple-element.1096) | copy-start | bytes 12292
  206.9 213.9 %copy-start.107 = (f32[1,1024]{1,0:T(1,128)S(1)}, f32[1,1024]{1,0:T(1,128)}, u32[]{:S(2)}) copy-start(f32[1,1024]{1,0:T(1,128)} %get-tuple-element.1098) | copy-start | bytes 12292
  206.9 365.5 %all-gather.28.cloned.1.call-start = ((), (), s32[]{:S(2)}) async-start(), calls=%async_computation.27 | async-start | bytes 2621440 | tf_op jit(solution)/shard_map/all_gather | solution.py:20
  422.5 196.7 %all-gather.34.cloned.1.call-start = ((), (), s32[]{:S(2)}) async-start(), calls=%async_computation.33 | async-start | bytes 2621440 | tf_op jit(solution)/shard_map/all_gather | solution.py:20
  423.0 243.0 %all-gather.20.cloned.1.call-start = ((), (), s32[]{:S(2)}) async-start(), calls=%async_computation.21 | async-start | bytes 2621440 | tf_op jit(solution)/shard_map/all_gather | solution.py:20
  423.8 288.5 %all-gather.42.cloned.1.call-start = ((), (), s32[]{:S(2)}) async-start(), calls=%async_computation.41 | async-start | bytes 2621440 | tf_op jit(solution)/shard_map/all_gather | solution.py:20
  424.4 334.1 %all-gather.32.cloned.1.call-start = ((), (), s32[]{:S(2)}) async-start(), calls=%async_computation.31 | async-start | bytes 2621440 | tf_op jit(solution)/shard_map/all_gather | solution.py:20
  424.9 411.2 %reduce-scatter.39.cloned.1.call-start = ((), (), s32[]{:S(2)}) async-start(), calls=%async_computation.38 | async-start | bytes 5242880 | tf_op jit(solution)/shard_map/reduce_scatter | solution.py:24
  524.8 58.9 %copy-start.136 = (bf16[1024,1024]{1,0:T(8,128)(2,1)S(1)}, bf16[1024,1024]{1,0:T(8,128)(2,1)}, u32[]{:S(2)}) copy-start(bf16[1024,1024]{1,0:T(8,128)(2,1)} %all-gather.22.cloned.1.call-done) | copy-start | bytes 6291460
  588.2 327.4 %reduce-scatter.35.cloned.1.call-start = ((), (), s32[]{:S(2)}) async-start(), calls=%async_computation.34 | async-start | bytes 5242880 | tf_op jit(solution)/shard_map/reduce_scatter | solution.py:24
  681.8 313.4 %reduce-scatter.29.cloned.1.call-start = ((), (), s32[]{:S(2)}) async-start(), calls=%async_computation.28 | async-start | bytes 5242880 | tf_op jit(solution)/shard_map/reduce_scatter | solution.py:24
  688.8 385.9 %reduce-scatter.43.cloned.1.call-start = ((), (), s32[]{:S(2)}) async-start(), calls=%async_computation.42 | async-start | bytes 5242880 | tf_op jit(solution)/shard_map/reduce_scatter | solution.py:24
  774.2 380.1 %reduce-scatter.25.cloned.1.call-start = ((), (), s32[]{:S(2)}) async-start(), calls=%async_computation.24 | async-start | bytes 5242880 | tf_op jit(solution)/shard_map/reduce_scatter | solution.py:24
  781.2 452.7 %reduce-scatter.33.cloned.1.call-start = ((), (), s32[]{:S(2)}) async-start(), calls=%async_computation.32 | async-start | bytes 5242880 | tf_op jit(solution)/shard_map/reduce_scatter | solution.py:24
  788.1 127.5 %copy-start.18 = (f32[256,1024]{1,0:T(8,128)S(1)}, f32[256,1024]{1,0:T(8,128)}, u32[]{:S(2)}) copy-start(f32[256,1024]{1,0:T(8,128)} %copy-done.17) | copy-start | bytes 3145732
  788.1 127.5 %copy-start.20 = (f32[256,1024]{1,0:T(8,128)S(1)}, f32[256,1024]{1,0:T(8,128)}, u32[]{:S(2)}) copy-start(f32[256,1024]{1,0:T(8,128)} %copy-done.19) | copy-start | bytes 3145732
  788.1 366.2 %copy-start.16 = (f32[256,1024]{1,0:T(8,128)S(1)}, f32[256,1024]{1,0:T(8,128)}, u32[]{:S(2)}) copy-start(f32[256,1024]{1,0:T(8,128)} %copy-done.15) | copy-start | bytes 3145732
  788.1 497.7 %all-gather.36.cloned.1.call-start = ((), (), s32[]{:S(2)}) async-start(), calls=%async_computation.35 | async-start | bytes 2621440 | tf_op jit(solution)/shard_map/all_gather | solution.py:20
  1159.3 78.4 %copy-start.29 = (f32[256,1024]{1,0:T(8,128)S(1)}, f32[256,1024]{1,0:T(8,128)}, u32[]{:S(2)}) copy-start(f32[256,1024]{1,0:T(8,128)} %get-tuple-element.1023) | copy-start | bytes 3145732
  1159.3 78.4 %copy-start.31 = (f32[256,1024]{1,0:T(8,128)S(1)}, f32[256,1024]{1,0:T(8,128)}, u32[]{:S(2)}) copy-start(f32[256,1024]{1,0:T(8,128)} %get-tuple-element.1089) | copy-start | bytes 3145732
  1159.3 77.8 %copy-start.114 = (f32[256]{0:T(256)}, f32[256]{0:T(256)S(1)}, u32[]{:S(2)}) copy-start(f32[256]{0:T(256)S(1)} %negate_multiply_fusion.3) | copy-start | bytes 3076
  1239.1 50.0 %copy-start.6 = (bf16[1024,2,128]{2,0,1:T(8,128)(2,1)S(1)}, bf16[1024,2,128]{2,0,1:T(8,128)(2,1)}, u32[]{:S(2)}) copy-start(bf16[1024,2,128]{2,0,1:T(8,128)(2,1)} %copy-done.5) | copy-start | bytes 1572868
  1239.1 50.0 %copy-start.12 = (bf16[1024,2,128]{2,0,1:T(8,128)(2,1)S(1)}, bf16[1024,2,128]{2,0,1:T(8,128)(2,1)}, u32[]{:S(2)}) copy-start(bf16[1024,2,128]{2,0,1:T(8,128)(2,1)} %copy-done.11) | copy-start | bytes 1572868
  1239.1 50.0 %copy-start.26 = (bf16[1024,2,128]{2,0,1:T(8,128)(2,1)S(1)}, bf16[1024,2,128]{2,0,1:T(8,128)(2,1)}, u32[]{:S(2)}) copy-start(bf16[1024,2,128]{2,0,1:T(8,128)(2,1)} %copy-done.25) | copy-start | bytes 1572868
  1239.2 50.0 %copy-start.56 = (s32[1024]{0:T(1024)S(1)}, s32[1024]{0:T(1024)}, u32[]{:S(2)}) copy-start(s32[1024]{0:T(1024)} %copy-done.55) | copy-start | bytes 12292
  1239.2 50.0 %copy-start.82 = (s32[1024]{0:T(1024)S(1)}, s32[1024]{0:T(1024)}, u32[]{:S(2)}) copy-start(s32[1024]{0:T(1024)} %copy-done.81) | copy-start | bytes 12292
  1239.2 50.0 %copy-start.85 = (f32[2,2,512]{2,1,0:T(2,128)S(1)}, f32[2,2,512]{2,1,0:T(2,128)}, u32[]{:S(2)}) copy-start(f32[2,2,512]{2,1,0:T(2,128)} %copy-done.84) | copy-start | bytes 24580
  1239.2 92.9 %all-gather.44.cloned.1.call-start = ((), (), s32[]{:S(2)}) async-start(), calls=%async_computation.43 | async-start | bytes 2621440 | tf_op jit(solution)/shard_map/all_gather | solution.py:20
  1239.9 139.3 %all-gather.40.cloned.1.call-start = ((), (), s32[]{:S(2)}) async-start(), calls=%async_computation.39 | async-start | bytes 2621440 | tf_op jit(solution)/shard_map/all_gather | solution.py:20
  1240.5 216.6 %reduce-scatter.37.cloned.1.call-start = ((), (), s32[]{:S(2)}) async-start(), calls=%async_computation.36 | async-start | bytes 5242880 | tf_op jit(solution)/shard_map/reduce_scatter | solution.py:24
  1320.3 216.2 %reduce-scatter.45.cloned.1.call-start = ((), (), s32[]{:S(2)}) async-start(), calls=%async_computation.44 | async-start | bytes 5242880 | tf_op jit(solution)/shard_map/reduce_scatter | solution.py:24
  1368.6 247.5 %reduce-scatter.41.cloned.1.call-start = ((), (), s32[]{:S(2)}) async-start(), calls=%async_computation.40 | async-start | bytes 5242880 | tf_op jit(solution)/shard_map/reduce_scatter | solution.py:24
  1413.7 257.6 %reduce-scatter.53.cloned.1.call-start = ((), (), s32[]{:S(2)}) async-start(), calls=%async_computation.48 | async-start | bytes 4718592 | tf_op jit(solution)/shard_map/reduce_scatter | solution.py:262
  1428.2 293.7 %reduce-scatter.47.cloned.1.call-start = ((), (), s32[]{:S(2)}) async-start(), calls=%async_computation.45 | async-start | bytes 3538944 | tf_op jit(solution)/shard_map/reduce_scatter | solution.py:259
  1438.0 321.0 %reduce-scatter.55.cloned.1.call-start = ((), (), s32[]{:S(2)}) async-start(), calls=%async_computation.49 | async-start | bytes 589824
  1444.2 171.9 %copy-start.2 = (f32[3,256,1024]{2,1,0:T(8,128)S(1)}, f32[3,256,1024]{2,1,0:T(8,128)}, u32[]{:S(2)}) copy-start(f32[3,256,1024]{2,1,0:T(8,128)} %param.22) | copy-start | bytes 9437188
  1444.2 171.9 %copy-start.91 = (f32[1,1024]{1,0:T(1,128)S(1)}, f32[1,1024]{1,0:T(1,128)}, u32[]{:S(2)}) copy-start(f32[1,1024]{1,0:T(1,128)} %copy-done.90) | copy-start | bytes 12292
  1444.2 171.9 %copy-start.94 = (f32[256]{0:T(256)S(1)}, f32[256]{0:T(256)}, u32[]{:S(2)}) copy-start(f32[256]{0:T(256)} %copy-done.93) | copy-start | bytes 3076
  1444.2 171.9 %copy-start.96 = (f32[256]{0:T(256)S(1)}, f32[256]{0:T(256)}, u32[]{:S(2)}) copy-start(f32[256]{0:T(256)} %copy-done.95) | copy-start | bytes 3076
  1444.2 171.9 %copy-start.98 = (f32[256]{0:T(256)S(1)}, f32[256]{0:T(256)}, u32[]{:S(2)}) copy-start(f32[256]{0:T(256)} %copy-done.97) | copy-start | bytes 3076
  1444.3 171.9 %copy-start.102 = (f32[256]{0:T(256)S(1)}, f32[256]{0:T(256)}, u32[]{:S(2)}) copy-start(f32[256]{0:T(256)} %copy-done.101) | copy-start | bytes 3076
  1444.3 171.8 %copy-start.104 = (f32[256]{0:T(256)S(1)}, f32[256]{0:T(256)}, u32[]{:S(2)}) copy-start(f32[256]{0:T(256)} %copy-done.103) | copy-start | bytes 3076
  1444.3 171.8 %copy-start.106 = (f32[256]{0:T(256)S(1)}, f32[256]{0:T(256)}, u32[]{:S(2)}) copy-start(f32[256]{0:T(256)} %copy-done.105) | copy-start | bytes 3076
  1448.8 170.0 %copy-start.100 = (f32[1024]{0:T(1024)S(1)}, f32[1024]{0:T(1024)}, u32[]{:S(2)}) copy-start(f32[1024]{0:T(1024)} %get-tuple-element.1092) | copy-start | bytes 12292
  1448.8 170.0 %copy-start.110 = (f32[1024]{0:T(1024)S(1)}, f32[1024]{0:T(1024)}, u32[]{:S(2)}) copy-start(f32[1024]{0:T(1024)} %get-tuple-element.878) | copy-start | bytes 12292
  1448.8 170.0 %copy-start.111 = (f32[1024]{0:T(1024)S(1)}, f32[1024]{0:T(1024)}, u32[]{:S(2)}) copy-start(f32[1024]{0:T(1024)} %get-tuple-element.1095) | copy-start | bytes 12292
  1448.8 171.2 %copy-start.99 = (f32[1024]{0:T(1024)S(1)}, f32[1024]{0:T(1024)}, u32[]{:S(2)}) copy-start(f32[1024]{0:T(1024)} %get-tuple-element.1090) | copy-start | bytes 12292
  1448.8 171.2 %copy-start.108 = (f32[1024]{0:T(1024)S(1)}, f32[1024]{0:T(1024)}, u32[]{:S(2)}) copy-start(f32[1024]{0:T(1024)} %get-tuple-element.885) | copy-start | bytes 12292
  1448.8 171.2 %copy-start.109 = (f32[1024]{0:T(1024)S(1)}, f32[1024]{0:T(1024)}, u32[]{:S(2)}) copy-start(f32[1024]{0:T(1024)} %get-tuple-element.1093) | copy-start | bytes 12292
  1619.9 176.6 %reduce-scatter.57.cloned.1.call-start = ((), (), s32[]{:S(2)}) async-start(), calls=%async_computation.50 | async-start | bytes 589824
  1621.1 230.8 %reduce-scatter.51.cloned.1.call-start = ((), (), s32[]{:S(2)}) async-start(), calls=%async_computation.47 | async-start | bytes 4718592 | tf_op jit(solution)/shard_map/reduce_scatter | solution.py:261
  1630.9 260.9 %reduce-scatter.49.cloned.1.call-start = ((), (), s32[]{:S(2)}) async-start(), calls=%async_computation.46 | async-start | bytes 1179648 | tf_op jit(solution)/shard_map/reduce_scatter | solution.py:260
  (128 other events, 886.1 us)
Sparse Core Ops, SparseCore 0:
  10.5 28.5 all-gather.17
  41.2 45.9 all-gather.15
  89.3 44.6 all-gather.25
  136.1 44.6 all-gather.29
  182.9 75.4 reduce-scatter.22
  260.7 77.2 reduce-scatter.26
  340.2 77.2 reduce-scatter.30
  419.8 46.4 all-gather.37
  468.3 26.6 all-gather.23
  496.8 27.8 all-gather.21
  526.4 45.9 all-gather.27
  574.5 44.6 all-gather.33
  621.4 44.6 all-gather.19
  667.6 44.6 all-gather.41
  713.7 44.6 all-gather.31
  760.7 75.4 reduce-scatter.38
  838.3 77.2 reduce-scatter.34
  917.9 77.2 reduce-scatter.28
  997.5 77.2 reduce-scatter.42
  1077.0 77.2 reduce-scatter.24
  1156.6 77.2 reduce-scatter.32
  1239.3 46.4 all-gather.35
  1287.5 44.6 all-gather.43
  1334.2 44.9 all-gather.39
  1381.6 75.4 reduce-scatter.36
  1459.2 77.2 reduce-scatter.44
  1538.8 77.2 reduce-scatter.40
  1619.4 51.8 reduce-scatter.52
  1675.6 46.2 reduce-scatter.46
  1724.8 34.1 reduce-scatter.54
  1762.4 34.1 reduce-scatter.56
  1800.5 51.3 reduce-scatter.50
  1855.7 36.0 reduce-scatter.48
where the time goes:
time: 1910 us; the launch traced here: 1900 us
  waiting for transfers between devices  1480 us (77%)
  matrix products  225 us (12%)
  other arithmetic  57.3 us (3%)
  local copies, waits for them, and re-layouts  50.1 us (3%)
  blocking collectives  40.2 us (2%)
  loops' own time  20.7 us (1%)
    reduce_scatter x12, waiting for transfers between devices, settle_rows(): return lax.psum_scatter(partial_rows, 'mp', scatter_dimension=0, tiled=True)  815 us
    all_gather x12, waiting for transfers between devices, spread_rows(): return lax.all_gather(rows_local, 'mp', axis=0, tiled=True)  384 us
    unnamed x35, waiting for transfers between devices  71.6 us
    reduce_scatter x1, waiting for transfers between devices, body(): lax.psum_scatter(partials[2], 'dp', scatter_dimension=0, tiled=True)  42.1 us
    reduce_scatter x1, waiting for transfers between devices, body(): lax.psum_scatter(partials[3], 'dp', scatter_dimension=0, tiled=True)  40.3 us
    reduce_scatter x1, waiting for transfers between devices, body(): lax.psum_scatter(partials[1], 'dp', scatter_dimension=0, tiled=True)  40 us
    reduce_scatter x1, waiting for transfers between devices, body(): lax.psum_scatter(partials[0], 'dp', scatter_dimension=1, tiled=True)  39.2 us
  transfers between devices with their start and end apart: 33, of which 32 were waited for; matrix products, arithmetic and copies ran while one was open for 17% of the time, Pallas kernels for 0%

commit v1 on v0

v1 whole, which is shorter than its diff:
```python
import jax
import jax.numpy as jnp
from jax import lax
from jax.sharding import PartitionSpec as P

HEAD_DIM = 128
HALO = 128
EPSILON = 1e-05
LOW = jnp.bfloat16


def dot(left, right, dims, kind=jnp.float32):
    return lax.dot_general(
        left, right, ((dims[:1], dims[1:]), ((), ())), preferred_element_type=kind
    )


def swap(value, bit, count):
    return lax.ppermute(value, "dp", [(i, i ^ bit) for i in range(count)])


def shift(value, step, count):
    return lax.ppermute(value, "mp", [(i, (i + step) % count) for i in range(count)])


class Plan:
    def __init__(self, mesh):
        self.dp = mesh.shape["dp"]
        self.mp = mesh.shape["mp"]
        bits = [1 << i for i in range(self.dp.bit_length() - 1)]
        core, others = bits[:1], bits[1:]
        self.orders = (others + core, others[::-1] + core)
        self.major = core + others[::-1]
        relative = [0]
        for bit in self.major[::-1]:
            relative = relative + [r ^ bit for r in relative]
        self.relative = relative

    def own(self):
        return lax.axis_index("dp")

    def enter(self, value):
        width = value.shape[-1] // self.dp
        axis = value.ndim - 1
        return jnp.concatenate(
            [
                lax.dynamic_slice_in_dim(value, (self.own() ^ r) * width, width, axis)
                for r in self.relative
            ],
            axis=axis,
        )

    def leave(self, value):
        width = value.shape[-1] // self.dp
        axis = value.ndim - 1
        inverse = {r: p for p, r in enumerate(self.relative)}
        table = jnp.array([inverse[r] for r in range(self.dp)], jnp.int32)
        return jnp.concatenate(
            [
                lax.dynamic_slice_in_dim(value, table[self.own() ^ n] * width, width, axis)
                for n in range(self.dp)
            ],
            axis=axis,
        )

    def gather_rows(self, value, order):
        block = value.shape[0]
        known = [0]
        held = [value]
        for i, bit in enumerate(order):
            if i + 3 < len(order):
                held = [jnp.concatenate([held[0], swap(held[0], bit, self.dp)], axis=0)]
            else:
                held = held + [swap(part, bit, self.dp) for part in held]
            known = known + [r ^ bit for r in known]
        spans = held[0].shape[0] // block

        def piece(r):
            at, inner = divmod(known.index(r), spans)
            return held[at] if spans == 1 else held[at][inner * block : (inner + 1) * block]

        return jnp.concatenate([piece(r) for r in self.relative], axis=0)

    def gather(self, local):
        parts = [local] + [shift(local, -k, self.mp) for k in range(1, self.mp)]
        half = self.mp // 2
        return [
            self.gather_rows(jnp.concatenate(parts[i * half : (i + 1) * half], axis=1), order)
            for i, order in enumerate(self.orders)
        ]

    def scatter_rows(self, produce, order):
        first = order[-1]
        rest = order[:-1][::-1]
        sent = produce(1).astype(LOW)
        kept = produce(0) + swap(sent, first, self.dp).astype(jnp.float32)
        left = [bit for bit in self.major if bit != first]
        for bit in rest:
            place = left.index(bit)
            block = kept.shape[0] >> (place + 1)
            shaped = kept.reshape((1 << place), 2, block, kept.shape[1])
            sent = shaped[:, 1].reshape(-1, kept.shape[1]).astype(LOW)
            kept = shaped[:, 0].reshape(-1, kept.shape[1])
            kept = kept + swap(sent, bit, self.dp).astype(jnp.float32)
            left.remove(bit)
        return kept

    def scatter(self, produces):
        half = self.mp // 2
        blocks = []
        for produce, order in zip(produces, self.orders):
            rows = self.scatter_rows(produce, order)
            width = rows.shape[1] // half
            blocks += [rows[:, i * width : (i + 1) * width] for i in range(half)]
        total = blocks[0]
        for k in range(1, self.mp):
            total = total + shift(blocks[k].astype(LOW), k, self.mp).astype(jnp.float32)
        return total


def statistics(values):
    mean = jnp.mean(values, axis=-1, keepdims=True)
    centred = values - mean
    variance = jnp.mean(centred * centred, axis=-1, keepdims=True)
    return centred, lax.rsqrt(variance + EPSILON)


def norm_rows(values, gain, bias):
    centred, scale = statistics(values)
    return centred * scale * gain + bias


def norm_back(values, gain, grad):
    centred, scale = statistics(values)
    normed = centred * scale
    inner = grad * gain
    first = jnp.mean(inner, axis=-1, keepdims=True)
    second = jnp.mean(inner * normed, axis=-1, keepdims=True)
    return (
        (inner - first - normed * second) * scale,
        jnp.sum(grad * normed, axis=0),
        jnp.sum(grad, axis=0),
    )


def halo(value, count):
    before = lax.ppermute(value[:, -HALO:], "mp", [(i, i + 1) for i in range(count - 1)])
    after = lax.ppermute(value[:, :HALO], "mp", [(i + 1, i) for i in range(count - 1)])
    return jnp.concatenate([before, value, after], axis=1)


def solution(mesh):
    plan = Plan(mesh)

    def body(latents, group_ids, pad_mask, w_qkv, w_out, w_up, w_down, norm_gain, norm_bias, out_grad):
        micro, rows, width = latents.shape
        total = micro * rows
        mp = plan.mp
        factor = HEAD_DIM ** (-0.5)
        small = jnp.concatenate([norm_gain, norm_bias], axis=0).T
        small = plan.gather_rows(small, plan.orders[0]).T.astype(jnp.float32)
        gains, biases = small[:2], small[2:]

        local_qkv = jnp.concatenate([w_qkv[t] for t in range(3)], axis=1)
        qkv = plan.gather(local_qkv)
        out = plan.gather(w_out)
        up = plan.gather(w_up)
        down = plan.gather(w_down)

        entered = plan.enter(latents.reshape(total, width))
        grad_rows = plan.enter(out_grad.reshape(total, width))
        grad_z = grad_rows.astype(LOW)
        inputs_a = norm_rows(entered, gains[0], biases[0]).astype(LOW)
        window = halo(inputs_a.reshape(micro, rows, width), mp)
        span = rows + 2 * HALO
        first = lax.axis_index("mp") * rows - HALO
        pads = ((0, 0), (HALO, HALO))
        groups = lax.dynamic_slice_in_dim(
            jnp.pad(group_ids[:, 0], pads, constant_values=-1), first + HALO, span, 1
        )
        live = lax.dynamic_slice_in_dim(jnp.pad(pad_mask[:, 0], pads), first + HALO, span, 1)
        same = groups[:, :, None] == groups[:, None, :]
        diagonal = jnp.eye(span, dtype=bool)
        allowed = same & ((live[:, None, :] == 1) | diagonal[None])

        def heads(values):
            return values.reshape(micro, span, -1, HEAD_DIM)

        shaped = []
        attended = []
        flat_window = window.reshape(micro * span, width)
        for part in qkv:
            projected = dot(flat_window, part, (1, 0)).astype(LOW)
            projected = projected.reshape(micro, span, mp // 2, 3, -1)
            q, k, v = (heads(projected[:, :, :, t]) for t in range(3))
            scores = jnp.einsum(
                "bqhd,bkhd->bhqk", q, k, preferred_element_type=jnp.float32
            )
            scores = jnp.where(allowed[:, None], scores * factor, -1e30)
            peak = jnp.max(scores, axis=-1, keepdims=True)
            weights = jnp.exp(scores - peak)
            probabilities = weights / jnp.sum(weights, axis=-1, keepdims=True)
            mixture = jnp.einsum(
                "bhqk,bkhd->bqhd",
                probabilities[:, :, HALO : HALO + rows].astype(LOW),
                v,
                preferred_element_type=jnp.float32,
            )
            attended.append(mixture.reshape(total, -1).astype(LOW))
            shaped.append((q, k, v, probabilities))
        resid = entered + sum(dot(a, w, (1, 1)) for a, w in zip(attended, out))
        inputs_c = norm_rows(resid, gains[1], biases[1]).astype(LOW)
        hidden, slopes = [], []
        for part in up:
            upward = dot(inputs_c, part, (1, 0))
            value, pull = jax.vjp(jax.nn.gelu, upward)
            hidden.append(value.astype(LOW))
            slopes.append(pull(jnp.ones_like(upward))[0].astype(LOW))

        def rows_of(values, other):
            half = width // 2
            return lambda which: dot(values[:, which * half : (which + 1) * half], other, (0, 0))

        grad_down = plan.scatter([rows_of(grad_z, h) for h in hidden])
        latents_out = resid + sum(dot(h, w, (1, 1)) for h, w in zip(hidden, down))
        grad_upward = [
            (dot(grad_z, w, (1, 0)) * s.astype(jnp.float32)).astype(LOW)
            for w, s in zip(down, slopes)
        ]
        grad_up = plan.scatter([rows_of(inputs_c, g) for g in grad_upward])
        grad_norm_two = sum(dot(g, w, (1, 1)) for g, w in zip(grad_upward, up))
        part_two, gain_two, bias_two = norm_back(resid, gains[1], grad_norm_two)
        grad_resid = grad_rows + part_two
        grad_branch = grad_resid.astype(LOW)
        grad_out = plan.scatter([rows_of(grad_branch, a) for a in attended])
        branch_window = halo(grad_branch.reshape(micro, rows, width), mp)
        branch_window = branch_window.reshape(micro * span, width)
        grad_projected = []
        for (q, k, v, probabilities), w in zip(shaped, out):
            grad_att = heads(dot(branch_window, w, (1, 0)).astype(LOW))
            grad_probs = jnp.einsum(
                "bqhd,bkhd->bhqk", grad_att, v, preferred_element_type=jnp.float32
            )
            weighted = jnp.sum(probabilities * grad_probs, axis=-1, keepdims=True)
            grad_scores = (probabilities * (grad_probs - weighted)).astype(LOW)
            mine = slice(HALO, HALO + rows)
            grad_q = jnp.einsum(
                "bhqk,bkhd->bqhd", grad_scores[:, :, mine], k, preferred_element_type=jnp.float32
            )
            grad_k = jnp.einsum(
                "bhqk,bqhd->bkhd", grad_scores[:, :, :, mine], q, preferred_element_type=jnp.float32
            )
            grad_v = jnp.einsum(
                "bhqk,bqhd->bkhd",
                probabilities[:, :, :, mine].astype(LOW),
                grad_att,
                preferred_element_type=jnp.float32,
            )
            three = [
                (g * f).astype(LOW).reshape(total, mp // 2, -1)
                for g, f in ((grad_q, factor), (grad_k, factor), (grad_v, 1.0))
            ]
            grad_projected.append(jnp.stack(three, axis=2).reshape(total, -1))
        grad_qkv = plan.scatter([rows_of(inputs_a, g) for g in grad_projected])
        grad_qkv = jnp.stack(jnp.split(grad_qkv, 3, axis=1))
        grad_norm_one = sum(dot(g, w, (1, 1)) for g, w in zip(grad_projected, qkv))
        part_one, gain_one, bias_one = norm_back(entered, gains[0], grad_norm_one)
        latents_grad = grad_resid + part_one
        sums = jnp.stack([gain_one, gain_two, bias_one, bias_two]).T
        for bit in plan.major:
            half = sums.shape[0] // 2
            sums = sums[:half] + swap(sums[half:], bit, plan.dp)
        sums = lax.psum(sums, "mp").T
        shape = latents.shape
        return (
            plan.leave(latents_out).reshape(shape),
            plan.leave(latents_grad).reshape(shape),
            grad_qkv,
            grad_out,
            grad_up,
            grad_down,
            sums[:2],
            sums[2:],
        )

    return jax.shard_map(
        body,
        mesh=mesh,
        in_specs=(
            P(None, ("dp", "mp"), None),
            P(None, "dp", None),
            P(None, "dp", None),
            P(None, "dp", "mp"),
            P("dp", "mp"),
            P("dp", "mp"),
            P("dp", "mp"),
            P(None, "dp"),
            P(None, "dp"),
            P(None, ("dp", "mp"), None),
        ),
        out_specs=(
            P(None, ("dp", "mp"), None),
            P(None, ("dp", "mp"), None),
            P(None, "dp", "mp"),
            P("dp", "mp"),
            P("dp", "mp"),
            P("dp", "mp"),
            P(None, "dp"),
            P(None, "dp"),
        ),
        check_vma=False,
    )
```

time: 1910 us -> 950 us (0.50)
  waiting for transfers between devices: 1480 us -> 326 us
  local copies, waits for them, and re-layouts: 50.1 us -> 240 us
  starting transfers between devices: 4.23 us -> 83.7 us
  blocking collectives: 40.2 us -> 10.5 us
  loops' own time: 20.7 us -> 0 us
    reduce_scatter x16 -> x0, waiting for transfers between devices: 977 us -> none  [the longest x12 815 us: settle_rows(): return lax.psum_scatter(partial_rows, 'mp', scatter_dimension=0, tiled=True)]
    all_gather x15 -> x0, waiting for transfers between devices: 436 us -> none  [the longest x12 384 us: spread_rows(): return lax.all_gather(rows_local, 'mp', axis=0, tiled=True)]
    ppermute x0 -> x118, waiting for transfers between devices: none -> 326 us  [the longest x90 234 us: swap(): return lax.ppermute(value, 'dp', [(i, i ^ bit) for i in range(count)])]
    ppermute x0 -> x118, starting transfers between devices: none -> 83.7 us  [the longest x90 44.7 us: swap(): return lax.ppermute(value, 'dp', [(i, i ^ bit) for i in range(count)])]
    slice x7 -> x31, local copies, waits for them, and re-layouts: 1.56 us -> 84.7 us  [the longest x8 81.3 us: body(): q, k, v = (heads(projected[:, :, :, t]) for t in range(3))]
    dot_general x78 -> x40, matrix products: 225 us -> 151 us  [the longest x32 127 us: dot(): lax.dot_general(left, right, ((dims[:1], dims[1:]), ((), ())), preferred_...]
    unnamed x35 -> x0, waiting for transfers between devices: 71.6 us -> none
    sub x0 -> x4, matrix products: none -> 55.7 us  [the longest x2 32.7 us: body(): grad_scores = (probabilities * (grad_probs - weighted)).astype(LOW)]
  transfers between devices with their start and end apart: 33 -> 118, of which waited for: 32 -> 44; matrix products, arithmetic and copies ran while one was open for 17% -> 48% of each run, Pallas kernels for 0% -> 0%
where the time goes in v1:
time: 950 us; the launch traced here: 937 us
  waiting for transfers between devices  326 us (34%)
  local copies, waits for them, and re-layouts  240 us (25%)
  matrix products  207 us (22%)
  starting transfers between devices  83.7 us (9%)
  other arithmetic  61.5 us (6%)
  blocking collectives  10.5 us (1%)
    ppermute x90, waiting for transfers between devices, swap(): return lax.ppermute(value, 'dp', [(i, i ^ bit) for i in range(count)])  234 us
    dot_general x32, matrix products, dot(): lax.dot_general(left, right, ((dims[:1], dims[1:]), ((), ())), preferred_...  127 us
    slice x8, local copies, waits for them, and re-layouts, body(): q, k, v = (heads(projected[:, :, :, t]) for t in range(3))  81.3 us
    ppermute x24, waiting for transfers between devices, shift(): lax.ppermute(value, 'mp', [(i, (i + step) % count) for i in range(count)])  74.6 us
    unnamed x243, local copies, waits for them, and re-layouts  49.6 us
    ppermute x90, starting transfers between devices, swap(): return lax.ppermute(value, 'dp', [(i, i ^ bit) for i in range(count)])  44.7 us
    sub x2, matrix products, body(): grad_scores = (probabilities * (grad_probs - weighted)).astype(LOW)  32.7 us
    another operation x8, local copies, waits for them, and re-layouts, body(): grad_projected.append(jnp.stack(three, axis=2).reshape(total, -1))  32.1 us
  transfers between devices with their start and end apart: 118, of which 44 were waited for; matrix products, arithmetic and copies ran while one was open for 48% of the time, Pallas kernels for 0%

profile of v1, /device:TPU:0, one launch (start us, length us, event | category | flops | bytes accessed | tf_op | source)
XLA Modules:
  0.0 936.6 jit_solution(1220437611616459340)
XLA Ops:
  86.7 29.9 %collective-permute-done.68 = bf16[128,1024]{1,0:T(8,128)(2,1)S(1)} collective-permute-done((bf16[128,1024]{1,0:T(8,128)(2,1)S(1)}, bf16[128,1024]{1,0:T(8,128)(2,1)S(1)}, u32[]{:S(2)}, u32[]{:S(2)}) %collective-permute-start.68) | collective-permute-done | bytes 262176 | tf_op jit(solution)/shard_map/ppermute | solution.py:23
  116.7 5.5 collective-permute-done.59
  133.1 4.9 collective-permute-done.20
  142.9 6.8 collective-permute-done.10
  153.6 8.1 collective-permute-done.27
  162.8 10.1 %collective-permute-done.70 = bf16[128,2048]{1,0:T(8,128)(2,1)S(1)} collective-permute-done((bf16[128,2048]{1,0:T(8,128)(2,1)S(1)}, bf16[128,2048]{1,0:T(8,128)(2,1)S(1)}, u32[]{:S(2)}, u32[]{:S(2)}) %collective-permute-start.70) | collective-permute-done | bytes 524320 | tf_op jit(solution)/shard_map/ppermute | solution.py:19
  174.1 10.0 %collective-permute-done.61 = bf16[128,2048]{1,0:T(8,128)(2,1)S(1)} collective-permute-done((bf16[128,2048]{1,0:T(8,128)(2,1)S(1)}, bf16[128,2048]{1,0:T(8,128)(2,1)S(1)}, u32[]{:S(2)}, u32[]{:S(2)}) %collective-permute-start.61) | collective-permute-done | bytes 524320 | tf_op jit(solution)/shard_map/ppermute | solution.py:19
  185.4 10.0 %collective-permute-done.44 = bf16[128,2048]{1,0:T(8,128)(2,1)S(1)} collective-permute-done((bf16[128,2048]{1,0:T(8,128)(2,1)S(1)}, bf16[128,2048]{1,0:T(8,128)(2,1)S(1)}, u32[]{:S(2)}, u32[]{:S(2)}) %collective-permute-start.44) | collective-permute-done | bytes 524320 | tf_op jit(solution)/shard_map/ppermute | solution.py:19
  197.5 7.8 collective-permute-done.52
  209.2 8.5 collective-permute-done.12
  220.2 10.4 %collective-permute-done.29 = bf16[128,1536]{1,0:T(8,128)(2,1)S(1)} collective-permute-done((bf16[128,1536]{1,0:T(8,128)(2,1)S(1)}, bf16[128,1536]{1,0:T(8,128)(2,1)S(1)}, u32[]{:S(2)}, u32[]{:S(2)}) %collective-permute-start.29) | collective-permute-done | bytes 393248 | tf_op jit(solution)/shard_map/ppermute | solution.py:19
  233.0 12.2 %collective-permute-done.72 = bf16[128,2048]{1,0:T(8,128)(2,1)} collective-permute-done((bf16[128,2048]{1,0:T(8,128)(2,1)S(1)}, bf16[128,2048]{1,0:T(8,128)(2,1)}, u32[]{:S(2)}, u32[]{:S(2)}) %collective-permute-start.72) | collective-permute-done | bytes 524320 | tf_op jit(solution)/shard_map/ppermute | solution.py:19
  247.7 13.1 %collective-permute-done.63 = bf16[128,2048]{1,0:T(8,128)(2,1)} collective-permute-done((bf16[128,2048]{1,0:T(8,128)(2,1)S(1)}, bf16[128,2048]{1,0:T(8,128)(2,1)}, u32[]{:S(2)}, u32[]{:S(2)}) %collective-permute-start.63) | collective-permute-done | bytes 524320 | tf_op jit(solution)/shard_map/ppermute | solution.py:19
  263.2 13.1 %collective-permute-done.46 = bf16[128,2048]{1,0:T(8,128)(2,1)} collective-permute-done((bf16[128,2048]{1,0:T(8,128)(2,1)S(1)}, bf16[128,2048]{1,0:T(8,128)(2,1)}, u32[]{:S(2)}, u32[]{:S(2)}) %collective-permute-start.46) | collective-permute-done | bytes 524320 | tf_op jit(solution)/shard_map/ppermute | solution.py:19
  281.8 10.9 %collective-permute-done.54 = bf16[128,2048]{1,0:T(8,128)(2,1)} collective-permute-done((bf16[128,2048]{1,0:T(8,128)(2,1)S(1)}, bf16[128,2048]{1,0:T(8,128)(2,1)}, u32[]{:S(2)}, u32[]{:S(2)}) %collective-permute-start.54) | collective-permute-done | bytes 524320 | tf_op jit(solution)/shard_map/ppermute | solution.py:19
  298.2 6.9 convolution_convert_fusion
  306.8 6.8 convolution_convert_fusion.1
  313.6 11.9 %reshape.285 = bf16[3,512,2,3,256]{4,3,2,1,0:T(4,128)(2,1)} reshape(bf16[1536,1536]{1,0:T(8,128)(2,1)} %convolution_convert_fusion.1) | data formatting | bytes 9437184 | tf_op jit(solution)/shard_map/reshape | solution.py:194
  325.5 11.9 %reshape.286 = bf16[3,512,2,3,256]{4,3,2,1,0:T(4,128)(2,1)} reshape(bf16[1536,1536]{1,0:T(8,128)(2,1)} %convolution_convert_fusion) | data formatting | bytes 9437184 | tf_op jit(solution)/shard_map/reshape | solution.py:194
  337.3 15.8 %fusion.207 = (bf16[3,512,2,1,256]{4,3,2,1,0:T(2,128)(2,1)}, bf16[3,512,2,1,256]{4,3,2,1,0:T(2,128)(2,1)}, bf16[3,512,2,1,256]{4,3,2,1,0:T(2,128)(2,1)}) fusion(bf16[3,512,2,3,256]{4,3,2,1,0:T(4,128)(2,1)} %reshape.286), kind=kLoop, calls=%fused_computation.426 | loop fusion | bytes 9437184 | tf_op jit(solution)/shard_map/slice | solution.py:195
  353.2 8.2 copy.49
  361.4 8.2 copy.48
  369.5 8.1 copy.47
  377.7 16.1 %fusion.206 = (bf16[3,512,2,1,256]{4,3,2,1,0:T(2,128)(2,1)}, bf16[3,512,2,1,256]{4,3,2,1,0:T(2,128)(2,1)}, bf16[3,512,2,1,256]{4,3,2,1,0:T(2,128)(2,1)}) fusion(bf16[3,512,2,3,256]{4,3,2,1,0:T(4,128)(2,1)} %reshape.285), kind=kLoop, calls=%fused_computation.425 | loop fusion | bytes 9437184 | tf_op jit(solution)/shard_map/slice | solution.py:195
  393.8 8.2 copy.42
  401.9 8.2 copy.41
  410.1 8.5 copy.40
  418.6 11.5 %fusion.218 = (f32[3,4,512]{2,1,0:T(4,128)S(1)}, f32[3,4,512,512]{2,3,1,0:T(8,128)}) fusion(pred[3,512,512]{1,2,0:T(8,128)(4,1)} %or_and_fusion, bf16[3,512,4,128]{1,3,2,0:T(8,128)(2,1)} %bitcast.354, bf16[3,512,4,128]{1,3,2,0:T(8,128)(2,1)} %bitcast.352), kind=kOutput, calls=%fused_computation.437 | convolution fusion | flops 817889792 | bytes 16539648 | tf_op jit(solution)/shard_map/sub | solution.py:201
  430.1 9.2 fusion.195
  445.0 11.5 %fusion.217 = (f32[3,4,512]{2,1,0:T(4,128)S(1)}, f32[3,4,512,512]{2,3,1,0:T(8,128)}) fusion(pred[3,512,512]{1,2,0:T(8,128)(4,1)} %or_and_fusion, bf16[3,512,4,128]{1,3,2,0:T(8,128)(2,1)} %bitcast.348, bf16[3,512,4,128]{1,3,2,0:T(8,128)(2,1)} %bitcast.346), kind=kOutput, calls=%fused_computation.436 | convolution fusion | flops 817889792 | bytes 16539648 | tf_op jit(solution)/shard_map/sub | solution.py:201
  456.5 9.2 fusion.196
  478.8 6.4 multiply_convert_fusion.5
  486.7 10.7 %multiply_convert_fusion.3 = bf16[768,2048]{1,0:T(8,128)(2,1)S(1)} fusion(bf16[768,1024]{1,0:T(8,128)(2,1)S(1)} %copy-done.4, bf16[1024,2048]{1,0:T(8,128)(2,1)S(1)} %constant_dynamic-update-slice_fusion.78, f32[768,2048]{1,0:T(8,128)} %get-tuple-element.126), kind=kOutput, calls=%fused_computation.37 | convolution fusion | flops 3254255616 | bytes 15204352 | tf_op jit(solution)/shard_map/dot_general | solution.py:13
  498.9 6.4 multiply_convert_fusion.4
  510.5 9.3 multiply_convert_fusion.2
  519.8 5.1 fusion.221
  525.0 7.7 multiply_reduce_fusion.2
  539.9 5.1 fusion.220
  552.1 5.5 add_add_fusion
  558.3 5.4 collective-permute-start.77
  571.2 9.8 %collective-permute-done.77 = bf16[3,128,1024]{2,1,0:T(8,128)(2,1)S(1)} collective-permute-done((bf16[3,128,1024]{2,1,0:T(8,128)(2,1)S(1)}, bf16[3,128,1024]{2,1,0:T(8,128)(2,1)S(1)}, u32[]{:S(2)}, u32[]{:S(2)}) %collective-permute-start.77) | collective-permute-done | bytes 786464 | tf_op jit(solution)/shard_map/ppermute | solution.py:147
  581.4 6.8 collective-permute-done.78
  602.7 16.3 %multiply_convert_fusion.1 = bf16[3,4,512,512]{2,3,1,0:T(8,128)(2,1)} fusion(bf16[3,512,4,128]{1,3,2,0:T(8,128)(2,1)} %copy.60, bf16[3,512,4,128]{1,3,2,0:T(8,128)(2,1)} %bitcast.356, f32[3,4,512,512]{2,3,1,0:T(8,128)} %get-tuple-element.120, f32[3,4,512]{2,1,0:T(4,128)S(1)} %get-tuple-element.119), kind=kOutput, calls=%fused_computation.7 | convolution fusion | flops 1629493760 | bytes 22044672 | tf_op jit(solution)/shard_map/sub | solution.py:245
  619.1 4.6 fusion.74
  634.5 16.4 %multiply_convert_fusion = bf16[3,4,512,512]{2,3,1,0:T(8,128)(2,1)} fusion(bf16[3,512,4,128]{1,3,2,0:T(8,128)(2,1)} %copy.70, bf16[3,512,4,128]{1,3,2,0:T(8,128)(2,1)} %bitcast.350, f32[3,4,512,512]{2,3,1,0:T(8,128)} %get-tuple-element.118, f32[3,4,512]{2,1,0:T(4,128)S(1)} %get-tuple-element.117), kind=kOutput, calls=%fused_computation.4 | convolution fusion | flops 1629493760 | bytes 22044672 | tf_op jit(solution)/shard_map/sub | solution.py:245
  650.9 4.5 fusion.92
  680.7 6.7 pad_maximum_fusion.2
  687.4 6.8 copy.63
  709.7 6.7 pad_maximum_fusion.3
  716.4 6.9 copy.73
  723.4 5.4 fusion.222
  728.9 4.4 multiply_reduce_fusion.3
  748.3 10.5 %psum.7 = f32[4,128]{1,0:T(4,128)S(1)} all-reduce(f32[4,128]{1,0:T(4,128)S(1)} %fusion.190), channel_id=1, replica_groups=mesh['dp'=8,'mp'=4] {'mp'}, use_global_device_ids=true, to_apply=%region_25.26 | all-reduce | flops 512 | bytes 4096 | tf_op jit(solution)/shard_map/psum | solution.py:273
  771.6 4.5 convert_add_fusion
  798.6 26.2 %collective-permute-done.80 = bf16[256,1536]{1,0:T(8,128)(2,1)S(1)} collective-permute-done((bf16[256,1536]{1,0:T(8,128)(2,1)S(1)}, bf16[256,1536]{1,0:T(8,128)(2,1)S(1)}, u32[]{:S(2)}, u32[]{:S(2)}) %collective-permute-start.80) | collective-permute-done | bytes 786464 | tf_op jit(solution)/shard_map/ppermute | solution.py:19
  825.9 32.5 %collective-permute-done.84 = bf16[256,1536]{1,0:T(8,128)(2,1)S(1)} collective-permute-done((bf16[256,1536]{1,0:T(8,128)(2,1)S(1)}, bf16[256,1536]{1,0:T(8,128)(2,1)S(1)}, u32[]{:S(2)}, u32[]{:S(2)}) %collective-permute-start.84) | collective-permute-done | bytes 786464 | tf_op jit(solution)/shard_map/ppermute | solution.py:19
  865.7 4.8 collective-permute-done.81
  871.7 10.0 %collective-permute-done.108 = bf16[128,2048]{1,0:T(8,128)(2,1)S(1)} collective-permute-done((bf16[128,2048]{1,0:T(8,128)(2,1)S(1)}, bf16[128,2048]{1,0:T(8,128)(2,1)S(1)}, u32[]{:S(2)}, u32[]{:S(2)}) %collective-permute-start.108) | collective-permute-done | bytes 524320 | tf_op jit(solution)/shard_map/ppermute | solution.py:19
  881.9 8.3 collective-permute-done.99
  892.9 4.2 collective-permute-start.113
  897.1 12.1 %collective-permute-done.87 = bf16[128,768]{1,0:T(8,128)(2,1)S(1)} collective-permute-done((bf16[128,768]{1,0:T(8,128)(2,1)S(1)}, bf16[128,768]{1,0:T(8,128)(2,1)S(1)}, u32[]{:S(2)}, u32[]{:S(2)}) %collective-permute-start.87) | collective-permute-done | bytes 196640 | tf_op jit(solution)/shard_map/ppermute | solution.py:23
  910.1 4.6 collective-permute-start.105
  914.7 7.4 collective-permute-done.113
  923.1 12.1 %collective-permute-done.104 = bf16[128,1024]{1,0:T(8,128)(2,1)S(1)} collective-permute-done((bf16[128,1024]{1,0:T(8,128)(2,1)S(1)}, bf16[128,1024]{1,0:T(8,128)(2,1)S(1)}, u32[]{:S(2)}, u32[]{:S(2)}) %collective-permute-start.104) | collective-permute-done | bytes 262176 | tf_op jit(solution)/shard_map/ppermute | solution.py:23
  (608 shorter events, 312.4 us)
Async XLA Ops:
  2.0 55.9 %collective-permute-start.3 = (bf16[128,4]{0,1:T(4,128)(2,1)}, bf16[128,4]{0,1:T(4,128)(2,1)}, u32[]{:S(2)}, u32[]{:S(2)}) collective-permute-start(bf16[128,4]{0,1:T(4,128)(2,1)} %maximum_bitcast_fusion.1), channel_id=1, source_target_pairs={{0,4},{4,0},{8,12},{12,8},{16,20},{20,16},{24,28},{28,24},{1,5},{5... | collective-permute-start | bytes 3080 | tf_op jit(solution)/shard_map/ppermute | solution.py:19
  2.5 47.9 %collective-permute-start.1 = (bf16[128,4]{0,1:T(4,128)(2,1)}, bf16[128,4]{0,1:T(4,128)(2,1)}, u32[]{:S(2)}, u32[]{:S(2)}) collective-permute-start(bf16[128,4]{0,1:T(4,128)(2,1)} %maximum_bitcast_fusion.1), channel_id=1, source_target_pairs={{0,16},{4,20},{8,24},{12,28},{16,0},{20,4},{24,8},{28,12},{1,17},{... | collective-permute-start | bytes 3080 | tf_op jit(solution)/shard_map/ppermute | solution.py:19
  5.0 43.1 %collective-permute-start = (bf16[128,4]{0,1:T(4,128)(2,1)}, bf16[128,4]{0,1:T(4,128)(2,1)}, u32[]{:S(2)}, u32[]{:S(2)}) collective-permute-start(bf16[128,4]{0,1:T(4,128)(2,1)} %maximum_bitcast_fusion.1), channel_id=1, source_target_pairs={{0,8},{4,12},{8,0},{12,4},{16,24},{20,28},{24,16},{28,20},{1,9},{5... | collective-permute-start | bytes 3080 | tf_op jit(solution)/shard_map/ppermute | solution.py:19
  6.5 63.9 %collective-permute-start.17 = (bf16[128,256]{1,0:T(8,128)(2,1)}, bf16[128,256]{1,0:T(8,128)(2,1)}, u32[]{:S(2)}, u32[]{:S(2)}) collective-permute-start(bf16[128,256]{1,0:T(8,128)(2,1)} %param.16), channel_id=1, source_target_pairs={{0,3},{1,0},{2,1},{3,2},{4,7},{5,4},{6,5},{7,6},{8,11},{9,8},{10,9... | collective-permute-start | bytes 196616 | tf_op jit(solution)/shard_map/ppermute | solution.py:23
  10.1 58.7 %collective-permute-start.35 = (bf16[128,256]{1,0:T(8,128)(2,1)}, bf16[128,256]{1,0:T(8,128)(2,1)}, u32[]{:S(2)}, u32[]{:S(2)}) collective-permute-start(bf16[128,256]{1,0:T(8,128)(2,1)} %param.16), channel_id=1, source_target_pairs={{0,1},{1,2},{2,3},{3,0},{4,5},{5,6},{6,7},{7,4},{8,9},{9,10},{10,1... | collective-permute-start | bytes 196616 | tf_op jit(solution)/shard_map/ppermute | solution.py:23
  48.1 18.3 %collective-permute-start.34 = (bf16[128,256]{1,0:T(8,128)(2,1)}, bf16[128,256]{1,0:T(8,128)(2,1)S(1)}, u32[]{:S(2)}, u32[]{:S(2)}) collective-permute-start(bf16[128,256]{1,0:T(8,128)(2,1)} %param.16), channel_id=1, source_target_pairs={{0,2},{1,3},{2,0},{3,1},{4,6},{5,7},{6,4},{7,5},{8,10},{9,11},{10,... | collective-permute-start | bytes 196616 | tf_op jit(solution)/shard_map/ppermute | solution.py:23
  54.0 31.2 %collective-permute-start.26 = (bf16[128,768]{1,0:T(8,128)(2,1)}, bf16[128,768]{1,0:T(8,128)(2,1)S(1)}, u32[]{:S(2)}, u32[]{:S(2)}) collective-permute-start(bf16[128,768]{1,0:T(8,128)(2,1)} %pad_maximum_fusion.6), channel_id=1, source_target_pairs={{0,1},{1,2},{2,3},{3,0},{4,5},{5,6},{6,7},{7,4},{8,9},{9,10},{10,1... | collective-permute-start | bytes 589832 | tf_op jit(solution)/shard_map/ppermute | solution.py:23
  61.9 21.4 %collective-permute-start.25 = (bf16[128,768]{1,0:T(8,128)(2,1)}, bf16[128,768]{1,0:T(8,128)(2,1)S(1)}, u32[]{:S(2)}, u32[]{:S(2)}) collective-permute-start(bf16[128,768]{1,0:T(8,128)(2,1)} %pad_maximum_fusion.6), channel_id=1, source_target_pairs={{0,2},{1,3},{2,0},{3,1},{4,6},{5,7},{6,4},{7,5},{8,10},{9,11},{10,... | collective-permute-start | bytes 589832 | tf_op jit(solution)/shard_map/ppermute | solution.py:23
  79.8 45.3 %collective-permute-start.43 = (bf16[128,1024]{1,0:T(8,128)(2,1)S(1)}, bf16[128,1024]{1,0:T(8,128)(2,1)S(1)}, u32[]{:S(2)}, u32[]{:S(2)}) collective-permute-start(bf16[128,1024]{1,0:T(8,128)(2,1)S(1)} %copy-done.39), channel_id=1, source_target_pairs={{0,3},{1,0},{2,1},{3,2},{4,7},{5,4},{6,5},{7,6},{8,11},{9,8},{10,9... | collective-permute-start | bytes 786440 | tf_op jit(solution)/shard_map/ppermute | solution.py:23
  81.9 43.1 %collective-permute-start.60 = (bf16[128,1024]{1,0:T(8,128)(2,1)S(1)}, bf16[128,1024]{1,0:T(8,128)(2,1)S(1)}, u32[]{:S(2)}, u32[]{:S(2)}) collective-permute-start(bf16[128,1024]{1,0:T(8,128)(2,1)S(1)} %copy-done.39), channel_id=1, source_target_pairs={{0,1},{1,2},{2,3},{3,0},{4,5},{5,6},{6,7},{7,4},{8,9},{9,10},{10,1... | collective-permute-start | bytes 786440 | tf_op jit(solution)/shard_map/ppermute | solution.py:23
  82.0 34.6 %collective-permute-start.68 = (bf16[128,1024]{1,0:T(8,128)(2,1)S(1)}, bf16[128,1024]{1,0:T(8,128)(2,1)S(1)}, u32[]{:S(2)}, u32[]{:S(2)}) collective-permute-start(bf16[128,1024]{1,0:T(8,128)(2,1)S(1)} %copy-done.41), channel_id=1, source_target_pairs={{0,2},{1,3},{2,0},{3,1},{4,6},{5,7},{6,4},{7,5},{8,10},{9,11},{10,... | collective-permute-start | bytes 786440 | tf_op jit(solution)/shard_map/ppermute | solution.py:23
  83.2 39.0 %collective-permute-start.59 = (bf16[128,1024]{1,0:T(8,128)(2,1)S(1)}, bf16[128,1024]{1,0:T(8,128)(2,1)S(1)}, u32[]{:S(2)}, u32[]{:S(2)}) collective-permute-start(bf16[128,1024]{1,0:T(8,128)(2,1)S(1)} %copy-done.39), channel_id=1, source_target_pairs={{0,2},{1,3},{2,0},{3,1},{4,6},{5,7},{6,4},{7,5},{8,10},{9,11},{10,... | collective-permute-start | bytes 786440 | tf_op jit(solution)/shard_map/ppermute | solution.py:23
  85.2 38.4 %collective-permute-start.69 = (bf16[128,1024]{1,0:T(8,128)(2,1)S(1)}, bf16[128,1024]{1,0:T(8,128)(2,1)S(1)}, u32[]{:S(2)}, u32[]{:S(2)}) collective-permute-start(bf16[128,1024]{1,0:T(8,128)(2,1)S(1)} %copy-done.41), channel_id=1, source_target_pairs={{0,1},{1,2},{2,3},{3,0},{4,5},{5,6},{6,7},{7,4},{8,9},{9,10},{10,1... | collective-permute-start | bytes 786440 | tf_op jit(solution)/shard_map/ppermute | solution.py:23
  122.2 85.9 %collective-permute-start.7 = (bf16[3,128,1024]{2,1,0:T(8,128)(2,1)S(1)}, bf16[3,128,1024]{2,1,0:T(8,128)(2,1)S(1)}, u32[]{:S(2)}, u32[]{:S(2)}) collective-permute-start(bf16[3,128,1024]{2,1,0:T(8,128)(2,1)S(1)} %get-tuple-element.57), channel_id=1, source_target_pairs={{0,1},{1,2},{2,3},{4,5},{5,6},{6,7},{8,9},{9,10},{10,11},{12,13},{... | collective-permute-start | bytes 2359304 | tf_op jit(solution)/shard_map/ppermute | solution.py:147
  123.6 84.5 %collective-permute-start.8 = (bf16[3,128,1024]{2,1,0:T(8,128)(2,1)S(1)}, bf16[3,128,1024]{2,1,0:T(8,128)(2,1)S(1)}, u32[]{:S(2)}, u32[]{:S(2)}) collective-permute-start(bf16[3,128,1024]{2,1,0:T(8,128)(2,1)S(1)} %get-tuple-element.58), channel_id=1, source_target_pairs={{1,0},{2,1},{3,2},{5,4},{6,5},{7,6},{9,8},{10,9},{11,10},{13,12},{... | collective-permute-start | bytes 2359304 | tf_op jit(solution)/shard_map/ppermute | solution.py:148
  141.3 20.9 %collective-permute-start.28 = (bf16[128,1536]{1,0:T(8,128)(2,1)S(1)}, bf16[128,1536]{1,0:T(8,128)(2,1)S(1)}, u32[]{:S(2)}, u32[]{:S(2)}) collective-permute-start(bf16[128,1536]{1,0:T(8,128)(2,1)S(1)} %get-tuple-element.86), channel_id=1, source_target_pairs={{0,16},{4,20},{8,24},{12,28},{16,0},{20,4},{24,8},{28,12},{1,17},{... | collective-permute-start | bytes 1179656 | tf_op jit(solution)/shard_map/ppermute | solution.py:19
  152.7 20.2 %collective-permute-start.70 = (bf16[128,2048]{1,0:T(8,128)(2,1)S(1)}, bf16[128,2048]{1,0:T(8,128)(2,1)S(1)}, u32[]{:S(2)}, u32[]{:S(2)}) collective-permute-start(bf16[128,2048]{1,0:T(8,128)(2,1)S(1)} %get-tuple-element.78), channel_id=1, source_target_pairs={{0,8},{4,12},{8,0},{12,4},{16,24},{20,28},{24,16},{28,20},{1,9},{5... | collective-permute-start | bytes 1572872 | tf_op jit(solution)/shard_map/ppermute | solution.py:19
  162.2 21.9 %collective-permute-start.61 = (bf16[128,2048]{1,0:T(8,128)(2,1)S(1)}, bf16[128,2048]{1,0:T(8,128)(2,1)S(1)}, u32[]{:S(2)}, u32[]{:S(2)}) collective-permute-start(bf16[128,2048]{1,0:T(8,128)(2,1)S(1)} %get-tuple-element.82), channel_id=1, source_target_pairs={{0,8},{4,12},{8,0},{12,4},{16,24},{20,28},{24,16},{28,20},{1,9},{5... | collective-permute-start | bytes 1572872 | tf_op jit(solution)/shard_map/ppermute | solution.py:19
  173.5 21.9 %collective-permute-start.44 = (bf16[128,2048]{1,0:T(8,128)(2,1)S(1)}, bf16[128,2048]{1,0:T(8,128)(2,1)S(1)}, u32[]{:S(2)}, u32[]{:S(2)}) collective-permute-start(bf16[128,2048]{1,0:T(8,128)(2,1)S(1)} %get-tuple-element.74), channel_id=1, source_target_pairs={{0,8},{4,12},{8,0},{12,4},{16,24},{20,28},{24,16},{28,20},{1,9},{5... | collective-permute-start | bytes 1572872 | tf_op jit(solution)/shard_map/ppermute | solution.py:19
  184.7 20.6 %collective-permute-start.52 = (bf16[128,2048]{1,0:T(8,128)(2,1)S(1)}, bf16[128,2048]{1,0:T(8,128)(2,1)S(1)}, u32[]{:S(2)}, u32[]{:S(2)}) collective-permute-start(bf16[128,2048]{1,0:T(8,128)(2,1)S(1)} %get-tuple-element.70), channel_id=1, source_target_pairs={{0,8},{4,12},{8,0},{12,4},{16,24},{20,28},{24,16},{28,20},{1,9},{5... | collective-permute-start | bytes 1572872 | tf_op jit(solution)/shard_map/ppermute | solution.py:19
  196.7 21.1 %collective-permute-start.13 = (bf16[128,1536]{1,0:T(8,128)(2,1)S(1)}, bf16[128,1536]{1,0:T(8,128)(2,1)S(1)}, u32[]{:S(2)}, u32[]{:S(2)}) collective-permute-start(bf16[128,1536]{1,0:T(8,128)(2,1)S(1)} %get-tuple-element.68), channel_id=1, source_target_pairs={{0,4},{4,0},{8,12},{12,8},{16,20},{20,16},{24,28},{28,24},{1,5},{5... | collective-permute-start | bytes 1179656 | tf_op jit(solution)/shard_map/ppermute | solution.py:19
  205.3 25.3 %collective-permute-start.30 = (bf16[128,1536]{1,0:T(8,128)(2,1)S(1)}, bf16[128,1536]{1,0:T(8,128)(2,1)S(1)}, u32[]{:S(2)}, u32[]{:S(2)}) collective-permute-start(bf16[128,1536]{1,0:T(8,128)(2,1)S(1)} %get-tuple-element.86), channel_id=1, source_target_pairs={{0,4},{4,0},{8,12},{12,8},{16,20},{20,16},{24,28},{28,24},{1,5},{5... | collective-permute-start | bytes 1179656 | tf_op jit(solution)/shard_map/ppermute | solution.py:19
  208.1 38.1 %collective-permute-start.73 = (bf16[128,2048]{1,0:T(8,128)(2,1)S(1)}, bf16[128,2048]{1,0:T(8,128)(2,1)S(1)}, u32[]{:S(2)}, u32[]{:S(2)}) collective-permute-start(bf16[128,2048]{1,0:T(8,128)(2,1)S(1)} %get-tuple-element.78), channel_id=1, source_target_pairs={{0,4},{4,0},{8,12},{12,8},{16,20},{20,16},{24,28},{28,24},{1,5},{5... | collective-permute-start | bytes 1572872 | tf_op jit(solution)/shard_map/ppermute | solution.py:19
  208.1 53.7 %collective-permute-start.64 = (bf16[128,2048]{1,0:T(8,128)(2,1)S(1)}, bf16[128,2048]{1,0:T(8,128)(2,1)S(1)}, u32[]{:S(2)}, u32[]{:S(2)}) collective-permute-start(bf16[128,2048]{1,0:T(8,128)(2,1)S(1)} %get-tuple-element.82), channel_id=1, source_target_pairs={{0,4},{4,0},{8,12},{12,8},{16,20},{20,16},{24,28},{28,24},{1,5},{5... | collective-permute-start | bytes 1572872 | tf_op jit(solution)/shard_map/ppermute | solution.py:19
  232.3 45.9 %collective-permute-start.47 = (bf16[128,2048]{1,0:T(8,128)(2,1)S(1)}, bf16[128,2048]{1,0:T(8,128)(2,1)S(1)}, u32[]{:S(2)}, u32[]{:S(2)}) collective-permute-start(bf16[128,2048]{1,0:T(8,128)(2,1)S(1)} %get-tuple-element.74), channel_id=1, source_target_pairs={{0,4},{4,0},{8,12},{12,8},{16,20},{20,16},{24,28},{28,24},{1,5},{5... | collective-permute-start | bytes 1572872 | tf_op jit(solution)/shard_map/ppermute | solution.py:19
  246.9 47.7 %collective-permute-start.55 = (bf16[128,2048]{1,0:T(8,128)(2,1)S(1)}, bf16[128,2048]{1,0:T(8,128)(2,1)S(1)}, u32[]{:S(2)}, u32[]{:S(2)}) collective-permute-start(bf16[128,2048]{1,0:T(8,128)(2,1)S(1)} %get-tuple-element.70), channel_id=1, source_target_pairs={{0,4},{4,0},{8,12},{12,8},{16,20},{20,16},{24,28},{28,24},{1,5},{5... | collective-permute-start | bytes 1572872 | tf_op jit(solution)/shard_map/ppermute | solution.py:19
  262.5 18.2 %collective-permute-start.49 = (bf16[128,2048]{1,0:T(8,128)(2,1)S(1)}, bf16[128,2048]{1,0:T(8,128)(2,1)S(1)}, u32[]{:S(2)}, u32[]{:S(2)}) collective-permute-start(bf16[128,2048]{1,0:T(8,128)(2,1)S(1)} %collective-permute-done.45), channel_id=1, source_target_pairs={{0,4},{4,0},{8,12},{12,8},{16,20},{20,16},{24,28},{28,24},{1,5},{5... | collective-permute-start | bytes 1572872 | tf_op jit(solution)/shard_map/ppermute | solution.py:19
  262.8 16.8 %collective-permute-start.48 = (bf16[128,2048]{1,0:T(8,128)(2,1)S(1)}, bf16[128,2048]{1,0:T(8,128)(2,1)S(1)}, u32[]{:S(2)}, u32[]{:S(2)}) collective-permute-start(bf16[128,2048]{1,0:T(8,128)(2,1)S(1)} %collective-permute-done.44), channel_id=1, source_target_pairs={{0,4},{4,0},{8,12},{12,8},{16,20},{20,16},{24,28},{28,24},{1,5},{5... | collective-permute-start | bytes 1572872 | tf_op jit(solution)/shard_map/ppermute | solution.py:19
  276.3 20.4 %collective-permute-start.57 = (bf16[128,2048]{1,0:T(8,128)(2,1)S(1)}, bf16[128,2048]{1,0:T(8,128)(2,1)S(1)}, u32[]{:S(2)}, u32[]{:S(2)}) collective-permute-start(bf16[128,2048]{1,0:T(8,128)(2,1)S(1)} %collective-permute-done.53), channel_id=1, source_target_pairs={{0,4},{4,0},{8,12},{12,8},{16,20},{20,16},{24,28},{28,24},{1,5},{5... | collective-permute-start | bytes 1572872 | tf_op jit(solution)/shard_map/ppermute | solution.py:19
  279.6 16.3 %collective-permute-start.56 = (bf16[128,2048]{1,0:T(8,128)(2,1)S(1)}, bf16[128,2048]{1,0:T(8,128)(2,1)S(1)}, u32[]{:S(2)}, u32[]{:S(2)}) collective-permute-start(bf16[128,2048]{1,0:T(8,128)(2,1)S(1)} %collective-permute-done.52), channel_id=1, source_target_pairs={{0,4},{4,0},{8,12},{12,8},{16,20},{20,16},{24,28},{28,24},{1,5},{5... | collective-permute-start | bytes 1572872 | tf_op jit(solution)/shard_map/ppermute | solution.py:19
  280.7 24.4 %collective-permute-start.16 = (bf16[128,1536]{1,0:T(8,128)(2,1)S(1)}, bf16[128,1536]{1,0:T(8,128)(2,1)S(1)}, u32[]{:S(2)}, u32[]{:S(2)}) collective-permute-start(bf16[128,1536]{1,0:T(8,128)(2,1)S(1)} %collective-permute-done.12), channel_id=1, source_target_pairs={{0,4},{4,0},{8,12},{12,8},{16,20},{20,16},{24,28},{28,24},{1,5},{5... | collective-permute-start | bytes 1179656 | tf_op jit(solution)/shard_map/ppermute | solution.py:19
  294.6 214.0 %collective-permute-start.76 = (bf16[128,2048]{1,0:T(8,128)(2,1)}, bf16[128,2048]{1,0:T(8,128)(2,1)}, u32[]{:S(2)}, u32[]{:S(2)}) collective-permute-start(bf16[128,2048]{1,0:T(8,128)(2,1)} %collective-permute-done.72), channel_id=1, source_target_pairs={{0,4},{4,0},{8,12},{12,8},{16,20},{20,16},{24,28},{28,24},{1,5},{5... | collective-permute-start | bytes 1572872 | tf_op jit(solution)/shard_map/ppermute | solution.py:19
  296.0 201.5 %collective-permute-start.67 = (bf16[128,2048]{1,0:T(8,128)(2,1)}, bf16[128,2048]{1,0:T(8,128)(2,1)}, u32[]{:S(2)}, u32[]{:S(2)}) collective-permute-start(bf16[128,2048]{1,0:T(8,128)(2,1)} %collective-permute-done.63), channel_id=1, source_target_pairs={{0,4},{4,0},{8,12},{12,8},{16,20},{20,16},{24,28},{28,24},{1,5},{5... | collective-permute-start | bytes 1572872 | tf_op jit(solution)/shard_map/ppermute | solution.py:19
  296.8 179.3 %collective-permute-start.50 = (bf16[128,2048]{1,0:T(8,128)(2,1)}, bf16[128,2048]{1,0:T(8,128)(2,1)}, u32[]{:S(2)}, u32[]{:S(2)}) collective-permute-start(bf16[128,2048]{1,0:T(8,128)(2,1)} %collective-permute-done.46), channel_id=1, source_target_pairs={{0,4},{4,0},{8,12},{12,8},{16,20},{20,16},{24,28},{28,24},{1,5},{5... | collective-permute-start | bytes 1572872 | tf_op jit(solution)/shard_map/ppermute | solution.py:19
  298.2 187.0 %collective-permute-start.58 = (bf16[128,2048]{1,0:T(8,128)(2,1)}, bf16[128,2048]{1,0:T(8,128)(2,1)}, u32[]{:S(2)}, u32[]{:S(2)}) collective-permute-start(bf16[128,2048]{1,0:T(8,128)(2,1)} %collective-permute-done.54), channel_id=1, source_target_pairs={{0,4},{4,0},{8,12},{12,8},{16,20},{20,16},{24,28},{28,24},{1,5},{5... | collective-permute-start | bytes 1572872 | tf_op jit(solution)/shard_map/ppermute | solution.py:19
  551.6 224.8 %collective-permute-start.106 = (bf16[512,2048]{1,0:T(8,128)(2,1)}, bf16[512,2048]{1,0:T(8,128)(2,1)}, u32[]{:S(2)}, u32[]{:S(2)}) collective-permute-start(bf16[512,2048]{1,0:T(8,128)(2,1)} %convolution_convert_fusion.3), channel_id=1, source_target_pairs={{0,4},{4,0},{8,12},{12,8},{16,20},{20,16},{24,28},{28,24},{1,5},{5... | collective-permute-start | bytes 6291464 | tf_op jit(solution)/shard_map/ppermute | solution.py:19
  552.1 231.4 %collective-permute-start.97 = (bf16[512,2048]{1,0:T(8,128)(2,1)}, bf16[512,2048]{1,0:T(8,128)(2,1)}, u32[]{:S(2)}, u32[]{:S(2)}) collective-permute-start(bf16[512,2048]{1,0:T(8,128)(2,1)} %convolution_convert_fusion.5), channel_id=1, source_target_pairs={{0,4},{4,0},{8,12},{12,8},{16,20},{20,16},{24,28},{28,24},{1,5},{5... | collective-permute-start | bytes 6291464 | tf_op jit(solution)/shard_map/ppermute | solution.py:19
  558.3 22.6 %collective-permute-start.77 = (bf16[3,128,1024]{2,1,0:T(8,128)(2,1)S(1)}, bf16[3,128,1024]{2,1,0:T(8,128)(2,1)S(1)}, u32[]{:S(2)}, u32[]{:S(2)}) collective-permute-start(bf16[3,128,1024]{2,1,0:T(8,128)(2,1)S(1)} %get-tuple-element.55), channel_id=1, source_target_pairs={{0,1},{1,2},{2,3},{4,5},{5,6},{6,7},{8,9},{9,10},{10,11},{12,13},{... | collective-permute-start | bytes 2359304 | tf_op jit(solution)/shard_map/ppermute | solution.py:147
  566.0 22.3 %collective-permute-start.78 = (bf16[3,128,1024]{2,1,0:T(8,128)(2,1)S(1)}, bf16[3,128,1024]{2,1,0:T(8,128)(2,1)S(1)}, u32[]{:S(2)}, u32[]{:S(2)}) collective-permute-start(bf16[3,128,1024]{2,1,0:T(8,128)(2,1)S(1)} %get-tuple-element.56), channel_id=1, source_target_pairs={{1,0},{2,1},{3,2},{5,4},{6,5},{7,6},{9,8},{10,9},{11,10},{13,12},{... | collective-permute-start | bytes 2359304 | tf_op jit(solution)/shard_map/ppermute | solution.py:148
  569.5 201.6 %collective-permute-start.110 = (bf16[512,2048]{1,0:T(8,128)(2,1)}, bf16[512,2048]{1,0:T(8,128)(2,1)}, u32[]{:S(2)}, u32[]{:S(2)}) collective-permute-start(bf16[512,2048]{1,0:T(8,128)(2,1)} %convolution_convert_fusion.2), channel_id=1, source_target_pairs={{0,4},{4,0},{8,12},{12,8},{16,20},{20,16},{24,28},{28,24},{1,5},{5... | collective-permute-start | bytes 6291464 | tf_op jit(solution)/shard_map/ppermute | solution.py:19
  580.9 80.1 %collective-permute-start.89 = (bf16[256,512]{1,0:T(8,128)(2,1)}, bf16[256,512]{1,0:T(8,128)(2,1)}, u32[]{:S(2)}, u32[]{:S(2)}) collective-permute-start(bf16[256,512]{1,0:T(8,128)(2,1)} %fusion.181), channel_id=1, source_target_pairs={{0,16},{4,20},{8,24},{12,28},{16,0},{20,4},{24,8},{28,12},{1,17},{... | collective-permute-start | bytes 786440 | tf_op jit(solution)/shard_map/ppermute | solution.py:19
  588.3 150.3 %collective-permute-start.93 = (bf16[256,512]{1,0:T(8,128)(2,1)}, bf16[256,512]{1,0:T(8,128)(2,1)S(1)}, u32[]{:S(2)}, u32[]{:S(2)}) collective-permute-start(bf16[256,512]{1,0:T(8,128)(2,1)} %bitcast.71), channel_id=1, source_target_pairs={{0,8},{4,12},{8,0},{12,4},{16,24},{20,28},{24,16},{28,20},{1,9},{5... | collective-permute-start | bytes 786440 | tf_op jit(solution)/shard_map/ppermute | solution.py:19
  663.6 95.3 %collective-permute-start.90 = (bf16[128,512]{1,0:T(8,128)(2,1)}, bf16[128,512]{1,0:T(8,128)(2,1)S(1)}, u32[]{:S(2)}, u32[]{:S(2)}) collective-permute-start(bf16[128,512]{1,0:T(8,128)(2,1)} %fusion.185), channel_id=1, source_target_pairs={{0,8},{4,12},{8,0},{12,4},{16,24},{20,28},{24,16},{28,20},{1,9},{5... | collective-permute-start | bytes 393224 | tf_op jit(solution)/shard_map/ppermute | solution.py:19
  767.5 19.5 %collective-permute-start.101 = (bf16[512,2048]{1,0:T(8,128)(2,1)}, bf16[512,2048]{1,0:T(8,128)(2,1)S(1)}, u32[]{:S(2)}, u32[]{:S(2)}) collective-permute-start(bf16[512,2048]{1,0:T(8,128)(2,1)} %convolution_convert_fusion.4), channel_id=1, source_target_pairs={{0,4},{4,0},{8,12},{12,8},{16,20},{20,16},{24,28},{28,24},{1,5},{5... | collective-permute-start | bytes 6291464 | tf_op jit(solution)/shard_map/ppermute | solution.py:19
  770.4 18.9 %collective-permute-start.79 = (bf16[512,1536]{1,0:T(8,128)(2,1)}, bf16[512,1536]{1,0:T(8,128)(2,1)S(1)}, u32[]{:S(2)}, u32[]{:S(2)}) collective-permute-start(bf16[512,1536]{1,0:T(8,128)(2,1)} %convolution_convert_fusion.7), channel_id=1, source_target_pairs={{0,4},{4,0},{8,12},{12,8},{16,20},{20,16},{24,28},{28,24},{1,5},{5... | collective-permute-start | bytes 4718600 | tf_op jit(solution)/shard_map/ppermute | solution.py:19
  771.1 24.6 %collective-permute-start.83 = (bf16[512,1536]{1,0:T(8,128)(2,1)}, bf16[512,1536]{1,0:T(8,128)(2,1)S(1)}, u32[]{:S(2)}, u32[]{:S(2)}) collective-permute-start(bf16[512,1536]{1,0:T(8,128)(2,1)} %convolution_convert_fusion.6), channel_id=1, source_target_pairs={{0,4},{4,0},{8,12},{12,8},{16,20},{20,16},{24,28},{28,24},{1,5},{5... | collective-permute-start | bytes 4718600 | tf_op jit(solution)/shard_map/ppermute | solution.py:19
  781.8 77.7 %collective-permute-start.107 = (bf16[256,2048]{1,0:T(8,128)(2,1)S(1)}, bf16[256,2048]{1,0:T(8,128)(2,1)S(1)}, u32[]{:S(2)}, u32[]{:S(2)}) collective-permute-start(bf16[256,2048]{1,0:T(8,128)(2,1)S(1)} %fusion.104), channel_id=1, source_target_pairs={{0,16},{4,20},{8,24},{12,28},{16,0},{20,4},{24,8},{28,12},{1,17},{... | collective-permute-start | bytes 3145736 | tf_op jit(solution)/shard_map/ppermute | solution.py:19
  792.6 32.2 %collective-permute-start.80 = (bf16[256,1536]{1,0:T(8,128)(2,1)S(1)}, bf16[256,1536]{1,0:T(8,128)(2,1)S(1)}, u32[]{:S(2)}, u32[]{:S(2)}) collective-permute-start(bf16[256,1536]{1,0:T(8,128)(2,1)S(1)} %fusion.111), channel_id=1, source_target_pairs={{0,16},{4,20},{8,24},{12,28},{16,0},{20,4},{24,8},{28,12},{1,17},{... | collective-permute-start | bytes 2359304 | tf_op jit(solution)/shard_map/ppermute | solution.py:19
  793.4 67.2 %collective-permute-start.98 = (bf16[256,2048]{1,0:T(8,128)(2,1)S(1)}, bf16[256,2048]{1,0:T(8,128)(2,1)S(1)}, u32[]{:S(2)}, u32[]{:S(2)}) collective-permute-start(bf16[256,2048]{1,0:T(8,128)(2,1)S(1)} %fusion.103), channel_id=1, source_target_pairs={{0,16},{4,20},{8,24},{12,28},{16,0},{20,4},{24,8},{28,12},{1,17},{... | collective-permute-start | bytes 3145736 | tf_op jit(solution)/shard_map/ppermute | solution.py:19
  794.9 67.6 %collective-permute-start.111 = (bf16[256,2048]{1,0:T(8,128)(2,1)S(1)}, bf16[256,2048]{1,0:T(8,128)(2,1)S(1)}, u32[]{:S(2)}, u32[]{:S(2)}) collective-permute-start(bf16[256,2048]{1,0:T(8,128)(2,1)S(1)} %bitcast.358), channel_id=1, source_target_pairs={{0,8},{4,12},{8,0},{12,4},{16,24},{20,28},{24,16},{28,20},{1,9},{5... | collective-permute-start | bytes 3145736 | tf_op jit(solution)/shard_map/ppermute | solution.py:19
  795.7 68.2 %collective-permute-start.102 = (bf16[256,2048]{1,0:T(8,128)(2,1)S(1)}, bf16[256,2048]{1,0:T(8,128)(2,1)S(1)}, u32[]{:S(2)}, u32[]{:S(2)}) collective-permute-start(bf16[256,2048]{1,0:T(8,128)(2,1)S(1)} %bitcast.359), channel_id=1, source_target_pairs={{0,8},{4,12},{8,0},{12,4},{16,24},{20,28},{24,16},{28,20},{1,9},{5... | collective-permute-start | bytes 3145736 | tf_op jit(solution)/shard_map/ppermute | solution.py:19
  824.7 33.7 %collective-permute-start.84 = (bf16[256,1536]{1,0:T(8,128)(2,1)S(1)}, bf16[256,1536]{1,0:T(8,128)(2,1)S(1)}, u32[]{:S(2)}, u32[]{:S(2)}) collective-permute-start(bf16[256,1536]{1,0:T(8,128)(2,1)S(1)} %bitcast.360), channel_id=1, source_target_pairs={{0,8},{4,12},{8,0},{12,4},{16,24},{20,28},{24,16},{28,20},{1,9},{5... | collective-permute-start | bytes 2359304 | tf_op jit(solution)/shard_map/ppermute | solution.py:19
  860.6 21.1 %collective-permute-start.108 = (bf16[128,2048]{1,0:T(8,128)(2,1)S(1)}, bf16[128,2048]{1,0:T(8,128)(2,1)S(1)}, u32[]{:S(2)}, u32[]{:S(2)}) collective-permute-start(bf16[128,2048]{1,0:T(8,128)(2,1)S(1)} %fusion.170), channel_id=1, source_target_pairs={{0,8},{4,12},{8,0},{12,4},{16,24},{20,28},{24,16},{28,20},{1,9},{5... | collective-permute-start | bytes 1572872 | tf_op jit(solution)/shard_map/ppermute | solution.py:19
  862.5 27.7 %collective-permute-start.99 = (bf16[128,2048]{1,0:T(8,128)(2,1)S(1)}, bf16[128,2048]{1,0:T(8,128)(2,1)S(1)}, u32[]{:S(2)}, u32[]{:S(2)}) collective-permute-start(bf16[128,2048]{1,0:T(8,128)(2,1)S(1)} %fusion.168), channel_id=1, source_target_pairs={{0,8},{4,12},{8,0},{12,4},{16,24},{20,28},{24,16},{28,20},{1,9},{5... | collective-permute-start | bytes 1572872 | tf_op jit(solution)/shard_map/ppermute | solution.py:19
  863.9 28.2 %collective-permute-start.112 = (bf16[128,2048]{1,0:T(8,128)(2,1)S(1)}, bf16[128,2048]{1,0:T(8,128)(2,1)S(1)}, u32[]{:S(2)}, u32[]{:S(2)}) collective-permute-start(bf16[128,2048]{1,0:T(8,128)(2,1)S(1)} %fusion.171), channel_id=1, source_target_pairs={{0,16},{4,20},{8,24},{12,28},{16,0},{20,4},{24,8},{28,12},{1,17},{... | collective-permute-start | bytes 1572872 | tf_op jit(solution)/shard_map/ppermute | solution.py:19
  870.5 22.1 %collective-permute-start.103 = (bf16[128,2048]{1,0:T(8,128)(2,1)S(1)}, bf16[128,2048]{1,0:T(8,128)(2,1)S(1)}, u32[]{:S(2)}, u32[]{:S(2)}) collective-permute-start(bf16[128,2048]{1,0:T(8,128)(2,1)S(1)} %fusion.169), channel_id=1, source_target_pairs={{0,16},{4,20},{8,24},{12,28},{16,0},{20,4},{24,8},{28,12},{1,17},{... | collective-permute-start | bytes 1572872 | tf_op jit(solution)/shard_map/ppermute | solution.py:19
  871.6 21.3 %collective-permute-start.82 = (bf16[128,768]{1,0:T(8,128)(2,1)S(1)}, bf16[128,768]{1,0:T(8,128)(2,1)S(1)}, u32[]{:S(2)}, u32[]{:S(2)}) collective-permute-start(bf16[128,768]{1,0:T(8,128)(2,1)S(1)} %slice.702), channel_id=1, source_target_pairs={{0,1},{1,2},{2,3},{3,0},{4,5},{5,6},{6,7},{7,4},{8,9},{9,10},{10,1... | collective-permute-start | bytes 589832 | tf_op jit(solution)/shard_map/ppermute | solution.py:23
  890.2 19.0 %collective-permute-start.87 = (bf16[128,768]{1,0:T(8,128)(2,1)S(1)}, bf16[128,768]{1,0:T(8,128)(2,1)S(1)}, u32[]{:S(2)}, u32[]{:S(2)}) collective-permute-start(bf16[128,768]{1,0:T(8,128)(2,1)S(1)} %get-tuple-element.67), channel_id=1, source_target_pairs={{0,3},{1,0},{2,1},{3,2},{4,7},{5,4},{6,5},{7,6},{8,11},{9,8},{10,9... | collective-permute-start | bytes 589832 | tf_op jit(solution)/shard_map/ppermute | solution.py:23
  892.1 17.9 %collective-permute-start.109 = (bf16[128,1024]{1,0:T(8,128)(2,1)S(1)}, bf16[128,1024]{1,0:T(8,128)(2,1)S(1)}, u32[]{:S(2)}, u32[]{:S(2)}) collective-permute-start(bf16[128,1024]{1,0:T(8,128)(2,1)S(1)} %slice.699), channel_id=1, source_target_pairs={{0,1},{1,2},{2,3},{3,0},{4,5},{5,6},{6,7},{7,4},{8,9},{9,10},{10,1... | collective-permute-start | bytes 786440 | tf_op jit(solution)/shard_map/ppermute | solution.py:23
  892.6 30.5 %collective-permute-start.100 = (bf16[128,1024]{1,0:T(8,128)(2,1)S(1)}, bf16[128,1024]{1,0:T(8,128)(2,1)S(1)}, u32[]{:S(2)}, u32[]{:S(2)}) collective-permute-start(bf16[128,1024]{1,0:T(8,128)(2,1)S(1)} %slice.700), channel_id=1, source_target_pairs={{0,1},{1,2},{2,3},{3,0},{4,5},{5,6},{6,7},{7,4},{8,9},{9,10},{10,1... | collective-permute-start | bytes 786440 | tf_op jit(solution)/shard_map/ppermute | solution.py:23
  892.9 29.3 %collective-permute-start.113 = (bf16[128,1024]{1,0:T(8,128)(2,1)S(1)}, bf16[128,1024]{1,0:T(8,128)(2,1)S(1)}, u32[]{:S(2)}, u32[]{:S(2)}) collective-permute-start(bf16[128,1024]{1,0:T(8,128)(2,1)S(1)} %get-tuple-element.59), channel_id=1, source_target_pairs={{0,2},{1,3},{2,0},{3,1},{4,6},{5,7},{6,4},{7,5},{8,10},{9,11},{10,... | collective-permute-start | bytes 786440 | tf_op jit(solution)/shard_map/ppermute | solution.py:23
  897.1 25.1 %collective-permute-start.114 = (bf16[128,1024]{1,0:T(8,128)(2,1)S(1)}, bf16[128,1024]{1,0:T(8,128)(2,1)S(1)}, u32[]{:S(2)}, u32[]{:S(2)}) collective-permute-start(bf16[128,1024]{1,0:T(8,128)(2,1)S(1)} %get-tuple-element.60), channel_id=1, source_target_pairs={{0,3},{1,0},{2,1},{3,2},{4,7},{5,4},{6,5},{7,6},{8,11},{9,8},{10,9... | collective-permute-start | bytes 786440 | tf_op jit(solution)/shard_map/ppermute | solution.py:23
  909.2 26.0 %collective-permute-start.104 = (bf16[128,1024]{1,0:T(8,128)(2,1)S(1)}, bf16[128,1024]{1,0:T(8,128)(2,1)S(1)}, u32[]{:S(2)}, u32[]{:S(2)}) collective-permute-start(bf16[128,1024]{1,0:T(8,128)(2,1)S(1)} %get-tuple-element.61), channel_id=1, source_target_pairs={{0,2},{1,3},{2,0},{3,1},{4,6},{5,7},{6,4},{7,5},{8,10},{9,11},{10,... | collective-permute-start | bytes 786440 | tf_op jit(solution)/shard_map/ppermute | solution.py:23
  910.1 25.1 %collective-permute-start.105 = (bf16[128,1024]{1,0:T(8,128)(2,1)S(1)}, bf16[128,1024]{1,0:T(8,128)(2,1)S(1)}, u32[]{:S(2)}, u32[]{:S(2)}) collective-permute-start(bf16[128,1024]{1,0:T(8,128)(2,1)S(1)} %get-tuple-element.62), channel_id=1, source_target_pairs={{0,3},{1,0},{2,1},{3,2},{4,7},{5,4},{6,5},{7,6},{8,11},{9,8},{10,9... | collective-permute-start | bytes 786440 | tf_op jit(solution)/shard_map/ppermute | solution.py:23
  (127 other events, 1634.5 us)

commit v2 on v1

v2 whole, which is shorter than its diff:
```python
import jax
import jax.numpy as jnp
from jax import lax
from jax.experimental import pallas as pl
from jax.experimental.pallas import tpu as pltpu
from jax.sharding import PartitionSpec as P

HEAD_DIM = 128
HALO = 128
EPSILON = 1e-05
LOW = jnp.bfloat16


def dot(left, right, dims, kind=jnp.float32):
    return lax.dot_general(
        left, right, ((dims[:1], dims[1:]), ((), ())), preferred_element_type=kind
    )


def swap(value, bit, count):
    return lax.ppermute(value, "dp", [(i, i ^ bit) for i in range(count)])


def shift(value, step, count):
    return lax.ppermute(value, "mp", [(i, (i + step) % count) for i in range(count)])


class Plan:
    def __init__(self, mesh):
        self.dp = mesh.shape["dp"]
        self.mp = mesh.shape["mp"]
        bits = [1 << i for i in range(self.dp.bit_length() - 1)]
        core, others = bits[:1], bits[1:]
        self.orders = (others + core, others[::-1] + core)
        self.major = core + others[::-1]
        relative = [0]
        for bit in self.major[::-1]:
            relative = relative + [r ^ bit for r in relative]
        self.relative = relative

    def own(self):
        return lax.axis_index("dp")

    def enter(self, value):
        width = value.shape[-1] // self.dp
        axis = value.ndim - 1
        return jnp.concatenate(
            [
                lax.dynamic_slice_in_dim(value, (self.own() ^ r) * width, width, axis)
                for r in self.relative
            ],
            axis=axis,
        )

    def leave(self, value):
        width = value.shape[-1] // self.dp
        axis = value.ndim - 1
        inverse = {r: p for p, r in enumerate(self.relative)}
        table = jnp.array([inverse[r] for r in range(self.dp)], jnp.int32)
        return jnp.concatenate(
            [
                lax.dynamic_slice_in_dim(value, table[self.own() ^ n] * width, width, axis)
                for n in range(self.dp)
            ],
            axis=axis,
        )

    def gather_rows(self, value, order):
        block = value.shape[0]
        known = [0]
        held = [value]
        for i, bit in enumerate(order):
            if i + 3 < len(order):
                held = [jnp.concatenate([held[0], swap(held[0], bit, self.dp)], axis=0)]
            else:
                held = held + [swap(part, bit, self.dp) for part in held]
            known = known + [r ^ bit for r in known]
        spans = held[0].shape[0] // block

        def piece(r):
            at, inner = divmod(known.index(r), spans)
            return held[at] if spans == 1 else held[at][inner * block : (inner + 1) * block]

        return jnp.concatenate([piece(r) for r in self.relative], axis=0)

    def gather(self, local):
        parts = [local] + [shift(local, -k, self.mp) for k in range(1, self.mp)]
        half = self.mp // 2
        return [
            self.gather_rows(jnp.concatenate(parts[i * half : (i + 1) * half], axis=1), order)
            for i, order in enumerate(self.orders)
        ]

    def scatter_rows(self, produce, order):
        first = order[-1]
        rest = order[:-1][::-1]
        sent = produce(1).astype(LOW)
        kept = produce(0) + swap(sent, first, self.dp).astype(jnp.float32)
        left = [bit for bit in self.major if bit != first]
        for bit in rest:
            place = left.index(bit)
            block = kept.shape[0] >> (place + 1)
            shaped = kept.reshape((1 << place), 2, block, kept.shape[1])
            sent = shaped[:, 1].reshape(-1, kept.shape[1]).astype(LOW)
            kept = shaped[:, 0].reshape(-1, kept.shape[1])
            kept = kept + swap(sent, bit, self.dp).astype(jnp.float32)
            left.remove(bit)
        return kept

    def scatter(self, produces):
        half = self.mp // 2
        blocks = []
        for produce, order in zip(produces, self.orders):
            rows = self.scatter_rows(produce, order)
            width = rows.shape[1] // half
            blocks += [rows[:, i * width : (i + 1) * width] for i in range(half)]
        total = blocks[0]
        for k in range(1, self.mp):
            total = total + shift(blocks[k].astype(LOW), k, self.mp).astype(jnp.float32)
        return total


MEGA = 1 << 20
LOG2E = 1.4426950408889634


def params(limit=56):
    return pltpu.CompilerParams(vmem_limit_bytes=limit * MEGA)


def cost(flops, bytes_accessed, transcendentals=0):
    return pl.CostEstimate(
        flops=int(flops), bytes_accessed=int(bytes_accessed), transcendentals=int(transcendentals)
    )


def whole(*shape):
    return pl.BlockSpec(shape, lambda *_: (0,) * len(shape))


def statistics(values):
    mean = jnp.mean(values, axis=-1, keepdims=True)
    centred = values - mean
    variance = jnp.mean(centred * centred, axis=-1, keepdims=True)
    return centred, lax.rsqrt(variance + EPSILON)


def norm_rows(values, gain, bias):
    centred, scale = statistics(values)
    return centred * scale * gain + bias


def norm_back(values, gain, grad):
    centred, scale = statistics(values)
    normed = centred * scale
    inner = grad * gain
    first = jnp.mean(inner, axis=-1, keepdims=True)
    second = jnp.mean(inner * normed, axis=-1, keepdims=True)
    return (inner - first - normed * second) * scale, grad * normed, grad


def fold(rows):
    total = rows[:8]
    for i in range(1, rows.shape[0] // 8):
        total = total + rows[i * 8 : i * 8 + 8]
    return total


ROWS = 64


def store_blocks(ref, start, value, table, inverse=None):
    if table is None:
        ref[pl.ds(start, value.shape[0]), :] = value
        return
    count = table.shape[0]
    block = value.shape[1] // count
    for p in range(count):
        at = pl.multiple_of(table[p] * block, block)
        ref[pl.ds(start, value.shape[0]), pl.ds(at, block)] = value[:, p * block : (p + 1) * block]


def load_blocks(ref, start, size, table):
    if table is None:
        return ref[pl.ds(start, size), :]
    count = table.shape[0]
    block = ref.shape[1] // count
    parts = []
    for p in range(count):
        at = pl.multiple_of(table[p] * block, block)
        parts.append(ref[pl.ds(start, size), pl.ds(at, block)])
    return jnp.concatenate(parts, axis=1)


def enter_kernel(blocked):
    def kernel(table_ref, latents, grads, small, entered, entered_grads, grad_z, inputs_a):
        table = table_ref if blocked else None

        @pl.loop(0, latents.shape[0] // ROWS)
        def _(i):
            start = pl.multiple_of(i * ROWS, ROWS)
            at = pl.ds(start, ROWS)
            values = load_blocks(latents, start, ROWS, table)
            entered[at, :] = values
            inputs_a[at, :] = norm_rows(values, small[0:1], small[2:3]).astype(LOW)
            values = load_blocks(grads, start, ROWS, table)
            entered_grads[at, :] = values
            grad_z[at, :] = values.astype(LOW)

    return kernel


def enter_norm(table, blocked, latents, grads, small):
    total, width = latents.shape
    rows = 256
    spec = pl.BlockSpec((rows, width), lambda i, *_: (i, 0))
    shape = lambda kind: jax.ShapeDtypeStruct((total, width), kind)
    return pl.pallas_call(
        enter_kernel(blocked),
        name="enter",
        grid_spec=pltpu.PrefetchScalarGridSpec(
            num_scalar_prefetch=1,
            grid=(total // rows,),
            in_specs=[spec, spec, whole(4, width)],
            out_specs=[spec] * 4,
        ),
        out_shape=[shape(jnp.float32), shape(jnp.float32), shape(LOW), shape(LOW)],
        compiler_params=params(),
        cost_estimate=cost(total * width * 16, total * width * 20),
    )(table, latents, grads, small)


def attention_weights(q, k, bias, factor):
    scores = dot(q, k, (1, 1)) * factor + bias
    peak = jnp.max(scores, axis=-1, keepdims=True)
    weights = jnp.exp(scores - peak)
    return weights / jnp.sum(weights, axis=-1, keepdims=True)


def window_bias(group_column, key_row):
    span = group_column.shape[0]
    place = lax.broadcasted_iota(jnp.int32, (span, span), 0)
    other = lax.broadcasted_iota(jnp.int32, (span, span), 1)
    allowed = (group_column == key_row) | (place == other)
    return jnp.where(allowed, 0.0, -1e30)


def forward_kernel(rows, steps, local_heads, factor):
    def kernel(before, own, after, w_qkv, w_out, column, row, entered, small,
               saved, attended, resid, inputs_c, bias, total):
        step = pl.program_id(1)
        w = w_qkv[...]
        saved[0, 0:HALO] = dot(before[0], w, (1, 0)).astype(LOW)
        saved[0, HALO : HALO + rows] = dot(own[0], w, (1, 0)).astype(LOW)
        saved[0, HALO + rows :] = dot(after[0], w, (1, 0)).astype(LOW)

        @pl.when(step == 0)
        def _():
            bias[...] = window_bias(column[0], row[0])
            total[...] = entered[...]

        group = local_heads * HEAD_DIM
        mine = slice(HALO, HALO + rows)
        for h in range(local_heads):
            at = slice(h * HEAD_DIM, (h + 1) * HEAD_DIM)
            q = saved[0, mine, at]
            k = saved[0, :, group + h * HEAD_DIM : group + (h + 1) * HEAD_DIM]
            v = saved[0, :, 2 * group + h * HEAD_DIM : 2 * group + (h + 1) * HEAD_DIM]
            p = attention_weights(q, k, bias[mine, :], factor).astype(LOW)
            attended[:, at] = dot(p, v, (1, 0)).astype(LOW)
        total[...] += dot(attended[...], w_out[...], (1, 1))

        @pl.when(step == steps - 1)
        def _():
            @pl.loop(0, rows // ROWS)
            def _(i):
                at = pl.ds(pl.multiple_of(i * ROWS, ROWS), ROWS)
                values = total[at, :]
                resid[at, :] = values
                inputs_c[at, :] = norm_rows(values, small[1:2], small[3:4]).astype(LOW)

    return kernel


def forward_block(parts, w_qkv, w_out, column, row, entered, small, mp, factor):
    before, own, after = parts
    micro, rows, width = own.shape
    span = rows + 2 * HALO
    total = micro * rows
    c = w_qkv.shape[1] // mp
    g = w_out.shape[1] // mp
    per = lambda n: pl.BlockSpec((1, n, width), lambda i, k: (i, 0, 0))
    tall = pl.BlockSpec((rows, width), lambda i, k: (i, 0))
    return pl.pallas_call(
        forward_kernel(rows, mp, g // HEAD_DIM, factor),
        name="attention_forward",
        grid=(micro, mp),
        in_specs=[
            per(HALO), per(rows), per(HALO),
            pl.BlockSpec((width, c), lambda i, k: (0, k)),
            pl.BlockSpec((width, g), lambda i, k: (0, k)),
            pl.BlockSpec((1, span, 1), lambda i, k: (i, 0, 0)),
            pl.BlockSpec((1, 1, span), lambda i, k: (i, 0, 0)),
            tall,
            whole(4, width),
        ],
        out_specs=[
            pl.BlockSpec((1, span, c), lambda i, k: (i, 0, k)),
            pl.BlockSpec((rows, g), lambda i, k: (i, k)),
            tall,
            tall,
        ],
        out_shape=[
            jax.ShapeDtypeStruct((micro, span, c * mp), LOW),
            jax.ShapeDtypeStruct((total, g * mp), LOW),
            jax.ShapeDtypeStruct((total, width), jnp.float32),
            jax.ShapeDtypeStruct((total, width), LOW),
        ],
        scratch_shapes=[pltpu.VMEM((span, span), jnp.float32), pltpu.VMEM((rows, width), jnp.float32)],
        compiler_params=params(),
        cost_estimate=cost(
            2 * micro * (span * width * c * mp + total * width * width // micro + 2 * rows * span * width),
            40 * MEGA,
            micro * rows * span * mp * g // HEAD_DIM,
        ),
    )(before, own, after, w_qkv, w_out, column, row, entered, small)


def up_kernel(inputs, weight, hidden, slope):
    u = dot(inputs[...], weight[...], (1, 0))
    c = 0.7978845608028654
    square = u * u
    t = jnp.tanh(u * (c + c * 0.044715 * square))
    half = 0.5 + 0.5 * t
    hidden[...] = (u * half).astype(LOW)
    inner = 0.5 * c + 1.5 * c * 0.044715 * square
    slope[...] = (half + u * inner * (1.0 - t * t)).astype(LOW)


def feed_up(inputs, weight, tile=512):
    total, width = inputs.shape
    ff = weight.shape[1]
    block = pl.BlockSpec((total, tile), lambda j: (0, j))
    return pl.pallas_call(
        up_kernel,
        name="feed_up",
        grid=(ff // tile,),
        in_specs=[whole(total, width), pl.BlockSpec((width, tile), lambda j: (0, j))],
        out_specs=[block, block],
        out_shape=[jax.ShapeDtypeStruct((total, ff), LOW)] * 2,
        compiler_params=params(),
        cost_estimate=cost(2 * total * width * ff, 2 * (width * ff + 2 * total * ff), total * ff),
    )(inputs, weight)


def down_kernel(blocked, steps):
    def kernel(table_ref, hidden, weight, resid, out, total):
        step = pl.program_id(0)
        part = dot(hidden[...], weight[...], (1, 1))

        @pl.when(step == 0)
        def _():
            total[...] = resid[...] + part

        @pl.when(step > 0)
        def _():
            total[...] += part

        @pl.when(step == steps - 1)
        def _():
            @pl.loop(0, total.shape[0] // ROWS)
            def _(i):
                start = pl.multiple_of(i * ROWS, ROWS)
                store_blocks(out, start, total[pl.ds(start, ROWS), :], table_ref if blocked else None)

    return kernel


def feed_down(table, blocked, hidden, weight, resid, tile=512):
    total, width = resid.shape
    ff = weight.shape[1]
    return pl.pallas_call(
        down_kernel(blocked, ff // tile),
        name="feed_down",
        grid_spec=pltpu.PrefetchScalarGridSpec(
            num_scalar_prefetch=1,
            grid=(ff // tile,),
            in_specs=[
                pl.BlockSpec((total, tile), lambda j, *_: (0, j)),
                pl.BlockSpec((width, tile), lambda j, *_: (0, j)),
                whole(total, width),
            ],
            out_specs=whole(total, width),
            scratch_shapes=[pltpu.VMEM((total, width), jnp.float32)],
        ),
        out_shape=jax.ShapeDtypeStruct((total, width), jnp.float32),
        compiler_params=params(),
        cost_estimate=cost(2 * total * width * ff, 2 * (width * ff + total * ff) + 8 * total * width),
    )(table, hidden, weight, resid)


def feed_back_kernel(steps):
    def kernel(grad_z, down, up, slope, resid, grads, small, grad_upward, grad_resid, grad_branch, sums, total):
        step = pl.program_id(0)
        grad = dot(grad_z[...], down[...], (1, 0)) * slope[...].astype(jnp.float32)
        grad_upward[...] = grad.astype(LOW)
        part = dot(grad_upward[...], up[...], (1, 1))

        @pl.when(step == 0)
        def _():
            total[...] = part

        @pl.when(step > 0)
        def _():
            total[...] += part

        @pl.when(step == steps - 1)
        def _():
            sums[...] = jnp.zeros_like(sums)

            @pl.loop(0, total.shape[0] // ROWS)
            def _(i):
                at = pl.ds(pl.multiple_of(i * ROWS, ROWS), ROWS)
                back, by_gain, by_bias = norm_back(resid[at, :], small[1:2], total[at, :])
                back = back + grads[at, :]
                grad_resid[at, :] = back
                grad_branch[at, :] = back.astype(LOW)
                sums[0:8] += fold(by_gain)
                sums[8:16] += fold(by_bias)

    return kernel


def feed_back(grad_z, down, up, slope, resid, grads, small, tile=512):
    total, width = resid.shape
    ff = up.shape[1]
    wide = pl.BlockSpec((width, tile), lambda j: (0, j))
    block = pl.BlockSpec((total, tile), lambda j: (0, j))
    full = whole(total, width)
    return pl.pallas_call(
        feed_back_kernel(ff // tile),
        name="feed_back",
        grid=(ff // tile,),
        in_specs=[full, wide, wide, block, full, full, whole(4, width)],
        out_specs=[block, full, full, whole(16, width)],
        out_shape=[
            jax.ShapeDtypeStruct((total, ff), LOW),
            jax.ShapeDtypeStruct((total, width), jnp.float32),
            jax.ShapeDtypeStruct((total, width), LOW),
            jax.ShapeDtypeStruct((16, width), jnp.float32),
        ],
        scratch_shapes=[pltpu.VMEM((total, width), jnp.float32)],
        compiler_params=params(),
        cost_estimate=cost(4 * total * width * ff, 4 * (width * ff + total * ff) + 14 * total * width),
    )(grad_z, down, up, slope, resid, grads, small)


def backward_kernel(rows, steps, micro, local_heads, factor, blocked):
    def kernel(table_ref, before, own, after, w_qkv, w_out, column, row, saved, entered, grad_resid, small,
               grad_projected, latents_grad, sums, bias, total, grad_att):
        index, step = pl.program_id(0), pl.program_id(1)
        w = w_out[...]
        grad_att[0:HALO] = dot(before[0], w, (1, 0)).astype(LOW)
        grad_att[HALO : HALO + rows] = dot(own[0], w, (1, 0)).astype(LOW)
        grad_att[HALO + rows :] = dot(after[0], w, (1, 0)).astype(LOW)

        @pl.when(step == 0)
        def _():
            bias[...] = window_bias(column[0], row[0])

        group = local_heads * HEAD_DIM
        mine = slice(HALO, HALO + rows)
        for h in range(local_heads):
            at = slice(h * HEAD_DIM, (h + 1) * HEAD_DIM)
            at_k = slice(group + h * HEAD_DIM, group + (h + 1) * HEAD_DIM)
            at_v = slice(2 * group + h * HEAD_DIM, 2 * group + (h + 1) * HEAD_DIM)
            q, k, v = saved[0, :, at], saved[0, :, at_k], saved[0, :, at_v]
            grad_mix = grad_att[:, at]
            p = attention_weights(q, k, bias[...], factor)
            grad_p = dot(grad_mix, v, (1, 1))
            weighted = jnp.sum(p * grad_p, axis=-1, keepdims=True)
            grad_s = (p * (grad_p - weighted)).astype(LOW)
            grad_projected[:, at] = (dot(grad_s[mine], k, (1, 0)) * factor).astype(LOW)
            grad_projected[:, at_k] = (dot(grad_s[:, mine], q, (0, 0)) * factor).astype(LOW)
            grad_projected[:, at_v] = dot(p[:, mine].astype(LOW), grad_mix, (0, 0)).astype(LOW)
        part = dot(grad_projected[...], w_qkv[...], (1, 1))

        @pl.when(step == 0)
        def _():
            total[...] = part

        @pl.when(step > 0)
        def _():
            total[...] += part

        @pl.when((index == 0) & (step == 0))
        def _():
            sums[...] = jnp.zeros_like(sums)

        @pl.when(step == steps - 1)
        def _():
            @pl.loop(0, rows // ROWS)
            def _(i):
                start = pl.multiple_of(i * ROWS, ROWS)
                at = pl.ds(start, ROWS)
                back, by_gain, by_bias = norm_back(entered[at, :], small[0:1], total[at, :])
                store_blocks(latents_grad, start, back + grad_resid[at, :], table_ref if blocked else None)
                sums[0:8] += fold(by_gain)
                sums[8:16] += fold(by_bias)

    return kernel


def backward_block(table, blocked, parts, w_qkv, w_out, column, row, saved, entered, grad_resid, small, mp, factor):
    before, own, after = parts
    micro, rows, width = own.shape
    span = rows + 2 * HALO
    total = micro * rows
    c = w_qkv.shape[1] // mp
    g = w_out.shape[1] // mp
    per = lambda n: pl.BlockSpec((1, n, width), lambda i, k, *_: (i, 0, 0))
    tall = pl.BlockSpec((rows, width), lambda i, k, *_: (i, 0))
    return pl.pallas_call(
        backward_kernel(rows, mp, micro, g // HEAD_DIM, factor, blocked),
        name="attention_backward",
        grid_spec=pltpu.PrefetchScalarGridSpec(
            num_scalar_prefetch=1,
            grid=(micro, mp),
            in_specs=[
                per(HALO), per(rows), per(HALO),
                pl.BlockSpec((width, c), lambda i, k, *_: (0, k)),
                pl.BlockSpec((width, g), lambda i, k, *_: (0, k)),
                pl.BlockSpec((1, span, 1), lambda i, k, *_: (i, 0, 0)),
                pl.BlockSpec((1, 1, span), lambda i, k, *_: (i, 0, 0)),
                pl.BlockSpec((1, span, c), lambda i, k, *_: (i, 0, k)),
                tall,
                tall,
                whole(4, width),
            ],
            out_specs=[
                pl.BlockSpec((rows, c), lambda i, k, *_: (i, k)),
                tall,
                whole(16, width),
            ],
            scratch_shapes=[
                pltpu.VMEM((span, span), jnp.float32),
                pltpu.VMEM((rows, width), jnp.float32),
                pltpu.VMEM((span, g), LOW),
            ],
        ),
        out_shape=[
            jax.ShapeDtypeStruct((total, c * mp), LOW),
            jax.ShapeDtypeStruct((total, width), jnp.float32),
            jax.ShapeDtypeStruct((16, width), jnp.float32),
        ],
        compiler_params=params(),
        cost_estimate=cost(
            2 * micro * (span * width * width + rows * width * c * mp + 4 * span * span * width),
            50 * MEGA,
            micro * span * span * mp * g // HEAD_DIM,
        ),
    )(table, before, own, after, w_qkv, w_out, column, row, saved, entered, grad_resid, small)


def halo(value, count):
    before = lax.ppermute(value[:, -HALO:], "mp", [(i, i + 1) for i in range(count - 1)])
    after = lax.ppermute(value[:, :HALO], "mp", [(i + 1, i) for i in range(count - 1)])
    return before, value, after


def solution(mesh):
    plan = Plan(mesh)

    def body(latents, group_ids, pad_mask, w_qkv, w_out, w_up, w_down, norm_gain, norm_bias, out_grad):
        micro, rows, width = latents.shape
        total = micro * rows
        mp = plan.mp
        factor = HEAD_DIM ** (-0.5)
        small = jnp.concatenate([norm_gain, norm_bias], axis=0).T
        small = plan.gather_rows(small, plan.orders[0]).T.astype(jnp.float32)

        local_qkv = jnp.concatenate([w_qkv[t] for t in range(3)], axis=1)
        qkv = jnp.concatenate(plan.gather(local_qkv), axis=1)
        out = jnp.concatenate(plan.gather(w_out), axis=1)
        up = jnp.concatenate(plan.gather(w_up), axis=1)
        down = jnp.concatenate(plan.gather(w_down), axis=1)

        blocked = width // plan.dp % 128 == 0
        table = plan.own() ^ jnp.array(plan.relative, jnp.int32)
        rows_in = (latents.reshape(total, width), out_grad.reshape(total, width))
        if not blocked:
            rows_in = tuple(plan.enter(v) for v in rows_in)
        entered, grad_rows, grad_z, inputs_a = enter_norm(table, blocked, *rows_in, small)
        window = halo(inputs_a.reshape(micro, rows, width), mp)
        span = rows + 2 * HALO
        first = lax.axis_index("mp") * rows
        pads = ((0, 0), (HALO, HALO))
        groups = jnp.pad(group_ids[:, 0], pads, constant_values=-1)
        keys = jnp.where(jnp.pad(pad_mask[:, 0], pads) == 1, groups, -2)
        groups = lax.dynamic_slice_in_dim(groups, first, span, 1)
        keys = lax.dynamic_slice_in_dim(keys, first, span, 1)
        column, row = groups[:, :, None], keys[:, None, :]

        saved, attended, resid, inputs_c = forward_block(
            window, qkv, out, column, row, entered, small, mp, factor
        )
        hidden, slope = feed_up(inputs_c, up)

        def scatter(left, right):
            half, part = left.shape[1] // 2, right.shape[1] // 2

            def rows_of(i):
                other = right[:, i * part : (i + 1) * part]
                return lambda which: dot(left[:, which * half : (which + 1) * half], other, (0, 0))

            return plan.scatter([rows_of(0), rows_of(1)])

        grad_down = scatter(grad_z, hidden)
        latents_out = feed_down(table, blocked, hidden, down, resid)
        grad_upward, grad_resid, grad_branch, sums_two = feed_back(
            grad_z, down, up, slope, resid, grad_rows, small
        )
        grad_up = scatter(inputs_c, grad_upward)
        branch = halo(grad_branch.reshape(micro, rows, width), mp)
        grad_out = scatter(grad_branch, attended)
        grad_projected, latents_grad, sums_one = backward_block(
            table, blocked, branch, qkv, out, column, row, saved, entered, grad_resid, small, mp, factor
        )
        grad_qkv = scatter(inputs_a, grad_projected)
        grad_qkv = jnp.stack(jnp.split(grad_qkv, 3, axis=1))
        sums = jnp.stack([sums_one, sums_two], axis=0).reshape(2, 2, 8, width).sum(axis=2)
        sums = sums.transpose(1, 0, 2).reshape(4, width).T
        for bit in plan.major:
            half = sums.shape[0] // 2
            sums = sums[:half] + swap(sums[half:], bit, plan.dp)
        sums = lax.psum(sums, "mp").T
        if not blocked:
            latents_out, latents_grad = plan.leave(latents_out), plan.leave(latents_grad)
        shape = latents.shape
        return (
            latents_out.reshape(shape),
            latents_grad.reshape(shape),
            grad_qkv,
            grad_out,
            grad_up,
            grad_down,
            sums[:2],
            sums[2:],
        )

    return jax.shard_map(
        body,
        mesh=mesh,
        in_specs=(
            P(None, ("dp", "mp"), None),
            P(None, "dp", None),
            P(None, "dp", None),
            P(None, "dp", "mp"),
            P("dp", "mp"),
            P("dp", "mp"),
            P("dp", "mp"),
            P(None, "dp"),
            P(None, "dp"),
            P(None, ("dp", "mp"), None),
        ),
        out_specs=(
            P(None, ("dp", "mp"), None),
            P(None, ("dp", "mp"), None),
            P(None, "dp", "mp"),
            P("dp", "mp"),
            P("dp", "mp"),
            P("dp", "mp"),
            P(None, "dp"),
            P(None, "dp"),
        ),
        check_vma=False,
    )
```

time: 950 us -> 702 us (0.74)
  local copies, waits for them, and re-layouts: 240 us -> 45 us
  matrix products: 207 us -> 42.2 us
  Pallas kernels: 0 us -> 149 us
  other arithmetic: 61.5 us -> 33.3 us
    pallas_call x0 -> x6, Pallas kernels: none -> 149 us  [the longest x1 44 us: backward_block(): pl.pallas_call(backward_kernel(rows, mp, micro, g // HEAD_DIM, factor, bl...]
    dot_general x32 -> x16, matrix products: 127 us -> 42.2 us  [dot(): lax.dot_general(left, right, ((dims[:1], dims[1:]), ((), ())), preferred_...]
    slice x11 -> x2, local copies, waits for them, and re-layouts: 81.5 us -> 1.69 us  [halo(): value[:, :HALO]]
    sub x4 -> x0, matrix products: 55.7 us -> none  [the longest x2 32.7 us: body(): grad_scores = (probabilities * (grad_probs - weighted)).astype(LOW)]
    reshape x6 -> x1, local copies, waits for them, and re-layouts: 38.2 us -> 0.02 us  [body(): sums = sums.transpose(1, 0, 2).reshape(4, width).T]
    another operation x8 -> x0, local copies, waits for them, and re-layouts: 32.1 us -> none  [body(): grad_projected.append(jnp.stack(three, axis=2).reshape(total, -1))]
    another operation x8 -> x4, other arithmetic: 33 us -> 1.43 us
    dot_general x8 -> x0, matrix products: 24.9 us -> none  [the longest x2 6.7 us: body(): jnp.einsum('bhqk,bkhd->bqhd', probabilities[:, :, HALO:HALO + rows].astyp...]
  transfers between devices with their start and end apart: 118 -> 118, of which waited for: 44 -> 44; matrix products, arithmetic and copies ran while one was open for 48% -> 13% of each run, Pallas kernels for 0% -> 13%
where the time goes in v2:
time: 702 us; the launch traced here: 691 us
  waiting for transfers between devices  322 us (46%)
  Pallas kernels  149 us (21%)
  starting transfers between devices  86.3 us (12%)
  local copies, waits for them, and re-layouts  45 us (6%)
  matrix products  42.2 us (6%)
  other arithmetic  33.3 us (5%)
  blocking collectives  10.8 us (2%)
    ppermute x90, waiting for transfers between devices, swap(): return lax.ppermute(value, 'dp', [(i, i ^ bit) for i in range(count)])  235 us
    ppermute x24, waiting for transfers between devices, shift(): lax.ppermute(value, 'mp', [(i, (i + step) % count) for i in range(count)])  74.1 us
    ppermute x90, starting transfers between devices, swap(): return lax.ppermute(value, 'dp', [(i, i ^ bit) for i in range(count)])  46.7 us
    pallas_call x1, Pallas kernels, backward_block(): pl.pallas_call(backward_kernel(rows, mp, micro, g // HEAD_DIM, factor, bl...  44 us
    dot_general x16, matrix products, dot(): lax.dot_general(left, right, ((dims[:1], dims[1:]), ((), ())), preferred_...  42.2 us
    pallas_call x1, Pallas kernels, forward_block(): pl.pallas_call(forward_kernel(rows, mp, g // HEAD_DIM, factor), name='att...  35.3 us
    unnamed x124, local copies, waits for them, and re-layouts  30 us
    pallas_call x1, Pallas kernels, feed_back(): pl.pallas_call(feed_back_kernel(ff // tile), name='feed_back', grid=(ff /...  27.7 us
  transfers between devices with their start and end apart: 118, of which 44 were waited for; matrix products, arithmetic and copies ran while one was open for 13% of the time, Pallas kernels for 13%

profile of v2, /device:TPU:0, one launch (start us, length us, event | category | flops | bytes accessed | tf_op | source)
XLA Modules:
  0.0 690.9 jit_solution(12528108577354381191)
XLA Ops:
  1.8 2.6 collective-permute-start.1
  5.9 3.6 collective-permute-start.26
  20.8 3.1 collective-permute-done.2
  23.8 3.4 collective-permute-start.18
  31.3 9.3 %enter.1 = (f32[768,1024]{1,0:T(8,128)}, f32[768,1024]{1,0:T(8,128)}, bf16[768,1024]{1,0:T(8,128)(2,1)}, bf16[768,1024]{1,0:T(8,128)(2,1)}) custom-call(s32[8]{0:T(128)} %broadcast_xor_fusion.table_ref, f32[768,1024]{1,0:T(8,128)} %bitcast.170, f32[768,1024]{1,0:T(8,128)} %bitcast.171, f32[4,1024]{1,0:T(4,128)} %convert_bitcast_fusion.small), custom_call_target="tpu_custom_call" | custom-call | flops 12582912 | bytes 15728640 | tf_op jit(solution)/shard_map/enter/pallas_call | solution.py:218
  40.6 2.4 collective-permute-start.9
  45.8 2.3 collective-permute-done.36
  50.8 2.3 collective-permute-done.27
  53.1 2.0 collective-permute-start.43
  55.3 2.6 collective-permute-start.68
  60.0 29.6 %collective-permute-done.68 = bf16[128,1024]{1,0:T(8,128)(2,1)S(1)} collective-permute-done((bf16[128,1024]{1,0:T(8,128)(2,1)S(1)}, bf16[128,1024]{1,0:T(8,128)(2,1)S(1)}, u32[]{:S(2)}, u32[]{:S(2)}) %collective-permute-start.68) | collective-permute-done | bytes 262176 | tf_op jit(solution)/shard_map/ppermute | solution.py:25
  90.4 4.8 collective-permute-done.51
  97.3 5.4 collective-permute-start.7
  106.4 3.8 collective-permute-done.38
  112.2 4.9 collective-permute-done.29
  122.7 8.3 %collective-permute-done.10 = bf16[128,1536]{1,0:T(8,128)(2,1)S(1)} collective-permute-done((bf16[128,1536]{1,0:T(8,128)(2,1)S(1)}, bf16[128,1536]{1,0:T(8,128)(2,1)S(1)}, u32[]{:S(2)}, u32[]{:S(2)}) %collective-permute-start.10) | collective-permute-done | bytes 393248 | tf_op jit(solution)/shard_map/ppermute | solution.py:21
  131.3 1.8 collective-permute-start.70
  133.1 9.9 %collective-permute-done.19 = bf16[128,1536]{1,0:T(8,128)(2,1)S(1)} collective-permute-done((bf16[128,1536]{1,0:T(8,128)(2,1)S(1)}, bf16[128,1536]{1,0:T(8,128)(2,1)S(1)}, u32[]{:S(2)}, u32[]{:S(2)}) %collective-permute-start.19) | collective-permute-done | bytes 393248 | tf_op jit(solution)/shard_map/ppermute | solution.py:21
  144.4 9.9 %collective-permute-done.70 = bf16[128,2048]{1,0:T(8,128)(2,1)S(1)} collective-permute-done((bf16[128,2048]{1,0:T(8,128)(2,1)S(1)}, bf16[128,2048]{1,0:T(8,128)(2,1)S(1)}, u32[]{:S(2)}, u32[]{:S(2)}) %collective-permute-start.70) | collective-permute-done | bytes 524320 | tf_op jit(solution)/shard_map/ppermute | solution.py:21
  157.2 8.3 %collective-permute-done.53 = bf16[128,2048]{1,0:T(8,128)(2,1)S(1)} collective-permute-done((bf16[128,2048]{1,0:T(8,128)(2,1)S(1)}, bf16[128,2048]{1,0:T(8,128)(2,1)S(1)}, u32[]{:S(2)}, u32[]{:S(2)}) %collective-permute-start.53) | collective-permute-done | bytes 524320 | tf_op jit(solution)/shard_map/ppermute | solution.py:21
  168.5 8.3 %collective-permute-done.44 = bf16[128,2048]{1,0:T(8,128)(2,1)S(1)} collective-permute-done((bf16[128,2048]{1,0:T(8,128)(2,1)S(1)}, bf16[128,2048]{1,0:T(8,128)(2,1)S(1)}, u32[]{:S(2)}, u32[]{:S(2)}) %collective-permute-start.44) | collective-permute-done | bytes 524320 | tf_op jit(solution)/shard_map/ppermute | solution.py:21
  179.4 6.9 %collective-permute-done.61 = bf16[128,2048]{1,0:T(8,128)(2,1)S(1)} collective-permute-done((bf16[128,2048]{1,0:T(8,128)(2,1)S(1)}, bf16[128,2048]{1,0:T(8,128)(2,1)S(1)}, u32[]{:S(2)}, u32[]{:S(2)}) %collective-permute-start.61) | collective-permute-done | bytes 524320 | tf_op jit(solution)/shard_map/ppermute | solution.py:21
  189.0 6.7 collective-permute-done.12
  198.1 10.4 %collective-permute-done.21 = bf16[128,1536]{1,0:T(8,128)(2,1)S(1)} collective-permute-done((bf16[128,1536]{1,0:T(8,128)(2,1)S(1)}, bf16[128,1536]{1,0:T(8,128)(2,1)S(1)}, u32[]{:S(2)}, u32[]{:S(2)}) %collective-permute-start.21) | collective-permute-done | bytes 393248 | tf_op jit(solution)/shard_map/ppermute | solution.py:21
  210.9 12.1 %collective-permute-done.72 = bf16[128,2048]{1,0:T(8,128)(2,1)S(1)} collective-permute-done((bf16[128,2048]{1,0:T(8,128)(2,1)S(1)}, bf16[128,2048]{1,0:T(8,128)(2,1)S(1)}, u32[]{:S(2)}, u32[]{:S(2)}) %collective-permute-start.72) | collective-permute-done | bytes 524320 | tf_op jit(solution)/shard_map/ppermute | solution.py:21
  227.2 11.0 %collective-permute-done.55 = bf16[128,2048]{1,0:T(8,128)(2,1)S(1)} collective-permute-done((bf16[128,2048]{1,0:T(8,128)(2,1)S(1)}, bf16[128,2048]{1,0:T(8,128)(2,1)S(1)}, u32[]{:S(2)}, u32[]{:S(2)}) %collective-permute-start.55) | collective-permute-done | bytes 524320 | tf_op jit(solution)/shard_map/ppermute | solution.py:21
  243.2 10.2 %collective-permute-done.46 = bf16[128,2048]{1,0:T(8,128)(2,1)S(1)} collective-permute-done((bf16[128,2048]{1,0:T(8,128)(2,1)S(1)}, bf16[128,2048]{1,0:T(8,128)(2,1)S(1)}, u32[]{:S(2)}, u32[]{:S(2)}) %collective-permute-start.46) | collective-permute-done | bytes 524320 | tf_op jit(solution)/shard_map/ppermute | solution.py:21
  258.4 10.2 %collective-permute-done.63 = bf16[128,2048]{1,0:T(8,128)(2,1)S(1)} collective-permute-done((bf16[128,2048]{1,0:T(8,128)(2,1)S(1)}, bf16[128,2048]{1,0:T(8,128)(2,1)S(1)}, u32[]{:S(2)}, u32[]{:S(2)}) %collective-permute-start.63) | collective-permute-done | bytes 524320 | tf_op jit(solution)/shard_map/ppermute | solution.py:21
  273.6 3.6 pad_maximum_fusion.2.w_qkv
  277.3 35.3 %attention_forward.1 = (bf16[3,512,3072]{2,1,0:T(8,128)(2,1)}, bf16[768,1024]{1,0:T(8,128)(2,1)}, f32[768,1024]{1,0:T(8,128)}, bf16[768,1024]{1,0:T(8,128)(2,1)}) custom-call(bf16[3,128,1024]{2,1,0:T(8,128)(2,1)} %collective-permute-done.7.before, bf16[3,256,1024]{2,1,0:T(8,128)(2,1)} %bitcast.181, bf16[3,128,1024]{2,1,0:T(8,128)(2,1)} %collective-permute-done.8.after, ...), custom_call_target="tpu_custom_call" | custom-call | flops 12884901888 | bytes 41943040 | tf_op jit(solution)/shard_map/attention_forward/pallas_call | solution.py:294
  315.1 7.8 %pad_maximum_fusion.weight.up = bf16[1024,4096]{1,0:T(8,128)(2,1)} fusion(bf16[1024,2048]{1,0:T(8,128)(2,1)} %constant_dynamic-update-slice_fusion.62, bf16[1024,2048]{1,0:T(8,128)(2,1)} %constant_dynamic-update-slice_fusion.51), kind=kLoop, calls=%fused_computation | loop fusion | flops 16777216 | bytes 16777216 | tf_op jit(solution)/shard_map/concatenate | solution.py:585
  323.7 7.8 %pad_maximum_fusion.1.weight.down = bf16[1024,4096]{1,0:T(8,128)(2,1)} fusion(bf16[1024,2048]{1,0:T(8,128)(2,1)} %constant_dynamic-update-slice_fusion.84, bf16[1024,2048]{1,0:T(8,128)(2,1)} %constant_dynamic-update-slice_fusion.73), kind=kLoop, calls=%fused_computation.1 | loop fusion | flops 16777216 | bytes 16777216 | tf_op jit(solution)/shard_map/concatenate | solution.py:586
  331.6 16.6 %feed_up.1 = (bf16[768,4096]{1,0:T(8,128)(2,1)}, bf16[768,4096]{1,0:T(8,128)(2,1)}) custom-call(bf16[768,1024]{1,0:T(8,128)(2,1)} %get-tuple-element.27.inputs, bf16[1024,4096]{1,0:T(8,128)(2,1)} %pad_maximum_fusion.weight.up), custom_call_target="tpu_custom_call" | custom-call | flops 6442450944 | bytes 20971520 | tf_op jit(solution)/shard_map/feed_up/pallas_call | solution.py:344
  348.1 27.7 %feed_back.1 = (bf16[768,4096]{1,0:T(8,128)(2,1)}, f32[768,1024]{1,0:T(8,128)}, bf16[768,1024]{1,0:T(8,128)(2,1)}, f32[16,1024]{1,0:T(8,128)}) custom-call(bf16[768,1024]{1,0:T(8,128)(2,1)} %get-tuple-element.30.grad_z, bf16[1024,4096]{1,0:T(8,128)(2,1)} %pad_maximum_fusion.1.weight.down, bf16[1024,4096]{1,0:T(8,128)(2,1)} %pad_maximum_fusion.weight.up, ...), custom_call_target="tpu_custom_call" | custom-call | flops 12884901888 | bytes 40370176 | tf_op jit(solution)/shard_map/feed_back/pallas_call | solution.py:440
  375.8 2.7 convolution_convert_fusion.6
  378.5 2.5 convolution_convert_fusion.7
  381.1 3.2 convolution_convert_fusion.3
  384.3 3.2 convolution_convert_fusion.2
  387.5 16.7 %feed_down.1 = f32[768,1024]{1,0:T(8,128)} custom-call(s32[8]{0:T(128)} %broadcast_xor_fusion.table_ref, bf16[768,4096]{1,0:T(8,128)(2,1)} %get-tuple-element.28.hidden, bf16[1024,4096]{1,0:T(8,128)(2,1)} %pad_maximum_fusion.1.weight.down, f32[768,1024]{1,0:T(8,128)} %get-tuple-element.29.resid), custom_call_target="tpu_custom_call" | custom-call | flops 6442450944 | bytes 20971520 | tf_op jit(solution)/shard_map/feed_down/pallas_call | solution.py:382
  404.3 3.2 convolution_convert_fusion.1
  408.1 3.2 convolution_convert_fusion
  412.8 4.6 collective-permute-start.77
  420.2 13.0 %collective-permute-done.78.after = bf16[3,128,1024]{2,1,0:T(8,128)(2,1)S(1)} collective-permute-done((bf16[3,128,1024]{2,1,0:T(8,128)(2,1)S(1)}, bf16[3,128,1024]{2,1,0:T(8,128)(2,1)S(1)}, u32[]{:S(2)}, u32[]{:S(2)}) %collective-permute-start.78) | collective-permute-done | bytes 786464 | tf_op jit(solution)/shard_map/ppermute | solution.py:567
  435.3 44.0 %attention_backward.1 = (bf16[768,3072]{1,0:T(8,128)(2,1)}, f32[768,1024]{1,0:T(8,128)}, f32[16,1024]{1,0:T(8,128)}) custom-call(s32[8]{0:T(128)} %broadcast_xor_fusion.table_ref, bf16[3,128,1024]{2,1,0:T(8,128)(2,1)} %copy-done.17, bf16[3,256,1024]{2,1,0:T(8,128)(2,1)} %bitcast.182, bf16[3,128,1024]{2,1,0:T(8,128)(2,1)} %copy-done.16, ...), custom_call_target="tpu_custom_call" | custom-call | flops 14495514624 | bytes 52428800 | tf_op jit(solution)/shard_map/attention_backward/pallas_call | solution.py:523
  480.3 4.6 convolution_convert_fusion.5
  484.9 2.6 convolution_convert_fusion.4
  492.4 2.4 collective-permute-done.116
  495.7 2.7 collective-permute-done.117
  499.6 10.8 %psum.7 = f32[4,128]{1,0:T(4,128)S(1)} all-reduce(f32[4,128]{1,0:T(4,128)S(1)} %fusion.77), channel_id=1, replica_groups=mesh['dp'=8,'mp'=4] {'mp'}, use_global_device_ids=true, to_apply=%region_1.2 | all-reduce | flops 512 | bytes 4096 | tf_op jit(solution)/shard_map/psum | solution.py:636
  512.3 4.3 collective-permute-done.91
  517.9 3.1 collective-permute-done.96
  522.2 4.8 convert_add_fusion
  528.5 4.1 convert_add_fusion.2
  534.0 1.9 convert_add_fusion.1
  538.1 1.9 convert_add_fusion.3
  545.7 51.8 %collective-permute-done.84 = bf16[256,1536]{1,0:T(8,128)(2,1)S(1)} collective-permute-done((bf16[256,1536]{1,0:T(8,128)(2,1)S(1)}, bf16[256,1536]{1,0:T(8,128)(2,1)S(1)}, u32[]{:S(2)}, u32[]{:S(2)}) %collective-permute-start.84) | collective-permute-done | bytes 786464 | tf_op jit(solution)/shard_map/ppermute | solution.py:21
  598.6 17.5 %collective-permute-done.80 = bf16[256,1536]{1,0:T(8,128)(2,1)S(1)} collective-permute-done((bf16[256,1536]{1,0:T(8,128)(2,1)S(1)}, bf16[256,1536]{1,0:T(8,128)(2,1)S(1)}, u32[]{:S(2)}, u32[]{:S(2)}) %collective-permute-start.80) | collective-permute-done | bytes 786464 | tf_op jit(solution)/shard_map/ppermute | solution.py:21
  623.5 4.7 collective-permute-done.85
  629.5 11.1 %collective-permute-done.108 = bf16[128,2048]{1,0:T(8,128)(2,1)S(1)} collective-permute-done((bf16[128,2048]{1,0:T(8,128)(2,1)S(1)}, bf16[128,2048]{1,0:T(8,128)(2,1)S(1)}, u32[]{:S(2)}, u32[]{:S(2)}) %collective-permute-start.108) | collective-permute-done | bytes 524320 | tf_op jit(solution)/shard_map/ppermute | solution.py:21
  643.0 5.8 collective-permute-done.99
  649.0 2.1 collective-permute-start.114
  651.6 2.6 collective-permute-start.104
  656.9 13.5 %collective-permute-done.113 = bf16[128,1024]{1,0:T(8,128)(2,1)S(1)} collective-permute-done((bf16[128,1024]{1,0:T(8,128)(2,1)S(1)}, bf16[128,1024]{1,0:T(8,128)(2,1)S(1)}, u32[]{:S(2)}, u32[]{:S(2)}) %collective-permute-start.113) | collective-permute-done | bytes 262176 | tf_op jit(solution)/shard_map/ppermute | solution.py:25
  671.4 18.1 %collective-permute-done.104 = bf16[128,1024]{1,0:T(8,128)(2,1)S(1)} collective-permute-done((bf16[128,1024]{1,0:T(8,128)(2,1)S(1)}, bf16[128,1024]{1,0:T(8,128)(2,1)S(1)}, u32[]{:S(2)}, u32[]{:S(2)}) %collective-permute-start.104) | collective-permute-done | bytes 262176 | tf_op jit(solution)/shard_map/ppermute | solution.py:25
  (415 shorter events, 127.1 us)
Async XLA Ops:
  1.4 25.8 %collective-permute-start.3 = (bf16[128,4]{0,1:T(4,128)(2,1)S(1)}, bf16[128,4]{0,1:T(4,128)(2,1)S(1)}, u32[]{:S(2)}, u32[]{:S(2)}) collective-permute-start(bf16[128,4]{0,1:T(4,128)(2,1)S(1)} %maximum_bitcast_fusion), channel_id=1, source_target_pairs={{0,4},{4,0},{8,12},{12,8},{16,20},{20,16},{24,28},{28,24},{1,5},{5... | collective-permute-start | bytes 3080 | tf_op jit(solution)/shard_map/ppermute | solution.py:21
  1.8 18.4 %collective-permute-start.1 = (bf16[128,4]{0,1:T(4,128)(2,1)S(1)}, bf16[128,4]{0,1:T(4,128)(2,1)S(1)}, u32[]{:S(2)}, u32[]{:S(2)}) collective-permute-start(bf16[128,4]{0,1:T(4,128)(2,1)S(1)} %maximum_bitcast_fusion), channel_id=1, source_target_pairs={{0,16},{4,20},{8,24},{12,28},{16,0},{20,4},{24,8},{28,12},{1,17},{... | collective-permute-start | bytes 3080 | tf_op jit(solution)/shard_map/ppermute | solution.py:21
  4.4 14.9 %collective-permute-start = (bf16[128,4]{0,1:T(4,128)(2,1)S(1)}, bf16[128,4]{0,1:T(4,128)(2,1)S(1)}, u32[]{:S(2)}, u32[]{:S(2)}) collective-permute-start(bf16[128,4]{0,1:T(4,128)(2,1)S(1)} %maximum_bitcast_fusion), channel_id=1, source_target_pairs={{0,8},{4,12},{8,0},{12,4},{16,24},{20,28},{24,16},{28,20},{1,9},{5... | collective-permute-start | bytes 3080 | tf_op jit(solution)/shard_map/ppermute | solution.py:21
  5.9 39.3 %collective-permute-start.26 = (bf16[128,256]{1,0:T(8,128)(2,1)}, bf16[128,256]{1,0:T(8,128)(2,1)S(1)}, u32[]{:S(2)}, u32[]{:S(2)}) collective-permute-start(bf16[128,256]{1,0:T(8,128)(2,1)} %param.15), channel_id=1, source_target_pairs={{0,3},{1,0},{2,1},{3,2},{4,7},{5,4},{6,5},{7,6},{8,11},{9,8},{10,9... | collective-permute-start | bytes 196616 | tf_op jit(solution)/shard_map/ppermute | solution.py:25
  9.5 33.5 %collective-permute-start.35 = (bf16[128,256]{1,0:T(8,128)(2,1)}, bf16[128,256]{1,0:T(8,128)(2,1)S(1)}, u32[]{:S(2)}, u32[]{:S(2)}) collective-permute-start(bf16[128,256]{1,0:T(8,128)(2,1)} %param.15), channel_id=1, source_target_pairs={{0,1},{1,2},{2,3},{3,0},{4,5},{5,6},{6,7},{7,4},{8,9},{9,10},{10,1... | collective-permute-start | bytes 196616 | tf_op jit(solution)/shard_map/ppermute | solution.py:25
  19.3 21.3 %collective-permute-start.34 = (bf16[128,256]{1,0:T(8,128)(2,1)S(1)}, bf16[128,256]{1,0:T(8,128)(2,1)S(1)}, u32[]{:S(2)}, u32[]{:S(2)}) collective-permute-start(bf16[128,256]{1,0:T(8,128)(2,1)S(1)} %copy-done.14), channel_id=1, source_target_pairs={{0,2},{1,3},{2,0},{3,1},{4,6},{5,7},{6,4},{7,5},{8,10},{9,11},{10,... | collective-permute-start | bytes 196616 | tf_op jit(solution)/shard_map/ppermute | solution.py:25
  23.8 34.6 %collective-permute-start.18 = (bf16[128,768]{1,0:T(8,128)(2,1)S(1)}, bf16[128,768]{1,0:T(8,128)(2,1)S(1)}, u32[]{:S(2)}, u32[]{:S(2)}) collective-permute-start(bf16[128,768]{1,0:T(8,128)(2,1)S(1)} %pad_maximum_fusion.6), channel_id=1, source_target_pairs={{0,1},{1,2},{2,3},{3,0},{4,5},{5,6},{6,7},{7,4},{8,9},{9,10},{10,1... | collective-permute-start | bytes 589832 | tf_op jit(solution)/shard_map/ppermute | solution.py:25
  30.6 27.3 %collective-permute-start.17 = (bf16[128,768]{1,0:T(8,128)(2,1)S(1)}, bf16[128,768]{1,0:T(8,128)(2,1)S(1)}, u32[]{:S(2)}, u32[]{:S(2)}) collective-permute-start(bf16[128,768]{1,0:T(8,128)(2,1)S(1)} %pad_maximum_fusion.6), channel_id=1, source_target_pairs={{0,2},{1,3},{2,0},{3,1},{4,6},{5,7},{6,4},{7,5},{8,10},{9,11},{10,... | collective-permute-start | bytes 589832 | tf_op jit(solution)/shard_map/ppermute | solution.py:25
  40.6 14.7 %collective-permute-start.9 = (bf16[128,768]{1,0:T(8,128)(2,1)S(1)}, bf16[128,768]{1,0:T(8,128)(2,1)S(1)}, u32[]{:S(2)}, u32[]{:S(2)}) collective-permute-start(bf16[128,768]{1,0:T(8,128)(2,1)S(1)} %pad_maximum_fusion.6), channel_id=1, source_target_pairs={{0,3},{1,0},{2,1},{3,2},{4,7},{5,4},{6,5},{7,6},{8,11},{9,8},{10,9... | collective-permute-start | bytes 589832 | tf_op jit(solution)/shard_map/ppermute | solution.py:25
  53.1 51.2 %collective-permute-start.43 = (bf16[128,1024]{1,0:T(8,128)(2,1)S(1)}, bf16[128,1024]{1,0:T(8,128)(2,1)S(1)}, u32[]{:S(2)}, u32[]{:S(2)}) collective-permute-start(bf16[128,1024]{1,0:T(8,128)(2,1)S(1)} %copy-done.11), channel_id=1, source_target_pairs={{0,3},{1,0},{2,1},{3,2},{4,7},{5,4},{6,5},{7,6},{8,11},{9,8},{10,9... | collective-permute-start | bytes 786440 | tf_op jit(solution)/shard_map/ppermute | solution.py:25
  55.2 48.3 %collective-permute-start.52 = (bf16[128,1024]{1,0:T(8,128)(2,1)S(1)}, bf16[128,1024]{1,0:T(8,128)(2,1)S(1)}, u32[]{:S(2)}, u32[]{:S(2)}) collective-permute-start(bf16[128,1024]{1,0:T(8,128)(2,1)S(1)} %copy-done.11), channel_id=1, source_target_pairs={{0,1},{1,2},{2,3},{3,0},{4,5},{5,6},{6,7},{7,4},{8,9},{9,10},{10,1... | collective-permute-start | bytes 786440 | tf_op jit(solution)/shard_map/ppermute | solution.py:25
  55.3 34.3 %collective-permute-start.68 = (bf16[128,1024]{1,0:T(8,128)(2,1)S(1)}, bf16[128,1024]{1,0:T(8,128)(2,1)S(1)}, u32[]{:S(2)}, u32[]{:S(2)}) collective-permute-start(bf16[128,1024]{1,0:T(8,128)(2,1)S(1)} %copy-done.12), channel_id=1, source_target_pairs={{0,2},{1,3},{2,0},{3,1},{4,6},{5,7},{6,4},{7,5},{8,10},{9,11},{10,... | collective-permute-start | bytes 786440 | tf_op jit(solution)/shard_map/ppermute | solution.py:25
  57.9 37.2 %collective-permute-start.51 = (bf16[128,1024]{1,0:T(8,128)(2,1)S(1)}, bf16[128,1024]{1,0:T(8,128)(2,1)S(1)}, u32[]{:S(2)}, u32[]{:S(2)}) collective-permute-start(bf16[128,1024]{1,0:T(8,128)(2,1)S(1)} %copy-done.11), channel_id=1, source_target_pairs={{0,2},{1,3},{2,0},{3,1},{4,6},{5,7},{6,4},{7,5},{8,10},{9,11},{10,... | collective-permute-start | bytes 786440 | tf_op jit(solution)/shard_map/ppermute | solution.py:25
  58.4 38.9 %collective-permute-start.69 = (bf16[128,1024]{1,0:T(8,128)(2,1)S(1)}, bf16[128,1024]{1,0:T(8,128)(2,1)S(1)}, u32[]{:S(2)}, u32[]{:S(2)}) collective-permute-start(bf16[128,1024]{1,0:T(8,128)(2,1)S(1)} %copy-done.12), channel_id=1, source_target_pairs={{0,1},{1,2},{2,3},{3,0},{4,5},{5,6},{6,7},{7,4},{8,9},{9,10},{10,1... | collective-permute-start | bytes 786440 | tf_op jit(solution)/shard_map/ppermute | solution.py:25
  89.6 15.6 %collective-permute-start.60 = (bf16[128,1024]{1,0:T(8,128)(2,1)S(1)}, bf16[128,1024]{1,0:T(8,128)(2,1)S(1)}, u32[]{:S(2)}, u32[]{:S(2)}) collective-permute-start(bf16[128,1024]{1,0:T(8,128)(2,1)S(1)} %copy-done.12), channel_id=1, source_target_pairs={{0,3},{1,0},{2,1},{3,2},{4,7},{5,4},{6,5},{7,6},{8,11},{9,8},{10,9... | collective-permute-start | bytes 786440 | tf_op jit(solution)/shard_map/ppermute | solution.py:25
  95.2 182.1 %collective-permute-start.8 = (bf16[3,128,1024]{2,1,0:T(8,128)(2,1)S(1)}, bf16[3,128,1024]{2,1,0:T(8,128)(2,1)}, u32[]{:S(2)}, u32[]{:S(2)}) collective-permute-start(bf16[3,128,1024]{2,1,0:T(8,128)(2,1)S(1)} %get-tuple-element.44), channel_id=1, source_target_pairs={{1,0},{2,1},{3,2},{5,4},{6,5},{7,6},{9,8},{10,9},{11,10},{13,12},{... | collective-permute-start | bytes 2359304 | tf_op jit(solution)/shard_map/ppermute | solution.py:567
  97.3 180.0 %collective-permute-start.7 = (bf16[3,128,1024]{2,1,0:T(8,128)(2,1)S(1)}, bf16[3,128,1024]{2,1,0:T(8,128)(2,1)}, u32[]{:S(2)}, u32[]{:S(2)}) collective-permute-start(bf16[3,128,1024]{2,1,0:T(8,128)(2,1)S(1)} %get-tuple-element.45), channel_id=1, source_target_pairs={{0,1},{1,2},{2,3},{4,5},{5,6},{6,7},{8,9},{9,10},{10,11},{12,13},{... | collective-permute-start | bytes 2359304 | tf_op jit(solution)/shard_map/ppermute | solution.py:566
  117.1 14.2 %collective-permute-start.11 = (bf16[128,1536]{1,0:T(8,128)(2,1)S(1)}, bf16[128,1536]{1,0:T(8,128)(2,1)S(1)}, u32[]{:S(2)}, u32[]{:S(2)}) collective-permute-start(bf16[128,1536]{1,0:T(8,128)(2,1)S(1)} %get-tuple-element.55), channel_id=1, source_target_pairs={{0,16},{4,20},{8,24},{12,28},{16,0},{20,4},{24,8},{28,12},{1,17},{... | collective-permute-start | bytes 1179656 | tf_op jit(solution)/shard_map/ppermute | solution.py:21
  120.1 23.9 %collective-permute-start.20 = (bf16[128,1536]{1,0:T(8,128)(2,1)S(1)}, bf16[128,1536]{1,0:T(8,128)(2,1)S(1)}, u32[]{:S(2)}, u32[]{:S(2)}) collective-permute-start(bf16[128,1536]{1,0:T(8,128)(2,1)S(1)} %get-tuple-element.73), channel_id=1, source_target_pairs={{0,16},{4,20},{8,24},{12,28},{16,0},{20,4},{24,8},{28,12},{1,17},{... | collective-permute-start | bytes 1179656 | tf_op jit(solution)/shard_map/ppermute | solution.py:21
  131.3 23.0 %collective-permute-start.70 = (bf16[128,2048]{1,0:T(8,128)(2,1)S(1)}, bf16[128,2048]{1,0:T(8,128)(2,1)S(1)}, u32[]{:S(2)}, u32[]{:S(2)}) collective-permute-start(bf16[128,2048]{1,0:T(8,128)(2,1)S(1)} %get-tuple-element.61), channel_id=1, source_target_pairs={{0,8},{4,12},{8,0},{12,4},{16,24},{20,28},{24,16},{28,20},{1,9},{5... | collective-permute-start | bytes 1572872 | tf_op jit(solution)/shard_map/ppermute | solution.py:21
  144.0 21.5 %collective-permute-start.53 = (bf16[128,2048]{1,0:T(8,128)(2,1)S(1)}, bf16[128,2048]{1,0:T(8,128)(2,1)S(1)}, u32[]{:S(2)}, u32[]{:S(2)}) collective-permute-start(bf16[128,2048]{1,0:T(8,128)(2,1)S(1)} %get-tuple-element.69), channel_id=1, source_target_pairs={{0,8},{4,12},{8,0},{12,4},{16,24},{20,28},{24,16},{28,20},{1,9},{5... | collective-permute-start | bytes 1572872 | tf_op jit(solution)/shard_map/ppermute | solution.py:21
  156.1 20.7 %collective-permute-start.44 = (bf16[128,2048]{1,0:T(8,128)(2,1)S(1)}, bf16[128,2048]{1,0:T(8,128)(2,1)S(1)}, u32[]{:S(2)}, u32[]{:S(2)}) collective-permute-start(bf16[128,2048]{1,0:T(8,128)(2,1)S(1)} %get-tuple-element.65), channel_id=1, source_target_pairs={{0,8},{4,12},{8,0},{12,4},{16,24},{20,28},{24,16},{28,20},{1,9},{5... | collective-permute-start | bytes 1572872 | tf_op jit(solution)/shard_map/ppermute | solution.py:21
  167.3 18.9 %collective-permute-start.61 = (bf16[128,2048]{1,0:T(8,128)(2,1)S(1)}, bf16[128,2048]{1,0:T(8,128)(2,1)S(1)}, u32[]{:S(2)}, u32[]{:S(2)}) collective-permute-start(bf16[128,2048]{1,0:T(8,128)(2,1)S(1)} %get-tuple-element.57), channel_id=1, source_target_pairs={{0,8},{4,12},{8,0},{12,4},{16,24},{20,28},{24,16},{28,20},{1,9},{5... | collective-permute-start | bytes 1572872 | tf_op jit(solution)/shard_map/ppermute | solution.py:21
  178.5 17.2 %collective-permute-start.13 = (bf16[128,1536]{1,0:T(8,128)(2,1)S(1)}, bf16[128,1536]{1,0:T(8,128)(2,1)S(1)}, u32[]{:S(2)}, u32[]{:S(2)}) collective-permute-start(bf16[128,1536]{1,0:T(8,128)(2,1)S(1)} %get-tuple-element.55), channel_id=1, source_target_pairs={{0,4},{4,0},{8,12},{12,8},{16,20},{20,16},{24,28},{28,24},{1,5},{5... | collective-permute-start | bytes 1179656 | tf_op jit(solution)/shard_map/ppermute | solution.py:21
  188.2 20.4 %collective-permute-start.22 = (bf16[128,1536]{1,0:T(8,128)(2,1)S(1)}, bf16[128,1536]{1,0:T(8,128)(2,1)S(1)}, u32[]{:S(2)}, u32[]{:S(2)}) collective-permute-start(bf16[128,1536]{1,0:T(8,128)(2,1)S(1)} %get-tuple-element.73), channel_id=1, source_target_pairs={{0,4},{4,0},{8,12},{12,8},{16,20},{20,16},{24,28},{28,24},{1,5},{5... | collective-permute-start | bytes 1179656 | tf_op jit(solution)/shard_map/ppermute | solution.py:21
  208.6 14.4 %collective-permute-start.72 = (bf16[128,2048]{1,0:T(8,128)(2,1)S(1)}, bf16[128,2048]{1,0:T(8,128)(2,1)S(1)}, u32[]{:S(2)}, u32[]{:S(2)}) collective-permute-start(bf16[128,2048]{1,0:T(8,128)(2,1)S(1)} %collective-permute-done.71), channel_id=1, source_target_pairs={{0,8},{4,12},{8,0},{12,4},{16,24},{20,28},{24,16},{28,20},{1,9},{5... | collective-permute-start | bytes 1572872 | tf_op jit(solution)/shard_map/ppermute | solution.py:21
  210.5 14.5 %collective-permute-start.74 = (bf16[128,2048]{1,0:T(8,128)(2,1)S(1)}, bf16[128,2048]{1,0:T(8,128)(2,1)S(1)}, u32[]{:S(2)}, u32[]{:S(2)}) collective-permute-start(bf16[128,2048]{1,0:T(8,128)(2,1)S(1)} %collective-permute-done.70), channel_id=1, source_target_pairs={{0,4},{4,0},{8,12},{12,8},{16,20},{20,16},{24,28},{28,24},{1,5},{5... | collective-permute-start | bytes 1572872 | tf_op jit(solution)/shard_map/ppermute | solution.py:21
  223.9 14.3 %collective-permute-start.55 = (bf16[128,2048]{1,0:T(8,128)(2,1)S(1)}, bf16[128,2048]{1,0:T(8,128)(2,1)S(1)}, u32[]{:S(2)}, u32[]{:S(2)}) collective-permute-start(bf16[128,2048]{1,0:T(8,128)(2,1)S(1)} %collective-permute-done.54), channel_id=1, source_target_pairs={{0,8},{4,12},{8,0},{12,4},{16,24},{20,28},{24,16},{28,20},{1,9},{5... | collective-permute-start | bytes 1572872 | tf_op jit(solution)/shard_map/ppermute | solution.py:21
  226.1 15.0 %collective-permute-start.57 = (bf16[128,2048]{1,0:T(8,128)(2,1)S(1)}, bf16[128,2048]{1,0:T(8,128)(2,1)S(1)}, u32[]{:S(2)}, u32[]{:S(2)}) collective-permute-start(bf16[128,2048]{1,0:T(8,128)(2,1)S(1)} %collective-permute-done.53), channel_id=1, source_target_pairs={{0,4},{4,0},{8,12},{12,8},{16,20},{20,16},{24,28},{28,24},{1,5},{5... | collective-permute-start | bytes 1572872 | tf_op jit(solution)/shard_map/ppermute | solution.py:21
  239.1 14.3 %collective-permute-start.46 = (bf16[128,2048]{1,0:T(8,128)(2,1)S(1)}, bf16[128,2048]{1,0:T(8,128)(2,1)S(1)}, u32[]{:S(2)}, u32[]{:S(2)}) collective-permute-start(bf16[128,2048]{1,0:T(8,128)(2,1)S(1)} %collective-permute-done.44), channel_id=1, source_target_pairs={{0,16},{4,20},{8,24},{12,28},{16,0},{20,4},{24,8},{28,12},{1,17},{... | collective-permute-start | bytes 1572872 | tf_op jit(solution)/shard_map/ppermute | solution.py:21
  242.1 14.1 %collective-permute-start.48 = (bf16[128,2048]{1,0:T(8,128)(2,1)S(1)}, bf16[128,2048]{1,0:T(8,128)(2,1)S(1)}, u32[]{:S(2)}, u32[]{:S(2)}) collective-permute-start(bf16[128,2048]{1,0:T(8,128)(2,1)S(1)} %collective-permute-done.44), channel_id=1, source_target_pairs={{0,4},{4,0},{8,12},{12,8},{16,20},{20,16},{24,28},{28,24},{1,5},{5... | collective-permute-start | bytes 1572872 | tf_op jit(solution)/shard_map/ppermute | solution.py:21
  254.2 14.3 %collective-permute-start.63 = (bf16[128,2048]{1,0:T(8,128)(2,1)S(1)}, bf16[128,2048]{1,0:T(8,128)(2,1)S(1)}, u32[]{:S(2)}, u32[]{:S(2)}) collective-permute-start(bf16[128,2048]{1,0:T(8,128)(2,1)S(1)} %collective-permute-done.61), channel_id=1, source_target_pairs={{0,16},{4,20},{8,24},{12,28},{16,0},{20,4},{24,8},{28,12},{1,17},{... | collective-permute-start | bytes 1572872 | tf_op jit(solution)/shard_map/ppermute | solution.py:21
  271.6 40.9 %collective-permute-start.76 = (bf16[128,2048]{1,0:T(8,128)(2,1)S(1)}, bf16[128,2048]{1,0:T(8,128)(2,1)S(1)}, u32[]{:S(2)}, u32[]{:S(2)}) collective-permute-start(bf16[128,2048]{1,0:T(8,128)(2,1)S(1)} %collective-permute-done.72), channel_id=1, source_target_pairs={{0,4},{4,0},{8,12},{12,8},{16,20},{20,16},{24,28},{28,24},{1,5},{5... | collective-permute-start | bytes 1572872 | tf_op jit(solution)/shard_map/ppermute | solution.py:21
  273.0 40.4 %collective-permute-start.59 = (bf16[128,2048]{1,0:T(8,128)(2,1)S(1)}, bf16[128,2048]{1,0:T(8,128)(2,1)S(1)}, u32[]{:S(2)}, u32[]{:S(2)}) collective-permute-start(bf16[128,2048]{1,0:T(8,128)(2,1)S(1)} %collective-permute-done.55), channel_id=1, source_target_pairs={{0,4},{4,0},{8,12},{12,8},{16,20},{20,16},{24,28},{28,24},{1,5},{5... | collective-permute-start | bytes 1572872 | tf_op jit(solution)/shard_map/ppermute | solution.py:21
  273.0 41.2 %collective-permute-start.50 = (bf16[128,2048]{1,0:T(8,128)(2,1)S(1)}, bf16[128,2048]{1,0:T(8,128)(2,1)S(1)}, u32[]{:S(2)}, u32[]{:S(2)}) collective-permute-start(bf16[128,2048]{1,0:T(8,128)(2,1)S(1)} %collective-permute-done.46), channel_id=1, source_target_pairs={{0,4},{4,0},{8,12},{12,8},{16,20},{20,16},{24,28},{28,24},{1,5},{5... | collective-permute-start | bytes 1572872 | tf_op jit(solution)/shard_map/ppermute | solution.py:21
  277.2 45.6 %collective-permute-start.67 = (bf16[128,2048]{1,0:T(8,128)(2,1)S(1)}, bf16[128,2048]{1,0:T(8,128)(2,1)S(1)}, u32[]{:S(2)}, u32[]{:S(2)}) collective-permute-start(bf16[128,2048]{1,0:T(8,128)(2,1)S(1)} %collective-permute-done.63), channel_id=1, source_target_pairs={{0,4},{4,0},{8,12},{12,8},{16,20},{20,16},{24,28},{28,24},{1,5},{5... | collective-permute-start | bytes 1572872 | tf_op jit(solution)/shard_map/ppermute | solution.py:21
  411.3 21.9 %collective-permute-start.78 = (bf16[3,128,1024]{2,1,0:T(8,128)(2,1)S(1)}, bf16[3,128,1024]{2,1,0:T(8,128)(2,1)S(1)}, u32[]{:S(2)}, u32[]{:S(2)}) collective-permute-start(bf16[3,128,1024]{2,1,0:T(8,128)(2,1)S(1)} %get-tuple-element.42), channel_id=1, source_target_pairs={{1,0},{2,1},{3,2},{5,4},{6,5},{7,6},{9,8},{10,9},{11,10},{13,12},{... | collective-permute-start | bytes 2359304 | tf_op jit(solution)/shard_map/ppermute | solution.py:567
  412.8 21.7 %collective-permute-start.77 = (bf16[3,128,1024]{2,1,0:T(8,128)(2,1)S(1)}, bf16[3,128,1024]{2,1,0:T(8,128)(2,1)S(1)}, u32[]{:S(2)}, u32[]{:S(2)}) collective-permute-start(bf16[3,128,1024]{2,1,0:T(8,128)(2,1)S(1)} %get-tuple-element.43), channel_id=1, source_target_pairs={{0,1},{1,2},{2,3},{4,5},{5,6},{6,7},{8,9},{9,10},{10,11},{12,13},{... | collective-permute-start | bytes 2359304 | tf_op jit(solution)/shard_map/ppermute | solution.py:566
  417.4 104.3 %collective-permute-start.110 = (bf16[512,2048]{1,0:T(8,128)(2,1)}, bf16[512,2048]{1,0:T(8,128)(2,1)}, u32[]{:S(2)}, u32[]{:S(2)}) collective-permute-start(bf16[512,2048]{1,0:T(8,128)(2,1)} %convolution_convert_fusion), channel_id=1, source_target_pairs={{0,4},{4,0},{8,12},{12,8},{16,20},{20,16},{24,28},{28,24},{1,5},{5... | collective-permute-start | bytes 6291464 | tf_op jit(solution)/shard_map/ppermute | solution.py:21
  417.5 116.4 %collective-permute-start.106 = (bf16[512,2048]{1,0:T(8,128)(2,1)}, bf16[512,2048]{1,0:T(8,128)(2,1)S(1)}, u32[]{:S(2)}, u32[]{:S(2)}) collective-permute-start(bf16[512,2048]{1,0:T(8,128)(2,1)} %convolution_convert_fusion.1), channel_id=1, source_target_pairs={{0,4},{4,0},{8,12},{12,8},{16,20},{20,16},{24,28},{28,24},{1,5},{5... | collective-permute-start | bytes 6291464 | tf_op jit(solution)/shard_map/ppermute | solution.py:21
  419.4 108.1 %collective-permute-start.101 = (bf16[512,2048]{1,0:T(8,128)(2,1)}, bf16[512,2048]{1,0:T(8,128)(2,1)}, u32[]{:S(2)}, u32[]{:S(2)}) collective-permute-start(bf16[512,2048]{1,0:T(8,128)(2,1)} %convolution_convert_fusion.2), channel_id=1, source_target_pairs={{0,4},{4,0},{8,12},{12,8},{16,20},{20,16},{24,28},{28,24},{1,5},{5... | collective-permute-start | bytes 6291464 | tf_op jit(solution)/shard_map/ppermute | solution.py:21
  433.3 54.3 %collective-permute-start.89 = (bf16[256,512]{1,0:T(8,128)(2,1)S(1)}, bf16[256,512]{1,0:T(8,128)(2,1)S(1)}, u32[]{:S(2)}, u32[]{:S(2)}) collective-permute-start(bf16[256,512]{1,0:T(8,128)(2,1)S(1)} %fusion.66), channel_id=1, source_target_pairs={{0,16},{4,20},{8,24},{12,28},{16,0},{20,4},{24,8},{28,12},{1,17},{... | collective-permute-start | bytes 786440 | tf_op jit(solution)/shard_map/ppermute | solution.py:21
  434.4 56.7 %collective-permute-start.93 = (bf16[256,512]{1,0:T(8,128)(2,1)}, bf16[256,512]{1,0:T(8,128)(2,1)S(1)}, u32[]{:S(2)}, u32[]{:S(2)}) collective-permute-start(bf16[256,512]{1,0:T(8,128)(2,1)} %bitcast.35), channel_id=1, source_target_pairs={{0,8},{4,12},{8,0},{12,4},{16,24},{20,28},{24,16},{28,20},{1,9},{5... | collective-permute-start | bytes 786440 | tf_op jit(solution)/shard_map/ppermute | solution.py:21
  490.0 20.4 %collective-permute-start.90 = (bf16[128,512]{1,0:T(8,128)(2,1)}, bf16[128,512]{1,0:T(8,128)(2,1)S(1)}, u32[]{:S(2)}, u32[]{:S(2)}) collective-permute-start(bf16[128,512]{1,0:T(8,128)(2,1)} %fusion.70), channel_id=1, source_target_pairs={{0,8},{4,12},{8,0},{12,4},{16,24},{20,28},{24,16},{28,20},{1,9},{5... | collective-permute-start | bytes 393224 | tf_op jit(solution)/shard_map/ppermute | solution.py:21
  517.9 19.0 %collective-permute-start.97 = (bf16[512,2048]{1,0:T(8,128)(2,1)}, bf16[512,2048]{1,0:T(8,128)(2,1)S(1)}, u32[]{:S(2)}, u32[]{:S(2)}) collective-permute-start(bf16[512,2048]{1,0:T(8,128)(2,1)} %convolution_convert_fusion.3), channel_id=1, source_target_pairs={{0,4},{4,0},{8,12},{12,8},{16,20},{20,16},{24,28},{28,24},{1,5},{5... | collective-permute-start | bytes 6291464 | tf_op jit(solution)/shard_map/ppermute | solution.py:21
  521.0 19.1 %collective-permute-start.83 = (bf16[512,1536]{1,0:T(8,128)(2,1)}, bf16[512,1536]{1,0:T(8,128)(2,1)S(1)}, u32[]{:S(2)}, u32[]{:S(2)}) collective-permute-start(bf16[512,1536]{1,0:T(8,128)(2,1)} %convolution_convert_fusion.4), channel_id=1, source_target_pairs={{0,4},{4,0},{8,12},{12,8},{16,20},{20,16},{24,28},{28,24},{1,5},{5... | collective-permute-start | bytes 4718600 | tf_op jit(solution)/shard_map/ppermute | solution.py:21
  521.7 21.4 %collective-permute-start.79 = (bf16[512,1536]{1,0:T(8,128)(2,1)}, bf16[512,1536]{1,0:T(8,128)(2,1)S(1)}, u32[]{:S(2)}, u32[]{:S(2)}) collective-permute-start(bf16[512,1536]{1,0:T(8,128)(2,1)} %convolution_convert_fusion.5), channel_id=1, source_target_pairs={{0,4},{4,0},{8,12},{12,8},{16,20},{20,16},{24,28},{28,24},{1,5},{5... | collective-permute-start | bytes 4718600 | tf_op jit(solution)/shard_map/ppermute | solution.py:21
  533.0 84.3 %collective-permute-start.111 = (bf16[256,2048]{1,0:T(8,128)(2,1)S(1)}, bf16[256,2048]{1,0:T(8,128)(2,1)S(1)}, u32[]{:S(2)}, u32[]{:S(2)}) collective-permute-start(bf16[256,2048]{1,0:T(8,128)(2,1)S(1)} %bitcast.185), channel_id=1, source_target_pairs={{0,8},{4,12},{8,0},{12,4},{16,24},{20,28},{24,16},{28,20},{1,9},{5... | collective-permute-start | bytes 3145736 | tf_op jit(solution)/shard_map/ppermute | solution.py:21
  536.1 82.6 %collective-permute-start.107 = (bf16[256,2048]{1,0:T(8,128)(2,1)S(1)}, bf16[256,2048]{1,0:T(8,128)(2,1)S(1)}, u32[]{:S(2)}, u32[]{:S(2)}) collective-permute-start(bf16[256,2048]{1,0:T(8,128)(2,1)S(1)} %fusion.22), channel_id=1, source_target_pairs={{0,16},{4,20},{8,24},{12,28},{16,0},{20,4},{24,8},{28,12},{1,17},{... | collective-permute-start | bytes 3145736 | tf_op jit(solution)/shard_map/ppermute | solution.py:21
  537.0 83.5 %collective-permute-start.102 = (bf16[256,2048]{1,0:T(8,128)(2,1)S(1)}, bf16[256,2048]{1,0:T(8,128)(2,1)S(1)}, u32[]{:S(2)}, u32[]{:S(2)}) collective-permute-start(bf16[256,2048]{1,0:T(8,128)(2,1)S(1)} %bitcast.184), channel_id=1, source_target_pairs={{0,8},{4,12},{8,0},{12,4},{16,24},{20,28},{24,16},{28,20},{1,9},{5... | collective-permute-start | bytes 3145736 | tf_op jit(solution)/shard_map/ppermute | solution.py:21
  540.2 82.0 %collective-permute-start.98 = (bf16[256,2048]{1,0:T(8,128)(2,1)S(1)}, bf16[256,2048]{1,0:T(8,128)(2,1)S(1)}, u32[]{:S(2)}, u32[]{:S(2)}) collective-permute-start(bf16[256,2048]{1,0:T(8,128)(2,1)S(1)} %fusion.21), channel_id=1, source_target_pairs={{0,16},{4,20},{8,24},{12,28},{16,0},{20,4},{24,8},{28,12},{1,17},{... | collective-permute-start | bytes 3145736 | tf_op jit(solution)/shard_map/ppermute | solution.py:21
  543.1 54.4 %collective-permute-start.84 = (bf16[256,1536]{1,0:T(8,128)(2,1)S(1)}, bf16[256,1536]{1,0:T(8,128)(2,1)S(1)}, u32[]{:S(2)}, u32[]{:S(2)}) collective-permute-start(bf16[256,1536]{1,0:T(8,128)(2,1)S(1)} %bitcast.186), channel_id=1, source_target_pairs={{0,8},{4,12},{8,0},{12,4},{16,24},{20,28},{24,16},{28,20},{1,9},{5... | collective-permute-start | bytes 2359304 | tf_op jit(solution)/shard_map/ppermute | solution.py:21
  597.5 18.6 %collective-permute-start.80 = (bf16[256,1536]{1,0:T(8,128)(2,1)S(1)}, bf16[256,1536]{1,0:T(8,128)(2,1)S(1)}, u32[]{:S(2)}, u32[]{:S(2)}) collective-permute-start(bf16[256,1536]{1,0:T(8,128)(2,1)S(1)} %fusion.29), channel_id=1, source_target_pairs={{0,16},{4,20},{8,24},{12,28},{16,0},{20,4},{24,8},{28,12},{1,17},{... | collective-permute-start | bytes 2359304 | tf_op jit(solution)/shard_map/ppermute | solution.py:21
  618.6 23.9 %collective-permute-start.112 = (bf16[128,2048]{1,0:T(8,128)(2,1)S(1)}, bf16[128,2048]{1,0:T(8,128)(2,1)S(1)}, u32[]{:S(2)}, u32[]{:S(2)}) collective-permute-start(bf16[128,2048]{1,0:T(8,128)(2,1)S(1)} %fusion.56), channel_id=1, source_target_pairs={{0,16},{4,20},{8,24},{12,28},{16,0},{20,4},{24,8},{28,12},{1,17},{... | collective-permute-start | bytes 1572872 | tf_op jit(solution)/shard_map/ppermute | solution.py:21
  620.5 20.1 %collective-permute-start.108 = (bf16[128,2048]{1,0:T(8,128)(2,1)S(1)}, bf16[128,2048]{1,0:T(8,128)(2,1)S(1)}, u32[]{:S(2)}, u32[]{:S(2)}) collective-permute-start(bf16[128,2048]{1,0:T(8,128)(2,1)S(1)} %fusion.55), channel_id=1, source_target_pairs={{0,8},{4,12},{8,0},{12,4},{16,24},{20,28},{24,16},{28,20},{1,9},{5... | collective-permute-start | bytes 1572872 | tf_op jit(solution)/shard_map/ppermute | solution.py:21
  622.2 26.8 %collective-permute-start.103 = (bf16[128,2048]{1,0:T(8,128)(2,1)S(1)}, bf16[128,2048]{1,0:T(8,128)(2,1)S(1)}, u32[]{:S(2)}, u32[]{:S(2)}) collective-permute-start(bf16[128,2048]{1,0:T(8,128)(2,1)S(1)} %fusion.54), channel_id=1, source_target_pairs={{0,16},{4,20},{8,24},{12,28},{16,0},{20,4},{24,8},{28,12},{1,17},{... | collective-permute-start | bytes 1572872 | tf_op jit(solution)/shard_map/ppermute | solution.py:21
  628.2 20.6 %collective-permute-start.99 = (bf16[128,2048]{1,0:T(8,128)(2,1)S(1)}, bf16[128,2048]{1,0:T(8,128)(2,1)S(1)}, u32[]{:S(2)}, u32[]{:S(2)}) collective-permute-start(bf16[128,2048]{1,0:T(8,128)(2,1)S(1)} %fusion.53), channel_id=1, source_target_pairs={{0,8},{4,12},{8,0},{12,4},{16,24},{20,28},{24,16},{28,20},{1,9},{5... | collective-permute-start | bytes 1572872 | tf_op jit(solution)/shard_map/ppermute | solution.py:21
  629.4 21.8 %collective-permute-start.86 = (bf16[128,768]{1,0:T(8,128)(2,1)S(1)}, bf16[128,768]{1,0:T(8,128)(2,1)S(1)}, u32[]{:S(2)}, u32[]{:S(2)}) collective-permute-start(bf16[128,768]{1,0:T(8,128)(2,1)S(1)} %get-tuple-element.53), channel_id=1, source_target_pairs={{0,2},{1,3},{2,0},{3,1},{4,6},{5,7},{6,4},{7,5},{8,10},{9,11},{10,... | collective-permute-start | bytes 589832 | tf_op jit(solution)/shard_map/ppermute | solution.py:25
  648.8 21.6 %collective-permute-start.113 = (bf16[128,1024]{1,0:T(8,128)(2,1)S(1)}, bf16[128,1024]{1,0:T(8,128)(2,1)S(1)}, u32[]{:S(2)}, u32[]{:S(2)}) collective-permute-start(bf16[128,1024]{1,0:T(8,128)(2,1)S(1)} %get-tuple-element.46), channel_id=1, source_target_pairs={{0,2},{1,3},{2,0},{3,1},{4,6},{5,7},{6,4},{7,5},{8,10},{9,11},{10,... | collective-permute-start | bytes 786440 | tf_op jit(solution)/shard_map/ppermute | solution.py:25
  649.0 21.5 %collective-permute-start.114 = (bf16[128,1024]{1,0:T(8,128)(2,1)S(1)}, bf16[128,1024]{1,0:T(8,128)(2,1)S(1)}, u32[]{:S(2)}, u32[]{:S(2)}) collective-permute-start(bf16[128,1024]{1,0:T(8,128)(2,1)S(1)} %get-tuple-element.47), channel_id=1, source_target_pairs={{0,3},{1,0},{2,1},{3,2},{4,7},{5,4},{6,5},{7,6},{8,11},{9,8},{10,9... | collective-permute-start | bytes 786440 | tf_op jit(solution)/shard_map/ppermute | solution.py:25
  651.2 19.2 %collective-permute-start.109 = (bf16[128,1024]{1,0:T(8,128)(2,1)S(1)}, bf16[128,1024]{1,0:T(8,128)(2,1)S(1)}, u32[]{:S(2)}, u32[]{:S(2)}) collective-permute-start(bf16[128,1024]{1,0:T(8,128)(2,1)S(1)} %slice.597), channel_id=1, source_target_pairs={{0,1},{1,2},{2,3},{3,0},{4,5},{5,6},{6,7},{7,4},{8,9},{9,10},{10,1... | collective-permute-start | bytes 786440 | tf_op jit(solution)/shard_map/ppermute | solution.py:25
  651.6 37.9 %collective-permute-start.104 = (bf16[128,1024]{1,0:T(8,128)(2,1)S(1)}, bf16[128,1024]{1,0:T(8,128)(2,1)S(1)}, u32[]{:S(2)}, u32[]{:S(2)}) collective-permute-start(bf16[128,1024]{1,0:T(8,128)(2,1)S(1)} %get-tuple-element.48), channel_id=1, source_target_pairs={{0,2},{1,3},{2,0},{3,1},{4,6},{5,7},{6,4},{7,5},{8,10},{9,11},{10,... | collective-permute-start | bytes 786440 | tf_op jit(solution)/shard_map/ppermute | solution.py:25
  654.2 35.3 %collective-permute-start.105 = (bf16[128,1024]{1,0:T(8,128)(2,1)S(1)}, bf16[128,1024]{1,0:T(8,128)(2,1)S(1)}, u32[]{:S(2)}, u32[]{:S(2)}) collective-permute-start(bf16[128,1024]{1,0:T(8,128)(2,1)S(1)} %get-tuple-element.49), channel_id=1, source_target_pairs={{0,3},{1,0},{2,1},{3,2},{4,7},{5,4},{6,5},{7,6},{8,11},{9,8},{10,9... | collective-permute-start | bytes 786440 | tf_op jit(solution)/shard_map/ppermute | solution.py:25
  670.4 19.1 %collective-permute-start.100 = (bf16[128,1024]{1,0:T(8,128)(2,1)S(1)}, bf16[128,1024]{1,0:T(8,128)(2,1)S(1)}, u32[]{:S(2)}, u32[]{:S(2)}) collective-permute-start(bf16[128,1024]{1,0:T(8,128)(2,1)S(1)} %slice.598), channel_id=1, source_target_pairs={{0,1},{1,2},{2,3},{3,0},{4,5},{5,6},{6,7},{7,4},{8,9},{9,10},{10,1... | collective-permute-start | bytes 786440 | tf_op jit(solution)/shard_map/ppermute | solution.py:25
  (85 other events, 688.9 us)

commit v3 on v2

v3 whole, which is shorter than its diff:
```python
import jax
import jax.numpy as jnp
from jax import lax
from jax.experimental import pallas as pl
from jax.experimental.pallas import tpu as pltpu
from jax.sharding import PartitionSpec as P

HEAD_DIM = 128
HALO = 128
EPSILON = 1e-05
LOW = jnp.bfloat16


def dot(left, right, dims, kind=jnp.float32):
    return lax.dot_general(
        left, right, ((dims[:1], dims[1:]), ((), ())), preferred_element_type=kind
    )


class Links:
    def __init__(self, dp, mp):
        self.dp, self.mp = dp, mp
        self.last = {}

    def send(self, value, axis, pairs, link, depth):
        before = self.last.setdefault(link, [])
        if depth and len(before) >= depth:
            value, _ = lax.optimization_barrier((value, before[-depth]))
        result = lax.ppermute(value, axis, pairs)
        before.append(result)
        return result

    def swap(self, value, bit, depth=0):
        return self.send(value, "dp", [(i, i ^ bit) for i in range(self.dp)], bit, depth)

    def shift(self, value, step, depth=3):
        pairs = [(i, (i + step) % self.mp) for i in range(self.mp)]
        return self.send(value, "mp", pairs, "z", depth)

    def halo(self, value, depth=0):
        count = self.mp
        before = self.send(value[:, -HALO:], "mp", [(i, i + 1) for i in range(count - 1)], "z", depth)
        after = self.send(value[:, :HALO], "mp", [(i + 1, i) for i in range(count - 1)], "z", depth)
        return before, value, after


class Plan:
    def __init__(self, mesh):
        self.dp = mesh.shape["dp"]
        self.mp = mesh.shape["mp"]
        bits = [1 << i for i in range(self.dp.bit_length() - 1)]
        core, others = bits[:1], bits[1:]
        self.orders = (others + core, others[::-1] + core)
        self.major = core + others[::-1]
        relative = [0]
        for bit in self.major[::-1]:
            relative = relative + [r ^ bit for r in relative]
        self.relative = relative

    def own(self):
        return lax.axis_index("dp")

    def enter(self, value):
        width = value.shape[-1] // self.dp
        axis = value.ndim - 1
        return jnp.concatenate(
            [
                lax.dynamic_slice_in_dim(value, (self.own() ^ r) * width, width, axis)
                for r in self.relative
            ],
            axis=axis,
        )

    def leave(self, value):
        width = value.shape[-1] // self.dp
        axis = value.ndim - 1
        inverse = {r: p for p, r in enumerate(self.relative)}
        table = jnp.array([inverse[r] for r in range(self.dp)], jnp.int32)
        return jnp.concatenate(
            [
                lax.dynamic_slice_in_dim(value, table[self.own() ^ n] * width, width, axis)
                for n in range(self.dp)
            ],
            axis=axis,
        )

    def gather_small(self, links, value):
        for bit in self.major[::-1]:
            value = jnp.concatenate([value, links.swap(value, bit, 0)], axis=0)
        return value

    def spread_columns(self, links, local):
        parts = [local] + [links.shift(local, -k, 0) for k in range(1, self.mp)]
        return self.halves(parts)

    def halves(self, parts):
        half = self.mp // 2
        return [jnp.concatenate(parts[i * half : (i + 1) * half], axis=1) for i in range(2)]


class Gather:
    def __init__(self, plan, links, held):
        self.plan, self.links = plan, links
        self.block = held[0].shape[0]
        self.held = [[h] for h in held]
        self.known = [[0], [0]]
        self.steps = [list(order[:-1]) for order in plan.orders]

    def pieces(self, i, order):
        span = self.held[i][0].shape[0] // self.block
        at = [self.known[i].index(r) for r in order]
        pieces = []
        while at:
            n = at.pop(0)
            count = 1
            while at and at[0] == n + count and (n + count) % span:
                at.pop(0)
                count += 1
            held = self.held[i][n // span]
            first = n % span * self.block
            pieces.append(held if count == span else held[first : first + count * self.block])
        return pieces

    def join(self, i, order):
        pieces = self.pieces(i, order)
        return pieces[0] if len(pieces) == 1 else jnp.concatenate(pieces, axis=0)

    def step(self, tokens=()):
        for i in range(2):
            bit = self.steps[i][0]
            value = self.join(i, self.known[i])
            self.held[i] = [value, self.links.swap(after(value, *tokens), bit)]
            self.known[i] = self.known[i] + [r ^ bit for r in self.known[i]]
            self.steps[i] = self.steps[i][1:]
        return [h[1] for h in self.held]

    def steps_but_last(self, tokens=()):
        received = []
        while len(self.steps[0]) > 1:
            received = self.step(tokens)
        return received

    def hold(self, tokens):
        for i in range(2):
            self.held[i][1] = after(self.held[i][1], *tokens)

    def finish(self):
        order = self.plan.relative[: self.plan.dp // 2]
        mine = [self.join(i, order) for i in range(2)]
        return [(m, self.links.swap(m, self.plan.major[0])) for m in mine]


class Scatter:
    def __init__(self, plan, links, pairs):
        self.plan, self.links = plan, links
        self.pairs = pairs
        self.kept = [None, None]
        self.bits = [list(order[:-1][::-1]) for order in plan.orders]
        self.remain = [list(plan.major[1:]), list(plan.major[1:])]

    def core(self, i):
        self.kept[i] = []
        for left, rights in self.pairs:
            middle = left.shape[1] // 2
            sent = dot(left[:, middle:], rights[i], (0, 0)).astype(LOW)
            kept = dot(left[:, :middle], rights[i], (0, 0))
            self.kept[i].append((kept, self.links.swap(sent, self.plan.major[0])))

    def hold(self, i, tokens):
        self.kept[i] = [(k, after(r, *tokens)) for k, r in self.kept[i]]

    def add(self, i):
        self.kept[i] = [
            k[0] + k[1].astype(jnp.float32) if isinstance(k, tuple) else k for k in self.kept[i]
        ]
        return self.kept[i]

    def step(self, i, tokens=()):
        values = self.add(i)
        bit = self.bits[i].pop(0)
        block = values[0].shape[0] >> (self.remain[i].index(bit) + 1)
        shaped = [v.reshape(-1, 2, block, v.shape[1]) for v in values]
        out = [x[:, 1].reshape(-1, v.shape[1]).astype(LOW) for x, v in zip(shaped, values)]
        stay = [x[:, 0].reshape(-1, v.shape[1]) for x, v in zip(shaped, values)]
        out = out[0] if len(out) == 1 else jnp.concatenate(out, axis=1)
        received = self.links.swap(after(out, *tokens), bit)
        self.kept[i], at = [], 0
        for x in stay:
            self.kept[i].append((x, received[:, at : at + x.shape[1]]))
            at += x.shape[1]
        self.remain[i].remove(bit)
        return out

    def steps_but_last(self, i, tokens=()):
        out = None
        while len(self.bits[i]) > 1:
            out = self.step(i, tokens)
        return out

    def rows(self):
        half = self.plan.mp // 2
        result = []
        for pair in zip(*[self.add(i) for i in range(2)]):
            width = pair[0].shape[1] // half
            result.append([r[:, j * width : (j + 1) * width] for r in pair for j in range(half)])
        return result

    def shifts(self, natural, tokens=()):
        mp = self.plan.mp
        products = self.rows()
        own = lax.axis_index("mp")
        for n, rows in enumerate(products):
            if natural[n]:
                joined = jnp.stack(rows)
                products[n] = [
                    lax.dynamic_index_in_dim(joined, lax.rem(own + k, mp), 0, keepdims=False)
                    for k in range(mp)
                ]
        self.total = [rows[0] for rows in products]
        outs = []
        for k in range(1, mp):
            out = [rows[k].astype(LOW) for rows in products]
            outs.append(out[0] if len(out) == 1 else jnp.concatenate(out, axis=1))
        self.received = [
            self.links.shift(after(value, *tokens), k + 1, 0) for k, value in enumerate(outs)
        ]
        return outs

    def finish(self):
        result, at = [], 0
        for total in self.total:
            for part in self.received:
                total = total + part[:, at : at + total.shape[1]].astype(jnp.float32)
            result.append(total)
            at += total.shape[1]
        return result

    def reduce_columns(self):
        joined = jnp.stack(self.rows()[0])
        return lax.psum_scatter(joined, "mp", scatter_dimension=0, tiled=False)


def after(value, *tokens):
    if not tokens:
        return value
    return lax.optimization_barrier((value, *tokens))[0]


def split_dot(left, top, bottom):
    half = top.shape[0]
    return dot(left[:, :half], top, (1, 0)) + dot(left[:, half:], bottom, (1, 0))


MEGA = 1 << 20
LOG2E = 1.4426950408889634
VM_FWD = 36
VM_UP = 20
VM_DOWN = 20
VM_BACK = 32
VM_BWD = 36
VM_ENTER = 20


def params(limit=56):
    return pltpu.CompilerParams(vmem_limit_bytes=limit * MEGA)


def cost(flops, bytes_accessed, transcendentals=0):
    return pl.CostEstimate(
        flops=int(flops), bytes_accessed=int(bytes_accessed), transcendentals=int(transcendentals)
    )


def whole(*shape):
    return pl.BlockSpec(shape, lambda *_: (0,) * len(shape), pipeline_mode=pl.Buffered(1))


def statistics(values):
    mean = jnp.mean(values, axis=-1, keepdims=True)
    centred = values - mean
    variance = jnp.mean(centred * centred, axis=-1, keepdims=True)
    return centred, lax.rsqrt(variance + EPSILON)


def norm_rows(values, gain, bias):
    centred, scale = statistics(values)
    return centred * scale * gain + bias


def norm_back(values, gain, grad):
    centred, scale = statistics(values)
    normed = centred * scale
    inner = grad * gain
    first = jnp.mean(inner, axis=-1, keepdims=True)
    second = jnp.mean(inner * normed, axis=-1, keepdims=True)
    return (inner - first - normed * second) * scale, grad * normed, grad


def fold(rows):
    total = rows[:8]
    for i in range(1, rows.shape[0] // 8):
        total = total + rows[i * 8 : i * 8 + 8]
    return total


ROWS = 64


def store_blocks(ref, start, value, table, inverse=None):
    if table is None:
        ref[pl.ds(start, value.shape[0]), :] = value
        return
    count = table.shape[0]
    block = value.shape[1] // count
    for p in range(count):
        at = pl.multiple_of(table[p] * block, block)
        ref[pl.ds(start, value.shape[0]), pl.ds(at, block)] = value[:, p * block : (p + 1) * block]


def load_blocks(ref, start, size, table):
    if table is None:
        return ref[pl.ds(start, size), :]
    count = table.shape[0]
    block = ref.shape[1] // count
    parts = []
    for p in range(count):
        at = pl.multiple_of(table[p] * block, block)
        parts.append(ref[pl.ds(start, size), pl.ds(at, block)])
    return jnp.concatenate(parts, axis=1)


def enter_kernel(blocked):
    def kernel(table_ref, latents, grads, small, entered, entered_grads, grad_z, inputs_a):
        table = table_ref if blocked else None

        @pl.loop(0, latents.shape[0] // ROWS)
        def _(i):
            start = pl.multiple_of(i * ROWS, ROWS)
            at = pl.ds(start, ROWS)
            values = load_blocks(latents, start, ROWS, table)
            entered[at, :] = values
            inputs_a[at, :] = norm_rows(values, small[0:1], small[2:3]).astype(LOW)
            values = load_blocks(grads, start, ROWS, table)
            entered_grads[at, :] = values
            grad_z[at, :] = values.astype(LOW)

    return kernel


def enter_norm(table, blocked, latents, grads, small):
    total, width = latents.shape
    rows = 256
    spec = pl.BlockSpec((rows, width), lambda i, *_: (i, 0))
    shape = lambda kind: jax.ShapeDtypeStruct((total, width), kind)
    return pl.pallas_call(
        enter_kernel(blocked),
        name="enter",
        grid_spec=pltpu.PrefetchScalarGridSpec(
            num_scalar_prefetch=1,
            grid=(total // rows,),
            in_specs=[spec, spec, whole(4, width)],
            out_specs=[spec] * 4,
        ),
        out_shape=[shape(jnp.float32), shape(jnp.float32), shape(LOW), shape(LOW)],
        compiler_params=params(VM_ENTER),
        cost_estimate=cost(total * width * 16, total * width * 20),
    )(table, latents, grads, small)


def attention_weights(q, k, bias, factor):
    scores = dot(q, k, (1, 1)) * (factor * LOG2E) + bias
    peak = jnp.max(scores, axis=-1, keepdims=True)
    weights = jnp.exp2(scores - peak)
    return weights * (1.0 / jnp.sum(weights, axis=-1, keepdims=True))


def window_bias(group_column, key_row):
    span = group_column.shape[0]
    place = lax.broadcasted_iota(jnp.int32, (span, span), 0)
    other = lax.broadcasted_iota(jnp.int32, (span, span), 1)
    allowed = (group_column == key_row) | (place == other)
    return jnp.where(allowed, 0.0, -1e30)


def column_halves(rows, tile, count):
    return (
        pl.BlockSpec((rows, tile), lambda k, *_: (0, jnp.minimum(k, count - 1))),
        pl.BlockSpec((rows, tile), lambda k, *_: (0, jnp.clip(k - count, 0, count - 1))),
    )


def either(step, count, work, first, second):
    @pl.when(step < count)
    def _():
        work(*first)

    @pl.when((step >= count) & (step < 2 * count))
    def _():
        work(*second)


def project(window, w_top, w_bottom, target, index, rows):
    before, own, after = window
    target[0:HALO] = split_dot(before[index], w_top, w_bottom).astype(LOW)
    target[HALO : HALO + rows] = split_dot(own[index], w_top, w_bottom).astype(LOW)
    target[HALO + rows :] = split_dot(after[index], w_top, w_bottom).astype(LOW)


def forward_kernel(rows, steps, local_heads, factor):
    def kernel(before, own, after, top_a, bottom_a, top_b, bottom_b, column, row, start, small,
               saved, attended, resid, inputs_c, bias, total):
        step, index = pl.program_id(0), pl.program_id(1)
        group = local_heads * HEAD_DIM
        wide = 3 * group
        half = top_a.shape[0]
        target = saved.at[0]

        @pl.when(step == 0)
        def _():
            bias[index] = window_bias(column[index], row[index])
            total[index] = jnp.zeros((rows, 2 * half), jnp.float32)

        mine = slice(HALO, HALO + rows)

        def work(top, bottom):
            project((before, own, after), top[:, :wide], bottom[:, :wide], target, index, rows)
            for h in range(local_heads):
                at = slice(h * HEAD_DIM, (h + 1) * HEAD_DIM)
                q = target[mine, at]
                k = target[:, group + h * HEAD_DIM : group + (h + 1) * HEAD_DIM]
                v = target[:, 2 * group + h * HEAD_DIM : 2 * group + (h + 1) * HEAD_DIM]
                p = attention_weights(q, k, bias[index, mine, :], factor).astype(LOW)
                attended[0, :, at] = dot(p, v, (1, 0)).astype(LOW)
            total[index, :, :half] += dot(attended[0], top[:, wide:], (1, 1))
            total[index, :, half:] += dot(attended[0], bottom[:, wide:], (1, 1))

        @pl.when(step < steps // 2)
        def _():
            work(top_a, bottom_a)

        @pl.when(step >= steps // 2)
        def _():
            work(top_b, bottom_b)

        @pl.when(step == steps - 1)
        def _():
            @pl.loop(0, rows // ROWS)
            def _(i):
                at = pl.ds(pl.multiple_of(i * ROWS, ROWS), ROWS)
                values = total[index, at, :] + start[at, :]
                resid[at, :] = values
                inputs_c[at, :] = norm_rows(values, small[1:2], small[3:4]).astype(LOW)

    return kernel


def forward_block(window, weights, column, row, start, small, steps, factor):
    before, own, after = window
    micro, rows, width = own.shape
    span = rows + 2 * HALO
    total = micro * rows
    half = steps // 2
    c = weights[0][0].shape[1] // half
    g = c // 4
    late = pl.BlockSpec((rows, width), lambda k, i: (jnp.where(k == steps - 1, i, 0), 0))
    weight_a, weight_b = column_halves(width // 2, c, half)
    return pl.pallas_call(
        forward_kernel(rows, steps, g // HEAD_DIM, factor),
        name="attention_forward",
        grid=(steps, micro),
        in_specs=[
            whole(*before.shape), whole(*own.shape), whole(*after.shape),
            weight_a, weight_a, weight_b, weight_b,
            whole(*column.shape), whole(*row.shape),
            late,
            whole(4, width),
        ],
        out_specs=[
            pl.BlockSpec((1, span, 3 * g), lambda k, i: (i, 0, k)),
            pl.BlockSpec((1, rows, g), lambda k, i: (k // half, i, k % half)),
            late,
            late,
        ],
        out_shape=[
            jax.ShapeDtypeStruct((micro, span, 3 * g * steps), LOW),
            jax.ShapeDtypeStruct((2, total, g * half), LOW),
            jax.ShapeDtypeStruct((total, width), jnp.float32),
            jax.ShapeDtypeStruct((total, width), LOW),
        ],
        scratch_shapes=[
            pltpu.VMEM((micro, span, span), jnp.float32),
            pltpu.VMEM((micro, rows, width), jnp.float32),
        ],
        compiler_params=params(VM_FWD),
        cost_estimate=cost(
            2 * micro * steps * g * (span * width * 3 + rows * width + 2 * rows * span),
            30 * MEGA,
            micro * rows * span * steps * g // HEAD_DIM,
        ),
    )(before, own, after, *weights[0], *weights[1], column, row, start, small)


def up_kernel(count):
    def kernel(inputs, top_a, bottom_a, top_b, bottom_b, hidden, slope):
        def work(top, bottom):
            u = split_dot(inputs[...], top[...], bottom[...])
            c = 0.7978845608028654
            square = u * u
            t = jnp.tanh(u * (c + c * 0.044715 * square))
            half = 0.5 + 0.5 * t
            hidden[0] = (u * half).astype(LOW)
            inner = 0.5 * c + 1.5 * c * 0.044715 * square
            slope[0] = (half + u * inner * (1.0 - t * t)).astype(LOW)

        either(pl.program_id(0), count, work, (top_a, bottom_a), (top_b, bottom_b))

    return kernel


def feed_up(inputs, weights, tile=512):
    total, width = inputs.shape
    ff = 2 * weights[0][0].shape[1]
    count = ff // 2 // tile
    block = pl.BlockSpec((1, total, tile), lambda j: (j // count, 0, j % count))
    weight_a, weight_b = column_halves(width // 2, tile, count)
    return pl.pallas_call(
        up_kernel(count),
        name="feed_up",
        grid=(ff // tile,),
        in_specs=[whole(total, width), weight_a, weight_a, weight_b, weight_b],
        out_specs=[block, block],
        out_shape=[jax.ShapeDtypeStruct((2, total, ff // 2), LOW)] * 2,
        compiler_params=params(VM_UP),
        cost_estimate=cost(2 * total * width * ff, 2 * (width * ff + 2 * total * ff), total * ff),
    )(inputs, *weights[0], *weights[1])


LATE = 256


def down_kernel(blocked, steps):
    def kernel(table_ref, hidden, top_a, bottom_a, top_b, bottom_b, start_rows, out, total):
        step = pl.program_id(0)
        half = top_a.shape[0]

        @pl.when(step == 0)
        def _():
            total[...] = jnp.zeros_like(total)

        def work(top, bottom):
            total[:, :half] += dot(hidden[0], top[...], (1, 1))
            total[:, half:] += dot(hidden[0], bottom[...], (1, 1))

        either(step, steps // 2, work, (top_a, bottom_a), (top_b, bottom_b))

        @pl.when(step >= steps)
        def _():
            base = (step - steps) * LATE

            @pl.loop(0, LATE // ROWS)
            def _(i):
                start = pl.multiple_of(i * ROWS, ROWS)
                at = pl.ds(pl.multiple_of(base + start, ROWS), ROWS)
                values = total[at, :] + start_rows[pl.ds(start, ROWS), :]
                store_blocks(out, start, values, table_ref if blocked else None)

    return kernel


def feed_down(table, blocked, hidden, weights, start, tile=512):
    total, width = start.shape
    ff = 2 * hidden.shape[2]
    steps = ff // tile
    count = steps // 2
    clip = lambda j: jnp.minimum(j, steps - 1)
    late = pl.BlockSpec((LATE, width), lambda j, *_: (jnp.maximum(j - steps, 0), 0))
    weight_a, weight_b = column_halves(width // 2, tile, count)
    return pl.pallas_call(
        down_kernel(blocked, steps),
        name="feed_down",
        grid_spec=pltpu.PrefetchScalarGridSpec(
            num_scalar_prefetch=1,
            grid=(steps + total // LATE,),
            in_specs=[
                pl.BlockSpec((1, total, tile), lambda j, *_: (clip(j) // count, 0, clip(j) % count)),
                weight_a, weight_a, weight_b, weight_b,
                late,
            ],
            out_specs=late,
            scratch_shapes=[pltpu.VMEM((total, width), jnp.float32)],
        ),
        out_shape=jax.ShapeDtypeStruct((total, width), jnp.float32),
        compiler_params=params(VM_DOWN),
        cost_estimate=cost(2 * total * width * ff, 2 * (width * ff + total * ff) + 8 * total * width),
    )(table, hidden, *weights[0], *weights[1], start)


def feed_back_kernel(steps):
    def kernel(grad_z, down_top_a, down_bottom_a, down_top_b, down_bottom_b,
               up_top_a, up_bottom_a, up_top_b, up_bottom_b, slope, resid, grads, small,
               grad_upward, grad_resid, grad_branch, sums, total):
        step = pl.program_id(0)
        half = up_top_a.shape[0]

        @pl.when(step == 0)
        def _():
            total[...] = jnp.zeros_like(total)
            sums[...] = jnp.zeros_like(sums)

        def work(down_top, down_bottom, up_top, up_bottom):
            grad = split_dot(grad_z[...], down_top[...], down_bottom[...]) * slope[0].astype(jnp.float32)
            grad_upward[0] = grad.astype(LOW)
            total[:, :half] += dot(grad_upward[0], up_top[...], (1, 1))
            total[:, half:] += dot(grad_upward[0], up_bottom[...], (1, 1))

        either(
            step, steps // 2, work,
            (down_top_a, down_bottom_a, up_top_a, up_bottom_a),
            (down_top_b, down_bottom_b, up_top_b, up_bottom_b),
        )

        @pl.when(step >= steps)
        def _():
            base = (step - steps) * LATE

            @pl.loop(0, LATE // ROWS)
            def _(i):
                start = pl.multiple_of(i * ROWS, ROWS)
                at = pl.ds(start, ROWS)
                grad = total[pl.ds(pl.multiple_of(base + start, ROWS), ROWS), :]
                back, by_gain, by_bias = norm_back(resid[at, :], small[1:2], grad)
                back = back + grads[at, :]
                grad_resid[at, :] = back
                grad_branch[at, :] = back.astype(LOW)
                sums[0:8] += fold(by_gain)
                sums[8:16] += fold(by_bias)

    return kernel


def feed_back(grad_z, down, up, slope, resid, grads, small, tile=512):
    total, width = grad_z.shape
    ff = 2 * slope.shape[2]
    steps = ff // tile
    count = steps // 2
    clip = lambda j: jnp.minimum(j, steps - 1)
    wide_a, wide_b = column_halves(width // 2, tile, count)
    block = pl.BlockSpec((1, total, tile), lambda j: (clip(j) // count, 0, clip(j) % count))
    late = pl.BlockSpec((LATE, width), lambda j: (jnp.maximum(j - steps, 0), 0))
    return pl.pallas_call(
        feed_back_kernel(steps),
        name="feed_back",
        grid=(steps + total // LATE,),
        in_specs=[whole(total, width), wide_a, wide_a, wide_b, wide_b, wide_a, wide_a, wide_b, wide_b, block, late, late, whole(4, width)],
        out_specs=[block, late, late, whole(16, width)],
        out_shape=[
            jax.ShapeDtypeStruct((2, total, ff // 2), LOW),
            jax.ShapeDtypeStruct((total, width), jnp.float32),
            jax.ShapeDtypeStruct((total, width), LOW),
            jax.ShapeDtypeStruct((16, width), jnp.float32),
        ],
        scratch_shapes=[pltpu.VMEM((total, width), jnp.float32)],
        compiler_params=params(VM_BACK),
        cost_estimate=cost(4 * total * width * ff, 4 * (width * ff + total * ff) + 14 * total * width),
    )(grad_z, *down[0], *down[1], *up[0], *up[1], slope, resid, grads, small)


def backward_kernel(rows, steps, local_heads, factor):
    def kernel(before, own, after, top_a, bottom_a, top_b, bottom_b, column, row, saved,
               grad_projected, out, bias, grad_att):
        step, index = pl.program_id(0), pl.program_id(1)
        group = local_heads * HEAD_DIM
        wide = 3 * group
        half = top_a.shape[0]
        at_rows = pl.ds(pl.multiple_of(index * rows, rows), rows)

        @pl.when(step == 0)
        def _():
            bias[index] = window_bias(column[index], row[index])
            out[at_rows, :] = jnp.zeros((rows, 2 * half), jnp.float32)

        mine = slice(HALO, HALO + rows)

        def work(top, bottom):
            project((before, own, after), top[:, wide:], bottom[:, wide:], grad_att, index, rows)
            for h in range(local_heads):
                at = slice(h * HEAD_DIM, (h + 1) * HEAD_DIM)
                at_k = slice(group + h * HEAD_DIM, group + (h + 1) * HEAD_DIM)
                at_v = slice(2 * group + h * HEAD_DIM, 2 * group + (h + 1) * HEAD_DIM)
                q, k, v = saved[0, :, at], saved[0, :, at_k], saved[0, :, at_v]
                grad_mix = grad_att[:, at]
                p = attention_weights(q, k, bias[index], factor)
                grad_p = dot(grad_mix, v, (1, 1))
                weighted = jnp.sum(p * grad_p, axis=-1, keepdims=True)
                grad_s = (p * (grad_p - weighted)).astype(LOW)
                grad_projected[0, :, at] = (dot(grad_s[mine], k, (1, 0)) * factor).astype(LOW)
                grad_projected[0, :, at_k] = (dot(grad_s[:, mine], q, (0, 0)) * factor).astype(LOW)
                grad_projected[0, :, at_v] = dot(p[:, mine].astype(LOW), grad_mix, (0, 0)).astype(LOW)
            out[at_rows, :half] += dot(grad_projected[0], top[:, :wide], (1, 1))
            out[at_rows, half:] += dot(grad_projected[0], bottom[:, :wide], (1, 1))

        either(step, steps // 2, work, (top_a, bottom_a), (top_b, bottom_b))

    return kernel


def backward_block(window, weights, column, row, saved, steps, factor):
    before, own, after = window
    micro, rows, width = own.shape
    span = rows + 2 * HALO
    total = micro * rows
    half = steps // 2
    c = weights[0][0].shape[1] // half
    g = c // 4
    weight_a, weight_b = column_halves(width // 2, c, half)
    return pl.pallas_call(
        backward_kernel(rows, steps, g // HEAD_DIM, factor),
        name="attention_backward",
        grid=(steps, micro),
        in_specs=[
            whole(*before.shape), whole(*own.shape), whole(*after.shape),
            weight_a, weight_a, weight_b, weight_b,
            whole(*column.shape), whole(*row.shape),
            pl.BlockSpec((1, span, 3 * g), lambda k, i: (i, 0, k)),
        ],
        out_specs=[
            pl.BlockSpec((1, rows, 3 * g), lambda k, i: (k // half, i, k % half)),
            whole(total, width),
        ],
        scratch_shapes=[
            pltpu.VMEM((micro, span, span), jnp.float32),
            pltpu.VMEM((span, g), LOW),
        ],
        out_shape=[
            jax.ShapeDtypeStruct((2, total, 3 * g * half), LOW),
            jax.ShapeDtypeStruct((total, width), jnp.float32),
        ],
        compiler_params=params(VM_BWD),
        cost_estimate=cost(
            2 * micro * steps * g * (span * width + rows * width * 3 + 4 * span * span),
            35 * MEGA,
            micro * span * span * steps * g // HEAD_DIM,
        ),
    )(before, own, after, *weights[0], *weights[1], column, row, saved)


def leave_kernel(blocked):
    def kernel(table_ref, norm_one, entered, grad_resid, small, latents_grad, sums):
        @pl.when(pl.program_id(0) == 0)
        def _():
            sums[...] = jnp.zeros_like(sums)

        @pl.loop(0, entered.shape[0] // ROWS)
        def _(i):
            start = pl.multiple_of(i * ROWS, ROWS)
            at = pl.ds(start, ROWS)
            back, by_gain, by_bias = norm_back(entered[at, :], small[0:1], norm_one[at, :])
            store_blocks(latents_grad, start, back + grad_resid[at, :], table_ref if blocked else None)
            sums[0:8] += fold(by_gain)
            sums[8:16] += fold(by_bias)

    return kernel


def leave_norm(table, blocked, norm_one, entered, grad_resid, small):
    total, width = entered.shape
    rows = 128
    spec = pl.BlockSpec((rows, width), lambda i, *_: (i, 0))
    return pl.pallas_call(
        leave_kernel(blocked),
        name="leave",
        grid_spec=pltpu.PrefetchScalarGridSpec(
            num_scalar_prefetch=1,
            grid=(total // rows,),
            in_specs=[spec, spec, spec, whole(4, width)],
            out_specs=[spec, whole(16, width)],
        ),
        out_shape=[
            jax.ShapeDtypeStruct((total, width), jnp.float32),
            jax.ShapeDtypeStruct((16, width), jnp.float32),
        ],
        compiler_params=params(VM_ENTER),
        cost_estimate=cost(total * width * 30, total * width * 16),
    )(table, norm_one, entered, grad_resid, small)


def solution(mesh):
    plan = Plan(mesh)

    def body(latents, group_ids, pad_mask, w_qkv, w_out, w_up, w_down, norm_gain, norm_bias, out_grad):
        micro, rows, width = latents.shape
        total = micro * rows
        mp = plan.mp
        factor = HEAD_DIM ** (-0.5)
        links = Links(plan.dp, mp)
        small = jnp.concatenate([norm_gain, norm_bias], axis=0).T
        small = plan.gather_small(links, small).T.astype(jnp.float32)

        blocked = width // plan.dp % 128 == 0
        table = plan.own() ^ jnp.array(plan.relative, jnp.int32)
        rows_in = (latents.reshape(total, width), out_grad.reshape(total, width))
        if not blocked:
            rows_in = tuple(plan.enter(v) for v in rows_in)
        entered, grad_rows, grad_z, inputs_a = enter_norm(table, blocked, *rows_in, small)

        local = jnp.concatenate([w_qkv[0], w_qkv[1], w_qkv[2], w_out], axis=1)
        gather_attention = Gather(plan, links, plan.spread_columns(links, local))
        columns_up = lax.all_gather(w_up, "mp", axis=0)
        columns_down = lax.all_gather(w_down, "mp", axis=0)
        gather_up = Gather(plan, links, plan.halves([columns_up[k] for k in range(mp)]))
        gather_down = Gather(plan, links, plan.halves([columns_down[k] for k in range(mp)]))
        gather_attention.steps_but_last([small])
        window = links.halo(inputs_a.reshape(micro, rows, width))
        gather_attention.step([inputs_a])
        attention = gather_attention.finish()
        tokens = gather_up.steps_but_last([inputs_a])

        span = rows + 2 * HALO
        first = lax.axis_index("mp") * rows
        pads = ((0, 0), (HALO, HALO))
        groups = jnp.pad(group_ids[:, 0], pads, constant_values=-1)
        keys = jnp.where(jnp.pad(pad_mask[:, 0], pads) == 1, groups, -2)
        groups = lax.dynamic_slice_in_dim(groups, first, span, 1)
        keys = lax.dynamic_slice_in_dim(keys, first, span, 1)
        column, row = groups[:, :, None], keys[:, None, :]

        saved, attended, resid, inputs_c = forward_block(
            window, attention, after(column, *tokens, columns_down), row, entered, small, mp, factor
        )
        gather_up.step()
        tokens = gather_down.steps_but_last()
        gather_up.hold([inputs_c])
        up = gather_up.finish()
        gather_down.hold([inputs_c])
        hidden, slope = feed_up(after(inputs_c, *tokens), up)
        gather_down.step()
        gather_down.hold([hidden])
        down = gather_down.finish()
        grad_down = Scatter(plan, links, [(grad_z, [hidden[0], hidden[1]])])
        for i in range(2):
            grad_down.core(i)
        tokens = [grad_down.steps_but_last(i) for i in range(2)]
        upward, grad_resid, grad_branch, sums_two = feed_back(
            after(grad_z, *tokens), down, up, slope, resid, grad_rows, small
        )
        branch = links.halo(grad_branch.reshape(micro, rows, width))
        for i in range(2):
            grad_down.hold(i, [grad_branch])
        tokens = [grad_down.step(i) for i in range(2)]
        left = after(inputs_c, *tokens)
        grad_up = Scatter(
            plan, links, [(left, [upward[0], upward[1]]), (grad_branch, [attended[0], attended[1]])]
        )
        for i in range(2):
            grad_up.core(i)
        tokens = [grad_up.steps_but_last(i) for i in range(2)]
        grad_down = grad_down.reduce_columns()
        projected, norm_one = backward_block(
            branch, attention, after(column, *tokens), row, saved, mp, factor
        )
        for i in range(2):
            grad_up.hold(i, [norm_one])
        tokens = [grad_up.step(i) for i in range(2)]
        left = after(inputs_a, *tokens)
        grad_qkv = Scatter(plan, links, [(left, [projected[0], projected[1]])])
        for i in range(2):
            grad_qkv.core(i)
        tokens = [grad_qkv.steps_but_last(i) for i in range(2)]
        latents_grad, sums_one = leave_norm(
            table, blocked, after(norm_one, *tokens), entered, grad_resid, small
        )
        for i in range(2):
            grad_up.hold(i, [latents_grad])
        tokens = grad_up.shifts([True, False])
        latents_out = feed_down(table, blocked, after(hidden, sums_one, *tokens), down, resid)
        for i in range(2):
            grad_qkv.hold(i, [latents_out])
            grad_qkv.step(i)
        grad_qkv.shifts([False])
        grad_up, grad_out = grad_up.finish()
        grad_qkv = grad_qkv.finish()[0]
        grad_qkv = jnp.stack(jnp.split(grad_qkv, 3, axis=1))
        sums = jnp.stack([sums_one, sums_two], axis=0).reshape(2, 2, 8, width).sum(axis=2)
        sums = sums.transpose(1, 0, 2).reshape(4, width).T
        for bit in plan.major:
            middle = sums.shape[0] // 2
            sums = sums[:middle] + links.swap(sums[middle:], bit, 0)
        for bit in [1 << i for i in range(mp.bit_length() - 1)]:
            sums = sums + lax.ppermute(sums, "mp", [(i, i ^ bit) for i in range(mp)])
        sums = sums.T
        if not blocked:
            latents_out, latents_grad = plan.leave(latents_out), plan.leave(latents_grad)
        shape = latents.shape
        return (
            latents_out.reshape(shape),
            latents_grad.reshape(shape),
            grad_qkv,
            grad_out,
            grad_up,
            grad_down,
            sums[:2],
            sums[2:],
        )

    return jax.shard_map(
        body,
        mesh=mesh,
        in_specs=(
            P(None, ("dp", "mp"), None),
            P(None, "dp", None),
            P(None, "dp", None),
            P(None, "dp", "mp"),
            P("dp", "mp"),
            P("dp", "mp"),
            P("dp", "mp"),
            P(None, "dp"),
            P(None, "dp"),
            P(None, ("dp", "mp"), None),
        ),
        out_specs=(
            P(None, ("dp", "mp"), None),
            P(None, ("dp", "mp"), None),
            P(None, "dp", "mp"),
            P("dp", "mp"),
            P("dp", "mp"),
            P("dp", "mp"),
            P(None, "dp"),
            P(None, "dp"),
        ),
        check_vma=False,
    )
```

time: 702 us -> 510 us (0.73)
  waiting for transfers between devices: 322 us -> 151 us
  starting transfers between devices: 86.3 us -> 66.8 us
  local copies, waits for them, and re-layouts: 45 us -> 62.3 us
  between operations: 2.28 us -> 15.5 us
  Pallas kernels: 149 us -> 137 us
  blocking collectives: 10.8 us -> 0 us
    ppermute x118 -> x59, waiting for transfers between devices: 322 us -> 150 us  [the longest x57 144 us: send(): result = lax.ppermute(value, axis, pairs)]
    ppermute x118 -> x59, starting transfers between devices: 86.3 us -> 66.7 us  [the longest x57 61.8 us: send(): result = lax.ppermute(value, axis, pairs)]
    slice x19 -> x28, local copies, waits for them, and re-layouts: 1.9 us -> 19.6 us  [the longest x8 11.9 us: step(): self.kept[i].append((x, received[:, at:at + x.shape[1]]))]
    psum x1 -> x0, blocking collectives: 10.8 us -> none  [body(): sums = lax.psum(sums, 'mp').T]
    pallas_call x5 -> x6, Pallas kernels: 140 us -> 133 us  [the longest x1 36.2 us: forward_block(): pl.pallas_call(forward_kernel(rows, steps, g // HEAD_DIM, factor), name='...]
    unnamed x124 -> x168, local copies, waits for them, and re-layouts: 30 us -> 32.4 us
    concatenate x6 -> x26, other arithmetic: 21 us -> 19.8 us  [the longest x12 13.6 us: join(): return pieces[0] if len(pieces) == 1 else jnp.concatenate(pieces, axis=0)]
  transfers between devices with their start and end apart: 118 -> 62, of which waited for: 44 -> 22; matrix products, arithmetic and copies ran while one was open for 13% -> 21% of each run, Pallas kernels for 13% -> 27%
where the time goes in v3:
time: 510 us; the launch traced here: 504 us
  waiting for transfers between devices  151 us (30%)
  Pallas kernels  137 us (27%)
  starting transfers between devices  66.8 us (13%)
  local copies, waits for them, and re-layouts  62.3 us (12%)
  matrix products  36.7 us (7%)
  other arithmetic  35.8 us (7%)
  between operations  15.5 us (3%)
    ppermute x57, waiting for transfers between devices, send(): result = lax.ppermute(value, axis, pairs)  144 us
    ppermute x57, starting transfers between devices, send(): result = lax.ppermute(value, axis, pairs)  61.8 us
    dot_general x16, matrix products, dot(): lax.dot_general(left, right, ((dims[:1], dims[1:]), ((), ())), preferred_...  36.7 us
    pallas_call x1, Pallas kernels, forward_block(): pl.pallas_call(forward_kernel(rows, steps, g // HEAD_DIM, factor), name='...  36.2 us
    pallas_call x1, Pallas kernels, backward_block(): pl.pallas_call(backward_kernel(rows, steps, g // HEAD_DIM, factor), name=...  35 us
    unnamed x168, local copies, waits for them, and re-layouts  32.4 us
    pallas_call x1, Pallas kernels, feed_back(): pl.pallas_call(feed_back_kernel(steps), name='feed_back', grid=(steps + t...  24.9 us
    pallas_call x1, Pallas kernels, feed_up(): pl.pallas_call(up_kernel(count), name='feed_up', grid=(ff // tile,), in_s...  16.5 us
  transfers between devices with their start and end apart: 62, of which 22 were waited for; matrix products, arithmetic and copies ran while one was open for 21% of the time, Pallas kernels for 27%

profile of v3, /device:TPU:0, one launch (start us, length us, event | category | flops | bytes accessed | tf_op | source)
XLA Modules:
  0.0 504.3 jit_solution(8920448754203836873)
XLA Ops:
  7.9 2.9 collective-permute-start
  12.7 1.6 collective-permute-start.10
  14.3 2.6 collective-permute-start.9
  18.2 1.6 collective-permute-start.1
  23.1 10.6 %collective-permute-done.9 = bf16[128,1024]{1,0:T(8,128)(2,1)S(1)} collective-permute-done((bf16[128,1024]{1,0:T(8,128)(2,1)S(1)}, bf16[128,1024]{1,0:T(8,128)(2,1)S(1)}, u32[]{:S(2)}, u32[]{:S(2)}) %collective-permute-start.9) | collective-permute-done | bytes 262176 | tf_op jit(solution)/shard_map/ppermute | solution.py:29
  33.8 1.6 collective-permute-start.11
  36.2 1.9 copy-done.1
  38.1 1.9 copy-done.2
  40.0 4.0 enter.1
  44.0 1.7 copy-done.3
  48.1 1.6 copy-done.23
  53.0 11.6 %collective-permute-done.6 = bf16[128,2048]{1,0:T(8,128)(2,1)S(1)} collective-permute-done((bf16[128,2048]{1,0:T(8,128)(2,1)S(1)}, bf16[128,2048]{1,0:T(8,128)(2,1)S(1)}, u32[]{:S(2)}, u32[]{:S(2)}) %collective-permute-start.6) | collective-permute-done | bytes 524320 | tf_op jit(solution)/shard_map/ppermute | solution.py:29
  65.3 20.4 %collective-permute-done.12 = bf16[256,2048]{1,0:T(8,128)(2,1)S(1)} collective-permute-done((bf16[256,2048]{1,0:T(8,128)(2,1)}, bf16[256,2048]{1,0:T(8,128)(2,1)S(1)}, u32[]{:S(2)}, u32[]{:S(2)}) %collective-permute-start.12) | collective-permute-done | bytes 1048608 | tf_op jit(solution)/shard_map/ppermute | solution.py:29
  92.2 2.7 fusion.115
  96.3 9.4 %collective-permute-done.14 = bf16[128,2048]{1,0:T(8,128)(2,1)} collective-permute-done((bf16[128,2048]{1,0:T(8,128)(2,1)}, bf16[128,2048]{1,0:T(8,128)(2,1)}, u32[]{:S(2)}, u32[]{:S(2)}) %collective-permute-start.14) | collective-permute-done | bytes 524320 | tf_op jit(solution)/shard_map/ppermute | solution.py:29
  105.6 5.8 %collective-permute-start.3 = (bf16[3,128,1024]{2,1,0:T(8,128)(2,1)}, bf16[3,128,1024]{2,1,0:T(8,128)(2,1)}, u32[]{:S(2)}, u32[]{:S(2)}) collective-permute-start(bf16[3,128,1024]{2,1,0:T(8,128)(2,1)} %get-tuple-element.114), channel_id=1, source_target_pairs={{0,1},{1,2},{2,3},{4,5},{5,6},{6,7},{8,9},{9,10},{10,11},{12,13},{... | collective-permute-start | bytes 2359304 | tf_op jit(solution)/shard_map/ppermute | solution.py:29
  114.7 19.6 %collective-permute-done.4.after = bf16[3,128,1024]{2,1,0:T(8,128)(2,1)} collective-permute-done((bf16[3,128,1024]{2,1,0:T(8,128)(2,1)}, bf16[3,128,1024]{2,1,0:T(8,128)(2,1)}, u32[]{:S(2)}, u32[]{:S(2)}) %collective-permute-start.4) | collective-permute-done | bytes 786464 | tf_op jit(solution)/shard_map/ppermute | solution.py:29
  135.9 36.2 %attention_forward.1 = (bf16[3,512,3072]{2,1,0:T(8,128)(2,1)}, bf16[2,768,512]{2,1,0:T(8,128)(2,1)S(1)}, f32[768,1024]{1,0:T(8,128)S(1)}, bf16[768,1024]{1,0:T(8,128)(2,1)S(1)}) custom-call(bf16[3,128,1024]{2,1,0:T(8,128)(2,1)} %collective-permute-done.3.before, bf16[3,256,1024]{2,1,0:T(8,128)(2,1)S(1)} %bitcast.236, ...), custom_call_target="tpu_custom_call" | custom-call | flops 12884901888 | bytes 31457280 | tf_op jit(solution)/shard_map/attention_forward/pallas_call | solution.py:467
  172.2 1.7 copy-done.30
  173.9 1.6 pad_maximum_fusion.2.top_a.up_top_a
  175.7 3.0 pad_maximum_fusion.3.top_b.up_top_b
  183.6 10.8 %collective-permute-done.17 = bf16[128,2048]{1,0:T(8,128)(2,1)S(1)} collective-permute-done((bf16[128,2048]{1,0:T(8,128)(2,1)S(1)}, bf16[128,2048]{1,0:T(8,128)(2,1)S(1)}, u32[]{:S(2)}, u32[]{:S(2)}) %collective-permute-start.17) | collective-permute-done | bytes 524320 | tf_op jit(solution)/shard_map/ppermute | solution.py:29
  198.1 16.5 %feed_up.1 = (bf16[2,768,2048]{2,1,0:T(8,128)(2,1)S(1)}, bf16[2,768,2048]{2,1,0:T(8,128)(2,1)S(1)}) custom-call(bf16[768,1024]{1,0:T(8,128)(2,1)S(1)} %copy-done.14, bf16[512,2048]{1,0:T(8,128)(2,1)S(1)} %pad_maximum_fusion.2.top_a.up_top_a, bf16[512,2048]{1,0:T(8,128)(2,1)} %collective-permute-done.19.bottom_a.up_bottom_a, ...), custom_call_target="tpu_custom_call" | custom-call | flops 6442450944 | bytes 20971520 | tf_op jit(solution)/shard_map/feed_up/pallas_call | solution.py:526
  214.6 2.6 copy-done.32
  217.2 3.3 fusion.27
  220.5 3.2 fusion.24
  225.7 3.0 pad_maximum_fusion.5.down_top_b.top_b
  229.2 4.8 convert_add_fusion.2
  236.6 3.5 convert_add_fusion.3
  243.3 24.9 %feed_back.1 = (bf16[2,768,2048]{2,1,0:T(8,128)(2,1)}, f32[768,1024]{1,0:T(8,128)}, bf16[768,1024]{1,0:T(8,128)(2,1)S(1)}, f32[16,1024]{1,0:T(8,128)S(1)}) custom-call(bf16[768,1024]{1,0:T(8,128)(2,1)S(1)} %copy-done.12, bf16[512,2048]{1,0:T(8,128)(2,1)} %pad_maximum_fusion.4.down_top_a.top_a, ...), custom_call_target="tpu_custom_call" | custom-call | flops 12884901888 | bytes 40370176 | tf_op jit(solution)/shard_map/feed_back/pallas_call | solution.py:650
  268.4 1.8 copy-done.29
  273.6 2.2 bitcast_add_fusion.1
  276.0 1.9 fusion.30
  277.9 1.9 fusion.33
  283.0 5.0 collective-permute-start.28
  291.7 11.4 %collective-permute-done.53 = bf16[128,2048]{1,0:T(8,128)(2,1)S(1)} collective-permute-done((bf16[128,2048]{1,0:T(8,128)(2,1)S(1)}, bf16[128,2048]{1,0:T(8,128)(2,1)S(1)}, u32[]{:S(2)}, u32[]{:S(2)}) %collective-permute-start.53) | collective-permute-done | bytes 524320 | tf_op jit(solution)/shard_map/ppermute | solution.py:29
  305.0 1.9 convert_add_fusion.1
  306.9 1.9 convert_add_fusion
  318.8 1.6 copy-done.7
  325.2 35.0 %attention_backward.1 = (bf16[2,768,1536]{2,1,0:T(8,128)(2,1)}, f32[768,1024]{1,0:T(8,128)S(1)}) custom-call(bf16[3,128,1024]{2,1,0:T(8,128)(2,1)S(1)} %copy-done.27, bf16[3,256,1024]{2,1,0:T(8,128)(2,1)S(1)} %bitcast.238, bf16[3,128,1024]{2,1,0:T(8,128)(2,1)S(1)} %copy-done.25, bf16[512,2048]{1,0:T(8,128)(2,1)} %pad_maximum_fusion.top_a, ...), custom_call_target="tpu_custom_call" | custom-call | flops 14495514624 | bytes 36700160 | tf_op jit(solution)/shard_map/attention_backward/pallas_call | solution.py:716
  361.4 1.6 slice.491
  363.5 2.2 slice.497
  370.8 2.6 convolution_convert_fusion.1
  375.9 2.7 convolution_convert_fusion
  380.3 11.8 %collective-permute-done.40 = bf16[128,2560]{1,0:T(8,128)(2,1)} collective-permute-done((bf16[128,2560]{1,0:T(8,128)(2,1)}, bf16[128,2560]{1,0:T(8,128)(2,1)}, u32[]{:S(2)}, u32[]{:S(2)}) %collective-permute-start.40) | collective-permute-done | bytes 655392 | tf_op jit(solution)/shard_map/ppermute | solution.py:29
  393.0 1.9 slice.505
  395.9 2.0 slice.509
  397.9 3.7 convolution_add_fusion.1
  403.7 3.0 convolution_add_fusion
  407.8 5.9 %leave.1 = (f32[768,1024]{1,0:T(8,128)}, f32[16,1024]{1,0:T(8,128)S(1)}) custom-call(s32[8]{0:T(128)S(1)} %broadcast_xor_fusion.table_ref, f32[768,1024]{1,0:T(8,128)S(1)} %get-tuple-element.96.norm_one, f32[768,1024]{1,0:T(8,128)S(1)} %copy-done.4, f32[768,1024]{1,0:T(8,128)S(1)} %copy-done.5, f32[4,1024]{1,0:T(4,128)S(1)} %convert_bitcast_fusion.small), custom_call_target="tpu_custom_call" | custom-call | flops 23592960 | bytes 12582912 | tf_op jit(solution)/shard_map/leave/pallas_call | solution.py:769
  415.7 1.6 fusion.59
  420.6 1.7 collective-permute-start.49
  423.6 2.8 collective-permute-start.50
  426.5 1.6 collective-permute-start.57
  428.2 2.5 collective-permute-start.51
  430.7 6.8 %collective-permute-done.57 = f32[128,4]{0,1:T(4,128)S(1)} collective-permute-done((f32[128,4]{0,1:T(4,128)S(1)}, f32[128,4]{0,1:T(4,128)S(1)}, u32[]{:S(2)}, u32[]{:S(2)}) %collective-permute-start.57) | collective-permute-done | bytes 2080 | tf_op jit(solution)/shard_map/ppermute | solution.py:889
  437.5 3.2 collective-permute-start.58
  440.7 14.2 %feed_down.1 = f32[768,1024]{1,0:T(8,128)} custom-call(s32[8]{0:T(128)S(1)} %broadcast_xor_fusion.table_ref, bf16[2,768,2048]{2,1,0:T(8,128)(2,1)S(1)} %bitcast.232, bf16[512,2048]{1,0:T(8,128)(2,1)} %pad_maximum_fusion.4.down_top_a.top_a, bf16[512,2048]{1,0:T(8,128)(2,1)} %collective-permute-done.25.down_bottom_a.bottom_a, ...), custom_call_target="tpu_custom_call" | custom-call | flops 6442450944 | bytes 20971520 | tf_op jit(solution)/shard_map/feed_down/pallas_call | solution.py:578
  460.0 15.5 %collective-permute-done.45 = bf16[256,1536]{1,0:T(8,128)(2,1)S(1)} collective-permute-done((bf16[256,1536]{1,0:T(8,128)(2,1)S(1)}, bf16[256,1536]{1,0:T(8,128)(2,1)S(1)}, u32[]{:S(2)}, u32[]{:S(2)}) %collective-permute-start.45) | collective-permute-done | bytes 786464 | tf_op jit(solution)/shard_map/ppermute | solution.py:29
  476.7 4.7 collective-permute-done.43
  481.7 1.9 collective-permute-done.46
  484.1 1.7 collective-permute-start.48
  486.4 4.9 collective-permute-done.44
  491.3 5.2 %collective-permute-done.47 = bf16[128,768]{1,0:T(8,128)(2,1)S(1)} collective-permute-done((bf16[128,768]{1,0:T(8,128)(2,1)S(1)}, bf16[128,768]{1,0:T(8,128)(2,1)S(1)}, u32[]{:S(2)}, u32[]{:S(2)}) %collective-permute-start.47) | collective-permute-done | bytes 196640 | tf_op jit(solution)/shard_map/ppermute | solution.py:29
  (374 shorter events, 101.8 us)
Async XLA Ops:
  7.2 81.5 %all-gather.5.cloned.1.call-start = ((), (), s32[]{:S(2)}) async-start(), calls=%async_computation.2 | async-start | bytes 1310720 | tf_op jit(solution)/shard_map/all_gather | solution.py:808
  7.9 10.3 %collective-permute-start = (bf16[128,4]{0,1:T(4,128)(2,1)S(1)}, bf16[128,4]{0,1:T(4,128)(2,1)S(1)}, u32[]{:S(2)}, u32[]{:S(2)}) collective-permute-start(bf16[128,4]{0,1:T(4,128)(2,1)S(1)} %maximum_bitcast_fusion), channel_id=1, source_target_pairs={{0,8},{4,12},{8,0},{12,4},{16,24},{20,28},{24,16},{28,20},{1,9},{5... | collective-permute-start | bytes 3080 | tf_op jit(solution)/shard_map/ppermute | solution.py:29
  12.7 21.1 %collective-permute-start.10 = (bf16[128,1024]{1,0:T(8,128)(2,1)S(1)}, bf16[128,1024]{1,0:T(8,128)(2,1)S(1)}, u32[]{:S(2)}, u32[]{:S(2)}) collective-permute-start(bf16[128,1024]{1,0:T(8,128)(2,1)S(1)} %pad_maximum_fusion.26), channel_id=1, source_target_pairs={{0,1},{1,2},{2,3},{3,0},{4,5},{5,6},{6,7},{7,4},{8,9},{9,10},{10,1... | collective-permute-start | bytes 786440 | tf_op jit(solution)/shard_map/ppermute | solution.py:29
  14.3 19.4 %collective-permute-start.9 = (bf16[128,1024]{1,0:T(8,128)(2,1)S(1)}, bf16[128,1024]{1,0:T(8,128)(2,1)S(1)}, u32[]{:S(2)}, u32[]{:S(2)}) collective-permute-start(bf16[128,1024]{1,0:T(8,128)(2,1)S(1)} %pad_maximum_fusion.26), channel_id=1, source_target_pairs={{0,2},{1,3},{2,0},{3,1},{4,6},{5,7},{6,4},{7,5},{8,10},{9,11},{10,... | collective-permute-start | bytes 786440 | tf_op jit(solution)/shard_map/ppermute | solution.py:29
  16.9 32.8 %collective-permute-start.5 = (bf16[128,1024]{1,0:T(8,128)(2,1)S(1)}, bf16[128,1024]{1,0:T(8,128)(2,1)S(1)}, u32[]{:S(2)}, u32[]{:S(2)}) collective-permute-start(bf16[128,1024]{1,0:T(8,128)(2,1)S(1)} %pad_maximum_fusion.26), channel_id=1, source_target_pairs={{0,3},{1,0},{2,1},{3,2},{4,7},{5,4},{6,5},{7,6},{8,11},{9,8},{10,9... | collective-permute-start | bytes 786440 | tf_op jit(solution)/shard_map/ppermute | solution.py:29
  18.2 3.7 collective-permute-start.1
  21.9 1.2 collective-permute-start.2
  33.8 16.6 %collective-permute-start.11 = (bf16[128,2048]{1,0:T(8,128)(2,1)S(1)}, bf16[128,2048]{1,0:T(8,128)(2,1)S(1)}, u32[]{:S(2)}, u32[]{:S(2)}) collective-permute-start(bf16[128,2048]{1,0:T(8,128)(2,1)S(1)} %constant_dynamic-update-slice_fusion.5), channel_id=1, source_target_pairs={{0,16},{4,20},{8,24},{12,28},{16,0},{20,4},{24,8},{28,12},{1,17},{... | collective-permute-start | bytes 1572872 | tf_op jit(solution)/shard_map/ppermute | solution.py:29
  49.7 14.9 %collective-permute-start.6 = (bf16[128,2048]{1,0:T(8,128)(2,1)S(1)}, bf16[128,2048]{1,0:T(8,128)(2,1)S(1)}, u32[]{:S(2)}, u32[]{:S(2)}) collective-permute-start(bf16[128,2048]{1,0:T(8,128)(2,1)S(1)} %constant_dynamic-update-slice_fusion), channel_id=1, source_target_pairs={{0,8},{4,12},{8,0},{12,4},{16,24},{20,28},{24,16},{28,20},{1,9},{5... | collective-permute-start | bytes 1572872 | tf_op jit(solution)/shard_map/ppermute | solution.py:29
  51.4 34.3 %collective-permute-start.12 = (bf16[256,2048]{1,0:T(8,128)(2,1)}, bf16[256,2048]{1,0:T(8,128)(2,1)S(1)}, u32[]{:S(2)}, u32[]{:S(2)}) collective-permute-start(bf16[256,2048]{1,0:T(8,128)(2,1)} %pad_maximum_fusion.11), channel_id=1, source_target_pairs={{0,8},{4,12},{8,0},{12,4},{16,24},{20,28},{24,16},{28,20},{1,9},{5... | collective-permute-start | bytes 3145736 | tf_op jit(solution)/shard_map/ppermute | solution.py:29
  52.9 126.3 %all-gather.7.cloned.1.call-start = ((), (), s32[]{:S(2)}) async-start(), calls=%async_computation.3 | async-start | bytes 1310720 | tf_op jit(solution)/shard_map/all_gather | solution.py:809
  64.7 22.5 %collective-permute-start.7 = (bf16[256,2048]{1,0:T(8,128)(2,1)S(1)}, bf16[256,2048]{1,0:T(8,128)(2,1)S(1)}, u32[]{:S(2)}, u32[]{:S(2)}) collective-permute-start(bf16[256,2048]{1,0:T(8,128)(2,1)S(1)} %pad_maximum_fusion.10), channel_id=1, source_target_pairs={{0,16},{4,20},{8,24},{12,28},{16,0},{20,4},{24,8},{28,12},{1,17},{... | collective-permute-start | bytes 3145736 | tf_op jit(solution)/shard_map/ppermute | solution.py:29
  86.0 49.9 %copy-start.6 = (bf16[512,2048]{1,0:T(8,128)(2,1)}, bf16[512,2048]{1,0:T(8,128)(2,1)S(1)}, u32[]{:S(2)}) copy-start(bf16[512,2048]{1,0:T(8,128)(2,1)S(1)} %pad_maximum_fusion.1.top_b) | copy-start | bytes 6291460
  86.0 49.9 %collective-permute-start.13 = (bf16[512,2048]{1,0:T(8,128)(2,1)S(1)}, bf16[512,2048]{1,0:T(8,128)(2,1)}, u32[]{:S(2)}, u32[]{:S(2)}) collective-permute-start(bf16[512,2048]{1,0:T(8,128)(2,1)S(1)} %pad_maximum_fusion.1.top_b), channel_id=1, source_target_pairs={{0,4},{4,0},{8,12},{12,8},{16,20},{20,16},{24,28},{28,24},{1,5},{5... | collective-permute-start | bytes 6291464 | tf_op jit(solution)/shard_map/ppermute | solution.py:29
  88.7 47.2 %collective-permute-start.8 = (bf16[512,2048]{1,0:T(8,128)(2,1)}, bf16[512,2048]{1,0:T(8,128)(2,1)}, u32[]{:S(2)}, u32[]{:S(2)}) collective-permute-start(bf16[512,2048]{1,0:T(8,128)(2,1)} %pad_maximum_fusion.top_a), channel_id=1, source_target_pairs={{0,4},{4,0},{8,12},{12,8},{16,20},{20,16},{24,28},{28,24},{1,5},{5... | collective-permute-start | bytes 6291464 | tf_op jit(solution)/shard_map/ppermute | solution.py:29
  91.0 14.7 %collective-permute-start.14 = (bf16[128,2048]{1,0:T(8,128)(2,1)}, bf16[128,2048]{1,0:T(8,128)(2,1)}, u32[]{:S(2)}, u32[]{:S(2)}) collective-permute-start(bf16[128,2048]{1,0:T(8,128)(2,1)} %pad_maximum_fusion.18), channel_id=1, source_target_pairs={{0,8},{4,12},{8,0},{12,4},{16,24},{20,28},{24,16},{28,20},{1,9},{5... | collective-permute-start | bytes 1572872 | tf_op jit(solution)/shard_map/ppermute | solution.py:29
  91.5 406.0 %reduce-scatter.2.cloned.1.call-start = ((), (), s32[]{:S(2)}) async-start(), calls=%async_computation.1 | async-start | bytes 2621440 | tf_op jit(solution)/shard_map/reduce_scatter | solution.py:240
  91.6 19.8 %collective-permute-start.15 = (bf16[128,2048]{1,0:T(8,128)(2,1)S(1)}, bf16[128,2048]{1,0:T(8,128)(2,1)S(1)}, u32[]{:S(2)}, u32[]{:S(2)}) collective-permute-start(bf16[128,2048]{1,0:T(8,128)(2,1)S(1)} %pad_maximum_fusion.19), channel_id=1, source_target_pairs={{0,16},{4,20},{8,24},{12,28},{16,0},{20,4},{24,8},{28,12},{1,17},{... | collective-permute-start | bytes 1572872 | tf_op jit(solution)/shard_map/ppermute | solution.py:29
  95.0 39.4 %collective-permute-start.4 = (bf16[3,128,1024]{2,1,0:T(8,128)(2,1)}, bf16[3,128,1024]{2,1,0:T(8,128)(2,1)}, u32[]{:S(2)}, u32[]{:S(2)}) collective-permute-start(bf16[3,128,1024]{2,1,0:T(8,128)(2,1)} %get-tuple-element.113), channel_id=1, source_target_pairs={{1,0},{2,1},{3,2},{5,4},{6,5},{7,6},{9,8},{10,9},{11,10},{13,12},{... | collective-permute-start | bytes 2359304 | tf_op jit(solution)/shard_map/ppermute | solution.py:29
  105.6 30.3 %collective-permute-start.3 = (bf16[3,128,1024]{2,1,0:T(8,128)(2,1)}, bf16[3,128,1024]{2,1,0:T(8,128)(2,1)}, u32[]{:S(2)}, u32[]{:S(2)}) collective-permute-start(bf16[3,128,1024]{2,1,0:T(8,128)(2,1)} %get-tuple-element.114), channel_id=1, source_target_pairs={{0,1},{1,2},{2,3},{4,5},{5,6},{6,7},{8,9},{9,10},{10,11},{12,13},{... | collective-permute-start | bytes 2359304 | tf_op jit(solution)/shard_map/ppermute | solution.py:29
  114.0 59.8 %collective-permute-start.18 = (bf16[256,2048]{1,0:T(8,128)(2,1)S(1)}, bf16[256,2048]{1,0:T(8,128)(2,1)S(1)}, u32[]{:S(2)}, u32[]{:S(2)}) collective-permute-start(bf16[256,2048]{1,0:T(8,128)(2,1)S(1)} %pad_maximum_fusion.12), channel_id=1, source_target_pairs={{0,16},{4,20},{8,24},{12,28},{16,0},{20,4},{24,8},{28,12},{1,17},{... | collective-permute-start | bytes 3145736 | tf_op jit(solution)/shard_map/ppermute | solution.py:29
  134.3 39.5 %collective-permute-start.20 = (bf16[256,2048]{1,0:T(8,128)(2,1)S(1)}, bf16[256,2048]{1,0:T(8,128)(2,1)S(1)}, u32[]{:S(2)}, u32[]{:S(2)}) collective-permute-start(bf16[256,2048]{1,0:T(8,128)(2,1)S(1)} %pad_maximum_fusion.13), channel_id=1, source_target_pairs={{0,8},{4,12},{8,0},{12,4},{16,24},{20,28},{24,16},{28,20},{1,9},{5... | collective-permute-start | bytes 3145736 | tf_op jit(solution)/shard_map/ppermute | solution.py:29
  135.9 38.0 %copy-start.47 = (bf16[128,1024]{1,0:T(8,128)(2,1)S(1)}, bf16[128,1024]{1,0:T(8,128)(2,1)}, u32[]{:S(2)}) copy-start(bf16[128,1024]{1,0:T(8,128)(2,1)} %copy-done.46) | copy-start | bytes 786436
  175.6 22.5 %collective-permute-start.19 = (bf16[512,2048]{1,0:T(8,128)(2,1)S(1)}, bf16[512,2048]{1,0:T(8,128)(2,1)}, u32[]{:S(2)}, u32[]{:S(2)}) collective-permute-start(bf16[512,2048]{1,0:T(8,128)(2,1)S(1)} %pad_maximum_fusion.2.top_a.up_top_a), channel_id=1, source_target_pairs={{0,4},{4,0},{8,12},{12,8},{16,20},{20,16},{24,28},{28,24},{1,5},{5... | collective-permute-start | bytes 6291464 | tf_op jit(solution)/shard_map/ppermute | solution.py:29
  178.7 19.4 %collective-permute-start.21 = (bf16[512,2048]{1,0:T(8,128)(2,1)}, bf16[512,2048]{1,0:T(8,128)(2,1)}, u32[]{:S(2)}, u32[]{:S(2)}) collective-permute-start(bf16[512,2048]{1,0:T(8,128)(2,1)} %pad_maximum_fusion.3.top_b.up_top_b), channel_id=1, source_target_pairs={{0,4},{4,0},{8,12},{12,8},{16,20},{20,16},{24,28},{28,24},{1,5},{5... | collective-permute-start | bytes 6291464 | tf_op jit(solution)/shard_map/ppermute | solution.py:29
  180.5 13.9 %collective-permute-start.17 = (bf16[128,2048]{1,0:T(8,128)(2,1)S(1)}, bf16[128,2048]{1,0:T(8,128)(2,1)S(1)}, u32[]{:S(2)}, u32[]{:S(2)}) collective-permute-start(bf16[128,2048]{1,0:T(8,128)(2,1)S(1)} %pad_maximum_fusion.21), channel_id=1, source_target_pairs={{0,16},{4,20},{8,24},{12,28},{16,0},{20,4},{24,8},{28,12},{1,17},{... | collective-permute-start | bytes 1572872 | tf_op jit(solution)/shard_map/ppermute | solution.py:29
  182.1 13.6 %collective-permute-start.16 = (bf16[128,2048]{1,0:T(8,128)(2,1)S(1)}, bf16[128,2048]{1,0:T(8,128)(2,1)S(1)}, u32[]{:S(2)}, u32[]{:S(2)}) collective-permute-start(bf16[128,2048]{1,0:T(8,128)(2,1)S(1)} %pad_maximum_fusion.20), channel_id=1, source_target_pairs={{0,8},{4,12},{8,0},{12,4},{16,24},{20,28},{24,16},{28,20},{1,9},{5... | collective-permute-start | bytes 1572872 | tf_op jit(solution)/shard_map/ppermute | solution.py:29
  195.8 28.3 %collective-permute-start.26 = (bf16[256,2048]{1,0:T(8,128)(2,1)S(1)}, bf16[256,2048]{1,0:T(8,128)(2,1)S(1)}, u32[]{:S(2)}, u32[]{:S(2)}) collective-permute-start(bf16[256,2048]{1,0:T(8,128)(2,1)S(1)} %pad_maximum_fusion.15), channel_id=1, source_target_pairs={{0,8},{4,12},{8,0},{12,4},{16,24},{20,28},{24,16},{28,20},{1,9},{5... | collective-permute-start | bytes 3145736 | tf_op jit(solution)/shard_map/ppermute | solution.py:29
  197.5 26.7 %collective-permute-start.24 = (bf16[256,2048]{1,0:T(8,128)(2,1)S(1)}, bf16[256,2048]{1,0:T(8,128)(2,1)S(1)}, u32[]{:S(2)}, u32[]{:S(2)}) collective-permute-start(bf16[256,2048]{1,0:T(8,128)(2,1)S(1)} %pad_maximum_fusion.14), channel_id=1, source_target_pairs={{0,16},{4,20},{8,24},{12,28},{16,0},{20,4},{24,8},{28,12},{1,17},{... | collective-permute-start | bytes 3145736 | tf_op jit(solution)/shard_map/ppermute | solution.py:29
  220.5 8.8 %collective-permute-start.23 = (bf16[512,2048]{1,0:T(8,128)(2,1)}, bf16[512,2048]{1,0:T(8,128)(2,1)}, u32[]{:S(2)}, u32[]{:S(2)}) collective-permute-start(bf16[512,2048]{1,0:T(8,128)(2,1)} %fusion.27), channel_id=1, source_target_pairs={{0,4},{4,0},{8,12},{12,8},{16,20},{20,16},{24,28},{28,24},{1,5},{5... | collective-permute-start | bytes 6291464 | tf_op jit(solution)/shard_map/ppermute | solution.py:29
  223.6 12.7 %collective-permute-start.22 = (bf16[512,2048]{1,0:T(8,128)(2,1)}, bf16[512,2048]{1,0:T(8,128)(2,1)}, u32[]{:S(2)}, u32[]{:S(2)}) collective-permute-start(bf16[512,2048]{1,0:T(8,128)(2,1)} %fusion.24), channel_id=1, source_target_pairs={{0,4},{4,0},{8,12},{12,8},{16,20},{20,16},{24,28},{28,24},{1,5},{5... | collective-permute-start | bytes 6291464 | tf_op jit(solution)/shard_map/ppermute | solution.py:29
  225.7 16.2 %collective-permute-start.25 = (bf16[512,2048]{1,0:T(8,128)(2,1)}, bf16[512,2048]{1,0:T(8,128)(2,1)}, u32[]{:S(2)}, u32[]{:S(2)}) collective-permute-start(bf16[512,2048]{1,0:T(8,128)(2,1)} %pad_maximum_fusion.4.down_top_a.top_a), channel_id=1, source_target_pairs={{0,4},{4,0},{8,12},{12,8},{16,20},{20,16},{24,28},{28,24},{1,5},{5... | collective-permute-start | bytes 6291464 | tf_op jit(solution)/shard_map/ppermute | solution.py:29
  228.7 13.2 %collective-permute-start.27 = (bf16[512,2048]{1,0:T(8,128)(2,1)}, bf16[512,2048]{1,0:T(8,128)(2,1)}, u32[]{:S(2)}, u32[]{:S(2)}) collective-permute-start(bf16[512,2048]{1,0:T(8,128)(2,1)} %pad_maximum_fusion.5.down_top_b.top_b), channel_id=1, source_target_pairs={{0,4},{4,0},{8,12},{12,8},{16,20},{20,16},{24,28},{28,24},{1,5},{5... | collective-permute-start | bytes 6291464 | tf_op jit(solution)/shard_map/ppermute | solution.py:29
  235.3 36.8 %collective-permute-start.31 = (bf16[256,2048]{1,0:T(8,128)(2,1)}, bf16[256,2048]{1,0:T(8,128)(2,1)}, u32[]{:S(2)}, u32[]{:S(2)}) collective-permute-start(bf16[256,2048]{1,0:T(8,128)(2,1)} %bitcast.14), channel_id=1, source_target_pairs={{0,8},{4,12},{8,0},{12,4},{16,24},{20,28},{24,16},{28,20},{1,9},{5... | collective-permute-start | bytes 3145736 | tf_op jit(solution)/shard_map/ppermute | solution.py:29
  240.3 31.7 %collective-permute-start.30 = (bf16[256,2048]{1,0:T(8,128)(2,1)S(1)}, bf16[256,2048]{1,0:T(8,128)(2,1)S(1)}, u32[]{:S(2)}, u32[]{:S(2)}) collective-permute-start(bf16[256,2048]{1,0:T(8,128)(2,1)S(1)} %fusion.55), channel_id=1, source_target_pairs={{0,16},{4,20},{8,24},{12,28},{16,0},{20,4},{24,8},{28,12},{1,17},{... | collective-permute-start | bytes 3145736 | tf_op jit(solution)/shard_map/ppermute | solution.py:29
  270.8 18.8 %collective-permute-start.33 = (bf16[512,512]{1,0:T(8,128)(2,1)S(1)}, bf16[512,512]{1,0:T(8,128)(2,1)S(1)}, u32[]{:S(2)}, u32[]{:S(2)}) collective-permute-start(bf16[512,512]{1,0:T(8,128)(2,1)S(1)} %convolution_convert_fusion.3), channel_id=1, source_target_pairs={{0,4},{4,0},{8,12},{12,8},{16,20},{20,16},{24,28},{28,24},{1,5},{5... | collective-permute-start | bytes 1572872 | tf_op jit(solution)/shard_map/ppermute | solution.py:29
  271.5 11.5 %collective-permute-start.35 = (bf16[512,512]{1,0:T(8,128)(2,1)S(1)}, bf16[512,512]{1,0:T(8,128)(2,1)S(1)}, u32[]{:S(2)}, u32[]{:S(2)}) collective-permute-start(bf16[512,512]{1,0:T(8,128)(2,1)S(1)} %convolution_convert_fusion.2), channel_id=1, source_target_pairs={{0,4},{4,0},{8,12},{12,8},{16,20},{20,16},{24,28},{28,24},{1,5},{5... | collective-permute-start | bytes 1572872 | tf_op jit(solution)/shard_map/ppermute | solution.py:29
  277.8 27.1 %collective-permute-start.32 = (bf16[512,2048]{1,0:T(8,128)(2,1)S(1)}, bf16[512,2048]{1,0:T(8,128)(2,1)S(1)}, u32[]{:S(2)}, u32[]{:S(2)}) collective-permute-start(bf16[512,2048]{1,0:T(8,128)(2,1)S(1)} %fusion.30), channel_id=1, source_target_pairs={{0,4},{4,0},{8,12},{12,8},{16,20},{20,16},{24,28},{28,24},{1,5},{5... | collective-permute-start | bytes 6291464 | tf_op jit(solution)/shard_map/ppermute | solution.py:29
  279.8 27.1 %collective-permute-start.34 = (bf16[512,2048]{1,0:T(8,128)(2,1)S(1)}, bf16[512,2048]{1,0:T(8,128)(2,1)S(1)}, u32[]{:S(2)}, u32[]{:S(2)}) collective-permute-start(bf16[512,2048]{1,0:T(8,128)(2,1)S(1)} %fusion.33), channel_id=1, source_target_pairs={{0,4},{4,0},{8,12},{12,8},{16,20},{20,16},{24,28},{28,24},{1,5},{5... | collective-permute-start | bytes 6291464 | tf_op jit(solution)/shard_map/ppermute | solution.py:29
  281.7 35.2 %collective-permute-start.29 = (bf16[3,128,1024]{2,1,0:T(8,128)(2,1)}, bf16[3,128,1024]{2,1,0:T(8,128)(2,1)S(1)}, u32[]{:S(2)}, u32[]{:S(2)}) collective-permute-start(bf16[3,128,1024]{2,1,0:T(8,128)(2,1)} %get-tuple-element.111), channel_id=1, source_target_pairs={{1,0},{2,1},{3,2},{5,4},{6,5},{7,6},{9,8},{10,9},{11,10},{13,12},{... | collective-permute-start | bytes 2359304 | tf_op jit(solution)/shard_map/ppermute | solution.py:29
  283.0 34.8 %collective-permute-start.28 = (bf16[3,128,1024]{2,1,0:T(8,128)(2,1)}, bf16[3,128,1024]{2,1,0:T(8,128)(2,1)S(1)}, u32[]{:S(2)}, u32[]{:S(2)}) collective-permute-start(bf16[3,128,1024]{2,1,0:T(8,128)(2,1)} %get-tuple-element.112), channel_id=1, source_target_pairs={{0,1},{1,2},{2,3},{4,5},{5,6},{6,7},{8,9},{9,10},{10,11},{12,13},{... | collective-permute-start | bytes 2359304 | tf_op jit(solution)/shard_map/ppermute | solution.py:29
  289.6 13.6 %collective-permute-start.53 = (bf16[128,2048]{1,0:T(8,128)(2,1)S(1)}, bf16[128,2048]{1,0:T(8,128)(2,1)S(1)}, u32[]{:S(2)}, u32[]{:S(2)}) collective-permute-start(bf16[128,2048]{1,0:T(8,128)(2,1)S(1)} %fusion.90), channel_id=1, source_target_pairs={{0,16},{4,20},{8,24},{12,28},{16,0},{20,4},{24,8},{28,12},{1,17},{... | collective-permute-start | bytes 1572872 | tf_op jit(solution)/shard_map/ppermute | solution.py:29
  303.1 70.3 %collective-permute-start.52 = (bf16[128,2048]{1,0:T(8,128)(2,1)}, bf16[128,2048]{1,0:T(8,128)(2,1)}, u32[]{:S(2)}, u32[]{:S(2)}) collective-permute-start(bf16[128,2048]{1,0:T(8,128)(2,1)} %fusion.89), channel_id=1, source_target_pairs={{0,8},{4,12},{8,0},{12,4},{16,24},{20,28},{24,16},{28,20},{1,9},{5... | collective-permute-start | bytes 1572872 | tf_op jit(solution)/shard_map/ppermute | solution.py:29
  311.8 48.4 %collective-permute-start.36 = (bf16[256,2560]{1,0:T(8,128)(2,1)}, bf16[256,2560]{1,0:T(8,128)(2,1)}, u32[]{:S(2)}, u32[]{:S(2)}) collective-permute-start(bf16[256,2560]{1,0:T(8,128)(2,1)} %pad_maximum_fusion.8), channel_id=1, source_target_pairs={{0,16},{4,20},{8,24},{12,28},{16,0},{20,4},{24,8},{28,12},{1,17},{... | collective-permute-start | bytes 3932168 | tf_op jit(solution)/shard_map/ppermute | solution.py:29
  314.5 49.0 %collective-permute-start.37 = (bf16[256,2560]{1,0:T(8,128)(2,1)}, bf16[256,2560]{1,0:T(8,128)(2,1)}, u32[]{:S(2)}, u32[]{:S(2)}) collective-permute-start(bf16[256,2560]{1,0:T(8,128)(2,1)} %pad_maximum_fusion.9), channel_id=1, source_target_pairs={{0,8},{4,12},{8,0},{12,4},{16,24},{20,28},{24,16},{28,20},{1,9},{5... | collective-permute-start | bytes 3932168 | tf_op jit(solution)/shard_map/ppermute | solution.py:29
  373.4 24.5 %collective-permute-start.38 = (bf16[512,1536]{1,0:T(8,128)(2,1)}, bf16[512,1536]{1,0:T(8,128)(2,1)}, u32[]{:S(2)}, u32[]{:S(2)}) collective-permute-start(bf16[512,1536]{1,0:T(8,128)(2,1)} %convolution_convert_fusion.1), channel_id=1, source_target_pairs={{0,4},{4,0},{8,12},{12,8},{16,20},{20,16},{24,28},{28,24},{1,5},{5... | collective-permute-start | bytes 4718600 | tf_op jit(solution)/shard_map/ppermute | solution.py:29
  374.6 17.5 %collective-permute-start.40 = (bf16[128,2560]{1,0:T(8,128)(2,1)}, bf16[128,2560]{1,0:T(8,128)(2,1)}, u32[]{:S(2)}, u32[]{:S(2)}) collective-permute-start(bf16[128,2560]{1,0:T(8,128)(2,1)} %pad_maximum_fusion.16), channel_id=1, source_target_pairs={{0,8},{4,12},{8,0},{12,4},{16,24},{20,28},{24,16},{28,20},{1,9},{5... | collective-permute-start | bytes 1966088 | tf_op jit(solution)/shard_map/ppermute | solution.py:29
  375.4 19.6 %collective-permute-start.41 = (bf16[128,2560]{1,0:T(8,128)(2,1)}, bf16[128,2560]{1,0:T(8,128)(2,1)}, u32[]{:S(2)}, u32[]{:S(2)}) collective-permute-start(bf16[128,2560]{1,0:T(8,128)(2,1)} %pad_maximum_fusion.17), channel_id=1, source_target_pairs={{0,16},{4,20},{8,24},{12,28},{16,0},{20,4},{24,8},{28,12},{1,17},{... | collective-permute-start | bytes 1966088 | tf_op jit(solution)/shard_map/ppermute | solution.py:29
  378.6 25.1 %collective-permute-start.39 = (bf16[512,1536]{1,0:T(8,128)(2,1)}, bf16[512,1536]{1,0:T(8,128)(2,1)}, u32[]{:S(2)}, u32[]{:S(2)}) collective-permute-start(bf16[512,1536]{1,0:T(8,128)(2,1)} %convolution_convert_fusion), channel_id=1, source_target_pairs={{0,4},{4,0},{8,12},{12,8},{16,20},{20,16},{24,28},{28,24},{1,5},{5... | collective-permute-start | bytes 4718600 | tf_op jit(solution)/shard_map/ppermute | solution.py:29
  402.7 54.4 %collective-permute-start.42 = (bf16[256,1536]{1,0:T(8,128)(2,1)}, bf16[256,1536]{1,0:T(8,128)(2,1)}, u32[]{:S(2)}, u32[]{:S(2)}) collective-permute-start(bf16[256,1536]{1,0:T(8,128)(2,1)} %fusion.61), channel_id=1, source_target_pairs={{0,16},{4,20},{8,24},{12,28},{16,0},{20,4},{24,8},{28,12},{1,17},{... | collective-permute-start | bytes 2359304 | tf_op jit(solution)/shard_map/ppermute | solution.py:29
  418.1 1.2 collective-permute-start.54
  419.3 3.6 collective-permute-start.55
  420.6 35.6 %collective-permute-start.49 = (bf16[128,1280]{1,0:T(8,128)(2,1)S(1)}, bf16[128,1280]{1,0:T(8,128)(2,1)S(1)}, u32[]{:S(2)}, u32[]{:S(2)}) collective-permute-start(bf16[128,1280]{1,0:T(8,128)(2,1)S(1)} %pad_maximum_fusion.23), channel_id=1, source_target_pairs={{0,1},{1,2},{2,3},{3,0},{4,5},{5,6},{6,7},{7,4},{8,9},{9,10},{10,1... | collective-permute-start | bytes 983048 | tf_op jit(solution)/shard_map/ppermute | solution.py:29
  422.9 3.6 collective-permute-start.56
  423.6 32.6 %collective-permute-start.50 = (bf16[128,1280]{1,0:T(8,128)(2,1)S(1)}, bf16[128,1280]{1,0:T(8,128)(2,1)S(1)}, u32[]{:S(2)}, u32[]{:S(2)}) collective-permute-start(bf16[128,1280]{1,0:T(8,128)(2,1)S(1)} %pad_maximum_fusion.24), channel_id=1, source_target_pairs={{0,2},{1,3},{2,0},{3,1},{4,6},{5,7},{6,4},{7,5},{8,10},{9,11},{10,... | collective-permute-start | bytes 983048 | tf_op jit(solution)/shard_map/ppermute | solution.py:29
  426.5 10.9 %collective-permute-start.57 = (f32[128,4]{0,1:T(4,128)S(1)}, f32[128,4]{0,1:T(4,128)S(1)}, u32[]{:S(2)}, u32[]{:S(2)}) collective-permute-start(f32[128,4]{0,1:T(4,128)S(1)} %slice_add_fusion.4), channel_id=1, source_target_pairs={{0,1},{1,0},{2,3},{3,2},{4,5},{5,4},{6,7},{7,6},{8,9},{9,8},{10,11... | collective-permute-start | bytes 6152 | tf_op jit(solution)/shard_map/ppermute | solution.py:889
  428.2 28.0 %collective-permute-start.51 = (bf16[128,1280]{1,0:T(8,128)(2,1)S(1)}, bf16[128,1280]{1,0:T(8,128)(2,1)S(1)}, u32[]{:S(2)}, u32[]{:S(2)}) collective-permute-start(bf16[128,1280]{1,0:T(8,128)(2,1)S(1)} %pad_maximum_fusion.25), channel_id=1, source_target_pairs={{0,3},{1,0},{2,1},{3,2},{4,7},{5,4},{6,5},{7,6},{8,11},{9,8},{10,9... | collective-permute-start | bytes 983048 | tf_op jit(solution)/shard_map/ppermute | solution.py:29
  437.5 17.5 %collective-permute-start.58 = (f32[128,4]{0,1:T(4,128)S(1)}, f32[128,4]{0,1:T(4,128)S(1)}, u32[]{:S(2)}, u32[]{:S(2)}) collective-permute-start(f32[128,4]{0,1:T(4,128)S(1)} %add.190), channel_id=1, source_target_pairs={{0,2},{1,3},{2,0},{3,1},{4,6},{5,7},{6,4},{7,5},{8,10},{9,11},{10,... | collective-permute-start | bytes 6152 | tf_op jit(solution)/shard_map/ppermute | solution.py:889
  454.9 20.5 %collective-permute-start.45 = (bf16[256,1536]{1,0:T(8,128)(2,1)S(1)}, bf16[256,1536]{1,0:T(8,128)(2,1)S(1)}, u32[]{:S(2)}, u32[]{:S(2)}) collective-permute-start(bf16[256,1536]{1,0:T(8,128)(2,1)S(1)} %bitcast.273), channel_id=1, source_target_pairs={{0,8},{4,12},{8,0},{12,4},{16,24},{20,28},{24,16},{28,20},{1,9},{5... | collective-permute-start | bytes 2359304 | tf_op jit(solution)/shard_map/ppermute | solution.py:29
  458.5 23.0 %collective-permute-start.43 = (bf16[128,1536]{1,0:T(8,128)(2,1)S(1)}, bf16[128,1536]{1,0:T(8,128)(2,1)S(1)}, u32[]{:S(2)}, u32[]{:S(2)}) collective-permute-start(bf16[128,1536]{1,0:T(8,128)(2,1)S(1)} %fusion.96), channel_id=1, source_target_pairs={{0,8},{4,12},{8,0},{12,4},{16,24},{20,28},{24,16},{28,20},{1,9},{5... | collective-permute-start | bytes 1179656 | tf_op jit(solution)/shard_map/ppermute | solution.py:29
  475.7 7.8 %collective-permute-start.46 = (bf16[128,1536]{1,0:T(8,128)(2,1)S(1)}, bf16[128,1536]{1,0:T(8,128)(2,1)S(1)}, u32[]{:S(2)}, u32[]{:S(2)}) collective-permute-start(bf16[128,1536]{1,0:T(8,128)(2,1)S(1)} %fusion.97), channel_id=1, source_target_pairs={{0,16},{4,20},{8,24},{12,28},{16,0},{20,4},{24,8},{28,12},{1,17},{... | collective-permute-start | bytes 1179656 | tf_op jit(solution)/shard_map/ppermute | solution.py:29
  481.6 9.7 %collective-permute-start.44 = (bf16[128,768]{1,0:T(8,128)(2,1)S(1)}, bf16[128,768]{1,0:T(8,128)(2,1)S(1)}, u32[]{:S(2)}, u32[]{:S(2)}) collective-permute-start(bf16[128,768]{1,0:T(8,128)(2,1)S(1)} %slice.766), channel_id=1, source_target_pairs={{0,1},{1,2},{2,3},{3,0},{4,5},{5,6},{6,7},{7,4},{8,9},{9,10},{10,1... | collective-permute-start | bytes 589832 | tf_op jit(solution)/shard_map/ppermute | solution.py:29
  483.7 12.9 %collective-permute-start.47 = (bf16[128,768]{1,0:T(8,128)(2,1)S(1)}, bf16[128,768]{1,0:T(8,128)(2,1)S(1)}, u32[]{:S(2)}, u32[]{:S(2)}) collective-permute-start(bf16[128,768]{1,0:T(8,128)(2,1)S(1)} %get-tuple-element.140), channel_id=1, source_target_pairs={{0,2},{1,3},{2,0},{3,1},{4,6},{5,7},{6,4},{7,5},{8,10},{9,11},{10,... | collective-permute-start | bytes 589832 | tf_op jit(solution)/shard_map/ppermute | solution.py:29
  484.1 12.5 %collective-permute-start.48 = (bf16[128,768]{1,0:T(8,128)(2,1)S(1)}, bf16[128,768]{1,0:T(8,128)(2,1)S(1)}, u32[]{:S(2)}, u32[]{:S(2)}) collective-permute-start(bf16[128,768]{1,0:T(8,128)(2,1)S(1)} %get-tuple-element.141), channel_id=1, source_target_pairs={{0,3},{1,0},{2,1},{3,2},{4,7},{5,4},{6,5},{7,6},{8,11},{9,8},{10,9... | collective-permute-start | bytes 589832 | tf_op jit(solution)/shard_map/ppermute | solution.py:29
  (79 other events, 669.3 us)
Sparse Core Ops, SparseCore 0:
  53.1 30.7 all-gather.4
  91.6 41.3 all-gather.6
  380.4 44.1 reduce-scatter.1

commit v4 on v3

--- a/solution.py
+++ b/solution.py
@@ -125,11 +125,12 @@
         pieces = self.pieces(i, order)
         return pieces[0] if len(pieces) == 1 else jnp.concatenate(pieces, axis=0)
 
-    def step(self, tokens=()):
+    def step(self, tokens=(), second=()):
         for i in range(2):
             bit = self.steps[i][0]
             value = self.join(i, self.known[i])
-            self.held[i] = [value, self.links.swap(after(value, *tokens), bit)]
+            value = after(value, *(second if i else tokens))
+            self.held[i] = [value, self.links.swap(value, bit)]
             self.known[i] = self.known[i] + [r ^ bit for r in self.known[i]]
             self.steps[i] = self.steps[i][1:]
         return [h[1] for h in self.held]
@@ -137,7 +138,7 @@
     def steps_but_last(self, tokens=()):
         received = []
         while len(self.steps[0]) > 1:
-            received = self.step(tokens)
+            received = self.step(tokens, tokens)
         return received
 
     def hold(self, tokens):
@@ -205,39 +206,34 @@
             result.append([r[:, j * width : (j + 1) * width] for r in pair for j in range(half)])
         return result
 
-    def shifts(self, natural, tokens=()):
-        mp = self.plan.mp
-        products = self.rows()
-        own = lax.axis_index("mp")
-        for n, rows in enumerate(products):
-            if natural[n]:
-                joined = jnp.stack(rows)
-                products[n] = [
-                    lax.dynamic_index_in_dim(joined, lax.rem(own + k, mp), 0, keepdims=False)
-                    for k in range(mp)
-                ]
-        self.total = [rows[0] for rows in products]
-        outs = []
-        for k in range(1, mp):
-            out = [rows[k].astype(LOW) for rows in products]
-            outs.append(out[0] if len(out) == 1 else jnp.concatenate(out, axis=1))
-        self.received = [
-            self.links.shift(after(value, *tokens), k + 1, 0) for k, value in enumerate(outs)
-        ]
-        return outs
-
-    def finish(self):
-        result, at = [], 0
-        for total in self.total:
-            for part in self.received:
-                total = total + part[:, at : at + total.shape[1]].astype(jnp.float32)
-            result.append(total)
-            at += total.shape[1]
-        return result
-
-    def reduce_columns(self):
-        joined = jnp.stack(self.rows()[0])
-        return lax.psum_scatter(joined, "mp", scatter_dimension=0, tiled=False)
+
+def own_first(blocks):
+    joined = jnp.stack(blocks)
+    own = lax.axis_index("mp")
+    return [
+        lax.dynamic_index_in_dim(joined, lax.rem(own + k, len(blocks)), 0, keepdims=False)
+        for k in range(len(blocks))
+    ]
+
+
+def shift_blocks(plan, links, products, tokens=()):
+    received = []
+    for k in range(1, plan.mp):
+        out = [blocks[k].astype(LOW) for blocks in products]
+        out = out[0] if len(out) == 1 else jnp.concatenate(out, axis=1)
+        received.append(links.shift(after(out, *tokens), k, 0))
+    result, at = [], 0
+    for blocks in products:
+        total = blocks[0]
+        for part in received:
+            total = total + part[:, at : at + total.shape[1]].astype(jnp.float32)
+        result.append(total)
+        at += total.shape[1]
+    return result
+
+
+def reduce_blocks(blocks):
+    return lax.psum_scatter(jnp.stack(blocks), "mp", scatter_dimension=0, tiled=False)
 
 
 def after(value, *tokens):
@@ -251,6 +247,7 @@
     return dot(left[:, :half], top, (1, 0)) + dot(left[:, half:], bottom, (1, 0))
 
 
+C = {"z_up": 0, "z_down": 0, "g_zup": 0, "g_enter": 0, "g_x1": 1, "g_zdown": 0, "g_x2a": 2, "g_x2b": 1, "g_x1up": 1, "h_core": 4, "t_fwd": 2, "h_up": 1, "h_down": 1, "t_up": 1, "h_down2": 1, "t_back": 1, "h_d2": 1, "p_down": 1, "t_down0": 1, "g_u": 1, "g_o": 0, "merge": 1, "t_bwd": 1, "h_sd": 0, "h_u2": 1, "first_u2": 1, "g_q": 1, "t_leave": 1, "h_uz": 1, "z_u": 0, "t_down": 2, "h_q2": 1, "t_down2": 0, "g_sums": 0}
 MEGA = 1 << 20
 LOG2E = 1.4426950408889634
 VM_FWD = 36
@@ -801,19 +798,41 @@
         rows_in = (latents.reshape(total, width), out_grad.reshape(total, width))
         if not blocked:
             rows_in = tuple(plan.enter(v) for v in rows_in)
-        entered, grad_rows, grad_z, inputs_a = enter_norm(table, blocked, *rows_in, small)
-
         local = jnp.concatenate([w_qkv[0], w_qkv[1], w_qkv[2], w_out], axis=1)
-        gather_attention = Gather(plan, links, plan.spread_columns(links, local))
-        columns_up = lax.all_gather(w_up, "mp", axis=0)
-        columns_down = lax.all_gather(w_down, "mp", axis=0)
-        gather_up = Gather(plan, links, plan.halves([columns_up[k] for k in range(mp)]))
-        gather_down = Gather(plan, links, plan.halves([columns_down[k] for k in range(mp)]))
-        gather_attention.steps_but_last([small])
+
+        def pick(name, *choices):
+            chosen = choices[C[name]]
+            return [t for t in chosen if t is not None]
+
+        def columns_of(weight, name, tokens):
+            if C[name]:
+                return plan.spread_columns(links, after(weight, *tokens))
+            columns = lax.all_gather(after(weight, *tokens), "mp", axis=0)
+            return plan.halves([columns[k] for k in range(mp)])
+
+        halves = plan.spread_columns(links, local)
+        gather_attention = Gather(plan, links, halves)
+        up_halves = columns_of(w_up, "z_up", pick("g_zup", [], halves))
+        entered, grad_rows, grad_z, inputs_a = enter_norm(
+            table, blocked, *rows_in, after(small, *pick("g_enter", [], halves))
+        )
+        gather_attention.steps_but_last(pick("g_x1", [], [small], [inputs_a]))
         window = links.halo(inputs_a.reshape(micro, rows, width))
-        gather_attention.step([inputs_a])
+        down_halves = columns_of(
+            w_down, "z_down", pick("g_zdown", [], up_halves, [inputs_a], [window[0], window[2]])
+        )
+        halos = [window[0], window[2]]
+        gather_attention.step(
+            pick("g_x2a", [], [inputs_a], halos, up_halves, halos + up_halves),
+            pick("g_x2b", [], [inputs_a], halos, up_halves),
+        )
+        gather_up = Gather(plan, links, up_halves)
+        gather_down = Gather(plan, links, down_halves)
+        tokens_up = gather_up.steps_but_last(pick("g_x1up", [], [inputs_a], halos))
+        gather_attention.hold(
+            pick("h_core", [], tokens_up, down_halves, tokens_up + down_halves, halos)
+        )
         attention = gather_attention.finish()
-        tokens = gather_up.steps_but_last([inputs_a])
 
         span = rows + 2 * HALO
         first = lax.axis_index("mp") * rows
@@ -824,64 +843,123 @@
         keys = lax.dynamic_slice_in_dim(keys, first, span, 1)
         column, row = groups[:, :, None], keys[:, None, :]
 
+        tokens_down = gather_down.steps_but_last()
+        late_up = gather_up.step()
         saved, attended, resid, inputs_c = forward_block(
-            window, attention, after(column, *tokens, columns_down), row, entered, small, mp, factor
-        )
-        gather_up.step()
-        tokens = gather_down.steps_but_last()
-        gather_up.hold([inputs_c])
+            window,
+            attention,
+            after(
+                column,
+                *pick(
+                    "t_fwd",
+                    [],
+                    tokens_up,
+                    tokens_up + down_halves,
+                    tokens_down,
+                    late_up,
+                    late_up + tokens_down,
+                ),
+            ),
+            row, entered, small, mp, factor,
+        )
+        gather_up.hold(pick("h_up", [], [inputs_c]))
         up = gather_up.finish()
-        gather_down.hold([inputs_c])
+        late_down = gather_down.step()
+        gather_down.hold(pick("h_down", [], [inputs_c]))
+        tokens = pick("t_up", [], tokens_down, late_down)
         hidden, slope = feed_up(after(inputs_c, *tokens), up)
-        gather_down.step()
-        gather_down.hold([hidden])
+        gather_down.hold(pick("h_down2", [], [hidden]))
         down = gather_down.finish()
         grad_down = Scatter(plan, links, [(grad_z, [hidden[0], hidden[1]])])
         for i in range(2):
             grad_down.core(i)
         tokens = [grad_down.steps_but_last(i) for i in range(2)]
         upward, grad_resid, grad_branch, sums_two = feed_back(
-            after(grad_z, *tokens), down, up, slope, resid, grad_rows, small
+            after(grad_z, *pick("t_back", [], tokens)), down, up, slope, resid, grad_rows, small
         )
         branch = links.halo(grad_branch.reshape(micro, rows, width))
+        halos = [branch[0], branch[2]]
+        latents_out = None
+
+        def put_down(*tokens):
+            return feed_down(table, blocked, after(hidden, *tokens), down, resid)
+
         for i in range(2):
-            grad_down.hold(i, [grad_branch])
+            grad_down.hold(i, pick("h_d2", [], [grad_branch]))
         tokens = [grad_down.step(i) for i in range(2)]
-        left = after(inputs_c, *tokens)
-        grad_up = Scatter(
-            plan, links, [(left, [upward[0], upward[1]]), (grad_branch, [attended[0], attended[1]])]
-        )
-        for i in range(2):
-            grad_up.core(i)
-        tokens = [grad_up.steps_but_last(i) for i in range(2)]
-        grad_down = grad_down.reduce_columns()
+        if C["p_down"] == 0:
+            latents_out = put_down(grad_branch, *pick("t_down0", [], tokens))
+        middle = [latents_out]
+        left = after(inputs_c, *pick("g_u", [], tokens, halos, middle))
+        grad_up = Scatter(plan, links, [(left, [upward[0], upward[1]])])
+        left = after(grad_branch, *pick("g_o", [], tokens, halos, middle))
+        grad_out = Scatter(plan, links, [(left, [attended[0], attended[1]])])
+        if C["merge"]:
+            grad_up.pairs += grad_out.pairs
+        parts = [grad_up] if C["merge"] else [grad_up, grad_out]
+        for part in parts:
+            for i in range(2):
+                part.core(i)
+        tokens = [part.steps_but_last(i) for part in parts for i in range(2)]
+        down_rows = grad_down.rows()[0]
         projected, norm_one = backward_block(
-            branch, attention, after(column, *tokens), row, saved, mp, factor
-        )
-        for i in range(2):
-            grad_up.hold(i, [norm_one])
-        tokens = [grad_up.step(i) for i in range(2)]
-        left = after(inputs_a, *tokens)
+            branch,
+            attention,
+            after(
+                column,
+                *pick("t_bwd", [], tokens, tokens + down_rows, down_rows, tokens[:2], middle, tokens + middle),
+            ),
+            row, saved, mp, factor,
+        )
+        grad_down = reduce_blocks([after(r, *pick("h_sd", [], [norm_one])) for r in down_rows])
+        for part in parts:
+            for i in range(2):
+                part.hold(i, pick("h_u2", [], [norm_one]))
+        outs = []
+
+        def second(tokens):
+            for part in parts:
+                outs.extend(part.step(i, tokens) for i in range(2))
+
+        if C["first_u2"]:
+            second([])
+        left = after(inputs_a, *pick("g_q", [], outs))
         grad_qkv = Scatter(plan, links, [(left, [projected[0], projected[1]])])
         for i in range(2):
             grad_qkv.core(i)
         tokens = [grad_qkv.steps_but_last(i) for i in range(2)]
+        if not C["first_u2"]:
+            second(tokens)
         latents_grad, sums_one = leave_norm(
-            table, blocked, after(norm_one, *tokens), entered, grad_resid, small
-        )
+            table, blocked, after(norm_one, *pick("t_leave", [], tokens)), entered, grad_resid, small
+        )
+        for part in parts:
+            for i in range(2):
+                part.hold(i, pick("h_uz", [], [latents_grad]))
+        rows_uo = sum((part.rows() for part in parts), [])
+        up_rows, out_rows = rows_uo
+        if C["z_u"] == 0:
+            grad_up = reduce_blocks(up_rows)
+        elif C["z_u"] == 1:
+            grad_up = shift_blocks(plan, links, [own_first(up_rows)])[0]
+        else:
+            grad_up, grad_out = shift_blocks(plan, links, [own_first(up_rows), out_rows])
+        if C["p_down"] == 1:
+            latents_out = put_down(*pick("t_down", [], [sums_one], [sums_one] + up_rows, tokens))
         for i in range(2):
-            grad_up.hold(i, [latents_grad])
-        tokens = grad_up.shifts([True, False])
-        latents_out = feed_down(table, blocked, after(hidden, sums_one, *tokens), down, resid)
-        for i in range(2):
-            grad_qkv.hold(i, [latents_out])
+            grad_qkv.hold(i, pick("h_q2", [], [latents_out], [latents_grad]))
             grad_qkv.step(i)
-        grad_qkv.shifts([False])
-        grad_up, grad_out = grad_up.finish()
-        grad_qkv = grad_qkv.finish()[0]
+        qkv_rows = grad_qkv.rows()[0]
+        if C["p_down"] == 2:
+            latents_out = put_down(latents_grad, *pick("t_down2", [], up_rows, qkv_rows))
+        if C["z_u"] == 2:
+            grad_qkv = shift_blocks(plan, links, [qkv_rows])[0]
+        else:
+            grad_qkv, grad_out = shift_blocks(plan, links, [qkv_rows, out_rows])
         grad_qkv = jnp.stack(jnp.split(grad_qkv, 3, axis=1))
         sums = jnp.stack([sums_one, sums_two], axis=0).reshape(2, 2, 8, width).sum(axis=2)
         sums = sums.transpose(1, 0, 2).reshape(4, width).T
+        sums = after(sums, *pick("g_sums", [], qkv_rows, [latents_grad]))
         for bit in plan.major:
             middle = sums.shape[0] // 2
             sums = sums[:middle] + links.swap(sums[middle:], bit, 0)

time: 510 us -> 482 us (0.945)
  waiting for transfers between devices: 151 us -> 120 us
  local copies, waits for them, and re-layouts: 62.3 us -> 74.8 us
  other arithmetic: 35.8 us -> 29.8 us
  matrix products: 36.7 us -> 31 us
    ppermute x57 -> x54, waiting for transfers between devices: 144 us -> 119 us  [send(): result = lax.ppermute(value, axis, pairs)]
    unnamed x168 -> x178, local copies, waits for them, and re-layouts: 32.4 us -> 45.8 us
    ppermute x2, waiting for transfers between devices: 6.79 us -> 0.01 us  [body(): sums = sums + lax.ppermute(sums, 'mp', [(i, i ^ bit) for i in range(mp)])]
    concatenate x12 -> x10, other arithmetic: 13.6 us -> 7.58 us  [join(): return pieces[0] if len(pieces) == 1 else jnp.concatenate(pieces, axis=0)]
    dot_general x16, matrix products: 36.7 us -> 31 us  [dot(): lax.dot_general(left, right, ((dims[:1], dims[1:]), ((), ())), preferred_...]
    ppermute x57 -> x54, starting transfers between devices: 61.8 us -> 67 us  [send(): result = lax.ppermute(value, axis, pairs)]
  transfers between devices with their start and end apart: 62 -> 60, of which waited for: 22 -> 20; matrix products, arithmetic and copies ran while one was open for 21% -> 20% of each run, Pallas kernels for 27% -> 28%
where the time goes in v4:
time: 482 us; the launch traced here: 477 us
  Pallas kernels  135 us (28%)
  waiting for transfers between devices  120 us (25%)
  local copies, waits for them, and re-layouts  74.8 us (16%)
  starting transfers between devices  71.3 us (15%)
  matrix products  31 us (6%)
  other arithmetic  29.8 us (6%)
  between operations  15.5 us (3%)
    ppermute x54, waiting for transfers between devices, send(): result = lax.ppermute(value, axis, pairs)  119 us
    ppermute x54, starting transfers between devices, send(): result = lax.ppermute(value, axis, pairs)  67 us
    unnamed x178, local copies, waits for them, and re-layouts  45.8 us
    pallas_call x1, Pallas kernels, forward_block(): pl.pallas_call(forward_kernel(rows, steps, g // HEAD_DIM, factor), name='...  36 us
    pallas_call x1, Pallas kernels, backward_block(): pl.pallas_call(backward_kernel(rows, steps, g // HEAD_DIM, factor), name=...  35.7 us
    dot_general x16, matrix products, dot(): lax.dot_general(left, right, ((dims[:1], dims[1:]), ((), ())), preferred_...  31 us
    pallas_call x1, Pallas kernels, feed_back(): pl.pallas_call(feed_back_kernel(steps), name='feed_back', grid=(steps + t...  25.5 us
    pallas_call x1, Pallas kernels, feed_up(): pl.pallas_call(up_kernel(count), name='feed_up', grid=(ff // tile,), in_s...  15 us
  transfers between devices with their start and end apart: 60, of which 20 were waited for; matrix products, arithmetic and copies ran while one was open for 20% of the time, Pallas kernels for 28%

profile of v4, /device:TPU:0, one launch (start us, length us, event | category | flops | bytes accessed | tf_op | source)
XLA Modules:
  0.0 476.8 jit_solution(16433212945037943204)
XLA Ops:
  9.7 3.1 collective-permute-start.10
  12.8 2.6 collective-permute-start.9
  21.6 1.6 collective-permute-start.1
  26.4 1.9 copy-done.2
  28.3 1.9 copy-done.3
  30.2 4.0 enter.1
  35.4 1.6 copy-done.23
  37.0 6.1 %collective-permute-done.9 = bf16[128,1024]{1,0:T(8,128)(2,1)S(1)} collective-permute-done((bf16[128,1024]{1,0:T(8,128)(2,1)S(1)}, bf16[128,1024]{1,0:T(8,128)(2,1)S(1)}, u32[]{:S(2)}, u32[]{:S(2)}) %collective-permute-start.9) | collective-permute-done | bytes 262176 | tf_op jit(solution)/shard_map/ppermute | solution.py:29
  43.1 1.6 collective-permute-start.11
  47.4 11.4 %collective-permute-start.3 = (bf16[3,128,1024]{2,1,0:T(8,128)(2,1)S(1)}, bf16[3,128,1024]{2,1,0:T(8,128)(2,1)S(1)}, u32[]{:S(2)}, u32[]{:S(2)}) collective-permute-start(bf16[3,128,1024]{2,1,0:T(8,128)(2,1)S(1)} %get-tuple-element.115), channel_id=1, source_target_pairs={{0,1},{1,2},{2,3},{4,5},{5,6},{6,7},{8,9},{9,10},{10,11},{12,13},{... | collective-permute-start | bytes 2359304 | tf_op jit(solution)/shard_map/ppermute | solution.py:29
  58.8 1.6 collective-permute-start.6
  61.2 12.6 %collective-permute-done.6 = bf16[128,2048]{1,0:T(8,128)(2,1)S(1)} collective-permute-done((bf16[128,2048]{1,0:T(8,128)(2,1)S(1)}, bf16[128,2048]{1,0:T(8,128)(2,1)S(1)}, u32[]{:S(2)}, u32[]{:S(2)}) %collective-permute-start.6) | collective-permute-done | bytes 524320 | tf_op jit(solution)/shard_map/ppermute | solution.py:29
  73.9 9.7 %collective-permute-done.4.after = bf16[3,128,1024]{2,1,0:T(8,128)(2,1)S(1)} collective-permute-done((bf16[3,128,1024]{2,1,0:T(8,128)(2,1)S(1)}, bf16[3,128,1024]{2,1,0:T(8,128)(2,1)S(1)}, u32[]{:S(2)}, u32[]{:S(2)}) %collective-permute-start.4) | collective-permute-done | bytes 786464 | tf_op jit(solution)/shard_map/ppermute | solution.py:29
  85.1 5.7 %collective-permute-done.12 = bf16[256,2048]{1,0:T(8,128)(2,1)S(1)} collective-permute-done((bf16[256,2048]{1,0:T(8,128)(2,1)S(1)}, bf16[256,2048]{1,0:T(8,128)(2,1)S(1)}, u32[]{:S(2)}, u32[]{:S(2)}) %collective-permute-start.12) | collective-permute-done | bytes 1048608 | tf_op jit(solution)/shard_map/ppermute | solution.py:29
  91.2 7.3 %collective-permute-done.7 = bf16[256,2048]{1,0:T(8,128)(2,1)S(1)} collective-permute-done((bf16[256,2048]{1,0:T(8,128)(2,1)S(1)}, bf16[256,2048]{1,0:T(8,128)(2,1)S(1)}, u32[]{:S(2)}, u32[]{:S(2)}) %collective-permute-start.7) | collective-permute-done | bytes 1048608 | tf_op jit(solution)/shard_map/ppermute | solution.py:29
  106.4 9.0 %collective-permute-done.14 = bf16[128,2048]{1,0:T(8,128)(2,1)} collective-permute-done((bf16[128,2048]{1,0:T(8,128)(2,1)S(1)}, bf16[128,2048]{1,0:T(8,128)(2,1)}, u32[]{:S(2)}, u32[]{:S(2)}) %collective-permute-start.14) | collective-permute-done | bytes 524320 | tf_op jit(solution)/shard_map/ppermute | solution.py:29
  122.0 36.0 %attention_forward.1 = (bf16[3,512,3072]{2,1,0:T(8,128)(2,1)}, bf16[2,768,512]{2,1,0:T(8,128)(2,1)S(1)}, f32[768,1024]{1,0:T(8,128)S(1)}, bf16[768,1024]{1,0:T(8,128)(2,1)S(1)}) custom-call(bf16[3,128,1024]{2,1,0:T(8,128)(2,1)S(1)} %copy-done.31, bf16[3,256,1024]{2,1,0:T(8,128)(2,1)S(1)} %bitcast.221, bf16[3,128,1024]{2,1,0:T(8,128)(2,1)S(1)} %copy-done.29, ...), custom_call_target="tpu_custom_call" | custom-call | flops 12884901888 | bytes 31457280 | tf_op jit(solution)/shard_map/attention_forward/pallas_call | solution.py:464
  158.0 1.7 copy-done.38
  165.9 11.0 %collective-permute-done.16 = bf16[128,2048]{1,0:T(8,128)(2,1)S(1)} collective-permute-done((bf16[128,2048]{1,0:T(8,128)(2,1)S(1)}, bf16[128,2048]{1,0:T(8,128)(2,1)S(1)}, u32[]{:S(2)}, u32[]{:S(2)}) %collective-permute-start.16) | collective-permute-done | bytes 524320 | tf_op jit(solution)/shard_map/ppermute | solution.py:29
  177.1 1.6 collective-permute-start.24
  180.3 15.0 %feed_up.1 = (bf16[2,768,2048]{2,1,0:T(8,128)(2,1)S(1)}, bf16[2,768,2048]{2,1,0:T(8,128)(2,1)S(1)}) custom-call(bf16[768,1024]{1,0:T(8,128)(2,1)S(1)} %get-tuple-element.88.inputs, bf16[512,2048]{1,0:T(8,128)(2,1)S(1)} %constant_dynamic-update-slice_fusion.7.top_a.up_top_a, bf16[512,2048]{1,0:T(8,128)(2,1)S(1)} %collective-permute-done.19.bottom_a.up_bottom_a, ...), custom_call_target="tpu_custom_call" | custom-call | flops 6442450944 | bytes 20971520 | tf_op jit(solution)/shard_map/feed_up/pallas_call | solution.py:523
  195.3 2.6 copy-done.40
  197.9 3.3 fusion.27
  201.1 1.9 fusion.24
  204.0 2.5 pad_maximum_fusion.3.down_top_b.top_b
  207.1 1.9 convert_add_fusion.2
  211.0 1.9 convert_add_fusion.3
  214.9 25.5 %feed_back.1 = (bf16[2,768,2048]{2,1,0:T(8,128)(2,1)}, f32[768,1024]{1,0:T(8,128)}, bf16[768,1024]{1,0:T(8,128)(2,1)S(1)}, f32[16,1024]{1,0:T(8,128)S(1)}) custom-call(bf16[768,1024]{1,0:T(8,128)(2,1)S(1)} %copy-done.14, bf16[512,2048]{1,0:T(8,128)(2,1)S(1)} %pad_maximum_fusion.2.down_top_a.top_a, ...), custom_call_target="tpu_custom_call" | custom-call | flops 12884901888 | bytes 40370176 | tf_op jit(solution)/shard_map/feed_back/pallas_call | solution.py:647
  240.7 1.7 copy-done.37
  247.6 1.9 fusion.30
  249.6 1.9 fusion.33
  253.5 9.1 %collective-permute-start.28 = (bf16[3,128,1024]{2,1,0:T(8,128)(2,1)S(1)}, bf16[3,128,1024]{2,1,0:T(8,128)(2,1)S(1)}, u32[]{:S(2)}, u32[]{:S(2)}) collective-permute-start(bf16[3,128,1024]{2,1,0:T(8,128)(2,1)S(1)} %get-tuple-element.113), channel_id=1, source_target_pairs={{0,1},{1,2},{2,3},{4,5},{5,6},{6,7},{8,9},{9,10},{10,11},{12,13},{... | collective-permute-start | bytes 2359304 | tf_op jit(solution)/shard_map/ppermute | solution.py:29
  265.7 12.0 %collective-permute-done.50 = bf16[128,2048]{1,0:T(8,128)(2,1)S(1)} collective-permute-done((bf16[128,2048]{1,0:T(8,128)(2,1)S(1)}, bf16[128,2048]{1,0:T(8,128)(2,1)S(1)}, u32[]{:S(2)}, u32[]{:S(2)}) %collective-permute-start.50) | collective-permute-done | bytes 524320 | tf_op jit(solution)/shard_map/ppermute | solution.py:29
  279.7 1.9 convert_add_fusion.1
  281.7 1.9 convert_add_fusion
  292.9 1.6 copy-done.12
  299.3 35.7 %attention_backward.1 = (bf16[2,768,1536]{2,1,0:T(8,128)(2,1)}, f32[768,1024]{1,0:T(8,128)S(1)}) custom-call(bf16[3,128,1024]{2,1,0:T(8,128)(2,1)S(1)} %copy-done.35, bf16[3,256,1024]{2,1,0:T(8,128)(2,1)S(1)} %bitcast.223, bf16[3,128,1024]{2,1,0:T(8,128)(2,1)S(1)} %copy-done.33, bf16[512,2048]{1,0:T(8,128)(2,1)} %constant_dynamic-update-slice_fusion.5.top_a, ...), custom_call_target="tpu_custom_call" | custom-call | flops 14495514624 | bytes 36700160 | tf_op jit(solution)/shard_map/attention_backward/pallas_call | solution.py:713
  336.2 1.6 slice.497
  338.3 2.2 slice.503
  345.5 2.6 convolution_convert_fusion.1
  351.5 2.7 convolution_convert_fusion
  356.2 10.7 %collective-permute-done.40 = bf16[128,2560]{1,0:T(8,128)(2,1)} collective-permute-done((bf16[128,2560]{1,0:T(8,128)(2,1)}, bf16[128,2560]{1,0:T(8,128)(2,1)}, u32[]{:S(2)}, u32[]{:S(2)}) %collective-permute-start.40) | collective-permute-done | bytes 655392 | tf_op jit(solution)/shard_map/ppermute | solution.py:29
  367.8 1.9 slice.511
  370.6 2.1 slice.515
  372.7 3.6 convolution_add_fusion.1
  378.7 3.0 convolution_add_fusion
  383.7 5.7 %leave.1 = (f32[768,1024]{1,0:T(8,128)}, f32[16,1024]{1,0:T(8,128)S(1)}) custom-call(s32[8]{0:T(128)S(1)} %broadcast_xor_fusion.table_ref, f32[768,1024]{1,0:T(8,128)S(1)} %get-tuple-element.100.norm_one, f32[768,1024]{1,0:T(8,128)S(1)} %copy-done.5, f32[768,1024]{1,0:T(8,128)S(1)} %copy-done.6, f32[4,1024]{1,0:T(4,128)S(1)} %convert_bitcast_fusion.small), custom_call_target="tpu_custom_call" | custom-call | flops 23592960 | bytes 12582912 | tf_op jit(solution)/shard_map/leave/pallas_call | solution.py:766
  390.5 1.6 fusion.59
  394.7 2.7 collective-permute-done.52
  400.0 2.8 slice.527
  402.9 2.6 collective-permute-start.54
  405.4 2.8 copy-done.1
  408.2 1.9 copy-done.10
  410.1 1.6 copy-done.25
  411.7 1.6 copy-done.27
  413.3 1.9 copy-done.39
  415.2 12.9 %feed_down.1 = f32[768,1024]{1,0:T(8,128)} custom-call(s32[8]{0:T(128)S(1)} %broadcast_xor_fusion.table_ref, bf16[2,768,2048]{2,1,0:T(8,128)(2,1)S(1)} %copy-done.1, bf16[512,2048]{1,0:T(8,128)(2,1)S(1)} %copy-done.8, bf16[512,2048]{1,0:T(8,128)(2,1)S(1)} %copy-done.25, bf16[512,2048]{1,0:T(8,128)(2,1)S(1)} %copy-done.10, bf16[512,2048]{1,0:T(8,128)(2,1)S(1)} %copy-done.27, ...), custom_call_target="tpu_custom_call" | custom-call | flops 6442450944 | bytes 20971520 | tf_op jit(solution)/shard_map/feed_down/pallas_call | solution.py:575
  434.1 6.7 %collective-permute-done.43 = bf16[128,1536]{1,0:T(8,128)(2,1)S(1)} collective-permute-done((bf16[128,1536]{1,0:T(8,128)(2,1)S(1)}, bf16[128,1536]{1,0:T(8,128)(2,1)S(1)}, u32[]{:S(2)}, u32[]{:S(2)}) %collective-permute-start.43) | collective-permute-done | bytes 393248 | tf_op jit(solution)/shard_map/ppermute | solution.py:29
  441.0 1.9 collective-permute-start.44
  443.4 1.7 collective-permute-start.48
  445.1 1.6 collective-permute-start.47
  447.2 6.6 %collective-permute-done.44 = bf16[128,1024]{1,0:T(8,128)(2,1)S(1)} collective-permute-done((bf16[128,1024]{1,0:T(8,128)(2,1)S(1)}, bf16[128,1024]{1,0:T(8,128)(2,1)S(1)}, u32[]{:S(2)}, u32[]{:S(2)}) %collective-permute-start.44) | collective-permute-done | bytes 262176 | tf_op jit(solution)/shard_map/ppermute | solution.py:29
  453.8 3.0 collective-permute-done.48
  456.7 11.6 %collective-permute-done.47 = bf16[128,1024]{1,0:T(8,128)(2,1)S(1)} collective-permute-done((bf16[128,1024]{1,0:T(8,128)(2,1)S(1)}, bf16[128,1024]{1,0:T(8,128)(2,1)S(1)}, u32[]{:S(2)}, u32[]{:S(2)}) %collective-permute-start.47) | collective-permute-done | bytes 262176 | tf_op jit(solution)/shard_map/ppermute | solution.py:29
  (377 shorter events, 105.5 us)
Async XLA Ops:
  7.2 92.4 %all-gather.5.cloned.1.call-start = ((), (), s32[]{:S(2)}) async-start(), calls=%async_computation.4 | async-start | bytes 1310720 | tf_op jit(solution)/shard_map/all_gather | solution.py:810
  7.9 94.6 %all-gather.7.cloned.1.call-start = ((), (), s32[]{:S(2)}) async-start(), calls=%async_computation.5 | async-start | bytes 1310720 | tf_op jit(solution)/shard_map/all_gather | solution.py:810
  9.7 27.2 %collective-permute-start.10 = (bf16[128,1024]{1,0:T(8,128)(2,1)S(1)}, bf16[128,1024]{1,0:T(8,128)(2,1)S(1)}, u32[]{:S(2)}, u32[]{:S(2)}) collective-permute-start(bf16[128,1024]{1,0:T(8,128)(2,1)S(1)} %pad_maximum_fusion.22), channel_id=1, source_target_pairs={{0,1},{1,2},{2,3},{3,0},{4,5},{5,6},{6,7},{7,4},{8,9},{9,10},{10,1... | collective-permute-start | bytes 786440 | tf_op jit(solution)/shard_map/ppermute | solution.py:29
  12.8 30.2 %collective-permute-start.9 = (bf16[128,1024]{1,0:T(8,128)(2,1)S(1)}, bf16[128,1024]{1,0:T(8,128)(2,1)S(1)}, u32[]{:S(2)}, u32[]{:S(2)}) collective-permute-start(bf16[128,1024]{1,0:T(8,128)(2,1)S(1)} %pad_maximum_fusion.22), channel_id=1, source_target_pairs={{0,2},{1,3},{2,0},{3,1},{4,6},{5,7},{6,4},{7,5},{8,10},{9,11},{10,... | collective-permute-start | bytes 786440 | tf_op jit(solution)/shard_map/ppermute | solution.py:29
  15.4 43.4 %collective-permute-start.5 = (bf16[128,1024]{1,0:T(8,128)(2,1)S(1)}, bf16[128,1024]{1,0:T(8,128)(2,1)S(1)}, u32[]{:S(2)}, u32[]{:S(2)}) collective-permute-start(bf16[128,1024]{1,0:T(8,128)(2,1)S(1)} %pad_maximum_fusion.22), channel_id=1, source_target_pairs={{0,3},{1,0},{2,1},{3,2},{4,7},{5,4},{6,5},{7,6},{8,11},{9,8},{10,9... | collective-permute-start | bytes 786440 | tf_op jit(solution)/shard_map/ppermute | solution.py:29
  17.4 4.1 collective-permute-start
  19.0 451.0 %reduce-scatter.5.cloned.1.call-start = ((), (), s32[]{:S(2)}) async-start(), calls=%async_computation.3 | async-start | bytes 2621440 | tf_op jit(solution)/shard_map/reduce_scatter | solution.py:236
  21.6 3.7 collective-permute-start.1
  25.2 1.2 collective-permute-start.2
  43.1 17.3 %collective-permute-start.11 = (bf16[128,2048]{1,0:T(8,128)(2,1)S(1)}, bf16[128,2048]{1,0:T(8,128)(2,1)S(1)}, u32[]{:S(2)}, u32[]{:S(2)}) collective-permute-start(bf16[128,2048]{1,0:T(8,128)(2,1)S(1)} %pad_maximum_fusion.16), channel_id=1, source_target_pairs={{0,16},{4,20},{8,24},{12,28},{16,0},{20,4},{24,8},{28,12},{1,17},{... | collective-permute-start | bytes 1572872 | tf_op jit(solution)/shard_map/ppermute | solution.py:29
  46.1 37.5 %collective-permute-start.4 = (bf16[3,128,1024]{2,1,0:T(8,128)(2,1)S(1)}, bf16[3,128,1024]{2,1,0:T(8,128)(2,1)S(1)}, u32[]{:S(2)}, u32[]{:S(2)}) collective-permute-start(bf16[3,128,1024]{2,1,0:T(8,128)(2,1)S(1)} %get-tuple-element.114), channel_id=1, source_target_pairs={{1,0},{2,1},{3,2},{5,4},{6,5},{7,6},{9,8},{10,9},{11,10},{13,12},{... | collective-permute-start | bytes 2359304 | tf_op jit(solution)/shard_map/ppermute | solution.py:29
  47.4 36.3 %collective-permute-start.3 = (bf16[3,128,1024]{2,1,0:T(8,128)(2,1)S(1)}, bf16[3,128,1024]{2,1,0:T(8,128)(2,1)S(1)}, u32[]{:S(2)}, u32[]{:S(2)}) collective-permute-start(bf16[3,128,1024]{2,1,0:T(8,128)(2,1)S(1)} %get-tuple-element.115), channel_id=1, source_target_pairs={{0,1},{1,2},{2,3},{4,5},{5,6},{6,7},{8,9},{9,10},{10,11},{12,13},{... | collective-permute-start | bytes 2359304 | tf_op jit(solution)/shard_map/ppermute | solution.py:29
  58.8 14.9 %collective-permute-start.6 = (bf16[128,2048]{1,0:T(8,128)(2,1)S(1)}, bf16[128,2048]{1,0:T(8,128)(2,1)S(1)}, u32[]{:S(2)}, u32[]{:S(2)}) collective-permute-start(bf16[128,2048]{1,0:T(8,128)(2,1)S(1)} %constant_dynamic-update-slice_fusion), channel_id=1, source_target_pairs={{0,8},{4,12},{8,0},{12,4},{16,24},{20,28},{24,16},{28,20},{1,9},{5... | collective-permute-start | bytes 1572872 | tf_op jit(solution)/shard_map/ppermute | solution.py:29
  60.5 30.3 %collective-permute-start.12 = (bf16[256,2048]{1,0:T(8,128)(2,1)S(1)}, bf16[256,2048]{1,0:T(8,128)(2,1)S(1)}, u32[]{:S(2)}, u32[]{:S(2)}) collective-permute-start(bf16[256,2048]{1,0:T(8,128)(2,1)S(1)} %pad_maximum_fusion.9), channel_id=1, source_target_pairs={{0,8},{4,12},{8,0},{12,4},{16,24},{20,28},{24,16},{28,20},{1,9},{5... | collective-permute-start | bytes 3145736 | tf_op jit(solution)/shard_map/ppermute | solution.py:29
  83.7 14.8 %collective-permute-start.7 = (bf16[256,2048]{1,0:T(8,128)(2,1)S(1)}, bf16[256,2048]{1,0:T(8,128)(2,1)S(1)}, u32[]{:S(2)}, u32[]{:S(2)}) collective-permute-start(bf16[256,2048]{1,0:T(8,128)(2,1)S(1)} %pad_maximum_fusion.8), channel_id=1, source_target_pairs={{0,16},{4,20},{8,24},{12,28},{16,0},{20,4},{24,8},{28,12},{1,17},{... | collective-permute-start | bytes 3145736 | tf_op jit(solution)/shard_map/ppermute | solution.py:29
  91.1 30.8 %copy-start.11 = (bf16[512,2048]{1,0:T(8,128)(2,1)}, bf16[512,2048]{1,0:T(8,128)(2,1)S(1)}, u32[]{:S(2)}) copy-start(bf16[512,2048]{1,0:T(8,128)(2,1)S(1)} %pad_maximum_fusion.top_b) | copy-start | bytes 6291460
  91.1 30.8 %collective-permute-start.13 = (bf16[512,2048]{1,0:T(8,128)(2,1)S(1)}, bf16[512,2048]{1,0:T(8,128)(2,1)}, u32[]{:S(2)}, u32[]{:S(2)}) collective-permute-start(bf16[512,2048]{1,0:T(8,128)(2,1)S(1)} %pad_maximum_fusion.top_b), channel_id=1, source_target_pairs={{0,4},{4,0},{8,12},{12,8},{16,20},{20,16},{24,28},{28,24},{1,5},{5... | collective-permute-start | bytes 6291464 | tf_op jit(solution)/shard_map/ppermute | solution.py:29
  99.6 22.3 %collective-permute-start.8 = (bf16[512,2048]{1,0:T(8,128)(2,1)}, bf16[512,2048]{1,0:T(8,128)(2,1)}, u32[]{:S(2)}, u32[]{:S(2)}) collective-permute-start(bf16[512,2048]{1,0:T(8,128)(2,1)} %constant_dynamic-update-slice_fusion.5.top_a), channel_id=1, source_target_pairs={{0,4},{4,0},{8,12},{12,8},{16,20},{20,16},{24,28},{28,24},{1,5},{5... | collective-permute-start | bytes 6291464 | tf_op jit(solution)/shard_map/ppermute | solution.py:29
  100.9 14.5 %collective-permute-start.14 = (bf16[128,2048]{1,0:T(8,128)(2,1)S(1)}, bf16[128,2048]{1,0:T(8,128)(2,1)}, u32[]{:S(2)}, u32[]{:S(2)}) collective-permute-start(bf16[128,2048]{1,0:T(8,128)(2,1)S(1)} %get-tuple-element.67), channel_id=1, source_target_pairs={{0,8},{4,12},{8,0},{12,4},{16,24},{20,28},{24,16},{28,20},{1,9},{5... | collective-permute-start | bytes 1572872 | tf_op jit(solution)/shard_map/ppermute | solution.py:29
  102.5 14.2 %collective-permute-start.15 = (bf16[128,2048]{1,0:T(8,128)(2,1)S(1)}, bf16[128,2048]{1,0:T(8,128)(2,1)}, u32[]{:S(2)}, u32[]{:S(2)}) collective-permute-start(bf16[128,2048]{1,0:T(8,128)(2,1)S(1)} %get-tuple-element.68), channel_id=1, source_target_pairs={{0,16},{4,20},{8,24},{12,28},{16,0},{20,4},{24,8},{28,12},{1,17},{... | collective-permute-start | bytes 1572872 | tf_op jit(solution)/shard_map/ppermute | solution.py:29
  118.3 41.4 %collective-permute-start.18 = (bf16[256,2048]{1,0:T(8,128)(2,1)S(1)}, bf16[256,2048]{1,0:T(8,128)(2,1)S(1)}, u32[]{:S(2)}, u32[]{:S(2)}) collective-permute-start(bf16[256,2048]{1,0:T(8,128)(2,1)S(1)} %pad_maximum_fusion.10), channel_id=1, source_target_pairs={{0,16},{4,20},{8,24},{12,28},{16,0},{20,4},{24,8},{28,12},{1,17},{... | collective-permute-start | bytes 3145736 | tf_op jit(solution)/shard_map/ppermute | solution.py:29
  120.2 39.5 %collective-permute-start.20 = (bf16[256,2048]{1,0:T(8,128)(2,1)S(1)}, bf16[256,2048]{1,0:T(8,128)(2,1)S(1)}, u32[]{:S(2)}, u32[]{:S(2)}) collective-permute-start(bf16[256,2048]{1,0:T(8,128)(2,1)S(1)} %pad_maximum_fusion.11), channel_id=1, source_target_pairs={{0,8},{4,12},{8,0},{12,4},{16,24},{20,28},{24,16},{28,20},{1,9},{5... | collective-permute-start | bytes 3145736 | tf_op jit(solution)/shard_map/ppermute | solution.py:29
  160.8 19.5 %collective-permute-start.19 = (bf16[512,2048]{1,0:T(8,128)(2,1)S(1)}, bf16[512,2048]{1,0:T(8,128)(2,1)S(1)}, u32[]{:S(2)}, u32[]{:S(2)}) collective-permute-start(bf16[512,2048]{1,0:T(8,128)(2,1)S(1)} %constant_dynamic-update-slice_fusion.7.top_a.up_top_a), channel_id=1, source_target_pairs={{0,4},{4,0},{8,12},{12,8},{16,20},{20,16},{24,28},{28,24},{1,5},{5... | collective-permute-start | bytes 6291464 | tf_op jit(solution)/shard_map/ppermute | solution.py:29
  162.6 17.8 %collective-permute-start.21 = (bf16[512,2048]{1,0:T(8,128)(2,1)S(1)}, bf16[512,2048]{1,0:T(8,128)(2,1)S(1)}, u32[]{:S(2)}, u32[]{:S(2)}) collective-permute-start(bf16[512,2048]{1,0:T(8,128)(2,1)S(1)} %pad_maximum_fusion.1.top_b.up_top_b), channel_id=1, source_target_pairs={{0,4},{4,0},{8,12},{12,8},{16,20},{20,16},{24,28},{28,24},{1,5},{5... | collective-permute-start | bytes 6291464 | tf_op jit(solution)/shard_map/ppermute | solution.py:29
  162.9 14.1 %collective-permute-start.16 = (bf16[128,2048]{1,0:T(8,128)(2,1)S(1)}, bf16[128,2048]{1,0:T(8,128)(2,1)S(1)}, u32[]{:S(2)}, u32[]{:S(2)}) collective-permute-start(bf16[128,2048]{1,0:T(8,128)(2,1)S(1)} %copy-done.76), channel_id=1, source_target_pairs={{0,8},{4,12},{8,0},{12,4},{16,24},{20,28},{24,16},{28,20},{1,9},{5... | collective-permute-start | bytes 1572872 | tf_op jit(solution)/shard_map/ppermute | solution.py:29
  164.4 14.3 %collective-permute-start.17 = (bf16[128,2048]{1,0:T(8,128)(2,1)S(1)}, bf16[128,2048]{1,0:T(8,128)(2,1)S(1)}, u32[]{:S(2)}, u32[]{:S(2)}) collective-permute-start(bf16[128,2048]{1,0:T(8,128)(2,1)S(1)} %copy-done.75), channel_id=1, source_target_pairs={{0,16},{4,20},{8,24},{12,28},{16,0},{20,4},{24,8},{28,12},{1,17},{... | collective-permute-start | bytes 1572872 | tf_op jit(solution)/shard_map/ppermute | solution.py:29
  177.1 26.5 %collective-permute-start.24 = (bf16[256,2048]{1,0:T(8,128)(2,1)S(1)}, bf16[256,2048]{1,0:T(8,128)(2,1)S(1)}, u32[]{:S(2)}, u32[]{:S(2)}) collective-permute-start(bf16[256,2048]{1,0:T(8,128)(2,1)S(1)} %pad_maximum_fusion.12), channel_id=1, source_target_pairs={{0,16},{4,20},{8,24},{12,28},{16,0},{20,4},{24,8},{28,12},{1,17},{... | collective-permute-start | bytes 3145736 | tf_op jit(solution)/shard_map/ppermute | solution.py:29
  178.8 24.8 %collective-permute-start.26 = (bf16[256,2048]{1,0:T(8,128)(2,1)S(1)}, bf16[256,2048]{1,0:T(8,128)(2,1)S(1)}, u32[]{:S(2)}, u32[]{:S(2)}) collective-permute-start(bf16[256,2048]{1,0:T(8,128)(2,1)S(1)} %pad_maximum_fusion.13), channel_id=1, source_target_pairs={{0,8},{4,12},{8,0},{12,4},{16,24},{20,28},{24,16},{28,20},{1,9},{5... | collective-permute-start | bytes 3145736 | tf_op jit(solution)/shard_map/ppermute | solution.py:29
  201.1 6.0 %collective-permute-start.23 = (bf16[512,2048]{1,0:T(8,128)(2,1)}, bf16[512,2048]{1,0:T(8,128)(2,1)S(1)}, u32[]{:S(2)}, u32[]{:S(2)}) collective-permute-start(bf16[512,2048]{1,0:T(8,128)(2,1)} %fusion.27), channel_id=1, source_target_pairs={{0,4},{4,0},{8,12},{12,8},{16,20},{20,16},{24,28},{28,24},{1,5},{5... | collective-permute-start | bytes 6291464 | tf_op jit(solution)/shard_map/ppermute | solution.py:29
  203.0 8.0 %collective-permute-start.22 = (bf16[512,2048]{1,0:T(8,128)(2,1)S(1)}, bf16[512,2048]{1,0:T(8,128)(2,1)S(1)}, u32[]{:S(2)}, u32[]{:S(2)}) collective-permute-start(bf16[512,2048]{1,0:T(8,128)(2,1)S(1)} %fusion.24), channel_id=1, source_target_pairs={{0,4},{4,0},{8,12},{12,8},{16,20},{20,16},{24,28},{28,24},{1,5},{5... | collective-permute-start | bytes 6291464 | tf_op jit(solution)/shard_map/ppermute | solution.py:29
  203.8 9.8 %collective-permute-start.25 = (bf16[512,2048]{1,0:T(8,128)(2,1)S(1)}, bf16[512,2048]{1,0:T(8,128)(2,1)S(1)}, u32[]{:S(2)}, u32[]{:S(2)}) collective-permute-start(bf16[512,2048]{1,0:T(8,128)(2,1)S(1)} %pad_maximum_fusion.2.down_top_a.top_a), channel_id=1, source_target_pairs={{0,4},{4,0},{8,12},{12,8},{16,20},{20,16},{24,28},{28,24},{1,5},{5... | collective-permute-start | bytes 6291464 | tf_op jit(solution)/shard_map/ppermute | solution.py:29
  206.6 7.7 %collective-permute-start.27 = (bf16[512,2048]{1,0:T(8,128)(2,1)S(1)}, bf16[512,2048]{1,0:T(8,128)(2,1)S(1)}, u32[]{:S(2)}, u32[]{:S(2)}) collective-permute-start(bf16[512,2048]{1,0:T(8,128)(2,1)S(1)} %pad_maximum_fusion.3.down_top_b.top_b), channel_id=1, source_target_pairs={{0,4},{4,0},{8,12},{12,8},{16,20},{20,16},{24,28},{28,24},{1,5},{5... | collective-permute-start | bytes 6291464 | tf_op jit(solution)/shard_map/ppermute | solution.py:29
  209.2 35.1 %collective-permute-start.31 = (bf16[256,2048]{1,0:T(8,128)(2,1)S(1)}, bf16[256,2048]{1,0:T(8,128)(2,1)S(1)}, u32[]{:S(2)}, u32[]{:S(2)}) collective-permute-start(bf16[256,2048]{1,0:T(8,128)(2,1)S(1)} %bitcast.258), channel_id=1, source_target_pairs={{0,8},{4,12},{8,0},{12,4},{16,24},{20,28},{24,16},{28,20},{1,9},{5... | collective-permute-start | bytes 3145736 | tf_op jit(solution)/shard_map/ppermute | solution.py:29
  213.1 31.2 %collective-permute-start.30 = (bf16[256,2048]{1,0:T(8,128)(2,1)S(1)}, bf16[256,2048]{1,0:T(8,128)(2,1)S(1)}, u32[]{:S(2)}, u32[]{:S(2)}) collective-permute-start(bf16[256,2048]{1,0:T(8,128)(2,1)S(1)} %fusion.55), channel_id=1, source_target_pairs={{0,16},{4,20},{8,24},{12,28},{16,0},{20,4},{24,8},{28,12},{1,17},{... | collective-permute-start | bytes 3145736 | tf_op jit(solution)/shard_map/ppermute | solution.py:29
  213.7 26.7 %copy-start.24 = (bf16[512,2048]{1,0:T(8,128)(2,1)}, bf16[512,2048]{1,0:T(8,128)(2,1)S(1)}, u32[]{:S(2)}) copy-start(bf16[512,2048]{1,0:T(8,128)(2,1)S(1)} %collective-permute-done.25.down_bottom_a.bottom_a) | copy-start | bytes 6291460
  214.3 26.1 %copy-start.26 = (bf16[512,2048]{1,0:T(8,128)(2,1)}, bf16[512,2048]{1,0:T(8,128)(2,1)S(1)}, u32[]{:S(2)}) copy-start(bf16[512,2048]{1,0:T(8,128)(2,1)S(1)} %collective-permute-done.27.down_bottom_b.bottom_b) | copy-start | bytes 6291460
  243.0 21.1 %collective-permute-start.33 = (bf16[512,512]{1,0:T(8,128)(2,1)S(1)}, bf16[512,512]{1,0:T(8,128)(2,1)S(1)}, u32[]{:S(2)}, u32[]{:S(2)}) collective-permute-start(bf16[512,512]{1,0:T(8,128)(2,1)S(1)} %convolution_convert_fusion.3), channel_id=1, source_target_pairs={{0,4},{4,0},{8,12},{12,8},{16,20},{20,16},{24,28},{28,24},{1,5},{5... | collective-permute-start | bytes 1572872 | tf_op jit(solution)/shard_map/ppermute | solution.py:29
  243.8 9.8 %collective-permute-start.35 = (bf16[512,512]{1,0:T(8,128)(2,1)S(1)}, bf16[512,512]{1,0:T(8,128)(2,1)S(1)}, u32[]{:S(2)}, u32[]{:S(2)}) collective-permute-start(bf16[512,512]{1,0:T(8,128)(2,1)S(1)} %convolution_convert_fusion.2), channel_id=1, source_target_pairs={{0,4},{4,0},{8,12},{12,8},{16,20},{20,16},{24,28},{28,24},{1,5},{5... | collective-permute-start | bytes 1572872 | tf_op jit(solution)/shard_map/ppermute | solution.py:29
  249.5 30.2 %collective-permute-start.32 = (bf16[512,2048]{1,0:T(8,128)(2,1)S(1)}, bf16[512,2048]{1,0:T(8,128)(2,1)S(1)}, u32[]{:S(2)}, u32[]{:S(2)}) collective-permute-start(bf16[512,2048]{1,0:T(8,128)(2,1)S(1)} %fusion.30), channel_id=1, source_target_pairs={{0,4},{4,0},{8,12},{12,8},{16,20},{20,16},{24,28},{28,24},{1,5},{5... | collective-permute-start | bytes 6291464 | tf_op jit(solution)/shard_map/ppermute | solution.py:29
  251.5 30.2 %collective-permute-start.34 = (bf16[512,2048]{1,0:T(8,128)(2,1)S(1)}, bf16[512,2048]{1,0:T(8,128)(2,1)S(1)}, u32[]{:S(2)}, u32[]{:S(2)}) collective-permute-start(bf16[512,2048]{1,0:T(8,128)(2,1)S(1)} %fusion.33), channel_id=1, source_target_pairs={{0,4},{4,0},{8,12},{12,8},{16,20},{20,16},{24,28},{28,24},{1,5},{5... | collective-permute-start | bytes 6291464 | tf_op jit(solution)/shard_map/ppermute | solution.py:29
  252.2 38.8 %collective-permute-start.29 = (bf16[3,128,1024]{2,1,0:T(8,128)(2,1)S(1)}, bf16[3,128,1024]{2,1,0:T(8,128)(2,1)S(1)}, u32[]{:S(2)}, u32[]{:S(2)}) collective-permute-start(bf16[3,128,1024]{2,1,0:T(8,128)(2,1)S(1)} %get-tuple-element.112), channel_id=1, source_target_pairs={{1,0},{2,1},{3,2},{5,4},{6,5},{7,6},{9,8},{10,9},{11,10},{13,12},{... | collective-permute-start | bytes 2359304 | tf_op jit(solution)/shard_map/ppermute | solution.py:29
  253.5 38.4 %collective-permute-start.28 = (bf16[3,128,1024]{2,1,0:T(8,128)(2,1)S(1)}, bf16[3,128,1024]{2,1,0:T(8,128)(2,1)S(1)}, u32[]{:S(2)}, u32[]{:S(2)}) collective-permute-start(bf16[3,128,1024]{2,1,0:T(8,128)(2,1)S(1)} %get-tuple-element.113), channel_id=1, source_target_pairs={{0,1},{1,2},{2,3},{4,5},{5,6},{6,7},{8,9},{9,10},{10,11},{12,13},{... | collective-permute-start | bytes 2359304 | tf_op jit(solution)/shard_map/ppermute | solution.py:29
  264.1 13.6 %collective-permute-start.50 = (bf16[128,2048]{1,0:T(8,128)(2,1)S(1)}, bf16[128,2048]{1,0:T(8,128)(2,1)S(1)}, u32[]{:S(2)}, u32[]{:S(2)}) collective-permute-start(bf16[128,2048]{1,0:T(8,128)(2,1)S(1)} %fusion.90), channel_id=1, source_target_pairs={{0,16},{4,20},{8,24},{12,28},{16,0},{20,4},{24,8},{28,12},{1,17},{... | collective-permute-start | bytes 1572872 | tf_op jit(solution)/shard_map/ppermute | solution.py:29
  277.7 70.5 %collective-permute-start.49 = (bf16[128,2048]{1,0:T(8,128)(2,1)}, bf16[128,2048]{1,0:T(8,128)(2,1)}, u32[]{:S(2)}, u32[]{:S(2)}) collective-permute-start(bf16[128,2048]{1,0:T(8,128)(2,1)} %fusion.89), channel_id=1, source_target_pairs={{0,8},{4,12},{8,0},{12,4},{16,24},{20,28},{24,16},{28,20},{1,9},{5... | collective-permute-start | bytes 1572872 | tf_op jit(solution)/shard_map/ppermute | solution.py:29
  286.6 48.3 %collective-permute-start.36 = (bf16[256,2560]{1,0:T(8,128)(2,1)}, bf16[256,2560]{1,0:T(8,128)(2,1)}, u32[]{:S(2)}, u32[]{:S(2)}) collective-permute-start(bf16[256,2560]{1,0:T(8,128)(2,1)} %pad_maximum_fusion.6), channel_id=1, source_target_pairs={{0,16},{4,20},{8,24},{12,28},{16,0},{20,4},{24,8},{28,12},{1,17},{... | collective-permute-start | bytes 3932168 | tf_op jit(solution)/shard_map/ppermute | solution.py:29
  288.7 49.6 %collective-permute-start.37 = (bf16[256,2560]{1,0:T(8,128)(2,1)}, bf16[256,2560]{1,0:T(8,128)(2,1)}, u32[]{:S(2)}, u32[]{:S(2)}) collective-permute-start(bf16[256,2560]{1,0:T(8,128)(2,1)} %pad_maximum_fusion.7), channel_id=1, source_target_pairs={{0,8},{4,12},{8,0},{12,4},{16,24},{20,28},{24,16},{28,20},{1,9},{5... | collective-permute-start | bytes 3932168 | tf_op jit(solution)/shard_map/ppermute | solution.py:29
  299.3 36.8 %copy-start.74 = (f32[512,512]{1,0:T(8,128)S(1)}, f32[512,512]{1,0:T(8,128)}, u32[]{:S(2)}) copy-start(f32[512,512]{1,0:T(8,128)} %copy-done.73) | copy-start | bytes 3145732
  348.2 24.5 %collective-permute-start.38 = (bf16[512,1536]{1,0:T(8,128)(2,1)}, bf16[512,1536]{1,0:T(8,128)(2,1)}, u32[]{:S(2)}, u32[]{:S(2)}) collective-permute-start(bf16[512,1536]{1,0:T(8,128)(2,1)} %convolution_convert_fusion.1), channel_id=1, source_target_pairs={{0,4},{4,0},{8,12},{12,8},{16,20},{20,16},{24,28},{28,24},{1,5},{5... | collective-permute-start | bytes 4718600 | tf_op jit(solution)/shard_map/ppermute | solution.py:29
  349.4 17.5 %collective-permute-start.40 = (bf16[128,2560]{1,0:T(8,128)(2,1)}, bf16[128,2560]{1,0:T(8,128)(2,1)}, u32[]{:S(2)}, u32[]{:S(2)}) collective-permute-start(bf16[128,2560]{1,0:T(8,128)(2,1)} %pad_maximum_fusion.14), channel_id=1, source_target_pairs={{0,8},{4,12},{8,0},{12,4},{16,24},{20,28},{24,16},{28,20},{1,9},{5... | collective-permute-start | bytes 1966088 | tf_op jit(solution)/shard_map/ppermute | solution.py:29
  350.3 19.3 %collective-permute-start.41 = (bf16[128,2560]{1,0:T(8,128)(2,1)}, bf16[128,2560]{1,0:T(8,128)(2,1)}, u32[]{:S(2)}, u32[]{:S(2)}) collective-permute-start(bf16[128,2560]{1,0:T(8,128)(2,1)} %pad_maximum_fusion.15), channel_id=1, source_target_pairs={{0,16},{4,20},{8,24},{12,28},{16,0},{20,4},{24,8},{28,12},{1,17},{... | collective-permute-start | bytes 1966088 | tf_op jit(solution)/shard_map/ppermute | solution.py:29
  354.2 24.5 %collective-permute-start.39 = (bf16[512,1536]{1,0:T(8,128)(2,1)}, bf16[512,1536]{1,0:T(8,128)(2,1)}, u32[]{:S(2)}, u32[]{:S(2)}) collective-permute-start(bf16[512,1536]{1,0:T(8,128)(2,1)} %convolution_convert_fusion), channel_id=1, source_target_pairs={{0,4},{4,0},{8,12},{12,8},{16,20},{20,16},{24,28},{28,24},{1,5},{5... | collective-permute-start | bytes 4718600 | tf_op jit(solution)/shard_map/ppermute | solution.py:29
  355.8 114.1 %reduce-scatter.3.cloned.1.call-start = ((), (), s32[]{:S(2)}) async-start(), calls=%async_computation.2 | async-start | bytes 2621440 | tf_op jit(solution)/shard_map/reduce_scatter | solution.py:236
  377.5 52.0 %collective-permute-start.42 = (bf16[256,1536]{1,0:T(8,128)(2,1)}, bf16[256,1536]{1,0:T(8,128)(2,1)}, u32[]{:S(2)}, u32[]{:S(2)}) collective-permute-start(bf16[256,1536]{1,0:T(8,128)(2,1)} %fusion.61), channel_id=1, source_target_pairs={{0,16},{4,20},{8,24},{12,28},{16,0},{20,4},{24,8},{28,12},{1,17},{... | collective-permute-start | bytes 2359304 | tf_op jit(solution)/shard_map/ppermute | solution.py:29
  382.7 49.0 %collective-permute-start.45 = (bf16[256,1536]{1,0:T(8,128)(2,1)}, bf16[256,1536]{1,0:T(8,128)(2,1)}, u32[]{:S(2)}, u32[]{:S(2)}) collective-permute-start(bf16[256,1536]{1,0:T(8,128)(2,1)} %bitcast.51), channel_id=1, source_target_pairs={{0,8},{4,12},{8,0},{12,4},{16,24},{20,28},{24,16},{28,20},{1,9},{5... | collective-permute-start | bytes 2359304 | tf_op jit(solution)/shard_map/ppermute | solution.py:29
  389.4 4.3 collective-permute-start.51
  393.8 3.7 collective-permute-start.52
  397.5 5.4 %collective-permute-start.53 = (f32[128,4]{0,1:T(4,128)S(1)}, f32[128,4]{0,1:T(4,128)S(1)}, u32[]{:S(2)}, u32[]{:S(2)}) collective-permute-start(f32[128,4]{0,1:T(4,128)S(1)} %slice.553), channel_id=1, source_target_pairs={{0,8},{4,12},{8,0},{12,4},{16,24},{20,28},{24,16},{28,20},{1,9},{5... | collective-permute-start | bytes 6152 | tf_op jit(solution)/shard_map/ppermute | solution.py:29
  402.9 25.3 %collective-permute-start.54 = (f32[128,4]{0,1:T(4,128)S(1)}, f32[128,4]{0,1:T(4,128)S(1)}, u32[]{:S(2)}, u32[]{:S(2)}) collective-permute-start(f32[128,4]{0,1:T(4,128)S(1)} %slice_add_fusion.4), channel_id=1, source_target_pairs={{0,1},{1,0},{2,3},{3,2},{4,5},{5,4},{6,7},{7,6},{8,9},{9,8},{10,11... | collective-permute-start | bytes 6152 | tf_op jit(solution)/shard_map/ppermute | solution.py:967
  428.1 18.5 %collective-permute-start.55 = (f32[128,4]{0,1:T(4,128)S(1)}, f32[128,4]{0,1:T(4,128)S(1)}, u32[]{:S(2)}, u32[]{:S(2)}) collective-permute-start(f32[128,4]{0,1:T(4,128)S(1)} %add.151), channel_id=1, source_target_pairs={{0,2},{1,3},{2,0},{3,1},{4,6},{5,7},{6,4},{7,5},{8,10},{9,11},{10,... | collective-permute-start | bytes 6152 | tf_op jit(solution)/shard_map/ppermute | solution.py:967
  430.8 10.0 %collective-permute-start.43 = (bf16[128,1536]{1,0:T(8,128)(2,1)S(1)}, bf16[128,1536]{1,0:T(8,128)(2,1)S(1)}, u32[]{:S(2)}, u32[]{:S(2)}) collective-permute-start(bf16[128,1536]{1,0:T(8,128)(2,1)S(1)} %fusion.94), channel_id=1, source_target_pairs={{0,8},{4,12},{8,0},{12,4},{16,24},{20,28},{24,16},{28,20},{1,9},{5... | collective-permute-start | bytes 1179656 | tf_op jit(solution)/shard_map/ppermute | solution.py:29
  433.2 10.0 %collective-permute-start.46 = (bf16[128,1536]{1,0:T(8,128)(2,1)S(1)}, bf16[128,1536]{1,0:T(8,128)(2,1)S(1)}, u32[]{:S(2)}, u32[]{:S(2)}) collective-permute-start(bf16[128,1536]{1,0:T(8,128)(2,1)S(1)} %fusion.95), channel_id=1, source_target_pairs={{0,16},{4,20},{8,24},{12,28},{16,0},{20,4},{24,8},{28,12},{1,17},{... | collective-permute-start | bytes 1179656 | tf_op jit(solution)/shard_map/ppermute | solution.py:29
  441.0 12.8 %collective-permute-start.44 = (bf16[128,1024]{1,0:T(8,128)(2,1)S(1)}, bf16[128,1024]{1,0:T(8,128)(2,1)S(1)}, u32[]{:S(2)}, u32[]{:S(2)}) collective-permute-start(bf16[128,1024]{1,0:T(8,128)(2,1)S(1)} %pad_maximum_fusion.23), channel_id=1, source_target_pairs={{0,1},{1,2},{2,3},{3,0},{4,5},{5,6},{6,7},{7,4},{8,9},{9,10},{10,1... | collective-permute-start | bytes 786440 | tf_op jit(solution)/shard_map/ppermute | solution.py:29
  443.4 13.4 %collective-permute-start.48 = (bf16[128,1024]{1,0:T(8,128)(2,1)S(1)}, bf16[128,1024]{1,0:T(8,128)(2,1)S(1)}, u32[]{:S(2)}, u32[]{:S(2)}) collective-permute-start(bf16[128,1024]{1,0:T(8,128)(2,1)S(1)} %pad_maximum_fusion.25), channel_id=1, source_target_pairs={{0,3},{1,0},{2,1},{3,2},{4,7},{5,4},{6,5},{7,6},{8,11},{9,8},{10,9... | collective-permute-start | bytes 786440 | tf_op jit(solution)/shard_map/ppermute | solution.py:29
  445.1 23.3 %collective-permute-start.47 = (bf16[128,1024]{1,0:T(8,128)(2,1)S(1)}, bf16[128,1024]{1,0:T(8,128)(2,1)S(1)}, u32[]{:S(2)}, u32[]{:S(2)}) collective-permute-start(bf16[128,1024]{1,0:T(8,128)(2,1)S(1)} %pad_maximum_fusion.24), channel_id=1, source_target_pairs={{0,2},{1,3},{2,0},{3,1},{4,6},{5,7},{6,4},{7,5},{8,10},{9,11},{10,... | collective-permute-start | bytes 786440 | tf_op jit(solution)/shard_map/ppermute | solution.py:29
  (81 other events, 472.8 us)
Sparse Core Ops, SparseCore 0:
  9.6 43.2 all-gather.4
  54.5 34.0 all-gather.6
  356.0 44.2 reduce-scatter.4
  403.1 45.2 reduce-scatter.2

commit v5 on v3

--- a/solution.py
+++ b/solution.py
@@ -30,8 +30,8 @@
         before.append(result)
         return result
 
-    def swap(self, value, bit, depth=0):
-        return self.send(value, "dp", [(i, i ^ bit) for i in range(self.dp)], bit, depth)
+    def swap(self, value, bit, depth=None):
+        return self.send(value, "dp", [(i, i ^ bit) for i in range(self.dp)], bit, 0)
 
     def shift(self, value, step, depth=3):
         pairs = [(i, (i + step) % self.mp) for i in range(self.mp)]
@@ -125,11 +125,12 @@
         pieces = self.pieces(i, order)
         return pieces[0] if len(pieces) == 1 else jnp.concatenate(pieces, axis=0)
 
-    def step(self, tokens=()):
+    def step(self, tokens=(), second=()):
         for i in range(2):
             bit = self.steps[i][0]
             value = self.join(i, self.known[i])
-            self.held[i] = [value, self.links.swap(after(value, *tokens), bit)]
+            value = after(value, *(second if i else tokens))
+            self.held[i] = [value, self.links.swap(value, bit)]
             self.known[i] = self.known[i] + [r ^ bit for r in self.known[i]]
             self.steps[i] = self.steps[i][1:]
         return [h[1] for h in self.held]
@@ -137,7 +138,7 @@
     def steps_but_last(self, tokens=()):
         received = []
         while len(self.steps[0]) > 1:
-            received = self.step(tokens)
+            received = self.step(tokens, tokens)
         return received
 
     def hold(self, tokens):
@@ -159,12 +160,14 @@
         self.remain = [list(plan.major[1:]), list(plan.major[1:])]
 
     def core(self, i):
-        self.kept[i] = []
+        self.kept[i], outs = [], []
         for left, rights in self.pairs:
             middle = left.shape[1] // 2
             sent = dot(left[:, middle:], rights[i], (0, 0)).astype(LOW)
             kept = dot(left[:, :middle], rights[i], (0, 0))
             self.kept[i].append((kept, self.links.swap(sent, self.plan.major[0])))
+            outs.append(sent)
+        return outs
 
     def hold(self, i, tokens):
         self.kept[i] = [(k, after(r, *tokens)) for k, r in self.kept[i]]
@@ -205,39 +208,35 @@
             result.append([r[:, j * width : (j + 1) * width] for r in pair for j in range(half)])
         return result
 
-    def shifts(self, natural, tokens=()):
-        mp = self.plan.mp
-        products = self.rows()
-        own = lax.axis_index("mp")
-        for n, rows in enumerate(products):
-            if natural[n]:
-                joined = jnp.stack(rows)
-                products[n] = [
-                    lax.dynamic_index_in_dim(joined, lax.rem(own + k, mp), 0, keepdims=False)
-                    for k in range(mp)
-                ]
-        self.total = [rows[0] for rows in products]
-        outs = []
-        for k in range(1, mp):
-            out = [rows[k].astype(LOW) for rows in products]
-            outs.append(out[0] if len(out) == 1 else jnp.concatenate(out, axis=1))
-        self.received = [
-            self.links.shift(after(value, *tokens), k + 1, 0) for k, value in enumerate(outs)
-        ]
-        return outs
-
-    def finish(self):
-        result, at = [], 0
-        for total in self.total:
-            for part in self.received:
-                total = total + part[:, at : at + total.shape[1]].astype(jnp.float32)
-            result.append(total)
-            at += total.shape[1]
-        return result
-
-    def reduce_columns(self):
-        joined = jnp.stack(self.rows()[0])
-        return lax.psum_scatter(joined, "mp", scatter_dimension=0, tiled=False)
+
+def own_first(blocks):
+    joined = jnp.stack(blocks)
+    own = lax.axis_index("mp")
+    return [
+        lax.dynamic_index_in_dim(joined, lax.rem(own + k, len(blocks)), 0, keepdims=False)
+        for k in range(len(blocks))
+    ]
+
+
+def shift_blocks(plan, links, products, tokens=()):
+    outs, received = [], []
+    for k in range(1, plan.mp):
+        out = [blocks[k].astype(LOW) for blocks in products]
+        out = out[0] if len(out) == 1 else jnp.concatenate(out, axis=1)
+        outs.append(out)
+        received.append(links.shift(after(out, *tokens), k, 0))
+    result, at = [], 0
+    for blocks in products:
+        total = blocks[0]
+        for part in received:
+            total = total + part[:, at : at + total.shape[1]].astype(jnp.float32)
+        result.append(total)
+        at += total.shape[1]
+    return result, outs
+
+
+def reduce_blocks(blocks):
+    return lax.psum_scatter(jnp.stack(blocks), "mp", scatter_dimension=0, tiled=False)
 
 
 def after(value, *tokens):
@@ -251,6 +250,13 @@
     return dot(left[:, :half], top, (1, 0)) + dot(left[:, half:], bottom, (1, 0))
 
 
+A_X2 = 1
+A_CORE = 0
+A_DOWN = 1
+B_DOWN = 1
+B_UADD = 1
+Z_LAST = 1
+D_SUMS = 1
 MEGA = 1 << 20
 LOG2E = 1.4426950408889634
 VM_FWD = 36
@@ -595,29 +601,51 @@
     )(table, hidden, *weights[0], *weights[1], start)
 
 
+def slope_kernel(count):
+    def kernel(grad_z, top_a, bottom_a, top_b, bottom_b, slope, grad_upward):
+        def work(top, bottom):
+            grad = split_dot(grad_z[...], top[...], bottom[...]) * slope[0].astype(jnp.float32)
+            grad_upward[0] = grad.astype(LOW)
+
+        either(pl.program_id(0), count, work, (top_a, bottom_a), (top_b, bottom_b))
+
+    return kernel
+
+
+def feed_slope(grad_z, down, slope, tile=512):
+    total, width = grad_z.shape
+    ff = 2 * slope.shape[2]
+    count = ff // 2 // tile
+    block = pl.BlockSpec((1, total, tile), lambda j: (j // count, 0, j % count))
+    weight_a, weight_b = column_halves(width // 2, tile, count)
+    return pl.pallas_call(
+        slope_kernel(count),
+        name="feed_slope",
+        grid=(ff // tile,),
+        in_specs=[whole(total, width), weight_a, weight_a, weight_b, weight_b, block],
+        out_specs=block,
+        out_shape=jax.ShapeDtypeStruct((2, total, ff // 2), LOW),
+        compiler_params=params(VM_UP),
+        cost_estimate=cost(2 * total * width * ff, 2 * (width * ff + 2 * total * ff)),
+    )(grad_z, *down[0], *down[1], slope)
+
+
 def feed_back_kernel(steps):
-    def kernel(grad_z, down_top_a, down_bottom_a, down_top_b, down_bottom_b,
-               up_top_a, up_bottom_a, up_top_b, up_bottom_b, slope, resid, grads, small,
-               grad_upward, grad_resid, grad_branch, sums, total):
+    def kernel(upward, top_a, bottom_a, top_b, bottom_b, resid, grads, small,
+               grad_resid, grad_branch, sums, total):
         step = pl.program_id(0)
-        half = up_top_a.shape[0]
+        half = top_a.shape[0]
 
         @pl.when(step == 0)
         def _():
             total[...] = jnp.zeros_like(total)
             sums[...] = jnp.zeros_like(sums)
 
-        def work(down_top, down_bottom, up_top, up_bottom):
-            grad = split_dot(grad_z[...], down_top[...], down_bottom[...]) * slope[0].astype(jnp.float32)
-            grad_upward[0] = grad.astype(LOW)
-            total[:, :half] += dot(grad_upward[0], up_top[...], (1, 1))
-            total[:, half:] += dot(grad_upward[0], up_bottom[...], (1, 1))
-
-        either(
-            step, steps // 2, work,
-            (down_top_a, down_bottom_a, up_top_a, up_bottom_a),
-            (down_top_b, down_bottom_b, up_top_b, up_bottom_b),
-        )
+        def work(top, bottom):
+            total[:, :half] += dot(upward[0], top[...], (1, 1))
+            total[:, half:] += dot(upward[0], bottom[...], (1, 1))
+
+        either(step, steps // 2, work, (top_a, bottom_a), (top_b, bottom_b))
 
         @pl.when(step >= steps)
         def _():
@@ -638,31 +666,30 @@
     return kernel
 
 
-def feed_back(grad_z, down, up, slope, resid, grads, small, tile=512):
-    total, width = grad_z.shape
-    ff = 2 * slope.shape[2]
+def feed_back(upward, up, resid, grads, small, tile=512):
+    total, width = resid.shape
+    ff = 2 * upward.shape[2]
     steps = ff // tile
     count = steps // 2
     clip = lambda j: jnp.minimum(j, steps - 1)
-    wide_a, wide_b = column_halves(width // 2, tile, count)
+    weight_a, weight_b = column_halves(width // 2, tile, count)
     block = pl.BlockSpec((1, total, tile), lambda j: (clip(j) // count, 0, clip(j) % count))
     late = pl.BlockSpec((LATE, width), lambda j: (jnp.maximum(j - steps, 0), 0))
     return pl.pallas_call(
         feed_back_kernel(steps),
         name="feed_back",
         grid=(steps + total // LATE,),
-        in_specs=[whole(total, width), wide_a, wide_a, wide_b, wide_b, wide_a, wide_a, wide_b, wide_b, block, late, late, whole(4, width)],
-        out_specs=[block, late, late, whole(16, width)],
+        in_specs=[block, weight_a, weight_a, weight_b, weight_b, late, late, whole(4, width)],
+        out_specs=[late, late, whole(16, width)],
         out_shape=[
-            jax.ShapeDtypeStruct((2, total, ff // 2), LOW),
             jax.ShapeDtypeStruct((total, width), jnp.float32),
             jax.ShapeDtypeStruct((total, width), LOW),
             jax.ShapeDtypeStruct((16, width), jnp.float32),
         ],
         scratch_shapes=[pltpu.VMEM((total, width), jnp.float32)],
-        compiler_params=params(VM_BACK),
-        cost_estimate=cost(4 * total * width * ff, 4 * (width * ff + total * ff) + 14 * total * width),
-    )(grad_z, *down[0], *down[1], *up[0], *up[1], slope, resid, grads, small)
+        compiler_params=params(VM_DOWN),
+        cost_estimate=cost(2 * total * width * ff, 2 * (width * ff + total * ff) + 14 * total * width),
+    )(upward, *up[0], *up[1], resid, grads, small)
 
 
 def backward_kernel(rows, steps, local_heads, factor):
@@ -801,19 +828,26 @@
         rows_in = (latents.reshape(total, width), out_grad.reshape(total, width))
         if not blocked:
             rows_in = tuple(plan.enter(v) for v in rows_in)
+        local = jnp.concatenate([w_qkv[0], w_qkv[1], w_qkv[2], w_out], axis=1)
+
+        def columns_of(weight):
+            columns = lax.all_gather(weight, "mp", axis=0)
+            return plan.halves([columns[k] for k in range(mp)])
+
+        halves = plan.spread_columns(links, local)
+        gather_attention = Gather(plan, links, halves)
+        up_halves = columns_of(w_up)
         entered, grad_rows, grad_z, inputs_a = enter_norm(table, blocked, *rows_in, small)
-
-        local = jnp.concatenate([w_qkv[0], w_qkv[1], w_qkv[2], w_out], axis=1)
-        gather_attention = Gather(plan, links, plan.spread_columns(links, local))
-        columns_up = lax.all_gather(w_up, "mp", axis=0)
-        columns_down = lax.all_gather(w_down, "mp", axis=0)
-        gather_up = Gather(plan, links, plan.halves([columns_up[k] for k in range(mp)]))
-        gather_down = Gather(plan, links, plan.halves([columns_down[k] for k in range(mp)]))
         gather_attention.steps_but_last([small])
         window = links.halo(inputs_a.reshape(micro, rows, width))
-        gather_attention.step([inputs_a])
+        down_halves = columns_of(w_down)
+        halos = [window[0], window[2]]
+        gather_attention.step(halos if A_X2 else [inputs_a], [inputs_a])
+        gather_up = Gather(plan, links, up_halves)
+        gather_down = Gather(plan, links, down_halves)
+        tokens_up = gather_up.steps_but_last([inputs_a])
+        gather_attention.hold(tokens_up + halos if A_CORE else halos)
         attention = gather_attention.finish()
-        tokens = gather_up.steps_but_last([inputs_a])
 
         span = rows + 2 * HALO
         first = lax.axis_index("mp") * rows
@@ -825,68 +859,84 @@
         column, row = groups[:, :, None], keys[:, None, :]
 
         saved, attended, resid, inputs_c = forward_block(
-            window, attention, after(column, *tokens, columns_down), row, entered, small, mp, factor
+            window, attention, after(column, *tokens_up, *down_halves), row, entered, small, mp, factor
         )
+        early_down = gather_down.steps_but_last()
         gather_up.step()
-        tokens = gather_down.steps_but_last()
-        gather_up.hold([inputs_c])
+        gather_up.hold([inputs_c] + early_down * A_DOWN)
         up = gather_up.finish()
-        gather_down.hold([inputs_c])
-        hidden, slope = feed_up(after(inputs_c, *tokens), up)
-        gather_down.step()
+        late_down = gather_down.step()
+        hidden, slope = feed_up(after(inputs_c, *early_down), up)
         gather_down.hold([hidden])
         down = gather_down.finish()
-        grad_down = Scatter(plan, links, [(grad_z, [hidden[0], hidden[1]])])
+        left = after(grad_z, *late_down) if B_DOWN else grad_z
+        grad_down = Scatter(plan, links, [(left, [hidden[0], hidden[1]])])
+        sent = grad_down.core(0) + grad_down.core(1)
+        upward = feed_slope(after(grad_z, *sent), down, slope)
         for i in range(2):
-            grad_down.core(i)
+            grad_down.hold(i, [upward])
         tokens = [grad_down.steps_but_last(i) for i in range(2)]
-        upward, grad_resid, grad_branch, sums_two = feed_back(
-            after(grad_z, *tokens), down, up, slope, resid, grad_rows, small
+        left = after(inputs_c, *tokens)
+        grad_up = Scatter(plan, links, [(left, [upward[0], upward[1]])])
+        tokens = tokens + grad_up.core(0) + grad_up.core(1)
+        if B_UADD:
+            tokens += grad_up.add(0) + grad_up.add(1)
+        grad_resid, grad_branch, sums_two = feed_back(
+            upward, up, after(resid, *tokens), grad_rows, small
         )
         branch = links.halo(grad_branch.reshape(micro, rows, width))
+        halos = [branch[0], branch[2]]
         for i in range(2):
             grad_down.hold(i, [grad_branch])
         tokens = [grad_down.step(i) for i in range(2)]
-        left = after(inputs_c, *tokens)
-        grad_up = Scatter(
-            plan, links, [(left, [upward[0], upward[1]]), (grad_branch, [attended[0], attended[1]])]
+        latents_out = feed_down(table, blocked, after(hidden, *tokens), down, resid)
+        for i in range(2):
+            grad_down.hold(i, [latents_out])
+        tokens = halos + [latents_out]
+        left = after(grad_branch, *tokens)
+        grad_out = Scatter(plan, links, [(left, [attended[0], attended[1]])])
+        down_rows = grad_down.rows()[0]
+        for i in range(2):
+            if not B_UADD:
+                grad_up.hold(i, [latents_out])
+            grad_out.core(i)
+            grad_up.kept[i] += grad_out.kept[i]
+        tokens = [grad_up.steps_but_last(i) for i in range(2)]
+        projected, norm_one = backward_block(
+            branch, attention, after(column, *tokens, *down_rows), row, saved, mp, factor
         )
-        for i in range(2):
-            grad_up.core(i)
-        tokens = [grad_up.steps_but_last(i) for i in range(2)]
-        grad_down = grad_down.reduce_columns()
-        projected, norm_one = backward_block(
-            branch, attention, after(column, *tokens), row, saved, mp, factor
-        )
+        grad_down = reduce_blocks(down_rows)
         for i in range(2):
             grad_up.hold(i, [norm_one])
         tokens = [grad_up.step(i) for i in range(2)]
         left = after(inputs_a, *tokens)
         grad_qkv = Scatter(plan, links, [(left, [projected[0], projected[1]])])
+        grad_qkv.core(0)
+        grad_qkv.core(1)
+        tokens = [grad_qkv.steps_but_last(i) for i in range(2)]
         for i in range(2):
-            grad_qkv.core(i)
-        tokens = [grad_qkv.steps_but_last(i) for i in range(2)]
+            grad_up.hold(i, tokens)
+        up_rows, out_rows = grad_up.rows()
+        (grad_up,), outs = shift_blocks(plan, links, [own_first(up_rows)])
         latents_grad, sums_one = leave_norm(
-            table, blocked, after(norm_one, *tokens), entered, grad_resid, small
+            table, blocked, after(norm_one, *outs), entered, grad_resid, small
         )
         for i in range(2):
-            grad_up.hold(i, [latents_grad])
-        tokens = grad_up.shifts([True, False])
-        latents_out = feed_down(table, blocked, after(hidden, sums_one, *tokens), down, resid)
-        for i in range(2):
-            grad_qkv.hold(i, [latents_out])
-            grad_qkv.step(i)
-        grad_qkv.shifts([False])
-        grad_up, grad_out = grad_up.finish()
-        grad_qkv = grad_qkv.finish()[0]
-        grad_qkv = jnp.stack(jnp.split(grad_qkv, 3, axis=1))
+            grad_qkv.hold(i, [latents_grad])
+        tokens = [grad_qkv.step(i) for i in range(2)]
+        qkv_rows = grad_qkv.rows()[0]
+        (grad_qkv, grad_out), outs = shift_blocks(
+            plan, links, [qkv_rows, out_rows], [grad_up] if Z_LAST else []
+        )
         sums = jnp.stack([sums_one, sums_two], axis=0).reshape(2, 2, 8, width).sum(axis=2)
         sums = sums.transpose(1, 0, 2).reshape(4, width).T
+        sums = after(sums, *(tokens if D_SUMS == 1 else outs if D_SUMS == 3 else [grad_up]))
         for bit in plan.major:
             middle = sums.shape[0] // 2
             sums = sums[:middle] + links.swap(sums[middle:], bit, 0)
         for bit in [1 << i for i in range(mp.bit_length() - 1)]:
             sums = sums + lax.ppermute(sums, "mp", [(i, i ^ bit) for i in range(mp)])
+        grad_qkv = jnp.stack(jnp.split(grad_qkv, 3, axis=1))
         sums = sums.T
         if not blocked:
             latents_out, latents_grad = plan.leave(latents_out), plan.leave(latents_grad)

time: 510 us -> 473 us (0.927)
  waiting for transfers between devices: 151 us -> 108 us
  starting transfers between devices: 66.8 us -> 73.5 us
    ppermute x57, waiting for transfers between devices: 144 us -> 108 us  [send(): result = lax.ppermute(value, axis, pairs)]
    pallas_call x1, Pallas kernels: 24.9 us -> 14.2 us  [feed_back(): pl.pallas_call(feed_back_kernel(steps), name='feed_back', grid=(steps + t...]
    pallas_call x0 -> x1, Pallas kernels: none -> 10 us  [feed_slope(): pl.pallas_call(slope_kernel(count), name='feed_slope', grid=(ff // tile,)...]
    ppermute x57, starting transfers between devices: 61.8 us -> 70 us  [send(): result = lax.ppermute(value, axis, pairs)]
    ppermute x2, waiting for transfers between devices: 6.79 us -> 0.01 us  [body(): sums = sums + lax.ppermute(sums, 'mp', [(i, i ^ bit) for i in range(mp)])]
    unnamed x168 -> x202, local copies, waits for them, and re-layouts: 32.4 us -> 33.3 us
    concatenate x12 -> x10, other arithmetic: 13.6 us -> 13.7 us  [join(): return pieces[0] if len(pieces) == 1 else jnp.concatenate(pieces, axis=0)]
  transfers between devices with their start and end apart: 62 -> 62, of which waited for: 22 -> 21; matrix products, arithmetic and copies ran while one was open for 21% -> 20% of each run, Pallas kernels for 27% -> 29%
where the time goes in v5:
time: 473 us; the launch traced here: 466 us
  Pallas kernels  133 us (28%)
  waiting for transfers between devices  108 us (23%)
  starting transfers between devices  73.5 us (16%)
  local copies, waits for them, and re-layouts  64.3 us (14%)
  matrix products  36.2 us (8%)
  other arithmetic  34 us (7%)
  between operations  15.8 us (3%)
    ppermute x57, waiting for transfers between devices, send(): result = lax.ppermute(value, axis, pairs)  108 us
    ppermute x57, starting transfers between devices, send(): result = lax.ppermute(value, axis, pairs)  70 us
    dot_general x16, matrix products, dot(): lax.dot_general(left, right, ((dims[:1], dims[1:]), ((), ())), preferred_...  36.2 us
    pallas_call x1, Pallas kernels, forward_block(): pl.pallas_call(forward_kernel(rows, steps, g // HEAD_DIM, factor), name='...  35.9 us
    pallas_call x1, Pallas kernels, backward_block(): pl.pallas_call(backward_kernel(rows, steps, g // HEAD_DIM, factor), name=...  35.7 us
    unnamed x202, local copies, waits for them, and re-layouts  33.3 us
    pallas_call x1, Pallas kernels, feed_up(): pl.pallas_call(up_kernel(count), name='feed_up', grid=(ff // tile,), in_s...  15 us
    pallas_call x1, Pallas kernels, feed_back(): pl.pallas_call(feed_back_kernel(steps), name='feed_back', grid=(steps + t...  14.2 us
  transfers between devices with their start and end apart: 62, of which 21 were waited for; matrix products, arithmetic and copies ran while one was open for 20% of the time, Pallas kernels for 29%

profile of v5, /device:TPU:0, one launch (start us, length us, event | category | flops | bytes accessed | tf_op | source)
XLA Modules:
  0.0 465.6 jit_solution(6794225799361408217)
XLA Ops:
  9.7 3.1 collective-permute-start.10
  12.8 2.6 collective-permute-start.9
  21.6 1.6 collective-permute-start.1
  26.4 1.9 copy-done.2
  28.3 1.9 copy-done.3
  30.2 4.0 enter.1
  35.3 1.6 copy-done.30
  37.0 6.1 %collective-permute-done.9 = bf16[128,1024]{1,0:T(8,128)(2,1)S(1)} collective-permute-done((bf16[128,1024]{1,0:T(8,128)(2,1)S(1)}, bf16[128,1024]{1,0:T(8,128)(2,1)S(1)}, u32[]{:S(2)}, u32[]{:S(2)}) %collective-permute-start.9) | collective-permute-done | bytes 262176 | tf_op jit(solution)/shard_map/ppermute | solution.py:29
  43.1 1.6 collective-permute-start.11
  46.1 10.8 %collective-permute-start.3 = (bf16[3,128,1024]{2,1,0:T(8,128)(2,1)S(1)}, bf16[3,128,1024]{2,1,0:T(8,128)(2,1)S(1)}, u32[]{:S(2)}, u32[]{:S(2)}) collective-permute-start(bf16[3,128,1024]{2,1,0:T(8,128)(2,1)S(1)} %get-tuple-element.134), channel_id=1, source_target_pairs={{0,1},{1,2},{2,3},{4,5},{5,6},{6,7},{8,9},{9,10},{10,11},{12,13},{... | collective-permute-start | bytes 2359304 | tf_op jit(solution)/shard_map/ppermute | solution.py:29
  60.6 12.6 %collective-permute-done.6 = bf16[128,2048]{1,0:T(8,128)(2,1)S(1)} collective-permute-done((bf16[128,2048]{1,0:T(8,128)(2,1)S(1)}, bf16[128,2048]{1,0:T(8,128)(2,1)S(1)}, u32[]{:S(2)}, u32[]{:S(2)}) %collective-permute-start.6) | collective-permute-done | bytes 524320 | tf_op jit(solution)/shard_map/ppermute | solution.py:29
  73.3 5.9 %collective-permute-done.3.before = bf16[3,128,1024]{2,1,0:T(8,128)(2,1)S(1)} collective-permute-done((bf16[3,128,1024]{2,1,0:T(8,128)(2,1)S(1)}, bf16[3,128,1024]{2,1,0:T(8,128)(2,1)S(1)}, u32[]{:S(2)}, u32[]{:S(2)}) %collective-permute-start.3) | collective-permute-done | bytes 786464 | tf_op jit(solution)/shard_map/ppermute | solution.py:29
  79.1 11.1 %collective-permute-done.4.after = bf16[3,128,1024]{2,1,0:T(8,128)(2,1)S(1)} collective-permute-done((bf16[3,128,1024]{2,1,0:T(8,128)(2,1)S(1)}, bf16[3,128,1024]{2,1,0:T(8,128)(2,1)S(1)}, u32[]{:S(2)}, u32[]{:S(2)}) %collective-permute-start.4) | collective-permute-done | bytes 786464 | tf_op jit(solution)/shard_map/ppermute | solution.py:29
  91.8 13.2 %collective-permute-done.7 = bf16[256,2048]{1,0:T(8,128)(2,1)S(1)} collective-permute-done((bf16[256,2048]{1,0:T(8,128)(2,1)S(1)}, bf16[256,2048]{1,0:T(8,128)(2,1)S(1)}, u32[]{:S(2)}, u32[]{:S(2)}) %collective-permute-start.7) | collective-permute-done | bytes 1048608 | tf_op jit(solution)/shard_map/ppermute | solution.py:29
  113.5 8.9 %collective-permute-done.14 = bf16[128,2048]{1,0:T(8,128)(2,1)} collective-permute-done((bf16[128,2048]{1,0:T(8,128)(2,1)S(1)}, bf16[128,2048]{1,0:T(8,128)(2,1)}, u32[]{:S(2)}, u32[]{:S(2)}) %collective-permute-start.14) | collective-permute-done | bytes 524320 | tf_op jit(solution)/shard_map/ppermute | solution.py:29
  128.3 1.9 collective-permute-start.18
  130.2 35.9 %attention_forward.1 = (bf16[3,512,3072]{2,1,0:T(8,128)(2,1)}, bf16[2,768,512]{2,1,0:T(8,128)(2,1)S(1)}, f32[768,1024]{1,0:T(8,128)S(1)}, bf16[768,1024]{1,0:T(8,128)(2,1)S(1)}) custom-call(bf16[3,128,1024]{2,1,0:T(8,128)(2,1)S(1)} %copy-done.41, bf16[3,256,1024]{2,1,0:T(8,128)(2,1)S(1)} %bitcast.226, bf16[3,128,1024]{2,1,0:T(8,128)(2,1)S(1)} %copy-done.43, ...), custom_call_target="tpu_custom_call" | custom-call | flops 12884901888 | bytes 31457280 | tf_op jit(solution)/shard_map/attention_forward/pallas_call | solution.py:473
  166.1 1.7 copy-done.50
  171.9 1.6 pad_maximum_fusion.13
  176.2 1.6 collective-permute-done.19.bottom_a
  177.8 15.0 %feed_up.1 = (bf16[2,768,2048]{2,1,0:T(8,128)(2,1)S(1)}, bf16[2,768,2048]{2,1,0:T(8,128)(2,1)S(1)}) custom-call(bf16[768,1024]{1,0:T(8,128)(2,1)S(1)} %get-tuple-element.93.inputs, bf16[512,2048]{1,0:T(8,128)(2,1)S(1)} %constant_dynamic-update-slice_fusion.7.top_a, bf16[512,2048]{1,0:T(8,128)(2,1)S(1)} %collective-permute-done.19.bottom_a, ...), custom_call_target="tpu_custom_call" | custom-call | flops 6442450944 | bytes 20971520 | tf_op jit(solution)/shard_map/feed_up/pallas_call | solution.py:532
  192.9 5.2 %collective-permute-done.23 = bf16[256,2048]{1,0:T(8,128)(2,1)S(1)} collective-permute-done((bf16[256,2048]{1,0:T(8,128)(2,1)S(1)}, bf16[256,2048]{1,0:T(8,128)(2,1)S(1)}, u32[]{:S(2)}, u32[]{:S(2)}) %collective-permute-start.23) | collective-permute-done | bytes 1048608 | tf_op jit(solution)/shard_map/ppermute | solution.py:29
  198.2 4.4 pad_maximum_fusion.3.top_b
  202.8 2.1 pad_maximum_fusion.2.top_a
  205.0 3.2 fusion.15
  208.7 1.8 fusion.12
  210.7 10.0 %feed_slope.1.upward = bf16[2,768,2048]{2,1,0:T(8,128)(2,1)S(1)} custom-call(bf16[768,1024]{1,0:T(8,128)(2,1)S(1)} %copy-done.17, bf16[512,2048]{1,0:T(8,128)(2,1)S(1)} %pad_maximum_fusion.2.top_a, bf16[512,2048]{1,0:T(8,128)(2,1)S(1)} %collective-permute-done.25.bottom_a, bf16[512,2048]{1,0:T(8,128)(2,1)S(1)} %pad_maximum_fusion.3.top_b, ...), custom_call_target="tpu_custom_call" | custom-call | flops 6442450944 | bytes 20971520 | tf_op jit(solution)/shard_map/feed_slope/pallas_call | solution.py:621
  220.7 2.0 convert_add_fusion.2
  224.0 1.9 convert_add_fusion.3
  227.2 3.2 convolution_convert_fusion.2
  230.9 3.2 convolution_convert_fusion.3
  235.0 1.9 slice.490
  237.5 4.5 convert_add_fusion
  243.7 1.9 convert_add_fusion.1
  246.7 2.4 copy-done.31
  249.7 14.2 %feed_back.1 = (f32[768,1024]{1,0:T(8,128)S(1)}, bf16[768,1024]{1,0:T(8,128)(2,1)S(1)}, f32[16,1024]{1,0:T(8,128)S(1)}) custom-call(bf16[2,768,2048]{2,1,0:T(8,128)(2,1)S(1)} %bitcast.222, bf16[512,2048]{1,0:T(8,128)(2,1)S(1)} %copy-done.29, bf16[512,2048]{1,0:T(8,128)(2,1)S(1)} %copy-done.37, bf16[512,2048]{1,0:T(8,128)(2,1)S(1)} %copy-done.11, ...), custom_call_target="tpu_custom_call" | custom-call | flops 6442450944 | bytes 25690112 | tf_op jit(solution)/shard_map/feed_back/pallas_call | solution.py:678
  267.2 1.7 collective-permute-start.37
  269.1 4.7 collective-permute-start.32
  275.1 12.9 %feed_down.1 = f32[768,1024]{1,0:T(8,128)} custom-call(s32[8]{0:T(128)S(1)} %broadcast_xor_fusion.table_ref, bf16[2,768,2048]{2,1,0:T(8,128)(2,1)S(1)} %bitcast.220, bf16[512,2048]{1,0:T(8,128)(2,1)S(1)} %copy-done.15, bf16[512,2048]{1,0:T(8,128)(2,1)S(1)} %copy-done.39, bf16[512,2048]{1,0:T(8,128)(2,1)S(1)} %copy-done.13, bf16[512,2048]{1,0:T(8,128)(2,1)S(1)} %copy-done.35, ...), custom_call_target="tpu_custom_call" | custom-call | flops 6442450944 | bytes 20971520 | tf_op jit(solution)/shard_map/feed_down/pallas_call | solution.py:584
  288.2 1.9 collective-permute-done.32.before
  290.1 4.2 collective-permute-done.33.after
  305.7 1.6 copy-done.9
  312.1 35.7 %attention_backward.1 = (bf16[2,768,1536]{2,1,0:T(8,128)(2,1)}, f32[768,1024]{1,0:T(8,128)S(1)}) custom-call(bf16[3,128,1024]{2,1,0:T(8,128)(2,1)S(1)} %copy-done.45, bf16[3,256,1024]{2,1,0:T(8,128)(2,1)S(1)} %bitcast.228, bf16[3,128,1024]{2,1,0:T(8,128)(2,1)S(1)} %copy-done.47, bf16[512,2048]{1,0:T(8,128)(2,1)} %constant_dynamic-update-slice_fusion.5.top_a, ...), custom_call_target="tpu_custom_call" | custom-call | flops 14495514624 | bytes 36700160 | tf_op jit(solution)/shard_map/attention_backward/pallas_call | solution.py:743
  349.3 2.4 slice.505
  352.2 2.0 slice.516
  359.4 2.6 convolution_convert_fusion
  362.0 2.7 convolution_convert_fusion.1
  366.4 1.6 collective-permute-start.43
  369.7 12.7 %collective-permute-done.39 = bf16[128,2560]{1,0:T(8,128)(2,1)} collective-permute-done((bf16[128,2560]{1,0:T(8,128)(2,1)}, bf16[128,2560]{1,0:T(8,128)(2,1)}, u32[]{:S(2)}, u32[]{:S(2)}) %collective-permute-start.39) | collective-permute-done | bytes 655392 | tf_op jit(solution)/shard_map/ppermute | solution.py:29
  386.7 3.7 convolution_add_fusion
  392.7 3.0 convolution_add_fusion.1
  397.7 1.6 collective-permute-start.44
  401.2 3.6 collective-permute-start.48
  404.8 5.7 %leave.1 = (f32[768,1024]{1,0:T(8,128)}, f32[16,1024]{1,0:T(8,128)S(1)}) custom-call(s32[8]{0:T(128)S(1)} %broadcast_xor_fusion.table_ref, f32[768,1024]{1,0:T(8,128)S(1)} %copy-done.7, f32[768,1024]{1,0:T(8,128)S(1)} %copy-done.5, f32[768,1024]{1,0:T(8,128)S(1)} %get-tuple-element.116.grad_resid, f32[4,1024]{1,0:T(4,128)S(1)} %convert_bitcast_fusion.small), custom_call_target="tpu_custom_call" | custom-call | flops 23592960 | bytes 12582912 | tf_op jit(solution)/shard_map/leave/pallas_call | solution.py:796
  410.6 5.1 %collective-permute-done.50 = bf16[256,1536]{1,0:T(8,128)(2,1)} collective-permute-done((bf16[256,1536]{1,0:T(8,128)(2,1)}, bf16[256,1536]{1,0:T(8,128)(2,1)}, u32[]{:S(2)}, u32[]{:S(2)}) %collective-permute-start.50) | collective-permute-done | bytes 786464 | tf_op jit(solution)/shard_map/ppermute | solution.py:29
  415.7 1.9 bitcast_add_fusion.2
  422.3 2.2 collective-permute-done.55
  428.5 2.2 fusion.73
  431.9 3.0 collective-permute-start.58
  435.9 1.7 collective-permute-start.49
  437.6 2.3 collective-permute-done.51
  440.1 4.3 collective-permute-start.52
  444.4 3.4 collective-permute-start.53
  448.4 8.8 %collective-permute-done.52 = bf16[128,1024]{1,0:T(8,128)(2,1)S(1)} collective-permute-done((bf16[128,1024]{1,0:T(8,128)(2,1)S(1)}, bf16[128,1024]{1,0:T(8,128)(2,1)S(1)}, u32[]{:S(2)}, u32[]{:S(2)}) %collective-permute-start.52) | collective-permute-done | bytes 262176 | tf_op jit(solution)/shard_map/ppermute | solution.py:29
  (408 shorter events, 104.1 us)
Async XLA Ops:
  7.2 99.0 %all-gather.5.cloned.1.call-start = ((), (), s32[]{:S(2)}) async-start(), calls=%async_computation.2 | async-start | bytes 1310720 | tf_op jit(solution)/shard_map/all_gather | solution.py:834
  7.9 101.2 %all-gather.7.cloned.1.call-start = ((), (), s32[]{:S(2)}) async-start(), calls=%async_computation.3 | async-start | bytes 1310720 | tf_op jit(solution)/shard_map/all_gather | solution.py:834
  9.7 27.2 %collective-permute-start.10 = (bf16[128,1024]{1,0:T(8,128)(2,1)S(1)}, bf16[128,1024]{1,0:T(8,128)(2,1)S(1)}, u32[]{:S(2)}, u32[]{:S(2)}) collective-permute-start(bf16[128,1024]{1,0:T(8,128)(2,1)S(1)} %pad_maximum_fusion.22), channel_id=1, source_target_pairs={{0,1},{1,2},{2,3},{3,0},{4,5},{5,6},{6,7},{7,4},{8,9},{9,10},{10,1... | collective-permute-start | bytes 786440 | tf_op jit(solution)/shard_map/ppermute | solution.py:29
  12.8 30.2 %collective-permute-start.9 = (bf16[128,1024]{1,0:T(8,128)(2,1)S(1)}, bf16[128,1024]{1,0:T(8,128)(2,1)S(1)}, u32[]{:S(2)}, u32[]{:S(2)}) collective-permute-start(bf16[128,1024]{1,0:T(8,128)(2,1)S(1)} %pad_maximum_fusion.22), channel_id=1, source_target_pairs={{0,2},{1,3},{2,0},{3,1},{4,6},{5,7},{6,4},{7,5},{8,10},{9,11},{10,... | collective-permute-start | bytes 786440 | tf_op jit(solution)/shard_map/ppermute | solution.py:29
  15.4 42.8 %collective-permute-start.5 = (bf16[128,1024]{1,0:T(8,128)(2,1)S(1)}, bf16[128,1024]{1,0:T(8,128)(2,1)S(1)}, u32[]{:S(2)}, u32[]{:S(2)}) collective-permute-start(bf16[128,1024]{1,0:T(8,128)(2,1)S(1)} %pad_maximum_fusion.22), channel_id=1, source_target_pairs={{0,3},{1,0},{2,1},{3,2},{4,7},{5,4},{6,5},{7,6},{8,11},{9,8},{10,9... | collective-permute-start | bytes 786440 | tf_op jit(solution)/shard_map/ppermute | solution.py:29
  17.4 4.1 collective-permute-start
  19.0 439.9 %reduce-scatter.2.cloned.1.call-start = ((), (), s32[]{:S(2)}) async-start(), calls=%async_computation.1 | async-start | bytes 2621440 | tf_op jit(solution)/shard_map/reduce_scatter | solution.py:239
  21.6 3.7 collective-permute-start.1
  25.2 1.2 collective-permute-start.2
  43.1 16.7 %collective-permute-start.11 = (bf16[128,2048]{1,0:T(8,128)(2,1)S(1)}, bf16[128,2048]{1,0:T(8,128)(2,1)S(1)}, u32[]{:S(2)}, u32[]{:S(2)}) collective-permute-start(bf16[128,2048]{1,0:T(8,128)(2,1)S(1)} %pad_maximum_fusion.16), channel_id=1, source_target_pairs={{0,16},{4,20},{8,24},{12,28},{16,0},{20,4},{24,8},{28,12},{1,17},{... | collective-permute-start | bytes 1572872 | tf_op jit(solution)/shard_map/ppermute | solution.py:29
  46.1 33.0 %collective-permute-start.3 = (bf16[3,128,1024]{2,1,0:T(8,128)(2,1)S(1)}, bf16[3,128,1024]{2,1,0:T(8,128)(2,1)S(1)}, u32[]{:S(2)}, u32[]{:S(2)}) collective-permute-start(bf16[3,128,1024]{2,1,0:T(8,128)(2,1)S(1)} %get-tuple-element.134), channel_id=1, source_target_pairs={{0,1},{1,2},{2,3},{4,5},{5,6},{6,7},{8,9},{9,10},{10,11},{12,13},{... | collective-permute-start | bytes 2359304 | tf_op jit(solution)/shard_map/ppermute | solution.py:29
  56.9 33.3 %collective-permute-start.4 = (bf16[3,128,1024]{2,1,0:T(8,128)(2,1)S(1)}, bf16[3,128,1024]{2,1,0:T(8,128)(2,1)S(1)}, u32[]{:S(2)}, u32[]{:S(2)}) collective-permute-start(bf16[3,128,1024]{2,1,0:T(8,128)(2,1)S(1)} %get-tuple-element.133), channel_id=1, source_target_pairs={{1,0},{2,1},{3,2},{5,4},{6,5},{7,6},{9,8},{10,9},{11,10},{13,12},{... | collective-permute-start | bytes 2359304 | tf_op jit(solution)/shard_map/ppermute | solution.py:29
  58.3 14.9 %collective-permute-start.6 = (bf16[128,2048]{1,0:T(8,128)(2,1)S(1)}, bf16[128,2048]{1,0:T(8,128)(2,1)S(1)}, u32[]{:S(2)}, u32[]{:S(2)}) collective-permute-start(bf16[128,2048]{1,0:T(8,128)(2,1)S(1)} %constant_dynamic-update-slice_fusion), channel_id=1, source_target_pairs={{0,8},{4,12},{8,0},{12,4},{16,24},{20,28},{24,16},{28,20},{1,9},{5... | collective-permute-start | bytes 1572872 | tf_op jit(solution)/shard_map/ppermute | solution.py:29
  60.0 31.5 %collective-permute-start.12 = (bf16[256,2048]{1,0:T(8,128)(2,1)S(1)}, bf16[256,2048]{1,0:T(8,128)(2,1)S(1)}, u32[]{:S(2)}, u32[]{:S(2)}) collective-permute-start(bf16[256,2048]{1,0:T(8,128)(2,1)S(1)} %pad_maximum_fusion.9), channel_id=1, source_target_pairs={{0,8},{4,12},{8,0},{12,4},{16,24},{20,28},{24,16},{28,20},{1,9},{5... | collective-permute-start | bytes 3145736 | tf_op jit(solution)/shard_map/ppermute | solution.py:29
  90.2 14.8 %collective-permute-start.7 = (bf16[256,2048]{1,0:T(8,128)(2,1)S(1)}, bf16[256,2048]{1,0:T(8,128)(2,1)S(1)}, u32[]{:S(2)}, u32[]{:S(2)}) collective-permute-start(bf16[256,2048]{1,0:T(8,128)(2,1)S(1)} %pad_maximum_fusion.8), channel_id=1, source_target_pairs={{0,16},{4,20},{8,24},{12,28},{16,0},{20,4},{24,8},{28,12},{1,17},{... | collective-permute-start | bytes 3145736 | tf_op jit(solution)/shard_map/ppermute | solution.py:29
  91.7 36.5 %collective-permute-start.13 = (bf16[512,2048]{1,0:T(8,128)(2,1)S(1)}, bf16[512,2048]{1,0:T(8,128)(2,1)}, u32[]{:S(2)}, u32[]{:S(2)}) collective-permute-start(bf16[512,2048]{1,0:T(8,128)(2,1)S(1)} %pad_maximum_fusion.top_b), channel_id=1, source_target_pairs={{0,4},{4,0},{8,12},{12,8},{16,20},{20,16},{24,28},{28,24},{1,5},{5... | collective-permute-start | bytes 6291464 | tf_op jit(solution)/shard_map/ppermute | solution.py:29
  106.2 24.0 %collective-permute-start.8 = (bf16[512,2048]{1,0:T(8,128)(2,1)}, bf16[512,2048]{1,0:T(8,128)(2,1)}, u32[]{:S(2)}, u32[]{:S(2)}) collective-permute-start(bf16[512,2048]{1,0:T(8,128)(2,1)} %constant_dynamic-update-slice_fusion.5.top_a), channel_id=1, source_target_pairs={{0,4},{4,0},{8,12},{12,8},{16,20},{20,16},{24,28},{28,24},{1,5},{5... | collective-permute-start | bytes 6291464 | tf_op jit(solution)/shard_map/ppermute | solution.py:29
  107.5 14.9 %collective-permute-start.14 = (bf16[128,2048]{1,0:T(8,128)(2,1)S(1)}, bf16[128,2048]{1,0:T(8,128)(2,1)}, u32[]{:S(2)}, u32[]{:S(2)}) collective-permute-start(bf16[128,2048]{1,0:T(8,128)(2,1)S(1)} %get-tuple-element.75), channel_id=1, source_target_pairs={{0,8},{4,12},{8,0},{12,4},{16,24},{20,28},{24,16},{28,20},{1,9},{5... | collective-permute-start | bytes 1572872 | tf_op jit(solution)/shard_map/ppermute | solution.py:29
  109.1 14.2 %collective-permute-start.15 = (bf16[128,2048]{1,0:T(8,128)(2,1)S(1)}, bf16[128,2048]{1,0:T(8,128)(2,1)}, u32[]{:S(2)}, u32[]{:S(2)}) collective-permute-start(bf16[128,2048]{1,0:T(8,128)(2,1)S(1)} %get-tuple-element.76), channel_id=1, source_target_pairs={{0,16},{4,20},{8,24},{12,28},{16,0},{20,4},{24,8},{28,12},{1,17},{... | collective-permute-start | bytes 1572872 | tf_op jit(solution)/shard_map/ppermute | solution.py:29
  111.3 56.5 %collective-permute-start.16 = (bf16[128,2048]{1,0:T(8,128)(2,1)}, bf16[128,2048]{1,0:T(8,128)(2,1)}, u32[]{:S(2)}, u32[]{:S(2)}) collective-permute-start(bf16[128,2048]{1,0:T(8,128)(2,1)} %pad_maximum_fusion.19), channel_id=1, source_target_pairs={{0,8},{4,12},{8,0},{12,4},{16,24},{20,28},{24,16},{28,20},{1,9},{5... | collective-permute-start | bytes 1572872 | tf_op jit(solution)/shard_map/ppermute | solution.py:29
  122.4 45.4 %collective-permute-start.17 = (bf16[128,2048]{1,0:T(8,128)(2,1)}, bf16[128,2048]{1,0:T(8,128)(2,1)}, u32[]{:S(2)}, u32[]{:S(2)}) collective-permute-start(bf16[128,2048]{1,0:T(8,128)(2,1)} %pad_maximum_fusion.20), channel_id=1, source_target_pairs={{0,16},{4,20},{8,24},{12,28},{16,0},{20,4},{24,8},{28,12},{1,17},{... | collective-permute-start | bytes 1572872 | tf_op jit(solution)/shard_map/ppermute | solution.py:29
  125.0 42.7 %collective-permute-start.20 = (bf16[256,2048]{1,0:T(8,128)(2,1)S(1)}, bf16[256,2048]{1,0:T(8,128)(2,1)S(1)}, u32[]{:S(2)}, u32[]{:S(2)}) collective-permute-start(bf16[256,2048]{1,0:T(8,128)(2,1)S(1)} %pad_maximum_fusion.11), channel_id=1, source_target_pairs={{0,8},{4,12},{8,0},{12,4},{16,24},{20,28},{24,16},{28,20},{1,9},{5... | collective-permute-start | bytes 3145736 | tf_op jit(solution)/shard_map/ppermute | solution.py:29
  128.3 42.4 %collective-permute-start.18 = (bf16[256,2048]{1,0:T(8,128)(2,1)S(1)}, bf16[256,2048]{1,0:T(8,128)(2,1)S(1)}, u32[]{:S(2)}, u32[]{:S(2)}) collective-permute-start(bf16[256,2048]{1,0:T(8,128)(2,1)S(1)} %pad_maximum_fusion.10), channel_id=1, source_target_pairs={{0,16},{4,20},{8,24},{12,28},{16,0},{20,4},{24,8},{28,12},{1,17},{... | collective-permute-start | bytes 3145736 | tf_op jit(solution)/shard_map/ppermute | solution.py:29
  167.8 63.2 %copy-start.18 = (bf16[768,1024]{1,0:T(8,128)(2,1)}, bf16[768,1024]{1,0:T(8,128)(2,1)S(1)}, u32[]{:S(2)}) copy-start(bf16[768,1024]{1,0:T(8,128)(2,1)S(1)} %get-tuple-element.93.inputs) | copy-start | bytes 4718596
  170.6 5.6 %collective-permute-start.21 = (bf16[512,2048]{1,0:T(8,128)(2,1)S(1)}, bf16[512,2048]{1,0:T(8,128)(2,1)S(1)}, u32[]{:S(2)}, u32[]{:S(2)}) collective-permute-start(bf16[512,2048]{1,0:T(8,128)(2,1)S(1)} %pad_maximum_fusion.1.top_b), channel_id=1, source_target_pairs={{0,4},{4,0},{8,12},{12,8},{16,20},{20,16},{24,28},{28,24},{1,5},{5... | collective-permute-start | bytes 6291464 | tf_op jit(solution)/shard_map/ppermute | solution.py:29
  170.8 7.0 %collective-permute-start.19 = (bf16[512,2048]{1,0:T(8,128)(2,1)S(1)}, bf16[512,2048]{1,0:T(8,128)(2,1)S(1)}, u32[]{:S(2)}, u32[]{:S(2)}) collective-permute-start(bf16[512,2048]{1,0:T(8,128)(2,1)S(1)} %constant_dynamic-update-slice_fusion.7.top_a), channel_id=1, source_target_pairs={{0,4},{4,0},{8,12},{12,8},{16,20},{20,16},{24,28},{28,24},{1,5},{5... | collective-permute-start | bytes 6291464 | tf_op jit(solution)/shard_map/ppermute | solution.py:29
  173.5 24.6 %collective-permute-start.23 = (bf16[256,2048]{1,0:T(8,128)(2,1)S(1)}, bf16[256,2048]{1,0:T(8,128)(2,1)S(1)}, u32[]{:S(2)}, u32[]{:S(2)}) collective-permute-start(bf16[256,2048]{1,0:T(8,128)(2,1)S(1)} %pad_maximum_fusion.13), channel_id=1, source_target_pairs={{0,8},{4,12},{8,0},{12,4},{16,24},{20,28},{24,16},{28,20},{1,9},{5... | collective-permute-start | bytes 3145736 | tf_op jit(solution)/shard_map/ppermute | solution.py:29
  175.6 27.1 %collective-permute-start.22 = (bf16[256,2048]{1,0:T(8,128)(2,1)S(1)}, bf16[256,2048]{1,0:T(8,128)(2,1)S(1)}, u32[]{:S(2)}, u32[]{:S(2)}) collective-permute-start(bf16[256,2048]{1,0:T(8,128)(2,1)S(1)} %pad_maximum_fusion.12), channel_id=1, source_target_pairs={{0,16},{4,20},{8,24},{12,28},{16,0},{20,4},{24,8},{28,12},{1,17},{... | collective-permute-start | bytes 3145736 | tf_op jit(solution)/shard_map/ppermute | solution.py:29
  202.7 7.9 %collective-permute-start.26 = (bf16[512,2048]{1,0:T(8,128)(2,1)S(1)}, bf16[512,2048]{1,0:T(8,128)(2,1)S(1)}, u32[]{:S(2)}, u32[]{:S(2)}) collective-permute-start(bf16[512,2048]{1,0:T(8,128)(2,1)S(1)} %pad_maximum_fusion.3.top_b), channel_id=1, source_target_pairs={{0,4},{4,0},{8,12},{12,8},{16,20},{20,16},{24,28},{28,24},{1,5},{5... | collective-permute-start | bytes 6291464 | tf_op jit(solution)/shard_map/ppermute | solution.py:29
  204.9 5.7 %collective-permute-start.25 = (bf16[512,2048]{1,0:T(8,128)(2,1)S(1)}, bf16[512,2048]{1,0:T(8,128)(2,1)S(1)}, u32[]{:S(2)}, u32[]{:S(2)}) collective-permute-start(bf16[512,2048]{1,0:T(8,128)(2,1)S(1)} %pad_maximum_fusion.2.top_a), channel_id=1, source_target_pairs={{0,4},{4,0},{8,12},{12,8},{16,20},{20,16},{24,28},{28,24},{1,5},{5... | collective-permute-start | bytes 6291464 | tf_op jit(solution)/shard_map/ppermute | solution.py:29
  208.2 12.5 %collective-permute-start.28 = (bf16[512,2048]{1,0:T(8,128)(2,1)}, bf16[512,2048]{1,0:T(8,128)(2,1)S(1)}, u32[]{:S(2)}, u32[]{:S(2)}) collective-permute-start(bf16[512,2048]{1,0:T(8,128)(2,1)} %fusion.15), channel_id=1, source_target_pairs={{0,4},{4,0},{8,12},{12,8},{16,20},{20,16},{24,28},{28,24},{1,5},{5... | collective-permute-start | bytes 6291464 | tf_op jit(solution)/shard_map/ppermute | solution.py:29
  210.5 13.5 %collective-permute-start.24 = (bf16[512,2048]{1,0:T(8,128)(2,1)S(1)}, bf16[512,2048]{1,0:T(8,128)(2,1)S(1)}, u32[]{:S(2)}, u32[]{:S(2)}) collective-permute-start(bf16[512,2048]{1,0:T(8,128)(2,1)S(1)} %fusion.12), channel_id=1, source_target_pairs={{0,4},{4,0},{8,12},{12,8},{16,20},{20,16},{24,28},{28,24},{1,5},{5... | collective-permute-start | bytes 6291464 | tf_op jit(solution)/shard_map/ppermute | solution.py:29
  230.4 7.0 %collective-permute-start.30 = (bf16[512,2048]{1,0:T(8,128)(2,1)}, bf16[512,2048]{1,0:T(8,128)(2,1)}, u32[]{:S(2)}, u32[]{:S(2)}) collective-permute-start(bf16[512,2048]{1,0:T(8,128)(2,1)} %convolution_convert_fusion.2), channel_id=1, source_target_pairs={{0,4},{4,0},{8,12},{12,8},{16,20},{20,16},{24,28},{28,24},{1,5},{5... | collective-permute-start | bytes 6291464 | tf_op jit(solution)/shard_map/ppermute | solution.py:29
  234.1 9.5 %collective-permute-start.29 = (bf16[512,2048]{1,0:T(8,128)(2,1)}, bf16[512,2048]{1,0:T(8,128)(2,1)S(1)}, u32[]{:S(2)}, u32[]{:S(2)}) collective-permute-start(bf16[512,2048]{1,0:T(8,128)(2,1)} %convolution_convert_fusion.3), channel_id=1, source_target_pairs={{0,4},{4,0},{8,12},{12,8},{16,20},{20,16},{24,28},{28,24},{1,5},{5... | collective-permute-start | bytes 6291464 | tf_op jit(solution)/shard_map/ppermute | solution.py:29
  234.2 29.8 %collective-permute-start.31 = (bf16[256,2048]{1,0:T(8,128)(2,1)}, bf16[256,2048]{1,0:T(8,128)(2,1)S(1)}, u32[]{:S(2)}, u32[]{:S(2)}) collective-permute-start(bf16[256,2048]{1,0:T(8,128)(2,1)} %bitcast.15), channel_id=1, source_target_pairs={{0,8},{4,12},{8,0},{12,4},{16,24},{20,28},{24,16},{28,20},{1,9},{5... | collective-permute-start | bytes 3145736 | tf_op jit(solution)/shard_map/ppermute | solution.py:29
  236.9 28.8 %collective-permute-start.27 = (bf16[256,2048]{1,0:T(8,128)(2,1)}, bf16[256,2048]{1,0:T(8,128)(2,1)S(1)}, u32[]{:S(2)}, u32[]{:S(2)}) collective-permute-start(bf16[256,2048]{1,0:T(8,128)(2,1)} %fusion.33), channel_id=1, source_target_pairs={{0,16},{4,20},{8,24},{12,28},{16,0},{20,4},{24,8},{28,12},{1,17},{... | collective-permute-start | bytes 3145736 | tf_op jit(solution)/shard_map/ppermute | solution.py:29
  245.6 42.5 %copy-start.52 = (f32[512,2048]{1,0:T(8,128)}, f32[512,2048]{1,0:T(8,128)S(1)}, u32[]{:S(2)}) copy-start(f32[512,2048]{1,0:T(8,128)S(1)} %convert_add_fusion.1) | copy-start | bytes 12582916
  266.2 22.0 %collective-permute-start.36 = (bf16[128,2048]{1,0:T(8,128)(2,1)S(1)}, bf16[128,2048]{1,0:T(8,128)(2,1)S(1)}, u32[]{:S(2)}, u32[]{:S(2)}) collective-permute-start(bf16[128,2048]{1,0:T(8,128)(2,1)S(1)} %fusion.67), channel_id=1, source_target_pairs={{0,8},{4,12},{8,0},{12,4},{16,24},{20,28},{24,16},{28,20},{1,9},{5... | collective-permute-start | bytes 1572872 | tf_op jit(solution)/shard_map/ppermute | solution.py:29
  267.2 30.1 %collective-permute-start.37 = (bf16[128,2048]{1,0:T(8,128)(2,1)S(1)}, bf16[128,2048]{1,0:T(8,128)(2,1)S(1)}, u32[]{:S(2)}, u32[]{:S(2)}) collective-permute-start(bf16[128,2048]{1,0:T(8,128)(2,1)S(1)} %fusion.68), channel_id=1, source_target_pairs={{0,16},{4,20},{8,24},{12,28},{16,0},{20,4},{24,8},{28,12},{1,17},{... | collective-permute-start | bytes 1572872 | tf_op jit(solution)/shard_map/ppermute | solution.py:29
  269.1 21.0 %collective-permute-start.32 = (bf16[3,128,1024]{2,1,0:T(8,128)(2,1)S(1)}, bf16[3,128,1024]{2,1,0:T(8,128)(2,1)S(1)}, u32[]{:S(2)}, u32[]{:S(2)}) collective-permute-start(bf16[3,128,1024]{2,1,0:T(8,128)(2,1)S(1)} %get-tuple-element.132), channel_id=1, source_target_pairs={{0,1},{1,2},{2,3},{4,5},{5,6},{6,7},{8,9},{9,10},{10,11},{12,13},{... | collective-permute-start | bytes 2359304 | tf_op jit(solution)/shard_map/ppermute | solution.py:29
  273.7 20.6 %collective-permute-start.33 = (bf16[3,128,1024]{2,1,0:T(8,128)(2,1)S(1)}, bf16[3,128,1024]{2,1,0:T(8,128)(2,1)S(1)}, u32[]{:S(2)}, u32[]{:S(2)}) collective-permute-start(bf16[3,128,1024]{2,1,0:T(8,128)(2,1)S(1)} %get-tuple-element.131), channel_id=1, source_target_pairs={{1,0},{2,1},{3,2},{5,4},{6,5},{7,6},{9,8},{10,9},{11,10},{13,12},{... | collective-permute-start | bytes 2359304 | tf_op jit(solution)/shard_map/ppermute | solution.py:29
  294.9 2.4 collective-permute-start.35
  295.7 2.5 collective-permute-start.34
  301.0 46.9 %collective-permute-start.38 = (bf16[256,2560]{1,0:T(8,128)(2,1)}, bf16[256,2560]{1,0:T(8,128)(2,1)}, u32[]{:S(2)}, u32[]{:S(2)}) collective-permute-start(bf16[256,2560]{1,0:T(8,128)(2,1)} %pad_maximum_fusion.6), channel_id=1, source_target_pairs={{0,16},{4,20},{8,24},{12,28},{16,0},{20,4},{24,8},{28,12},{1,17},{... | collective-permute-start | bytes 3932168 | tf_op jit(solution)/shard_map/ppermute | solution.py:29
  302.6 49.6 %collective-permute-start.40 = (bf16[256,2560]{1,0:T(8,128)(2,1)}, bf16[256,2560]{1,0:T(8,128)(2,1)}, u32[]{:S(2)}, u32[]{:S(2)}) collective-permute-start(bf16[256,2560]{1,0:T(8,128)(2,1)} %pad_maximum_fusion.7), channel_id=1, source_target_pairs={{0,8},{4,12},{8,0},{12,4},{16,24},{20,28},{24,16},{28,20},{1,9},{5... | collective-permute-start | bytes 3932168 | tf_op jit(solution)/shard_map/ppermute | solution.py:29
  362.0 24.7 %collective-permute-start.42 = (bf16[512,1536]{1,0:T(8,128)(2,1)}, bf16[512,1536]{1,0:T(8,128)(2,1)}, u32[]{:S(2)}, u32[]{:S(2)}) collective-permute-start(bf16[512,1536]{1,0:T(8,128)(2,1)} %convolution_convert_fusion), channel_id=1, source_target_pairs={{0,4},{4,0},{8,12},{12,8},{16,20},{20,16},{24,28},{28,24},{1,5},{5... | collective-permute-start | bytes 4718600 | tf_op jit(solution)/shard_map/ppermute | solution.py:29
  364.7 28.0 %collective-permute-start.41 = (bf16[512,1536]{1,0:T(8,128)(2,1)}, bf16[512,1536]{1,0:T(8,128)(2,1)}, u32[]{:S(2)}, u32[]{:S(2)}) collective-permute-start(bf16[512,1536]{1,0:T(8,128)(2,1)} %convolution_convert_fusion.1), channel_id=1, source_target_pairs={{0,4},{4,0},{8,12},{12,8},{16,20},{20,16},{24,28},{28,24},{1,5},{5... | collective-permute-start | bytes 4718600 | tf_op jit(solution)/shard_map/ppermute | solution.py:29
  365.3 17.0 %collective-permute-start.39 = (bf16[128,2560]{1,0:T(8,128)(2,1)}, bf16[128,2560]{1,0:T(8,128)(2,1)}, u32[]{:S(2)}, u32[]{:S(2)}) collective-permute-start(bf16[128,2560]{1,0:T(8,128)(2,1)} %pad_maximum_fusion.14), channel_id=1, source_target_pairs={{0,8},{4,12},{8,0},{12,4},{16,24},{20,28},{24,16},{28,20},{1,9},{5... | collective-permute-start | bytes 1966088 | tf_op jit(solution)/shard_map/ppermute | solution.py:29
  366.4 18.0 %collective-permute-start.43 = (bf16[128,2560]{1,0:T(8,128)(2,1)}, bf16[128,2560]{1,0:T(8,128)(2,1)}, u32[]{:S(2)}, u32[]{:S(2)}) collective-permute-start(bf16[128,2560]{1,0:T(8,128)(2,1)} %pad_maximum_fusion.15), channel_id=1, source_target_pairs={{0,16},{4,20},{8,24},{12,28},{16,0},{20,4},{24,8},{28,12},{1,17},{... | collective-permute-start | bytes 1966088 | tf_op jit(solution)/shard_map/ppermute | solution.py:29
  396.8 18.9 %collective-permute-start.50 = (bf16[256,1536]{1,0:T(8,128)(2,1)}, bf16[256,1536]{1,0:T(8,128)(2,1)}, u32[]{:S(2)}, u32[]{:S(2)}) collective-permute-start(bf16[256,1536]{1,0:T(8,128)(2,1)} %bitcast.55), channel_id=1, source_target_pairs={{0,8},{4,12},{8,0},{12,4},{16,24},{20,28},{24,16},{28,20},{1,9},{5... | collective-permute-start | bytes 2359304 | tf_op jit(solution)/shard_map/ppermute | solution.py:29
  397.7 20.0 %collective-permute-start.44 = (bf16[256,1536]{1,0:T(8,128)(2,1)}, bf16[256,1536]{1,0:T(8,128)(2,1)}, u32[]{:S(2)}, u32[]{:S(2)}) collective-permute-start(bf16[256,1536]{1,0:T(8,128)(2,1)} %fusion.39), channel_id=1, source_target_pairs={{0,16},{4,20},{8,24},{12,28},{16,0},{20,4},{24,8},{28,12},{1,17},{... | collective-permute-start | bytes 2359304 | tf_op jit(solution)/shard_map/ppermute | solution.py:29
  401.0 27.5 %collective-permute-start.46 = (bf16[128,1024]{1,0:T(8,128)(2,1)}, bf16[128,1024]{1,0:T(8,128)(2,1)}, u32[]{:S(2)}, u32[]{:S(2)}) collective-permute-start(bf16[128,1024]{1,0:T(8,128)(2,1)} %get-tuple-element.130), channel_id=1, source_target_pairs={{0,1},{1,2},{2,3},{3,0},{4,5},{5,6},{6,7},{7,4},{8,9},{9,10},{10,1... | collective-permute-start | bytes 786440 | tf_op jit(solution)/shard_map/ppermute | solution.py:29
  401.2 27.3 %collective-permute-start.47 = (bf16[128,1024]{1,0:T(8,128)(2,1)}, bf16[128,1024]{1,0:T(8,128)(2,1)}, u32[]{:S(2)}, u32[]{:S(2)}) collective-permute-start(bf16[128,1024]{1,0:T(8,128)(2,1)} %get-tuple-element.129), channel_id=1, source_target_pairs={{0,2},{1,3},{2,0},{3,1},{4,6},{5,7},{6,4},{7,5},{8,10},{9,11},{10,... | collective-permute-start | bytes 786440 | tf_op jit(solution)/shard_map/ppermute | solution.py:29
  401.2 27.3 %collective-permute-start.48 = (bf16[128,1024]{1,0:T(8,128)(2,1)}, bf16[128,1024]{1,0:T(8,128)(2,1)}, u32[]{:S(2)}, u32[]{:S(2)}) collective-permute-start(bf16[128,1024]{1,0:T(8,128)(2,1)} %get-tuple-element.128), channel_id=1, source_target_pairs={{0,3},{1,0},{2,1},{3,2},{4,7},{5,4},{6,5},{7,6},{8,11},{9,8},{10,9... | collective-permute-start | bytes 786440 | tf_op jit(solution)/shard_map/ppermute | solution.py:29
  419.7 1.2 collective-permute-start.54
  420.9 3.6 collective-permute-start.55
  424.5 3.6 collective-permute-start.56
  425.5 10.2 %collective-permute-start.45 = (bf16[128,1536]{1,0:T(8,128)(2,1)S(1)}, bf16[128,1536]{1,0:T(8,128)(2,1)S(1)}, u32[]{:S(2)}, u32[]{:S(2)}) collective-permute-start(bf16[128,1536]{1,0:T(8,128)(2,1)S(1)} %fusion.74), channel_id=1, source_target_pairs={{0,8},{4,12},{8,0},{12,4},{16,24},{20,28},{24,16},{28,20},{1,9},{5... | collective-permute-start | bytes 1179656 | tf_op jit(solution)/shard_map/ppermute | solution.py:29
  428.1 3.8 collective-permute-start.57
  430.7 9.2 %collective-permute-start.51 = (bf16[128,1536]{1,0:T(8,128)(2,1)S(1)}, bf16[128,1536]{1,0:T(8,128)(2,1)S(1)}, u32[]{:S(2)}, u32[]{:S(2)}) collective-permute-start(bf16[128,1536]{1,0:T(8,128)(2,1)S(1)} %fusion.75), channel_id=1, source_target_pairs={{0,16},{4,20},{8,24},{12,28},{16,0},{20,4},{24,8},{28,12},{1,17},{... | collective-permute-start | bytes 1179656 | tf_op jit(solution)/shard_map/ppermute | solution.py:29
  431.9 15.9 %collective-permute-start.58 = (f32[128,4]{0,1:T(4,128)S(1)}, f32[128,4]{0,1:T(4,128)S(1)}, u32[]{:S(2)}, u32[]{:S(2)}) collective-permute-start(f32[128,4]{0,1:T(4,128)S(1)} %add.190), channel_id=1, source_target_pairs={{0,2},{1,3},{2,0},{3,1},{4,6},{5,7},{6,4},{7,5},{8,10},{9,11},{10,... | collective-permute-start | bytes 6152 | tf_op jit(solution)/shard_map/ppermute | solution.py:938
  435.9 12.5 %collective-permute-start.49 = (bf16[128,1024]{1,0:T(8,128)(2,1)S(1)}, bf16[128,1024]{1,0:T(8,128)(2,1)S(1)}, u32[]{:S(2)}, u32[]{:S(2)}) collective-permute-start(bf16[128,1024]{1,0:T(8,128)(2,1)S(1)} %pad_maximum_fusion.23), channel_id=1, source_target_pairs={{0,1},{1,2},{2,3},{3,0},{4,5},{5,6},{6,7},{7,4},{8,9},{9,10},{10,1... | collective-permute-start | bytes 786440 | tf_op jit(solution)/shard_map/ppermute | solution.py:29
  440.1 17.1 %collective-permute-start.52 = (bf16[128,1024]{1,0:T(8,128)(2,1)S(1)}, bf16[128,1024]{1,0:T(8,128)(2,1)S(1)}, u32[]{:S(2)}, u32[]{:S(2)}) collective-permute-start(bf16[128,1024]{1,0:T(8,128)(2,1)S(1)} %pad_maximum_fusion.24), channel_id=1, source_target_pairs={{0,2},{1,3},{2,0},{3,1},{4,6},{5,7},{6,4},{7,5},{8,10},{9,11},{10,... | collective-permute-start | bytes 786440 | tf_op jit(solution)/shard_map/ppermute | solution.py:29
  444.4 12.8 %collective-permute-start.53 = (bf16[128,1024]{1,0:T(8,128)(2,1)S(1)}, bf16[128,1024]{1,0:T(8,128)(2,1)S(1)}, u32[]{:S(2)}, u32[]{:S(2)}) collective-permute-start(bf16[128,1024]{1,0:T(8,128)(2,1)S(1)} %pad_maximum_fusion.25), channel_id=1, source_target_pairs={{0,3},{1,0},{2,1},{3,2},{4,7},{5,4},{6,5},{7,6},{8,11},{9,8},{10,9... | collective-permute-start | bytes 786440 | tf_op jit(solution)/shard_map/ppermute | solution.py:29
  (95 other events, 649.4 us)
Sparse Core Ops, SparseCore 0:
  9.6 43.2 all-gather.4
  54.5 37.1 all-gather.6
  369.8 48.0 reduce-scatter.1

commit v6 on v5

--- a/solution.py
+++ b/solution.py
@@ -165,16 +165,17 @@
             middle = left.shape[1] // 2
             sent = dot(left[:, middle:], rights[i], (0, 0)).astype(LOW)
             kept = dot(left[:, :middle], rights[i], (0, 0))
-            self.kept[i].append((kept, self.links.swap(sent, self.plan.major[0])))
+            self.kept[i].append((kept, self.links.swap(sent, self.plan.major[0]), 0))
             outs.append(sent)
         return outs
 
     def hold(self, i, tokens):
-        self.kept[i] = [(k, after(r, *tokens)) for k, r in self.kept[i]]
+        self.kept[i] = [(k, after(r, *tokens), at) for k, r, at in self.kept[i]]
 
     def add(self, i):
         self.kept[i] = [
-            k[0] + k[1].astype(jnp.float32) if isinstance(k, tuple) else k for k in self.kept[i]
+            k[0] + k[1][:, k[2] : k[2] + k[0].shape[1]].astype(jnp.float32) if isinstance(k, tuple) else k
+            for k in self.kept[i]
         ]
         return self.kept[i]
 
@@ -189,7 +190,7 @@
         received = self.links.swap(after(out, *tokens), bit)
         self.kept[i], at = [], 0
         for x in stay:
-            self.kept[i].append((x, received[:, at : at + x.shape[1]]))
+            self.kept[i].append((x, received, at))
             at += x.shape[1]
         self.remain[i].remove(bit)
         return out
@@ -913,16 +914,16 @@
         grad_qkv = Scatter(plan, links, [(left, [projected[0], projected[1]])])
         grad_qkv.core(0)
         grad_qkv.core(1)
-        tokens = [grad_qkv.steps_but_last(i) for i in range(2)]
+        tokens += [grad_qkv.steps_but_last(i) for i in range(2)]
+        latents_grad, sums_one = leave_norm(
+            table, blocked, after(norm_one, *tokens), entered, grad_resid, small
+        )
         for i in range(2):
-            grad_up.hold(i, tokens)
+            grad_up.hold(i, [latents_grad])
         up_rows, out_rows = grad_up.rows()
         (grad_up,), outs = shift_blocks(plan, links, [own_first(up_rows)])
-        latents_grad, sums_one = leave_norm(
-            table, blocked, after(norm_one, *outs), entered, grad_resid, small
-        )
         for i in range(2):
-            grad_qkv.hold(i, [latents_grad])
+            grad_qkv.hold(i, outs)
         tokens = [grad_qkv.step(i) for i in range(2)]
         qkv_rows = grad_qkv.rows()[0]
         (grad_qkv, grad_out), outs = shift_blocks(

time: 473 us -> 469 us (level)
  local copies, waits for them, and re-layouts: 64.3 us -> 52.3 us
  other arithmetic: 34 us -> 42.7 us
    slice x8 -> x0, local copies, waits for them, and re-layouts: 11.4 us -> none  [step(): self.kept[i].append((x, received[:, at:at + x.shape[1]]))]
    add x14, other arithmetic: 6.35 us -> 15.4 us  [add(): k[0] + k[1][:, k[2]:k[2] + k[0].shape[1]].astype(jnp.float32)]
    unnamed x202 -> x198, local copies, waits for them, and re-layouts: 33.3 us -> 34 us
  transfers between devices with their start and end apart: 62 -> 62, of which waited for: 21 -> 19; matrix products, arithmetic and copies ran while one was open for 20% -> 19% of each run, Pallas kernels for 29% -> 29%
where the time goes in v6:
time: 469 us; the launch traced here: 462 us
  Pallas kernels  133 us (28%)
  waiting for transfers between devices  106 us (23%)
  starting transfers between devices  74.4 us (16%)
  local copies, waits for them, and re-layouts  52.3 us (11%)
  other arithmetic  42.7 us (9%)
  matrix products  37.4 us (8%)
  between operations  15.7 us (3%)
    ppermute x57, waiting for transfers between devices, send(): result = lax.ppermute(value, axis, pairs)  106 us
    ppermute x57, starting transfers between devices, send(): result = lax.ppermute(value, axis, pairs)  69.2 us
    dot_general x16, matrix products, dot(): lax.dot_general(left, right, ((dims[:1], dims[1:]), ((), ())), preferred_...  37.4 us
    pallas_call x1, Pallas kernels, forward_block(): pl.pallas_call(forward_kernel(rows, steps, g // HEAD_DIM, factor), name='...  35.9 us
    pallas_call x1, Pallas kernels, backward_block(): pl.pallas_call(backward_kernel(rows, steps, g // HEAD_DIM, factor), name=...  35.8 us
    unnamed x198, local copies, waits for them, and re-layouts  34 us
    add x14, other arithmetic, add(): k[0] + k[1][:, k[2]:k[2] + k[0].shape[1]].astype(jnp.float32)  15.4 us
    pallas_call x1, Pallas kernels, feed_up(): pl.pallas_call(up_kernel(count), name='feed_up', grid=(ff // tile,), in_s...  15 us
  transfers between devices with their start and end apart: 62, of which 19 were waited for; matrix products, arithmetic and copies ran while one was open for 19% of the time, Pallas kernels for 29%

profile of v6, /device:TPU:0, one launch (start us, length us, event | category | flops | bytes accessed | tf_op | source)
XLA Modules:
  0.0 462.4 jit_solution(5631353315652026970)
XLA Ops:
  9.7 3.1 collective-permute-start.10
  12.8 2.6 collective-permute-start.9
  21.6 1.6 collective-permute-start.1
  26.4 1.9 copy-done.2
  28.3 1.9 copy-done.3
  30.2 4.0 enter.1
  35.3 1.6 copy-done.30
  37.0 6.1 %collective-permute-done.9 = bf16[128,1024]{1,0:T(8,128)(2,1)S(1)} collective-permute-done((bf16[128,1024]{1,0:T(8,128)(2,1)S(1)}, bf16[128,1024]{1,0:T(8,128)(2,1)S(1)}, u32[]{:S(2)}, u32[]{:S(2)}) %collective-permute-start.9) | collective-permute-done | bytes 262176 | tf_op jit(solution)/shard_map/ppermute | solution.py:29
  43.1 1.6 collective-permute-start.11
  46.1 10.8 %collective-permute-start.3 = (bf16[3,128,1024]{2,1,0:T(8,128)(2,1)S(1)}, bf16[3,128,1024]{2,1,0:T(8,128)(2,1)S(1)}, u32[]{:S(2)}, u32[]{:S(2)}) collective-permute-start(bf16[3,128,1024]{2,1,0:T(8,128)(2,1)S(1)} %get-tuple-element.126), channel_id=1, source_target_pairs={{0,1},{1,2},{2,3},{4,5},{5,6},{6,7},{8,9},{9,10},{10,11},{12,13},{... | collective-permute-start | bytes 2359304 | tf_op jit(solution)/shard_map/ppermute | solution.py:29
  58.2 1.6 collective-permute-start.6
  60.6 12.6 %collective-permute-done.6 = bf16[128,2048]{1,0:T(8,128)(2,1)S(1)} collective-permute-done((bf16[128,2048]{1,0:T(8,128)(2,1)S(1)}, bf16[128,2048]{1,0:T(8,128)(2,1)S(1)}, u32[]{:S(2)}, u32[]{:S(2)}) %collective-permute-start.6) | collective-permute-done | bytes 524320 | tf_op jit(solution)/shard_map/ppermute | solution.py:29
  73.3 5.8 %collective-permute-done.3.before = bf16[3,128,1024]{2,1,0:T(8,128)(2,1)S(1)} collective-permute-done((bf16[3,128,1024]{2,1,0:T(8,128)(2,1)S(1)}, bf16[3,128,1024]{2,1,0:T(8,128)(2,1)S(1)}, u32[]{:S(2)}, u32[]{:S(2)}) %collective-permute-start.3) | collective-permute-done | bytes 786464 | tf_op jit(solution)/shard_map/ppermute | solution.py:29
  79.1 11.1 %collective-permute-done.4.after = bf16[3,128,1024]{2,1,0:T(8,128)(2,1)S(1)} collective-permute-done((bf16[3,128,1024]{2,1,0:T(8,128)(2,1)S(1)}, bf16[3,128,1024]{2,1,0:T(8,128)(2,1)S(1)}, u32[]{:S(2)}, u32[]{:S(2)}) %collective-permute-start.4) | collective-permute-done | bytes 786464 | tf_op jit(solution)/shard_map/ppermute | solution.py:29
  91.8 13.2 %collective-permute-done.7 = bf16[256,2048]{1,0:T(8,128)(2,1)S(1)} collective-permute-done((bf16[256,2048]{1,0:T(8,128)(2,1)S(1)}, bf16[256,2048]{1,0:T(8,128)(2,1)S(1)}, u32[]{:S(2)}, u32[]{:S(2)}) %collective-permute-start.7) | collective-permute-done | bytes 1048608 | tf_op jit(solution)/shard_map/ppermute | solution.py:29
  107.5 1.6 collective-permute-start.14
  113.4 8.9 %collective-permute-done.14 = bf16[128,2048]{1,0:T(8,128)(2,1)} collective-permute-done((bf16[128,2048]{1,0:T(8,128)(2,1)S(1)}, bf16[128,2048]{1,0:T(8,128)(2,1)}, u32[]{:S(2)}, u32[]{:S(2)}) %collective-permute-start.14) | collective-permute-done | bytes 524320 | tf_op jit(solution)/shard_map/ppermute | solution.py:29
  128.2 1.9 collective-permute-start.18
  130.2 35.9 %attention_forward.1 = (bf16[3,512,3072]{2,1,0:T(8,128)(2,1)}, bf16[2,768,512]{2,1,0:T(8,128)(2,1)S(1)}, f32[768,1024]{1,0:T(8,128)S(1)}, bf16[768,1024]{1,0:T(8,128)(2,1)S(1)}) custom-call(bf16[3,128,1024]{2,1,0:T(8,128)(2,1)S(1)} %copy-done.41, bf16[3,256,1024]{2,1,0:T(8,128)(2,1)S(1)} %bitcast.226, bf16[3,128,1024]{2,1,0:T(8,128)(2,1)S(1)} %copy-done.43, ...), custom_call_target="tpu_custom_call" | custom-call | flops 12884901888 | bytes 31457280 | tf_op jit(solution)/shard_map/attention_forward/pallas_call | solution.py:474
  166.1 1.7 copy-done.50
  172.0 1.6 pad_maximum_fusion.13
  176.2 1.6 collective-permute-done.19.bottom_a
  177.9 15.0 %feed_up.1 = (bf16[2,768,2048]{2,1,0:T(8,128)(2,1)S(1)}, bf16[2,768,2048]{2,1,0:T(8,128)(2,1)S(1)}) custom-call(bf16[768,1024]{1,0:T(8,128)(2,1)S(1)} %get-tuple-element.89.inputs, bf16[512,2048]{1,0:T(8,128)(2,1)S(1)} %constant_dynamic-update-slice_fusion.7.top_a, bf16[512,2048]{1,0:T(8,128)(2,1)S(1)} %collective-permute-done.19.bottom_a, ...), custom_call_target="tpu_custom_call" | custom-call | flops 6442450944 | bytes 20971520 | tf_op jit(solution)/shard_map/feed_up/pallas_call | solution.py:533
  192.9 5.2 %collective-permute-done.23 = bf16[256,2048]{1,0:T(8,128)(2,1)S(1)} collective-permute-done((bf16[256,2048]{1,0:T(8,128)(2,1)S(1)}, bf16[256,2048]{1,0:T(8,128)(2,1)S(1)}, u32[]{:S(2)}, u32[]{:S(2)}) %collective-permute-start.23) | collective-permute-done | bytes 1048608 | tf_op jit(solution)/shard_map/ppermute | solution.py:29
  198.2 4.4 pad_maximum_fusion.3.top_b
  202.8 2.1 pad_maximum_fusion.2.top_a
  205.1 3.2 fusion.15
  208.7 1.8 fusion.12
  210.7 10.0 %feed_slope.1.upward = bf16[2,768,2048]{2,1,0:T(8,128)(2,1)S(1)} custom-call(bf16[768,1024]{1,0:T(8,128)(2,1)S(1)} %copy-done.17, bf16[512,2048]{1,0:T(8,128)(2,1)S(1)} %pad_maximum_fusion.2.top_a, bf16[512,2048]{1,0:T(8,128)(2,1)S(1)} %collective-permute-done.25.bottom_a, bf16[512,2048]{1,0:T(8,128)(2,1)S(1)} %pad_maximum_fusion.3.top_b, ...), custom_call_target="tpu_custom_call" | custom-call | flops 6442450944 | bytes 20971520 | tf_op jit(solution)/shard_map/feed_slope/pallas_call | solution.py:622
  220.7 2.0 convert_add_fusion.2
  224.0 1.9 convert_add_fusion.3
  227.3 3.2 convolution_convert_fusion.2
  231.0 3.2 convolution_convert_fusion.3
  235.1 1.9 slice.490
  237.6 4.5 convert_add_fusion
  242.2 1.5 slice.508
  243.8 1.9 convert_add_fusion.1
  246.8 2.4 copy-done.31
  249.8 14.2 %feed_back.1 = (f32[768,1024]{1,0:T(8,128)S(1)}, bf16[768,1024]{1,0:T(8,128)(2,1)S(1)}, f32[16,1024]{1,0:T(8,128)S(1)}) custom-call(bf16[2,768,2048]{2,1,0:T(8,128)(2,1)S(1)} %bitcast.222, bf16[512,2048]{1,0:T(8,128)(2,1)S(1)} %copy-done.29, bf16[512,2048]{1,0:T(8,128)(2,1)S(1)} %copy-done.37, bf16[512,2048]{1,0:T(8,128)(2,1)S(1)} %copy-done.11, ...), custom_call_target="tpu_custom_call" | custom-call | flops 6442450944 | bytes 25690112 | tf_op jit(solution)/shard_map/feed_back/pallas_call | solution.py:679
  267.3 1.7 collective-permute-start.37
  269.2 4.7 %collective-permute-start.32 = (bf16[3,128,1024]{2,1,0:T(8,128)(2,1)S(1)}, bf16[3,128,1024]{2,1,0:T(8,128)(2,1)S(1)}, u32[]{:S(2)}, u32[]{:S(2)}) collective-permute-start(bf16[3,128,1024]{2,1,0:T(8,128)(2,1)S(1)} %get-tuple-element.124), channel_id=1, source_target_pairs={{0,1},{1,2},{2,3},{4,5},{5,6},{6,7},{8,9},{9,10},{10,11},{12,13},{... | collective-permute-start | bytes 2359304 | tf_op jit(solution)/shard_map/ppermute | solution.py:29
  275.2 12.9 %feed_down.1 = f32[768,1024]{1,0:T(8,128)} custom-call(s32[8]{0:T(128)S(1)} %broadcast_xor_fusion.table_ref, bf16[2,768,2048]{2,1,0:T(8,128)(2,1)S(1)} %bitcast.220, bf16[512,2048]{1,0:T(8,128)(2,1)S(1)} %copy-done.15, bf16[512,2048]{1,0:T(8,128)(2,1)S(1)} %copy-done.39, bf16[512,2048]{1,0:T(8,128)(2,1)S(1)} %copy-done.13, bf16[512,2048]{1,0:T(8,128)(2,1)S(1)} %copy-done.35, ...), custom_call_target="tpu_custom_call" | custom-call | flops 6442450944 | bytes 20971520 | tf_op jit(solution)/shard_map/feed_down/pallas_call | solution.py:585
  288.3 1.9 collective-permute-done.32.before
  290.3 4.2 collective-permute-done.33.after
  305.2 1.6 copy-done.9
  311.6 35.8 %attention_backward.1 = (bf16[2,768,1536]{2,1,0:T(8,128)(2,1)}, f32[768,1024]{1,0:T(8,128)S(1)}) custom-call(bf16[3,128,1024]{2,1,0:T(8,128)(2,1)S(1)} %copy-done.45, bf16[3,256,1024]{2,1,0:T(8,128)(2,1)S(1)} %bitcast.228, bf16[3,128,1024]{2,1,0:T(8,128)(2,1)S(1)} %copy-done.47, bf16[512,2048]{1,0:T(8,128)(2,1)} %constant_dynamic-update-slice_fusion.5.top_a, ...), custom_call_target="tpu_custom_call" | custom-call | flops 14495514624 | bytes 36700160 | tf_op jit(solution)/shard_map/attention_backward/pallas_call | solution.py:744
  348.7 1.7 fusion.26
  350.8 2.6 bitcast_add_fusion
  357.6 2.6 convolution_convert_fusion.1
  360.3 2.6 convolution_convert_fusion
  366.1 1.6 collective-permute-start.44
  367.7 4.2 convolution_add_fusion.1
  373.8 3.8 convolution_add_fusion
  381.0 5.6 %leave.1 = (f32[768,1024]{1,0:T(8,128)}, f32[16,1024]{1,0:T(8,128)S(1)}) custom-call(s32[8]{0:T(128)S(1)} %broadcast_xor_fusion.table_ref, f32[768,1024]{1,0:T(8,128)S(1)} %copy-done.7, f32[768,1024]{1,0:T(8,128)S(1)} %copy-done.5, f32[768,1024]{1,0:T(8,128)S(1)} %get-tuple-element.108.grad_resid, f32[4,1024]{1,0:T(4,128)S(1)} %convert_bitcast_fusion.small), custom_call_target="tpu_custom_call" | custom-call | flops 23592960 | bytes 12582912 | tf_op jit(solution)/shard_map/leave/pallas_call | solution.py:797
  386.8 1.6 fusion.36
  390.5 8.4 %collective-permute-done.50 = bf16[256,1536]{1,0:T(8,128)(2,1)} collective-permute-done((bf16[256,1536]{1,0:T(8,128)(2,1)}, bf16[256,1536]{1,0:T(8,128)(2,1)}, u32[]{:S(2)}, u32[]{:S(2)}) %collective-permute-start.50) | collective-permute-done | bytes 786464 | tf_op jit(solution)/shard_map/ppermute | solution.py:29
  398.9 1.6 bitcast_add_fusion.2
  403.9 3.4 collective-permute-start.48
  415.2 10.0 %collective-permute-done.47 = bf16[128,1024]{1,0:T(8,128)(2,1)S(1)} collective-permute-done((bf16[128,1024]{1,0:T(8,128)(2,1)S(1)}, bf16[128,1024]{1,0:T(8,128)(2,1)S(1)}, u32[]{:S(2)}, u32[]{:S(2)}) %collective-permute-start.47) | collective-permute-done | bytes 262176 | tf_op jit(solution)/shard_map/ppermute | solution.py:29
  427.4 4.5 collective-permute-start.58
  433.4 2.4 collective-permute-done.51
  436.0 5.2 %collective-permute-start.52 = (bf16[128,1024]{1,0:T(8,128)(2,1)S(1)}, bf16[128,1024]{1,0:T(8,128)(2,1)S(1)}, u32[]{:S(2)}, u32[]{:S(2)}) collective-permute-start(bf16[128,1024]{1,0:T(8,128)(2,1)S(1)} %pad_maximum_fusion.24), channel_id=1, source_target_pairs={{0,2},{1,3},{2,0},{3,1},{4,6},{5,7},{6,4},{7,5},{8,10},{9,11},{10,... | collective-permute-start | bytes 786440 | tf_op jit(solution)/shard_map/ppermute | solution.py:29
  441.2 3.4 collective-permute-start.53
  445.2 8.8 %collective-permute-done.52 = bf16[128,1024]{1,0:T(8,128)(2,1)S(1)} collective-permute-done((bf16[128,1024]{1,0:T(8,128)(2,1)S(1)}, bf16[128,1024]{1,0:T(8,128)(2,1)S(1)}, u32[]{:S(2)}, u32[]{:S(2)}) %collective-permute-start.52) | collective-permute-done | bytes 262176 | tf_op jit(solution)/shard_map/ppermute | solution.py:29
  (395 shorter events, 98.7 us)
Async XLA Ops:
  7.2 99.0 %all-gather.5.cloned.1.call-start = ((), (), s32[]{:S(2)}) async-start(), calls=%async_computation.2 | async-start | bytes 1310720 | tf_op jit(solution)/shard_map/all_gather | solution.py:835
  7.9 101.1 %all-gather.7.cloned.1.call-start = ((), (), s32[]{:S(2)}) async-start(), calls=%async_computation.3 | async-start | bytes 1310720 | tf_op jit(solution)/shard_map/all_gather | solution.py:835
  9.7 27.2 %collective-permute-start.10 = (bf16[128,1024]{1,0:T(8,128)(2,1)S(1)}, bf16[128,1024]{1,0:T(8,128)(2,1)S(1)}, u32[]{:S(2)}, u32[]{:S(2)}) collective-permute-start(bf16[128,1024]{1,0:T(8,128)(2,1)S(1)} %pad_maximum_fusion.22), channel_id=1, source_target_pairs={{0,1},{1,2},{2,3},{3,0},{4,5},{5,6},{6,7},{7,4},{8,9},{9,10},{10,1... | collective-permute-start | bytes 786440 | tf_op jit(solution)/shard_map/ppermute | solution.py:29
  12.8 30.2 %collective-permute-start.9 = (bf16[128,1024]{1,0:T(8,128)(2,1)S(1)}, bf16[128,1024]{1,0:T(8,128)(2,1)S(1)}, u32[]{:S(2)}, u32[]{:S(2)}) collective-permute-start(bf16[128,1024]{1,0:T(8,128)(2,1)S(1)} %pad_maximum_fusion.22), channel_id=1, source_target_pairs={{0,2},{1,3},{2,0},{3,1},{4,6},{5,7},{6,4},{7,5},{8,10},{9,11},{10,... | collective-permute-start | bytes 786440 | tf_op jit(solution)/shard_map/ppermute | solution.py:29
  15.4 42.8 %collective-permute-start.5 = (bf16[128,1024]{1,0:T(8,128)(2,1)S(1)}, bf16[128,1024]{1,0:T(8,128)(2,1)S(1)}, u32[]{:S(2)}, u32[]{:S(2)}) collective-permute-start(bf16[128,1024]{1,0:T(8,128)(2,1)S(1)} %pad_maximum_fusion.22), channel_id=1, source_target_pairs={{0,3},{1,0},{2,1},{3,2},{4,7},{5,4},{6,5},{7,6},{8,11},{9,8},{10,9... | collective-permute-start | bytes 786440 | tf_op jit(solution)/shard_map/ppermute | solution.py:29
  17.4 4.1 collective-permute-start
  19.0 436.7 %reduce-scatter.2.cloned.1.call-start = ((), (), s32[]{:S(2)}) async-start(), calls=%async_computation.1 | async-start | bytes 2621440 | tf_op jit(solution)/shard_map/reduce_scatter | solution.py:240
  21.6 3.7 collective-permute-start.1
  25.2 1.2 collective-permute-start.2
  43.1 16.7 %collective-permute-start.11 = (bf16[128,2048]{1,0:T(8,128)(2,1)S(1)}, bf16[128,2048]{1,0:T(8,128)(2,1)S(1)}, u32[]{:S(2)}, u32[]{:S(2)}) collective-permute-start(bf16[128,2048]{1,0:T(8,128)(2,1)S(1)} %pad_maximum_fusion.16), channel_id=1, source_target_pairs={{0,16},{4,20},{8,24},{12,28},{16,0},{20,4},{24,8},{28,12},{1,17},{... | collective-permute-start | bytes 1572872 | tf_op jit(solution)/shard_map/ppermute | solution.py:29
  46.1 33.0 %collective-permute-start.3 = (bf16[3,128,1024]{2,1,0:T(8,128)(2,1)S(1)}, bf16[3,128,1024]{2,1,0:T(8,128)(2,1)S(1)}, u32[]{:S(2)}, u32[]{:S(2)}) collective-permute-start(bf16[3,128,1024]{2,1,0:T(8,128)(2,1)S(1)} %get-tuple-element.126), channel_id=1, source_target_pairs={{0,1},{1,2},{2,3},{4,5},{5,6},{6,7},{8,9},{9,10},{10,11},{12,13},{... | collective-permute-start | bytes 2359304 | tf_op jit(solution)/shard_map/ppermute | solution.py:29
  56.9 33.3 %collective-permute-start.4 = (bf16[3,128,1024]{2,1,0:T(8,128)(2,1)S(1)}, bf16[3,128,1024]{2,1,0:T(8,128)(2,1)S(1)}, u32[]{:S(2)}, u32[]{:S(2)}) collective-permute-start(bf16[3,128,1024]{2,1,0:T(8,128)(2,1)S(1)} %get-tuple-element.125), channel_id=1, source_target_pairs={{1,0},{2,1},{3,2},{5,4},{6,5},{7,6},{9,8},{10,9},{11,10},{13,12},{... | collective-permute-start | bytes 2359304 | tf_op jit(solution)/shard_map/ppermute | solution.py:29
  58.2 14.9 %collective-permute-start.6 = (bf16[128,2048]{1,0:T(8,128)(2,1)S(1)}, bf16[128,2048]{1,0:T(8,128)(2,1)S(1)}, u32[]{:S(2)}, u32[]{:S(2)}) collective-permute-start(bf16[128,2048]{1,0:T(8,128)(2,1)S(1)} %constant_dynamic-update-slice_fusion), channel_id=1, source_target_pairs={{0,8},{4,12},{8,0},{12,4},{16,24},{20,28},{24,16},{28,20},{1,9},{5... | collective-permute-start | bytes 1572872 | tf_op jit(solution)/shard_map/ppermute | solution.py:29
  59.9 31.5 %collective-permute-start.12 = (bf16[256,2048]{1,0:T(8,128)(2,1)S(1)}, bf16[256,2048]{1,0:T(8,128)(2,1)S(1)}, u32[]{:S(2)}, u32[]{:S(2)}) collective-permute-start(bf16[256,2048]{1,0:T(8,128)(2,1)S(1)} %pad_maximum_fusion.9), channel_id=1, source_target_pairs={{0,8},{4,12},{8,0},{12,4},{16,24},{20,28},{24,16},{28,20},{1,9},{5... | collective-permute-start | bytes 3145736 | tf_op jit(solution)/shard_map/ppermute | solution.py:29
  90.2 14.8 %collective-permute-start.7 = (bf16[256,2048]{1,0:T(8,128)(2,1)S(1)}, bf16[256,2048]{1,0:T(8,128)(2,1)S(1)}, u32[]{:S(2)}, u32[]{:S(2)}) collective-permute-start(bf16[256,2048]{1,0:T(8,128)(2,1)S(1)} %pad_maximum_fusion.8), channel_id=1, source_target_pairs={{0,16},{4,20},{8,24},{12,28},{16,0},{20,4},{24,8},{28,12},{1,17},{... | collective-permute-start | bytes 3145736 | tf_op jit(solution)/shard_map/ppermute | solution.py:29
  91.7 36.5 %collective-permute-start.13 = (bf16[512,2048]{1,0:T(8,128)(2,1)S(1)}, bf16[512,2048]{1,0:T(8,128)(2,1)}, u32[]{:S(2)}, u32[]{:S(2)}) collective-permute-start(bf16[512,2048]{1,0:T(8,128)(2,1)S(1)} %pad_maximum_fusion.top_b), channel_id=1, source_target_pairs={{0,4},{4,0},{8,12},{12,8},{16,20},{20,16},{24,28},{28,24},{1,5},{5... | collective-permute-start | bytes 6291464 | tf_op jit(solution)/shard_map/ppermute | solution.py:29
  106.1 24.0 %collective-permute-start.8 = (bf16[512,2048]{1,0:T(8,128)(2,1)}, bf16[512,2048]{1,0:T(8,128)(2,1)}, u32[]{:S(2)}, u32[]{:S(2)}) collective-permute-start(bf16[512,2048]{1,0:T(8,128)(2,1)} %constant_dynamic-update-slice_fusion.5.top_a), channel_id=1, source_target_pairs={{0,4},{4,0},{8,12},{12,8},{16,20},{20,16},{24,28},{28,24},{1,5},{5... | collective-permute-start | bytes 6291464 | tf_op jit(solution)/shard_map/ppermute | solution.py:29
  107.5 14.9 %collective-permute-start.14 = (bf16[128,2048]{1,0:T(8,128)(2,1)S(1)}, bf16[128,2048]{1,0:T(8,128)(2,1)}, u32[]{:S(2)}, u32[]{:S(2)}) collective-permute-start(bf16[128,2048]{1,0:T(8,128)(2,1)S(1)} %get-tuple-element.71), channel_id=1, source_target_pairs={{0,8},{4,12},{8,0},{12,4},{16,24},{20,28},{24,16},{28,20},{1,9},{5... | collective-permute-start | bytes 1572872 | tf_op jit(solution)/shard_map/ppermute | solution.py:29
  109.0 14.2 %collective-permute-start.15 = (bf16[128,2048]{1,0:T(8,128)(2,1)S(1)}, bf16[128,2048]{1,0:T(8,128)(2,1)}, u32[]{:S(2)}, u32[]{:S(2)}) collective-permute-start(bf16[128,2048]{1,0:T(8,128)(2,1)S(1)} %get-tuple-element.72), channel_id=1, source_target_pairs={{0,16},{4,20},{8,24},{12,28},{16,0},{20,4},{24,8},{28,12},{1,17},{... | collective-permute-start | bytes 1572872 | tf_op jit(solution)/shard_map/ppermute | solution.py:29
  111.3 56.5 %collective-permute-start.16 = (bf16[128,2048]{1,0:T(8,128)(2,1)}, bf16[128,2048]{1,0:T(8,128)(2,1)}, u32[]{:S(2)}, u32[]{:S(2)}) collective-permute-start(bf16[128,2048]{1,0:T(8,128)(2,1)} %pad_maximum_fusion.19), channel_id=1, source_target_pairs={{0,8},{4,12},{8,0},{12,4},{16,24},{20,28},{24,16},{28,20},{1,9},{5... | collective-permute-start | bytes 1572872 | tf_op jit(solution)/shard_map/ppermute | solution.py:29
  122.4 45.4 %collective-permute-start.17 = (bf16[128,2048]{1,0:T(8,128)(2,1)}, bf16[128,2048]{1,0:T(8,128)(2,1)}, u32[]{:S(2)}, u32[]{:S(2)}) collective-permute-start(bf16[128,2048]{1,0:T(8,128)(2,1)} %pad_maximum_fusion.20), channel_id=1, source_target_pairs={{0,16},{4,20},{8,24},{12,28},{16,0},{20,4},{24,8},{28,12},{1,17},{... | collective-permute-start | bytes 1572872 | tf_op jit(solution)/shard_map/ppermute | solution.py:29
  125.0 42.8 %collective-permute-start.20 = (bf16[256,2048]{1,0:T(8,128)(2,1)S(1)}, bf16[256,2048]{1,0:T(8,128)(2,1)S(1)}, u32[]{:S(2)}, u32[]{:S(2)}) collective-permute-start(bf16[256,2048]{1,0:T(8,128)(2,1)S(1)} %pad_maximum_fusion.11), channel_id=1, source_target_pairs={{0,8},{4,12},{8,0},{12,4},{16,24},{20,28},{24,16},{28,20},{1,9},{5... | collective-permute-start | bytes 3145736 | tf_op jit(solution)/shard_map/ppermute | solution.py:29
  128.2 42.5 %collective-permute-start.18 = (bf16[256,2048]{1,0:T(8,128)(2,1)S(1)}, bf16[256,2048]{1,0:T(8,128)(2,1)S(1)}, u32[]{:S(2)}, u32[]{:S(2)}) collective-permute-start(bf16[256,2048]{1,0:T(8,128)(2,1)S(1)} %pad_maximum_fusion.10), channel_id=1, source_target_pairs={{0,16},{4,20},{8,24},{12,28},{16,0},{20,4},{24,8},{28,12},{1,17},{... | collective-permute-start | bytes 3145736 | tf_op jit(solution)/shard_map/ppermute | solution.py:29
  167.8 63.2 %copy-start.18 = (bf16[768,1024]{1,0:T(8,128)(2,1)}, bf16[768,1024]{1,0:T(8,128)(2,1)S(1)}, u32[]{:S(2)}) copy-start(bf16[768,1024]{1,0:T(8,128)(2,1)S(1)} %get-tuple-element.89.inputs) | copy-start | bytes 4718596
  170.6 5.6 %collective-permute-start.21 = (bf16[512,2048]{1,0:T(8,128)(2,1)S(1)}, bf16[512,2048]{1,0:T(8,128)(2,1)S(1)}, u32[]{:S(2)}, u32[]{:S(2)}) collective-permute-start(bf16[512,2048]{1,0:T(8,128)(2,1)S(1)} %pad_maximum_fusion.1.top_b), channel_id=1, source_target_pairs={{0,4},{4,0},{8,12},{12,8},{16,20},{20,16},{24,28},{28,24},{1,5},{5... | collective-permute-start | bytes 6291464 | tf_op jit(solution)/shard_map/ppermute | solution.py:29
  170.8 7.0 %collective-permute-start.19 = (bf16[512,2048]{1,0:T(8,128)(2,1)S(1)}, bf16[512,2048]{1,0:T(8,128)(2,1)S(1)}, u32[]{:S(2)}, u32[]{:S(2)}) collective-permute-start(bf16[512,2048]{1,0:T(8,128)(2,1)S(1)} %constant_dynamic-update-slice_fusion.7.top_a), channel_id=1, source_target_pairs={{0,4},{4,0},{8,12},{12,8},{16,20},{20,16},{24,28},{28,24},{1,5},{5... | collective-permute-start | bytes 6291464 | tf_op jit(solution)/shard_map/ppermute | solution.py:29
  173.6 24.6 %collective-permute-start.23 = (bf16[256,2048]{1,0:T(8,128)(2,1)S(1)}, bf16[256,2048]{1,0:T(8,128)(2,1)S(1)}, u32[]{:S(2)}, u32[]{:S(2)}) collective-permute-start(bf16[256,2048]{1,0:T(8,128)(2,1)S(1)} %pad_maximum_fusion.13), channel_id=1, source_target_pairs={{0,8},{4,12},{8,0},{12,4},{16,24},{20,28},{24,16},{28,20},{1,9},{5... | collective-permute-start | bytes 3145736 | tf_op jit(solution)/shard_map/ppermute | solution.py:29
  175.7 27.1 %collective-permute-start.22 = (bf16[256,2048]{1,0:T(8,128)(2,1)S(1)}, bf16[256,2048]{1,0:T(8,128)(2,1)S(1)}, u32[]{:S(2)}, u32[]{:S(2)}) collective-permute-start(bf16[256,2048]{1,0:T(8,128)(2,1)S(1)} %pad_maximum_fusion.12), channel_id=1, source_target_pairs={{0,16},{4,20},{8,24},{12,28},{16,0},{20,4},{24,8},{28,12},{1,17},{... | collective-permute-start | bytes 3145736 | tf_op jit(solution)/shard_map/ppermute | solution.py:29
  202.7 7.9 %collective-permute-start.26 = (bf16[512,2048]{1,0:T(8,128)(2,1)S(1)}, bf16[512,2048]{1,0:T(8,128)(2,1)S(1)}, u32[]{:S(2)}, u32[]{:S(2)}) collective-permute-start(bf16[512,2048]{1,0:T(8,128)(2,1)S(1)} %pad_maximum_fusion.3.top_b), channel_id=1, source_target_pairs={{0,4},{4,0},{8,12},{12,8},{16,20},{20,16},{24,28},{28,24},{1,5},{5... | collective-permute-start | bytes 6291464 | tf_op jit(solution)/shard_map/ppermute | solution.py:29
  205.0 5.7 %collective-permute-start.25 = (bf16[512,2048]{1,0:T(8,128)(2,1)S(1)}, bf16[512,2048]{1,0:T(8,128)(2,1)S(1)}, u32[]{:S(2)}, u32[]{:S(2)}) collective-permute-start(bf16[512,2048]{1,0:T(8,128)(2,1)S(1)} %pad_maximum_fusion.2.top_a), channel_id=1, source_target_pairs={{0,4},{4,0},{8,12},{12,8},{16,20},{20,16},{24,28},{28,24},{1,5},{5... | collective-permute-start | bytes 6291464 | tf_op jit(solution)/shard_map/ppermute | solution.py:29
  208.2 12.5 %collective-permute-start.28 = (bf16[512,2048]{1,0:T(8,128)(2,1)}, bf16[512,2048]{1,0:T(8,128)(2,1)S(1)}, u32[]{:S(2)}, u32[]{:S(2)}) collective-permute-start(bf16[512,2048]{1,0:T(8,128)(2,1)} %fusion.15), channel_id=1, source_target_pairs={{0,4},{4,0},{8,12},{12,8},{16,20},{20,16},{24,28},{28,24},{1,5},{5... | collective-permute-start | bytes 6291464 | tf_op jit(solution)/shard_map/ppermute | solution.py:29
  210.6 13.4 %collective-permute-start.24 = (bf16[512,2048]{1,0:T(8,128)(2,1)S(1)}, bf16[512,2048]{1,0:T(8,128)(2,1)S(1)}, u32[]{:S(2)}, u32[]{:S(2)}) collective-permute-start(bf16[512,2048]{1,0:T(8,128)(2,1)S(1)} %fusion.12), channel_id=1, source_target_pairs={{0,4},{4,0},{8,12},{12,8},{16,20},{20,16},{24,28},{28,24},{1,5},{5... | collective-permute-start | bytes 6291464 | tf_op jit(solution)/shard_map/ppermute | solution.py:29
  230.5 7.0 %collective-permute-start.30 = (bf16[512,2048]{1,0:T(8,128)(2,1)}, bf16[512,2048]{1,0:T(8,128)(2,1)}, u32[]{:S(2)}, u32[]{:S(2)}) collective-permute-start(bf16[512,2048]{1,0:T(8,128)(2,1)} %convolution_convert_fusion.2), channel_id=1, source_target_pairs={{0,4},{4,0},{8,12},{12,8},{16,20},{20,16},{24,28},{28,24},{1,5},{5... | collective-permute-start | bytes 6291464 | tf_op jit(solution)/shard_map/ppermute | solution.py:29
  234.2 9.5 %collective-permute-start.29 = (bf16[512,2048]{1,0:T(8,128)(2,1)}, bf16[512,2048]{1,0:T(8,128)(2,1)S(1)}, u32[]{:S(2)}, u32[]{:S(2)}) collective-permute-start(bf16[512,2048]{1,0:T(8,128)(2,1)} %convolution_convert_fusion.3), channel_id=1, source_target_pairs={{0,4},{4,0},{8,12},{12,8},{16,20},{20,16},{24,28},{28,24},{1,5},{5... | collective-permute-start | bytes 6291464 | tf_op jit(solution)/shard_map/ppermute | solution.py:29
  234.2 29.8 %collective-permute-start.31 = (bf16[256,2048]{1,0:T(8,128)(2,1)}, bf16[256,2048]{1,0:T(8,128)(2,1)S(1)}, u32[]{:S(2)}, u32[]{:S(2)}) collective-permute-start(bf16[256,2048]{1,0:T(8,128)(2,1)} %bitcast.15), channel_id=1, source_target_pairs={{0,8},{4,12},{8,0},{12,4},{16,24},{20,28},{24,16},{28,20},{1,9},{5... | collective-permute-start | bytes 3145736 | tf_op jit(solution)/shard_map/ppermute | solution.py:29
  237.0 28.8 %collective-permute-start.27 = (bf16[256,2048]{1,0:T(8,128)(2,1)}, bf16[256,2048]{1,0:T(8,128)(2,1)S(1)}, u32[]{:S(2)}, u32[]{:S(2)}) collective-permute-start(bf16[256,2048]{1,0:T(8,128)(2,1)} %fusion.33), channel_id=1, source_target_pairs={{0,16},{4,20},{8,24},{12,28},{16,0},{20,4},{24,8},{28,12},{1,17},{... | collective-permute-start | bytes 3145736 | tf_op jit(solution)/shard_map/ppermute | solution.py:29
  245.7 42.4 %copy-start.52 = (f32[512,2048]{1,0:T(8,128)}, f32[512,2048]{1,0:T(8,128)S(1)}, u32[]{:S(2)}) copy-start(f32[512,2048]{1,0:T(8,128)S(1)} %convert_add_fusion.1) | copy-start | bytes 12582916
  266.3 22.0 %collective-permute-start.36 = (bf16[128,2048]{1,0:T(8,128)(2,1)S(1)}, bf16[128,2048]{1,0:T(8,128)(2,1)S(1)}, u32[]{:S(2)}, u32[]{:S(2)}) collective-permute-start(bf16[128,2048]{1,0:T(8,128)(2,1)S(1)} %fusion.67), channel_id=1, source_target_pairs={{0,8},{4,12},{8,0},{12,4},{16,24},{20,28},{24,16},{28,20},{1,9},{5... | collective-permute-start | bytes 1572872 | tf_op jit(solution)/shard_map/ppermute | solution.py:29
  267.3 30.1 %collective-permute-start.37 = (bf16[128,2048]{1,0:T(8,128)(2,1)S(1)}, bf16[128,2048]{1,0:T(8,128)(2,1)S(1)}, u32[]{:S(2)}, u32[]{:S(2)}) collective-permute-start(bf16[128,2048]{1,0:T(8,128)(2,1)S(1)} %fusion.68), channel_id=1, source_target_pairs={{0,16},{4,20},{8,24},{12,28},{16,0},{20,4},{24,8},{28,12},{1,17},{... | collective-permute-start | bytes 1572872 | tf_op jit(solution)/shard_map/ppermute | solution.py:29
  269.2 21.1 %collective-permute-start.32 = (bf16[3,128,1024]{2,1,0:T(8,128)(2,1)S(1)}, bf16[3,128,1024]{2,1,0:T(8,128)(2,1)S(1)}, u32[]{:S(2)}, u32[]{:S(2)}) collective-permute-start(bf16[3,128,1024]{2,1,0:T(8,128)(2,1)S(1)} %get-tuple-element.124), channel_id=1, source_target_pairs={{0,1},{1,2},{2,3},{4,5},{5,6},{6,7},{8,9},{9,10},{10,11},{12,13},{... | collective-permute-start | bytes 2359304 | tf_op jit(solution)/shard_map/ppermute | solution.py:29
  273.9 20.6 %collective-permute-start.33 = (bf16[3,128,1024]{2,1,0:T(8,128)(2,1)S(1)}, bf16[3,128,1024]{2,1,0:T(8,128)(2,1)S(1)}, u32[]{:S(2)}, u32[]{:S(2)}) collective-permute-start(bf16[3,128,1024]{2,1,0:T(8,128)(2,1)S(1)} %get-tuple-element.123), channel_id=1, source_target_pairs={{1,0},{2,1},{3,2},{5,4},{6,5},{7,6},{9,8},{10,9},{11,10},{13,12},{... | collective-permute-start | bytes 2359304 | tf_op jit(solution)/shard_map/ppermute | solution.py:29
  295.1 2.4 collective-permute-start.35
  295.8 2.4 collective-permute-start.34
  301.3 49.2 %collective-permute-start.39 = (bf16[256,2560]{1,0:T(8,128)(2,1)}, bf16[256,2560]{1,0:T(8,128)(2,1)}, u32[]{:S(2)}, u32[]{:S(2)}) collective-permute-start(bf16[256,2560]{1,0:T(8,128)(2,1)} %pad_maximum_fusion.7), channel_id=1, source_target_pairs={{0,8},{4,12},{8,0},{12,4},{16,24},{20,28},{24,16},{28,20},{1,9},{5... | collective-permute-start | bytes 3932168 | tf_op jit(solution)/shard_map/ppermute | solution.py:29
  303.3 44.2 %collective-permute-start.38 = (bf16[256,2560]{1,0:T(8,128)(2,1)}, bf16[256,2560]{1,0:T(8,128)(2,1)}, u32[]{:S(2)}, u32[]{:S(2)}) collective-permute-start(bf16[256,2560]{1,0:T(8,128)(2,1)} %pad_maximum_fusion.6), channel_id=1, source_target_pairs={{0,16},{4,20},{8,24},{12,28},{16,0},{20,4},{24,8},{28,12},{1,17},{... | collective-permute-start | bytes 3932168 | tf_op jit(solution)/shard_map/ppermute | solution.py:29
  360.1 7.5 %collective-permute-start.40 = (bf16[512,1536]{1,0:T(8,128)(2,1)}, bf16[512,1536]{1,0:T(8,128)(2,1)}, u32[]{:S(2)}, u32[]{:S(2)}) collective-permute-start(bf16[512,1536]{1,0:T(8,128)(2,1)} %convolution_convert_fusion.1), channel_id=1, source_target_pairs={{0,4},{4,0},{8,12},{12,8},{16,20},{20,16},{24,28},{28,24},{1,5},{5... | collective-permute-start | bytes 4718600 | tf_op jit(solution)/shard_map/ppermute | solution.py:29
  362.9 11.0 %collective-permute-start.41 = (bf16[512,1536]{1,0:T(8,128)(2,1)}, bf16[512,1536]{1,0:T(8,128)(2,1)}, u32[]{:S(2)}, u32[]{:S(2)}) collective-permute-start(bf16[512,1536]{1,0:T(8,128)(2,1)} %convolution_convert_fusion), channel_id=1, source_target_pairs={{0,4},{4,0},{8,12},{12,8},{16,20},{20,16},{24,28},{28,24},{1,5},{5... | collective-permute-start | bytes 4718600 | tf_op jit(solution)/shard_map/ppermute | solution.py:29
  365.1 21.7 %collective-permute-start.43 = (bf16[128,2560]{1,0:T(8,128)(2,1)}, bf16[128,2560]{1,0:T(8,128)(2,1)}, u32[]{:S(2)}, u32[]{:S(2)}) collective-permute-start(bf16[128,2560]{1,0:T(8,128)(2,1)} %pad_maximum_fusion.14), channel_id=1, source_target_pairs={{0,8},{4,12},{8,0},{12,4},{16,24},{20,28},{24,16},{28,20},{1,9},{5... | collective-permute-start | bytes 1966088 | tf_op jit(solution)/shard_map/ppermute | solution.py:29
  366.1 22.3 %collective-permute-start.44 = (bf16[128,2560]{1,0:T(8,128)(2,1)}, bf16[128,2560]{1,0:T(8,128)(2,1)}, u32[]{:S(2)}, u32[]{:S(2)}) collective-permute-start(bf16[128,2560]{1,0:T(8,128)(2,1)} %pad_maximum_fusion.15), channel_id=1, source_target_pairs={{0,16},{4,20},{8,24},{12,28},{16,0},{20,4},{24,8},{28,12},{1,17},{... | collective-permute-start | bytes 1966088 | tf_op jit(solution)/shard_map/ppermute | solution.py:29
  379.9 19.0 %collective-permute-start.50 = (bf16[256,1536]{1,0:T(8,128)(2,1)}, bf16[256,1536]{1,0:T(8,128)(2,1)}, u32[]{:S(2)}, u32[]{:S(2)}) collective-permute-start(bf16[256,1536]{1,0:T(8,128)(2,1)} %bitcast.54), channel_id=1, source_target_pairs={{0,8},{4,12},{8,0},{12,4},{16,24},{20,28},{24,16},{28,20},{1,9},{5... | collective-permute-start | bytes 2359304 | tf_op jit(solution)/shard_map/ppermute | solution.py:29
  380.5 20.1 %collective-permute-start.42 = (bf16[256,1536]{1,0:T(8,128)(2,1)}, bf16[256,1536]{1,0:T(8,128)(2,1)}, u32[]{:S(2)}, u32[]{:S(2)}) collective-permute-start(bf16[256,1536]{1,0:T(8,128)(2,1)} %fusion.39), channel_id=1, source_target_pairs={{0,16},{4,20},{8,24},{12,28},{16,0},{20,4},{24,8},{28,12},{1,17},{... | collective-permute-start | bytes 2359304 | tf_op jit(solution)/shard_map/ppermute | solution.py:29
  402.4 4.9 %collective-permute-start.54 = (f32[512,4]{0,1:T(4,128)S(1)}, f32[512,4]{0,1:T(4,128)S(1)}, u32[]{:S(2)}, u32[]{:S(2)}) collective-permute-start(f32[512,4]{0,1:T(4,128)S(1)} %slice.459), channel_id=1, source_target_pairs={{0,4},{4,0},{8,12},{12,8},{16,20},{20,16},{24,28},{28,24},{1,5},{5... | collective-permute-start | bytes 24584 | tf_op jit(solution)/shard_map/ppermute | solution.py:29
  403.5 11.8 %collective-permute-start.46 = (bf16[128,1024]{1,0:T(8,128)(2,1)S(1)}, bf16[128,1024]{1,0:T(8,128)(2,1)S(1)}, u32[]{:S(2)}, u32[]{:S(2)}) collective-permute-start(bf16[128,1024]{1,0:T(8,128)(2,1)S(1)} %get-tuple-element.122), channel_id=1, source_target_pairs={{0,1},{1,2},{2,3},{3,0},{4,5},{5,6},{6,7},{7,4},{8,9},{9,10},{10,1... | collective-permute-start | bytes 786440 | tf_op jit(solution)/shard_map/ppermute | solution.py:29
  403.9 21.3 %collective-permute-start.47 = (bf16[128,1024]{1,0:T(8,128)(2,1)S(1)}, bf16[128,1024]{1,0:T(8,128)(2,1)S(1)}, u32[]{:S(2)}, u32[]{:S(2)}) collective-permute-start(bf16[128,1024]{1,0:T(8,128)(2,1)S(1)} %get-tuple-element.121), channel_id=1, source_target_pairs={{0,2},{1,3},{2,0},{3,1},{4,6},{5,7},{6,4},{7,5},{8,10},{9,11},{10,... | collective-permute-start | bytes 786440 | tf_op jit(solution)/shard_map/ppermute | solution.py:29
  403.9 21.3 %collective-permute-start.48 = (bf16[128,1024]{1,0:T(8,128)(2,1)S(1)}, bf16[128,1024]{1,0:T(8,128)(2,1)S(1)}, u32[]{:S(2)}, u32[]{:S(2)}) collective-permute-start(bf16[128,1024]{1,0:T(8,128)(2,1)S(1)} %get-tuple-element.120), channel_id=1, source_target_pairs={{0,3},{1,0},{2,1},{3,2},{4,7},{5,4},{6,5},{7,6},{8,11},{9,8},{10,9... | collective-permute-start | bytes 786440 | tf_op jit(solution)/shard_map/ppermute | solution.py:29
  407.4 3.7 collective-permute-start.55
  411.0 3.6 collective-permute-start.56
  412.0 19.9 %collective-permute-start.45 = (bf16[128,1536]{1,0:T(8,128)(2,1)S(1)}, bf16[128,1536]{1,0:T(8,128)(2,1)S(1)}, u32[]{:S(2)}, u32[]{:S(2)}) collective-permute-start(bf16[128,1536]{1,0:T(8,128)(2,1)S(1)} %fusion.74), channel_id=1, source_target_pairs={{0,8},{4,12},{8,0},{12,4},{16,24},{20,28},{24,16},{28,20},{1,9},{5... | collective-permute-start | bytes 1179656 | tf_op jit(solution)/shard_map/ppermute | solution.py:29
  414.7 12.7 %collective-permute-start.57 = (f32[128,4]{0,1:T(4,128)S(1)}, f32[128,4]{0,1:T(4,128)S(1)}, u32[]{:S(2)}, u32[]{:S(2)}) collective-permute-start(f32[128,4]{0,1:T(4,128)S(1)} %slice_add_fusion.4), channel_id=1, source_target_pairs={{0,1},{1,0},{2,3},{3,2},{4,5},{5,4},{6,7},{7,6},{8,9},{9,8},{10,11... | collective-permute-start | bytes 6152 | tf_op jit(solution)/shard_map/ppermute | solution.py:939
  426.1 9.7 %collective-permute-start.51 = (bf16[128,1536]{1,0:T(8,128)(2,1)S(1)}, bf16[128,1536]{1,0:T(8,128)(2,1)S(1)}, u32[]{:S(2)}, u32[]{:S(2)}) collective-permute-start(bf16[128,1536]{1,0:T(8,128)(2,1)S(1)} %fusion.75), channel_id=1, source_target_pairs={{0,16},{4,20},{8,24},{12,28},{16,0},{20,4},{24,8},{28,12},{1,17},{... | collective-permute-start | bytes 1179656 | tf_op jit(solution)/shard_map/ppermute | solution.py:29
  427.4 17.3 %collective-permute-start.58 = (f32[128,4]{0,1:T(4,128)S(1)}, f32[128,4]{0,1:T(4,128)S(1)}, u32[]{:S(2)}, u32[]{:S(2)}) collective-permute-start(f32[128,4]{0,1:T(4,128)S(1)} %add.190), channel_id=1, source_target_pairs={{0,2},{1,3},{2,0},{3,1},{4,6},{5,7},{6,4},{7,5},{8,10},{9,11},{10,... | collective-permute-start | bytes 6152 | tf_op jit(solution)/shard_map/ppermute | solution.py:939
  432.1 13.1 %collective-permute-start.49 = (bf16[128,1024]{1,0:T(8,128)(2,1)S(1)}, bf16[128,1024]{1,0:T(8,128)(2,1)S(1)}, u32[]{:S(2)}, u32[]{:S(2)}) collective-permute-start(bf16[128,1024]{1,0:T(8,128)(2,1)S(1)} %pad_maximum_fusion.23), channel_id=1, source_target_pairs={{0,1},{1,2},{2,3},{3,0},{4,5},{5,6},{6,7},{7,4},{8,9},{9,10},{10,1... | collective-permute-start | bytes 786440 | tf_op jit(solution)/shard_map/ppermute | solution.py:29
  436.0 18.1 %collective-permute-start.52 = (bf16[128,1024]{1,0:T(8,128)(2,1)S(1)}, bf16[128,1024]{1,0:T(8,128)(2,1)S(1)}, u32[]{:S(2)}, u32[]{:S(2)}) collective-permute-start(bf16[128,1024]{1,0:T(8,128)(2,1)S(1)} %pad_maximum_fusion.24), channel_id=1, source_target_pairs={{0,2},{1,3},{2,0},{3,1},{4,6},{5,7},{6,4},{7,5},{8,10},{9,11},{10,... | collective-permute-start | bytes 786440 | tf_op jit(solution)/shard_map/ppermute | solution.py:29
  441.2 12.8 %collective-permute-start.53 = (bf16[128,1024]{1,0:T(8,128)(2,1)S(1)}, bf16[128,1024]{1,0:T(8,128)(2,1)S(1)}, u32[]{:S(2)}, u32[]{:S(2)}) collective-permute-start(bf16[128,1024]{1,0:T(8,128)(2,1)S(1)} %pad_maximum_fusion.25), channel_id=1, source_target_pairs={{0,3},{1,0},{2,1},{3,2},{4,7},{5,4},{6,5},{7,6},{8,11},{9,8},{10,9... | collective-permute-start | bytes 786440 | tf_op jit(solution)/shard_map/ppermute | solution.py:29
  (93 other events, 698.6 us)
Sparse Core Ops, SparseCore 0:
  9.6 43.2 all-gather.4
  54.5 37.1 all-gather.6
  365.2 41.6 reduce-scatter.1

commit v7 on v6

--- a/solution.py
+++ b/solution.py
@@ -251,7 +251,7 @@
     return dot(left[:, :half], top, (1, 0)) + dot(left[:, half:], bottom, (1, 0))
 
 
-A_X2 = 1
+A_X2 = 2
 A_CORE = 0
 A_DOWN = 1
 B_DOWN = 1
@@ -843,7 +843,7 @@
         window = links.halo(inputs_a.reshape(micro, rows, width))
         down_halves = columns_of(w_down)
         halos = [window[0], window[2]]
-        gather_attention.step(halos if A_X2 else [inputs_a], [inputs_a])
+        gather_attention.step([] if A_X2 == 2 else halos if A_X2 else [inputs_a], [inputs_a])
         gather_up = Gather(plan, links, up_halves)
         gather_down = Gather(plan, links, down_halves)
         tokens_up = gather_up.steps_but_last([inputs_a])

time: 469 us -> 468 us (level)
  waiting for transfers between devices: 106 us -> 94.3 us
    ppermute x57, waiting for transfers between devices: 106 us -> 93.5 us  [send(): result = lax.ppermute(value, axis, pairs)]
    unnamed x198 -> x197, local copies, waits for them, and re-layouts: 34 us -> 35.5 us
  transfers between devices with their start and end apart: 62 -> 62, of which waited for: 19 -> 16; matrix products, arithmetic and copies ran while one was open for 19% -> 21% of each run, Pallas kernels for 29% -> 29%
where the time goes in v7:
time: 468 us; the launch traced here: 461 us
  Pallas kernels  133 us (28%)
  waiting for transfers between devices  94.3 us (20%)
  starting transfers between devices  78.9 us (17%)
  local copies, waits for them, and re-layouts  56.3 us (12%)
  other arithmetic  45 us (10%)
  matrix products  37.1 us (8%)
  between operations  15.7 us (3%)
    ppermute x57, waiting for transfers between devices, send(): result = lax.ppermute(value, axis, pairs)  93.5 us
    ppermute x57, starting transfers between devices, send(): result = lax.ppermute(value, axis, pairs)  73.7 us
    dot_general x16, matrix products, dot(): lax.dot_general(left, right, ((dims[:1], dims[1:]), ((), ())), preferred_...  37.1 us
    pallas_call x1, Pallas kernels, forward_block(): pl.pallas_call(forward_kernel(rows, steps, g // HEAD_DIM, factor), name='...  35.9 us
    pallas_call x1, Pallas kernels, backward_block(): pl.pallas_call(backward_kernel(rows, steps, g // HEAD_DIM, factor), name=...  35.8 us
    unnamed x197, local copies, waits for them, and re-layouts  35.5 us
    add x14, other arithmetic, add(): k[0] + k[1][:, k[2]:k[2] + k[0].shape[1]].astype(jnp.float32)  15.4 us
    pallas_call x1, Pallas kernels, feed_up(): pl.pallas_call(up_kernel(count), name='feed_up', grid=(ff // tile,), in_s...  15 us
  transfers between devices with their start and end apart: 62, of which 16 were waited for; matrix products, arithmetic and copies ran while one was open for 21% of the time, Pallas kernels for 29%

profile of v7, /device:TPU:0, one launch (start us, length us, event | category | flops | bytes accessed | tf_op | source)
XLA Modules:
  0.0 460.6 jit_solution(18201055554479901818)
XLA Ops:
  9.9 3.1 collective-permute-start.10
  13.0 2.6 collective-permute-start.9
  23.6 1.6 collective-permute-start.1
  28.5 14.9 %collective-permute-done.9 = bf16[128,1024]{1,0:T(8,128)(2,1)} collective-permute-done((bf16[128,1024]{1,0:T(8,128)(2,1)S(1)}, bf16[128,1024]{1,0:T(8,128)(2,1)}, u32[]{:S(2)}, u32[]{:S(2)}) %collective-permute-start.9) | collective-permute-done | bytes 262176 | tf_op jit(solution)/shard_map/ppermute | solution.py:29
  44.4 1.6 collective-permute-start.11
  46.7 1.9 copy-done.3
  48.6 4.0 enter.1
  52.6 1.6 copy-done.30
  54.2 2.2 constant_dynamic-update-slice_fusion
  56.4 1.5 collective-permute-start.6
  59.4 10.7 %collective-permute-start.3 = (bf16[3,128,1024]{2,1,0:T(8,128)(2,1)S(1)}, bf16[3,128,1024]{2,1,0:T(8,128)(2,1)S(1)}, u32[]{:S(2)}, u32[]{:S(2)}) collective-permute-start(bf16[3,128,1024]{2,1,0:T(8,128)(2,1)S(1)} %get-tuple-element.124), channel_id=1, source_target_pairs={{0,1},{1,2},{2,3},{4,5},{5,6},{6,7},{8,9},{9,10},{10,11},{12,13},{... | collective-permute-start | bytes 2359304 | tf_op jit(solution)/shard_map/ppermute | solution.py:29
  72.1 1.9 constant_dynamic-update-slice_fusion.7
  76.7 21.4 %collective-permute-done.3.before = bf16[3,128,1024]{2,1,0:T(8,128)(2,1)S(1)} collective-permute-done((bf16[3,128,1024]{2,1,0:T(8,128)(2,1)S(1)}, bf16[3,128,1024]{2,1,0:T(8,128)(2,1)S(1)}, u32[]{:S(2)}, u32[]{:S(2)}) %collective-permute-start.3) | collective-permute-done | bytes 786464 | tf_op jit(solution)/shard_map/ppermute | solution.py:29
  98.1 2.2 collective-permute-done.4.after
  104.3 1.5 collective-permute-start.14
  111.7 7.5 %collective-permute-done.14 = bf16[128,2048]{1,0:T(8,128)(2,1)} collective-permute-done((bf16[128,2048]{1,0:T(8,128)(2,1)S(1)}, bf16[128,2048]{1,0:T(8,128)(2,1)}, u32[]{:S(2)}, u32[]{:S(2)}) %collective-permute-start.14) | collective-permute-done | bytes 524320 | tf_op jit(solution)/shard_map/ppermute | solution.py:29
  122.5 1.5 collective-permute-start.20
  127.0 35.9 %attention_forward.1 = (bf16[3,512,3072]{2,1,0:T(8,128)(2,1)}, bf16[2,768,512]{2,1,0:T(8,128)(2,1)S(1)}, f32[768,1024]{1,0:T(8,128)S(1)}, bf16[768,1024]{1,0:T(8,128)(2,1)S(1)}) custom-call(bf16[3,128,1024]{2,1,0:T(8,128)(2,1)S(1)} %copy-done.41, bf16[3,256,1024]{2,1,0:T(8,128)(2,1)S(1)} %bitcast.226, bf16[3,128,1024]{2,1,0:T(8,128)(2,1)S(1)} %copy-done.43, ...), custom_call_target="tpu_custom_call" | custom-call | flops 12884901888 | bytes 31457280 | tf_op jit(solution)/shard_map/attention_forward/pallas_call | solution.py:474
  162.9 1.7 copy-done.50
  168.7 1.6 pad_maximum_fusion.13
  172.4 1.5 collective-permute-start.22
  174.6 15.0 %feed_up.1 = (bf16[2,768,2048]{2,1,0:T(8,128)(2,1)S(1)}, bf16[2,768,2048]{2,1,0:T(8,128)(2,1)S(1)}) custom-call(bf16[768,1024]{1,0:T(8,128)(2,1)S(1)} %get-tuple-element.87.inputs, bf16[512,2048]{1,0:T(8,128)(2,1)S(1)} %constant_dynamic-update-slice_fusion.8.top_a, bf16[512,2048]{1,0:T(8,128)(2,1)S(1)} %collective-permute-done.19.bottom_a, ...), custom_call_target="tpu_custom_call" | custom-call | flops 6442450944 | bytes 20971520 | tf_op jit(solution)/shard_map/feed_up/pallas_call | solution.py:533
  189.7 5.2 %collective-permute-done.23 = bf16[256,2048]{1,0:T(8,128)(2,1)S(1)} collective-permute-done((bf16[256,2048]{1,0:T(8,128)(2,1)S(1)}, bf16[256,2048]{1,0:T(8,128)(2,1)S(1)}, u32[]{:S(2)}, u32[]{:S(2)}) %collective-permute-start.23) | collective-permute-done | bytes 1048608 | tf_op jit(solution)/shard_map/ppermute | solution.py:29
  195.0 4.4 pad_maximum_fusion.3.top_b
  199.6 2.1 pad_maximum_fusion.2.top_a
  201.8 3.2 fusion.15
  205.5 1.8 fusion.12
  207.5 10.0 %feed_slope.1.upward = bf16[2,768,2048]{2,1,0:T(8,128)(2,1)S(1)} custom-call(bf16[768,1024]{1,0:T(8,128)(2,1)S(1)} %copy-done.17, bf16[512,2048]{1,0:T(8,128)(2,1)S(1)} %pad_maximum_fusion.2.top_a, bf16[512,2048]{1,0:T(8,128)(2,1)S(1)} %collective-permute-done.25.bottom_a, bf16[512,2048]{1,0:T(8,128)(2,1)S(1)} %pad_maximum_fusion.3.top_b, ...), custom_call_target="tpu_custom_call" | custom-call | flops 6442450944 | bytes 20971520 | tf_op jit(solution)/shard_map/feed_slope/pallas_call | solution.py:622
  217.6 2.0 convert_add_fusion.2
  220.8 1.9 convert_add_fusion.3
  224.2 3.2 convolution_convert_fusion.2
  227.8 3.2 convolution_convert_fusion.3
  231.9 1.9 slice.490
  233.8 1.5 collective-permute-start.27
  235.4 4.5 convert_add_fusion
  241.6 1.9 convert_add_fusion.1
  244.6 2.4 copy-done.31
  247.7 14.2 %feed_back.1 = (f32[768,1024]{1,0:T(8,128)S(1)}, bf16[768,1024]{1,0:T(8,128)(2,1)S(1)}, f32[16,1024]{1,0:T(8,128)S(1)}) custom-call(bf16[2,768,2048]{2,1,0:T(8,128)(2,1)S(1)} %bitcast.222, bf16[512,2048]{1,0:T(8,128)(2,1)S(1)} %copy-done.29, bf16[512,2048]{1,0:T(8,128)(2,1)S(1)} %copy-done.37, bf16[512,2048]{1,0:T(8,128)(2,1)S(1)} %copy-done.11, ...), custom_call_target="tpu_custom_call" | custom-call | flops 6442450944 | bytes 25690112 | tf_op jit(solution)/shard_map/feed_back/pallas_call | solution.py:679
  266.0 3.8 collective-permute-start.32
  271.2 12.9 %feed_down.1 = f32[768,1024]{1,0:T(8,128)} custom-call(s32[8]{0:T(128)S(1)} %broadcast_xor_fusion.table_ref, bf16[2,768,2048]{2,1,0:T(8,128)(2,1)S(1)} %bitcast.220, bf16[512,2048]{1,0:T(8,128)(2,1)S(1)} %copy-done.15, bf16[512,2048]{1,0:T(8,128)(2,1)S(1)} %copy-done.39, bf16[512,2048]{1,0:T(8,128)(2,1)S(1)} %copy-done.13, bf16[512,2048]{1,0:T(8,128)(2,1)S(1)} %copy-done.35, ...), custom_call_target="tpu_custom_call" | custom-call | flops 6442450944 | bytes 20971520 | tf_op jit(solution)/shard_map/feed_down/pallas_call | solution.py:585
  284.3 1.9 collective-permute-done.32.before
  286.3 4.2 collective-permute-done.33.after
  301.9 1.6 copy-done.9
  308.3 35.8 %attention_backward.1 = (bf16[2,768,1536]{2,1,0:T(8,128)(2,1)}, f32[768,1024]{1,0:T(8,128)S(1)}) custom-call(bf16[3,128,1024]{2,1,0:T(8,128)(2,1)S(1)} %copy-done.45, bf16[3,256,1024]{2,1,0:T(8,128)(2,1)S(1)} %bitcast.228, bf16[3,128,1024]{2,1,0:T(8,128)(2,1)S(1)} %copy-done.47, bf16[512,2048]{1,0:T(8,128)(2,1)} %constant_dynamic-update-slice_fusion.5.top_a, ...), custom_call_target="tpu_custom_call" | custom-call | flops 14495514624 | bytes 36700160 | tf_op jit(solution)/shard_map/attention_backward/pallas_call | solution.py:744
  345.4 1.7 fusion.26
  347.5 2.6 bitcast_add_fusion
  354.2 2.6 convolution_convert_fusion.1
  357.0 2.6 convolution_convert_fusion
  363.7 3.9 convolution_add_fusion.1
  369.6 3.7 convolution_add_fusion
  377.7 5.6 %leave.1 = (f32[768,1024]{1,0:T(8,128)}, f32[16,1024]{1,0:T(8,128)S(1)}) custom-call(s32[8]{0:T(128)S(1)} %broadcast_xor_fusion.table_ref, f32[768,1024]{1,0:T(8,128)S(1)} %copy-done.7, f32[768,1024]{1,0:T(8,128)S(1)} %copy-done.5, f32[768,1024]{1,0:T(8,128)S(1)} %get-tuple-element.106.grad_resid, f32[4,1024]{1,0:T(4,128)S(1)} %convert_bitcast_fusion.small), custom_call_target="tpu_custom_call" | custom-call | flops 23592960 | bytes 12582912 | tf_op jit(solution)/shard_map/leave/pallas_call | solution.py:797
  383.4 1.6 fusion.36
  387.2 8.4 %collective-permute-done.50 = bf16[256,1536]{1,0:T(8,128)(2,1)} collective-permute-done((bf16[256,1536]{1,0:T(8,128)(2,1)}, bf16[256,1536]{1,0:T(8,128)(2,1)}, u32[]{:S(2)}, u32[]{:S(2)}) %collective-permute-start.50) | collective-permute-done | bytes 786464 | tf_op jit(solution)/shard_map/ppermute | solution.py:29
  395.6 1.6 bitcast_add_fusion.2
  401.9 2.8 collective-permute-start.48
  406.6 1.8 collective-permute-done.55
  410.5 1.5 collective-permute-done.56
  412.0 10.0 %collective-permute-done.47 = bf16[128,1024]{1,0:T(8,128)(2,1)S(1)} collective-permute-done((bf16[128,1024]{1,0:T(8,128)(2,1)S(1)}, bf16[128,1024]{1,0:T(8,128)(2,1)S(1)}, u32[]{:S(2)}, u32[]{:S(2)}) %collective-permute-start.47) | collective-permute-done | bytes 262176 | tf_op jit(solution)/shard_map/ppermute | solution.py:29
  423.7 5.1 %collective-permute-start.58 = (f32[128,4]{0,1:T(4,128)S(1)}, f32[128,4]{0,1:T(4,128)S(1)}, u32[]{:S(2)}, u32[]{:S(2)}) collective-permute-start(f32[128,4]{0,1:T(4,128)S(1)} %add.190), channel_id=1, source_target_pairs={{0,2},{1,3},{2,0},{3,1},{4,6},{5,7},{6,4},{7,5},{8,10},{9,11},{10,... | collective-permute-start | bytes 6152 | tf_op jit(solution)/shard_map/ppermute | solution.py:939
  429.0 1.8 collective-permute-start.49
  430.8 3.2 collective-permute-done.51
  434.2 5.2 %collective-permute-start.52 = (bf16[128,1024]{1,0:T(8,128)(2,1)S(1)}, bf16[128,1024]{1,0:T(8,128)(2,1)S(1)}, u32[]{:S(2)}, u32[]{:S(2)}) collective-permute-start(bf16[128,1024]{1,0:T(8,128)(2,1)S(1)} %pad_maximum_fusion.24), channel_id=1, source_target_pairs={{0,2},{1,3},{2,0},{3,1},{4,6},{5,7},{6,4},{7,5},{8,10},{9,11},{10,... | collective-permute-start | bytes 786440 | tf_op jit(solution)/shard_map/ppermute | solution.py:29
  439.4 3.4 collective-permute-start.53
  443.4 8.8 %collective-permute-done.52 = bf16[128,1024]{1,0:T(8,128)(2,1)S(1)} collective-permute-done((bf16[128,1024]{1,0:T(8,128)(2,1)S(1)}, bf16[128,1024]{1,0:T(8,128)(2,1)S(1)}, u32[]{:S(2)}, u32[]{:S(2)}) %collective-permute-start.52) | collective-permute-done | bytes 262176 | tf_op jit(solution)/shard_map/ppermute | solution.py:29
  (394 shorter events, 105.5 us)
Async XLA Ops:
  7.2 95.8 %all-gather.5.cloned.1.call-start = ((), (), s32[]{:S(2)}) async-start(), calls=%async_computation.2 | async-start | bytes 1310720 | tf_op jit(solution)/shard_map/all_gather | solution.py:835
  7.9 99.4 %all-gather.7.cloned.1.call-start = ((), (), s32[]{:S(2)}) async-start(), calls=%async_computation.3 | async-start | bytes 1310720 | tf_op jit(solution)/shard_map/all_gather | solution.py:835
  9.9 18.5 %collective-permute-start.10 = (bf16[128,1024]{1,0:T(8,128)(2,1)S(1)}, bf16[128,1024]{1,0:T(8,128)(2,1)}, u32[]{:S(2)}, u32[]{:S(2)}) collective-permute-start(bf16[128,1024]{1,0:T(8,128)(2,1)S(1)} %pad_maximum_fusion.22), channel_id=1, source_target_pairs={{0,1},{1,2},{2,3},{3,0},{4,5},{5,6},{6,7},{7,4},{8,9},{9,10},{10,1... | collective-permute-start | bytes 786440 | tf_op jit(solution)/shard_map/ppermute | solution.py:29
  13.0 30.3 %collective-permute-start.9 = (bf16[128,1024]{1,0:T(8,128)(2,1)S(1)}, bf16[128,1024]{1,0:T(8,128)(2,1)}, u32[]{:S(2)}, u32[]{:S(2)}) collective-permute-start(bf16[128,1024]{1,0:T(8,128)(2,1)S(1)} %pad_maximum_fusion.22), channel_id=1, source_target_pairs={{0,2},{1,3},{2,0},{3,1},{4,6},{5,7},{6,4},{7,5},{8,10},{9,11},{10,... | collective-permute-start | bytes 786440 | tf_op jit(solution)/shard_map/ppermute | solution.py:29
  15.6 38.6 %collective-permute-start.5 = (bf16[128,1024]{1,0:T(8,128)(2,1)S(1)}, bf16[128,1024]{1,0:T(8,128)(2,1)}, u32[]{:S(2)}, u32[]{:S(2)}) collective-permute-start(bf16[128,1024]{1,0:T(8,128)(2,1)S(1)} %pad_maximum_fusion.22), channel_id=1, source_target_pairs={{0,3},{1,0},{2,1},{3,2},{4,7},{5,4},{6,5},{7,6},{8,11},{9,8},{10,9... | collective-permute-start | bytes 786440 | tf_op jit(solution)/shard_map/ppermute | solution.py:29
  17.6 6.0 %collective-permute-start = (bf16[128,4]{0,1:T(4,128)(2,1)S(1)}, bf16[128,4]{0,1:T(4,128)(2,1)S(1)}, u32[]{:S(2)}, u32[]{:S(2)}) collective-permute-start(bf16[128,4]{0,1:T(4,128)(2,1)S(1)} %maximum_bitcast_fusion), channel_id=1, source_target_pairs={{0,8},{4,12},{8,0},{12,4},{16,24},{20,28},{24,16},{28,20},{1,9},{5... | collective-permute-start | bytes 3080 | tf_op jit(solution)/shard_map/ppermute | solution.py:29
  19.1 434.7 %reduce-scatter.2.cloned.1.call-start = ((), (), s32[]{:S(2)}) async-start(), calls=%async_computation.1 | async-start | bytes 2621440 | tf_op jit(solution)/shard_map/reduce_scatter | solution.py:240
  23.6 3.7 collective-permute-start.1
  27.3 1.2 collective-permute-start.2
  44.4 26.9 %collective-permute-start.11 = (bf16[128,2048]{1,0:T(8,128)(2,1)S(1)}, bf16[128,2048]{1,0:T(8,128)(2,1)S(1)}, u32[]{:S(2)}, u32[]{:S(2)}) collective-permute-start(bf16[128,2048]{1,0:T(8,128)(2,1)S(1)} %pad_maximum_fusion.16), channel_id=1, source_target_pairs={{0,16},{4,20},{8,24},{12,28},{16,0},{20,4},{24,8},{28,12},{1,17},{... | collective-permute-start | bytes 1572872 | tf_op jit(solution)/shard_map/ppermute | solution.py:29
  56.4 17.5 %collective-permute-start.6 = (bf16[128,2048]{1,0:T(8,128)(2,1)}, bf16[128,2048]{1,0:T(8,128)(2,1)S(1)}, u32[]{:S(2)}, u32[]{:S(2)}) collective-permute-start(bf16[128,2048]{1,0:T(8,128)(2,1)} %constant_dynamic-update-slice_fusion), channel_id=1, source_target_pairs={{0,8},{4,12},{8,0},{12,4},{16,24},{20,28},{24,16},{28,20},{1,9},{5... | collective-permute-start | bytes 1572872 | tf_op jit(solution)/shard_map/ppermute | solution.py:29
  59.4 38.7 %collective-permute-start.3 = (bf16[3,128,1024]{2,1,0:T(8,128)(2,1)S(1)}, bf16[3,128,1024]{2,1,0:T(8,128)(2,1)S(1)}, u32[]{:S(2)}, u32[]{:S(2)}) collective-permute-start(bf16[3,128,1024]{2,1,0:T(8,128)(2,1)S(1)} %get-tuple-element.124), channel_id=1, source_target_pairs={{0,1},{1,2},{2,3},{4,5},{5,6},{6,7},{8,9},{9,10},{10,11},{12,13},{... | collective-permute-start | bytes 2359304 | tf_op jit(solution)/shard_map/ppermute | solution.py:29
  70.0 30.2 %collective-permute-start.4 = (bf16[3,128,1024]{2,1,0:T(8,128)(2,1)S(1)}, bf16[3,128,1024]{2,1,0:T(8,128)(2,1)S(1)}, u32[]{:S(2)}, u32[]{:S(2)}) collective-permute-start(bf16[3,128,1024]{2,1,0:T(8,128)(2,1)S(1)} %get-tuple-element.123), channel_id=1, source_target_pairs={{1,0},{2,1},{3,2},{5,4},{6,5},{7,6},{9,8},{10,9},{11,10},{13,12},{... | collective-permute-start | bytes 2359304 | tf_op jit(solution)/shard_map/ppermute | solution.py:29
  71.5 28.8 %collective-permute-start.12 = (bf16[256,2048]{1,0:T(8,128)(2,1)S(1)}, bf16[256,2048]{1,0:T(8,128)(2,1)S(1)}, u32[]{:S(2)}, u32[]{:S(2)}) collective-permute-start(bf16[256,2048]{1,0:T(8,128)(2,1)S(1)} %pad_maximum_fusion.9), channel_id=1, source_target_pairs={{0,8},{4,12},{8,0},{12,4},{16,24},{20,28},{24,16},{28,20},{1,9},{5... | collective-permute-start | bytes 3145736 | tf_op jit(solution)/shard_map/ppermute | solution.py:29
  75.2 26.2 %collective-permute-start.7 = (bf16[256,2048]{1,0:T(8,128)(2,1)S(1)}, bf16[256,2048]{1,0:T(8,128)(2,1)S(1)}, u32[]{:S(2)}, u32[]{:S(2)}) collective-permute-start(bf16[256,2048]{1,0:T(8,128)(2,1)S(1)} %pad_maximum_fusion.8), channel_id=1, source_target_pairs={{0,16},{4,20},{8,24},{12,28},{16,0},{20,4},{24,8},{28,12},{1,17},{... | collective-permute-start | bytes 3145736 | tf_op jit(solution)/shard_map/ppermute | solution.py:29
  101.3 25.1 %collective-permute-start.13 = (bf16[512,2048]{1,0:T(8,128)(2,1)S(1)}, bf16[512,2048]{1,0:T(8,128)(2,1)}, u32[]{:S(2)}, u32[]{:S(2)}) collective-permute-start(bf16[512,2048]{1,0:T(8,128)(2,1)S(1)} %pad_maximum_fusion.top_b), channel_id=1, source_target_pairs={{0,4},{4,0},{8,12},{12,8},{16,20},{20,16},{24,28},{28,24},{1,5},{5... | collective-permute-start | bytes 6291464 | tf_op jit(solution)/shard_map/ppermute | solution.py:29
  102.6 24.4 %collective-permute-start.8 = (bf16[512,2048]{1,0:T(8,128)(2,1)}, bf16[512,2048]{1,0:T(8,128)(2,1)}, u32[]{:S(2)}, u32[]{:S(2)}) collective-permute-start(bf16[512,2048]{1,0:T(8,128)(2,1)} %constant_dynamic-update-slice_fusion.5.top_a), channel_id=1, source_target_pairs={{0,4},{4,0},{8,12},{12,8},{16,20},{20,16},{24,28},{28,24},{1,5},{5... | collective-permute-start | bytes 6291464 | tf_op jit(solution)/shard_map/ppermute | solution.py:29
  104.3 14.9 %collective-permute-start.14 = (bf16[128,2048]{1,0:T(8,128)(2,1)S(1)}, bf16[128,2048]{1,0:T(8,128)(2,1)}, u32[]{:S(2)}, u32[]{:S(2)}) collective-permute-start(bf16[128,2048]{1,0:T(8,128)(2,1)S(1)} %get-tuple-element.69), channel_id=1, source_target_pairs={{0,8},{4,12},{8,0},{12,4},{16,24},{20,28},{24,16},{28,20},{1,9},{5... | collective-permute-start | bytes 1572872 | tf_op jit(solution)/shard_map/ppermute | solution.py:29
  105.8 14.9 %collective-permute-start.15 = (bf16[128,2048]{1,0:T(8,128)(2,1)S(1)}, bf16[128,2048]{1,0:T(8,128)(2,1)}, u32[]{:S(2)}, u32[]{:S(2)}) collective-permute-start(bf16[128,2048]{1,0:T(8,128)(2,1)S(1)} %get-tuple-element.70), channel_id=1, source_target_pairs={{0,16},{4,20},{8,24},{12,28},{16,0},{20,4},{24,8},{28,12},{1,17},{... | collective-permute-start | bytes 1572872 | tf_op jit(solution)/shard_map/ppermute | solution.py:29
  109.5 55.0 %collective-permute-start.16 = (bf16[128,2048]{1,0:T(8,128)(2,1)}, bf16[128,2048]{1,0:T(8,128)(2,1)}, u32[]{:S(2)}, u32[]{:S(2)}) collective-permute-start(bf16[128,2048]{1,0:T(8,128)(2,1)} %pad_maximum_fusion.19), channel_id=1, source_target_pairs={{0,8},{4,12},{8,0},{12,4},{16,24},{20,28},{24,16},{28,20},{1,9},{5... | collective-permute-start | bytes 1572872 | tf_op jit(solution)/shard_map/ppermute | solution.py:29
  119.2 45.3 %collective-permute-start.17 = (bf16[128,2048]{1,0:T(8,128)(2,1)}, bf16[128,2048]{1,0:T(8,128)(2,1)}, u32[]{:S(2)}, u32[]{:S(2)}) collective-permute-start(bf16[128,2048]{1,0:T(8,128)(2,1)} %pad_maximum_fusion.20), channel_id=1, source_target_pairs={{0,16},{4,20},{8,24},{12,28},{16,0},{20,4},{24,8},{28,12},{1,17},{... | collective-permute-start | bytes 1572872 | tf_op jit(solution)/shard_map/ppermute | solution.py:29
  122.5 42.0 %collective-permute-start.20 = (bf16[256,2048]{1,0:T(8,128)(2,1)S(1)}, bf16[256,2048]{1,0:T(8,128)(2,1)S(1)}, u32[]{:S(2)}, u32[]{:S(2)}) collective-permute-start(bf16[256,2048]{1,0:T(8,128)(2,1)S(1)} %pad_maximum_fusion.11), channel_id=1, source_target_pairs={{0,8},{4,12},{8,0},{12,4},{16,24},{20,28},{24,16},{28,20},{1,9},{5... | collective-permute-start | bytes 3145736 | tf_op jit(solution)/shard_map/ppermute | solution.py:29
  126.4 41.1 %collective-permute-start.18 = (bf16[256,2048]{1,0:T(8,128)(2,1)S(1)}, bf16[256,2048]{1,0:T(8,128)(2,1)S(1)}, u32[]{:S(2)}, u32[]{:S(2)}) collective-permute-start(bf16[256,2048]{1,0:T(8,128)(2,1)S(1)} %pad_maximum_fusion.10), channel_id=1, source_target_pairs={{0,16},{4,20},{8,24},{12,28},{16,0},{20,4},{24,8},{28,12},{1,17},{... | collective-permute-start | bytes 3145736 | tf_op jit(solution)/shard_map/ppermute | solution.py:29
  164.5 63.3 %copy-start.18 = (bf16[768,1024]{1,0:T(8,128)(2,1)}, bf16[768,1024]{1,0:T(8,128)(2,1)S(1)}, u32[]{:S(2)}) copy-start(bf16[768,1024]{1,0:T(8,128)(2,1)S(1)} %get-tuple-element.87.inputs) | copy-start | bytes 4718596
  167.4 6.6 %collective-permute-start.21 = (bf16[512,2048]{1,0:T(8,128)(2,1)S(1)}, bf16[512,2048]{1,0:T(8,128)(2,1)S(1)}, u32[]{:S(2)}, u32[]{:S(2)}) collective-permute-start(bf16[512,2048]{1,0:T(8,128)(2,1)S(1)} %pad_maximum_fusion.1.top_b), channel_id=1, source_target_pairs={{0,4},{4,0},{8,12},{12,8},{16,20},{20,16},{24,28},{28,24},{1,5},{5... | collective-permute-start | bytes 6291464 | tf_op jit(solution)/shard_map/ppermute | solution.py:29
  167.6 7.0 %collective-permute-start.19 = (bf16[512,2048]{1,0:T(8,128)(2,1)S(1)}, bf16[512,2048]{1,0:T(8,128)(2,1)S(1)}, u32[]{:S(2)}, u32[]{:S(2)}) collective-permute-start(bf16[512,2048]{1,0:T(8,128)(2,1)S(1)} %constant_dynamic-update-slice_fusion.8.top_a), channel_id=1, source_target_pairs={{0,4},{4,0},{8,12},{12,8},{16,20},{20,16},{24,28},{28,24},{1,5},{5... | collective-permute-start | bytes 6291464 | tf_op jit(solution)/shard_map/ppermute | solution.py:29
  170.3 24.6 %collective-permute-start.23 = (bf16[256,2048]{1,0:T(8,128)(2,1)S(1)}, bf16[256,2048]{1,0:T(8,128)(2,1)S(1)}, u32[]{:S(2)}, u32[]{:S(2)}) collective-permute-start(bf16[256,2048]{1,0:T(8,128)(2,1)S(1)} %pad_maximum_fusion.13), channel_id=1, source_target_pairs={{0,8},{4,12},{8,0},{12,4},{16,24},{20,28},{24,16},{28,20},{1,9},{5... | collective-permute-start | bytes 3145736 | tf_op jit(solution)/shard_map/ppermute | solution.py:29
  172.4 27.1 %collective-permute-start.22 = (bf16[256,2048]{1,0:T(8,128)(2,1)S(1)}, bf16[256,2048]{1,0:T(8,128)(2,1)S(1)}, u32[]{:S(2)}, u32[]{:S(2)}) collective-permute-start(bf16[256,2048]{1,0:T(8,128)(2,1)S(1)} %pad_maximum_fusion.12), channel_id=1, source_target_pairs={{0,16},{4,20},{8,24},{12,28},{16,0},{20,4},{24,8},{28,12},{1,17},{... | collective-permute-start | bytes 3145736 | tf_op jit(solution)/shard_map/ppermute | solution.py:29
  199.5 8.0 %collective-permute-start.26 = (bf16[512,2048]{1,0:T(8,128)(2,1)S(1)}, bf16[512,2048]{1,0:T(8,128)(2,1)S(1)}, u32[]{:S(2)}, u32[]{:S(2)}) collective-permute-start(bf16[512,2048]{1,0:T(8,128)(2,1)S(1)} %pad_maximum_fusion.3.top_b), channel_id=1, source_target_pairs={{0,4},{4,0},{8,12},{12,8},{16,20},{20,16},{24,28},{28,24},{1,5},{5... | collective-permute-start | bytes 6291464 | tf_op jit(solution)/shard_map/ppermute | solution.py:29
  201.7 5.7 %collective-permute-start.25 = (bf16[512,2048]{1,0:T(8,128)(2,1)S(1)}, bf16[512,2048]{1,0:T(8,128)(2,1)S(1)}, u32[]{:S(2)}, u32[]{:S(2)}) collective-permute-start(bf16[512,2048]{1,0:T(8,128)(2,1)S(1)} %pad_maximum_fusion.2.top_a), channel_id=1, source_target_pairs={{0,4},{4,0},{8,12},{12,8},{16,20},{20,16},{24,28},{28,24},{1,5},{5... | collective-permute-start | bytes 6291464 | tf_op jit(solution)/shard_map/ppermute | solution.py:29
  205.0 12.5 %collective-permute-start.28 = (bf16[512,2048]{1,0:T(8,128)(2,1)}, bf16[512,2048]{1,0:T(8,128)(2,1)S(1)}, u32[]{:S(2)}, u32[]{:S(2)}) collective-permute-start(bf16[512,2048]{1,0:T(8,128)(2,1)} %fusion.15), channel_id=1, source_target_pairs={{0,4},{4,0},{8,12},{12,8},{16,20},{20,16},{24,28},{28,24},{1,5},{5... | collective-permute-start | bytes 6291464 | tf_op jit(solution)/shard_map/ppermute | solution.py:29
  207.4 13.5 %collective-permute-start.24 = (bf16[512,2048]{1,0:T(8,128)(2,1)S(1)}, bf16[512,2048]{1,0:T(8,128)(2,1)S(1)}, u32[]{:S(2)}, u32[]{:S(2)}) collective-permute-start(bf16[512,2048]{1,0:T(8,128)(2,1)S(1)} %fusion.12), channel_id=1, source_target_pairs={{0,4},{4,0},{8,12},{12,8},{16,20},{20,16},{24,28},{28,24},{1,5},{5... | collective-permute-start | bytes 6291464 | tf_op jit(solution)/shard_map/ppermute | solution.py:29
  227.3 8.0 %collective-permute-start.30 = (bf16[512,2048]{1,0:T(8,128)(2,1)}, bf16[512,2048]{1,0:T(8,128)(2,1)}, u32[]{:S(2)}, u32[]{:S(2)}) collective-permute-start(bf16[512,2048]{1,0:T(8,128)(2,1)} %convolution_convert_fusion.2), channel_id=1, source_target_pairs={{0,4},{4,0},{8,12},{12,8},{16,20},{20,16},{24,28},{28,24},{1,5},{5... | collective-permute-start | bytes 6291464 | tf_op jit(solution)/shard_map/ppermute | solution.py:29
  231.1 10.5 %collective-permute-start.29 = (bf16[512,2048]{1,0:T(8,128)(2,1)}, bf16[512,2048]{1,0:T(8,128)(2,1)S(1)}, u32[]{:S(2)}, u32[]{:S(2)}) collective-permute-start(bf16[512,2048]{1,0:T(8,128)(2,1)} %convolution_convert_fusion.3), channel_id=1, source_target_pairs={{0,4},{4,0},{8,12},{12,8},{16,20},{20,16},{24,28},{28,24},{1,5},{5... | collective-permute-start | bytes 6291464 | tf_op jit(solution)/shard_map/ppermute | solution.py:29
  231.1 30.7 %collective-permute-start.31 = (bf16[256,2048]{1,0:T(8,128)(2,1)}, bf16[256,2048]{1,0:T(8,128)(2,1)S(1)}, u32[]{:S(2)}, u32[]{:S(2)}) collective-permute-start(bf16[256,2048]{1,0:T(8,128)(2,1)} %bitcast.15), channel_id=1, source_target_pairs={{0,8},{4,12},{8,0},{12,4},{16,24},{20,28},{24,16},{28,20},{1,9},{5... | collective-permute-start | bytes 3145736 | tf_op jit(solution)/shard_map/ppermute | solution.py:29
  233.8 29.8 %collective-permute-start.27 = (bf16[256,2048]{1,0:T(8,128)(2,1)}, bf16[256,2048]{1,0:T(8,128)(2,1)S(1)}, u32[]{:S(2)}, u32[]{:S(2)}) collective-permute-start(bf16[256,2048]{1,0:T(8,128)(2,1)} %fusion.33), channel_id=1, source_target_pairs={{0,16},{4,20},{8,24},{12,28},{16,0},{20,4},{24,8},{28,12},{1,17},{... | collective-permute-start | bytes 3145736 | tf_op jit(solution)/shard_map/ppermute | solution.py:29
  243.5 40.7 %copy-start.52 = (f32[512,2048]{1,0:T(8,128)}, f32[512,2048]{1,0:T(8,128)S(1)}, u32[]{:S(2)}) copy-start(f32[512,2048]{1,0:T(8,128)S(1)} %convert_add_fusion.1) | copy-start | bytes 12582916
  264.1 20.2 %collective-permute-start.36 = (bf16[128,2048]{1,0:T(8,128)(2,1)S(1)}, bf16[128,2048]{1,0:T(8,128)(2,1)S(1)}, u32[]{:S(2)}, u32[]{:S(2)}) collective-permute-start(bf16[128,2048]{1,0:T(8,128)(2,1)S(1)} %fusion.67), channel_id=1, source_target_pairs={{0,8},{4,12},{8,0},{12,4},{16,24},{20,28},{24,16},{28,20},{1,9},{5... | collective-permute-start | bytes 1572872 | tf_op jit(solution)/shard_map/ppermute | solution.py:29
  265.3 28.1 %collective-permute-start.37 = (bf16[128,2048]{1,0:T(8,128)(2,1)S(1)}, bf16[128,2048]{1,0:T(8,128)(2,1)S(1)}, u32[]{:S(2)}, u32[]{:S(2)}) collective-permute-start(bf16[128,2048]{1,0:T(8,128)(2,1)S(1)} %fusion.68), channel_id=1, source_target_pairs={{0,16},{4,20},{8,24},{12,28},{16,0},{20,4},{24,8},{28,12},{1,17},{... | collective-permute-start | bytes 1572872 | tf_op jit(solution)/shard_map/ppermute | solution.py:29
  266.0 20.2 %collective-permute-start.32 = (bf16[3,128,1024]{2,1,0:T(8,128)(2,1)S(1)}, bf16[3,128,1024]{2,1,0:T(8,128)(2,1)S(1)}, u32[]{:S(2)}, u32[]{:S(2)}) collective-permute-start(bf16[3,128,1024]{2,1,0:T(8,128)(2,1)S(1)} %get-tuple-element.122), channel_id=1, source_target_pairs={{0,1},{1,2},{2,3},{4,5},{5,6},{6,7},{8,9},{9,10},{10,11},{12,13},{... | collective-permute-start | bytes 2359304 | tf_op jit(solution)/shard_map/ppermute | solution.py:29
  269.9 20.6 %collective-permute-start.33 = (bf16[3,128,1024]{2,1,0:T(8,128)(2,1)S(1)}, bf16[3,128,1024]{2,1,0:T(8,128)(2,1)S(1)}, u32[]{:S(2)}, u32[]{:S(2)}) collective-permute-start(bf16[3,128,1024]{2,1,0:T(8,128)(2,1)S(1)} %get-tuple-element.121), channel_id=1, source_target_pairs={{1,0},{2,1},{3,2},{5,4},{6,5},{7,6},{9,8},{10,9},{11,10},{13,12},{... | collective-permute-start | bytes 2359304 | tf_op jit(solution)/shard_map/ppermute | solution.py:29
  291.1 2.4 collective-permute-start.35
  291.8 2.4 collective-permute-start.34
  297.2 50.0 %collective-permute-start.39 = (bf16[256,2560]{1,0:T(8,128)(2,1)}, bf16[256,2560]{1,0:T(8,128)(2,1)}, u32[]{:S(2)}, u32[]{:S(2)}) collective-permute-start(bf16[256,2560]{1,0:T(8,128)(2,1)} %pad_maximum_fusion.7), channel_id=1, source_target_pairs={{0,8},{4,12},{8,0},{12,4},{16,24},{20,28},{24,16},{28,20},{1,9},{5... | collective-permute-start | bytes 3932168 | tf_op jit(solution)/shard_map/ppermute | solution.py:29
  299.3 44.8 %collective-permute-start.38 = (bf16[256,2560]{1,0:T(8,128)(2,1)}, bf16[256,2560]{1,0:T(8,128)(2,1)}, u32[]{:S(2)}, u32[]{:S(2)}) collective-permute-start(bf16[256,2560]{1,0:T(8,128)(2,1)} %pad_maximum_fusion.6), channel_id=1, source_target_pairs={{0,16},{4,20},{8,24},{12,28},{16,0},{20,4},{24,8},{28,12},{1,17},{... | collective-permute-start | bytes 3932168 | tf_op jit(solution)/shard_map/ppermute | solution.py:29
  356.8 6.9 %collective-permute-start.40 = (bf16[512,1536]{1,0:T(8,128)(2,1)}, bf16[512,1536]{1,0:T(8,128)(2,1)}, u32[]{:S(2)}, u32[]{:S(2)}) collective-permute-start(bf16[512,1536]{1,0:T(8,128)(2,1)} %convolution_convert_fusion.1), channel_id=1, source_target_pairs={{0,4},{4,0},{8,12},{12,8},{16,20},{20,16},{24,28},{28,24},{1,5},{5... | collective-permute-start | bytes 4718600 | tf_op jit(solution)/shard_map/ppermute | solution.py:29
  359.6 10.0 %collective-permute-start.41 = (bf16[512,1536]{1,0:T(8,128)(2,1)}, bf16[512,1536]{1,0:T(8,128)(2,1)}, u32[]{:S(2)}, u32[]{:S(2)}) collective-permute-start(bf16[512,1536]{1,0:T(8,128)(2,1)} %convolution_convert_fusion), channel_id=1, source_target_pairs={{0,4},{4,0},{8,12},{12,8},{16,20},{20,16},{24,28},{28,24},{1,5},{5... | collective-permute-start | bytes 4718600 | tf_op jit(solution)/shard_map/ppermute | solution.py:29
  361.8 21.7 %collective-permute-start.43 = (bf16[128,2560]{1,0:T(8,128)(2,1)}, bf16[128,2560]{1,0:T(8,128)(2,1)}, u32[]{:S(2)}, u32[]{:S(2)}) collective-permute-start(bf16[128,2560]{1,0:T(8,128)(2,1)} %pad_maximum_fusion.14), channel_id=1, source_target_pairs={{0,8},{4,12},{8,0},{12,4},{16,24},{20,28},{24,16},{28,20},{1,9},{5... | collective-permute-start | bytes 1966088 | tf_op jit(solution)/shard_map/ppermute | solution.py:29
  363.0 22.1 %collective-permute-start.44 = (bf16[128,2560]{1,0:T(8,128)(2,1)}, bf16[128,2560]{1,0:T(8,128)(2,1)}, u32[]{:S(2)}, u32[]{:S(2)}) collective-permute-start(bf16[128,2560]{1,0:T(8,128)(2,1)} %pad_maximum_fusion.15), channel_id=1, source_target_pairs={{0,16},{4,20},{8,24},{12,28},{16,0},{20,4},{24,8},{28,12},{1,17},{... | collective-permute-start | bytes 1966088 | tf_op jit(solution)/shard_map/ppermute | solution.py:29
  375.6 20.0 %collective-permute-start.50 = (bf16[256,1536]{1,0:T(8,128)(2,1)}, bf16[256,1536]{1,0:T(8,128)(2,1)}, u32[]{:S(2)}, u32[]{:S(2)}) collective-permute-start(bf16[256,1536]{1,0:T(8,128)(2,1)} %bitcast.54), channel_id=1, source_target_pairs={{0,8},{4,12},{8,0},{12,4},{16,24},{20,28},{24,16},{28,20},{1,9},{5... | collective-permute-start | bytes 2359304 | tf_op jit(solution)/shard_map/ppermute | solution.py:29
  376.4 20.9 %collective-permute-start.42 = (bf16[256,1536]{1,0:T(8,128)(2,1)}, bf16[256,1536]{1,0:T(8,128)(2,1)}, u32[]{:S(2)}, u32[]{:S(2)}) collective-permute-start(bf16[256,1536]{1,0:T(8,128)(2,1)} %fusion.39), channel_id=1, source_target_pairs={{0,16},{4,20},{8,24},{12,28},{16,0},{20,4},{24,8},{28,12},{1,17},{... | collective-permute-start | bytes 2359304 | tf_op jit(solution)/shard_map/ppermute | solution.py:29
  399.2 5.5 %collective-permute-start.54 = (f32[512,4]{0,1:T(4,128)S(1)}, f32[512,4]{0,1:T(4,128)S(1)}, u32[]{:S(2)}, u32[]{:S(2)}) collective-permute-start(f32[512,4]{0,1:T(4,128)S(1)} %slice.459), channel_id=1, source_target_pairs={{0,4},{4,0},{8,12},{12,8},{16,20},{20,16},{24,28},{28,24},{1,5},{5... | collective-permute-start | bytes 24584 | tf_op jit(solution)/shard_map/ppermute | solution.py:29
  400.2 11.9 %collective-permute-start.46 = (bf16[128,1024]{1,0:T(8,128)(2,1)S(1)}, bf16[128,1024]{1,0:T(8,128)(2,1)S(1)}, u32[]{:S(2)}, u32[]{:S(2)}) collective-permute-start(bf16[128,1024]{1,0:T(8,128)(2,1)S(1)} %get-tuple-element.120), channel_id=1, source_target_pairs={{0,1},{1,2},{2,3},{3,0},{4,5},{5,6},{6,7},{7,4},{8,9},{9,10},{10,1... | collective-permute-start | bytes 786440 | tf_op jit(solution)/shard_map/ppermute | solution.py:29
  401.5 20.5 %collective-permute-start.47 = (bf16[128,1024]{1,0:T(8,128)(2,1)S(1)}, bf16[128,1024]{1,0:T(8,128)(2,1)S(1)}, u32[]{:S(2)}, u32[]{:S(2)}) collective-permute-start(bf16[128,1024]{1,0:T(8,128)(2,1)S(1)} %get-tuple-element.119), channel_id=1, source_target_pairs={{0,2},{1,3},{2,0},{3,1},{4,6},{5,7},{6,4},{7,5},{8,10},{9,11},{10,... | collective-permute-start | bytes 786440 | tf_op jit(solution)/shard_map/ppermute | solution.py:29
  401.9 20.2 %collective-permute-start.48 = (bf16[128,1024]{1,0:T(8,128)(2,1)S(1)}, bf16[128,1024]{1,0:T(8,128)(2,1)S(1)}, u32[]{:S(2)}, u32[]{:S(2)}) collective-permute-start(bf16[128,1024]{1,0:T(8,128)(2,1)S(1)} %get-tuple-element.118), channel_id=1, source_target_pairs={{0,3},{1,0},{2,1},{3,2},{4,7},{5,4},{6,5},{7,6},{8,11},{9,8},{10,9... | collective-permute-start | bytes 786440 | tf_op jit(solution)/shard_map/ppermute | solution.py:29
  404.7 3.7 collective-permute-start.55
  408.4 3.6 collective-permute-start.56
  409.6 19.2 %collective-permute-start.45 = (bf16[128,1536]{1,0:T(8,128)(2,1)S(1)}, bf16[128,1536]{1,0:T(8,128)(2,1)S(1)}, u32[]{:S(2)}, u32[]{:S(2)}) collective-permute-start(bf16[128,1536]{1,0:T(8,128)(2,1)S(1)} %fusion.74), channel_id=1, source_target_pairs={{0,8},{4,12},{8,0},{12,4},{16,24},{20,28},{24,16},{28,20},{1,9},{5... | collective-permute-start | bytes 1179656 | tf_op jit(solution)/shard_map/ppermute | solution.py:29
  412.0 11.7 %collective-permute-start.57 = (f32[128,4]{0,1:T(4,128)S(1)}, f32[128,4]{0,1:T(4,128)S(1)}, u32[]{:S(2)}, u32[]{:S(2)}) collective-permute-start(f32[128,4]{0,1:T(4,128)S(1)} %slice_add_fusion.4), channel_id=1, source_target_pairs={{0,1},{1,0},{2,3},{3,2},{4,5},{5,4},{6,7},{7,6},{8,9},{9,8},{10,11... | collective-permute-start | bytes 6152 | tf_op jit(solution)/shard_map/ppermute | solution.py:939
  423.0 11.0 %collective-permute-start.51 = (bf16[128,1536]{1,0:T(8,128)(2,1)S(1)}, bf16[128,1536]{1,0:T(8,128)(2,1)S(1)}, u32[]{:S(2)}, u32[]{:S(2)}) collective-permute-start(bf16[128,1536]{1,0:T(8,128)(2,1)S(1)} %fusion.75), channel_id=1, source_target_pairs={{0,16},{4,20},{8,24},{12,28},{16,0},{20,4},{24,8},{28,12},{1,17},{... | collective-permute-start | bytes 1179656 | tf_op jit(solution)/shard_map/ppermute | solution.py:29
  423.7 19.1 %collective-permute-start.58 = (f32[128,4]{0,1:T(4,128)S(1)}, f32[128,4]{0,1:T(4,128)S(1)}, u32[]{:S(2)}, u32[]{:S(2)}) collective-permute-start(f32[128,4]{0,1:T(4,128)S(1)} %add.190), channel_id=1, source_target_pairs={{0,2},{1,3},{2,0},{3,1},{4,6},{5,7},{6,4},{7,5},{8,10},{9,11},{10,... | collective-permute-start | bytes 6152 | tf_op jit(solution)/shard_map/ppermute | solution.py:939
  429.0 14.5 %collective-permute-start.49 = (bf16[128,1024]{1,0:T(8,128)(2,1)S(1)}, bf16[128,1024]{1,0:T(8,128)(2,1)S(1)}, u32[]{:S(2)}, u32[]{:S(2)}) collective-permute-start(bf16[128,1024]{1,0:T(8,128)(2,1)S(1)} %pad_maximum_fusion.23), channel_id=1, source_target_pairs={{0,1},{1,2},{2,3},{3,0},{4,5},{5,6},{6,7},{7,4},{8,9},{9,10},{10,1... | collective-permute-start | bytes 786440 | tf_op jit(solution)/shard_map/ppermute | solution.py:29
  434.2 18.1 %collective-permute-start.52 = (bf16[128,1024]{1,0:T(8,128)(2,1)S(1)}, bf16[128,1024]{1,0:T(8,128)(2,1)S(1)}, u32[]{:S(2)}, u32[]{:S(2)}) collective-permute-start(bf16[128,1024]{1,0:T(8,128)(2,1)S(1)} %pad_maximum_fusion.24), channel_id=1, source_target_pairs={{0,2},{1,3},{2,0},{3,1},{4,6},{5,7},{6,4},{7,5},{8,10},{9,11},{10,... | collective-permute-start | bytes 786440 | tf_op jit(solution)/shard_map/ppermute | solution.py:29
  439.4 12.8 %collective-permute-start.53 = (bf16[128,1024]{1,0:T(8,128)(2,1)S(1)}, bf16[128,1024]{1,0:T(8,128)(2,1)S(1)}, u32[]{:S(2)}, u32[]{:S(2)}) collective-permute-start(bf16[128,1024]{1,0:T(8,128)(2,1)S(1)} %pad_maximum_fusion.25), channel_id=1, source_target_pairs={{0,3},{1,0},{2,1},{3,2},{4,7},{5,4},{6,5},{7,6},{8,11},{9,8},{10,9... | collective-permute-start | bytes 786440 | tf_op jit(solution)/shard_map/ppermute | solution.py:29
  (92 other events, 731.8 us)
Sparse Core Ops, SparseCore 0:
  9.6 43.5 all-gather.4
  54.7 40.4 all-gather.6
  361.9 41.9 reduce-scatter.1
